TPU v7x, 32 devices: a whole 2x2x4 slice. The times are simulated.
32 devices in a mesh: dp: 4 (over y, x), fsdp: 8 (over z, core).
Axes of the slice: x: 2, y: 2, z: 4, core: 2. Of those that a mesh axis runs over, the one named last changes fastest.
Arguments:
- tokens: bfloat16 [8, 2048, 1792], P('dp', 'fsdp'), may hold values from -6 to 6
- cotangent: bfloat16 [8, 2048, 1792], P('dp', 'fsdp'), may hold values from -6 to 6
- lengths: int32 [8], P('dp'), may hold values from 1024 to 2048, as said below
- w_qk: float32 [1792, 512], P(('dp', 'fsdp')), may hold values from -0.125 to 0.125
- w_value: float32 [1792, 1792], P(('dp', 'fsdp')), may hold values from -0.125 to 0.125
- w_out: float32 [1792, 1792], P(('dp', 'fsdp')), may hold values from -1.5 to 1.5
- w_gu: float32 [1792, 9728], P(('dp', 'fsdp')), may hold values from -0.125 to 0.125
- w_down: float32 [1792, 4864], P(('dp', 'fsdp')), may hold values from -0.21875 to 0.21875
- small_params: float32 [1792, 5], P(('dp', 'fsdp')), may hold values from 0.5 to 1.5
- m_qk: float32 [1792, 512], P(('dp', 'fsdp')), may hold values from -28672 to 28672
- m_value: float32 [1792, 1792], P(('dp', 'fsdp')), may hold values from -14336 to 14336
- m_out: float32 [1792, 1792], P(('dp', 'fsdp')), may hold values from -1280 to 1280
- m_gu: float32 [1792, 9728], P(('dp', 'fsdp')), may hold values from -5120 to 5120
- m_down: float32 [1792, 4864], P(('dp', 'fsdp')), may hold values from -3584 to 3584
- m_small: float32 [1792, 5], P(('dp', 'fsdp')), may hold values from -19941.367 to 19941.367
- v_qk: float32 [1792, 512], P(('dp', 'fsdp')), may hold values from 12939.913 to 51759.652
- v_value: float32 [1792, 1792], P(('dp', 'fsdp')), may hold values from 3533.0715 to 14129.249
- v_out: float32 [1792, 1792], P(('dp', 'fsdp')), may hold values from 26.888407 to 107.54147
- v_gu: float32 [1792, 9728], P(('dp', 'fsdp')), may hold values from 448.69705 to 1795.236
- v_down: float32 [1792, 4864], P(('dp', 'fsdp')), may hold values from 233.0624 to 932.2496
- v_small: float32 [1792, 5], P(('dp', 'fsdp')), may hold values from 1163.5137 to 28711.144
Outputs:
- layer_out: bfloat16 [8, 2048, 1792], P('dp', 'fsdp')
- input_grad: float32 [8, 2048, 1792], P('dp', 'fsdp')
- grad_qk: float32 [1792, 512], P(('dp', 'fsdp'))
- grad_value: float32 [1792, 1792], P(('dp', 'fsdp'))
- grad_out: float32 [1792, 1792], P(('dp', 'fsdp'))
- grad_gu: float32 [1792, 9728], P(('dp', 'fsdp'))
- grad_down: float32 [1792, 4864], P(('dp', 'fsdp'))
- grad_small: float32 [1792, 5], P(('dp', 'fsdp'))
- new_qk: float32 [1792, 512], P(('dp', 'fsdp'))
- new_value: float32 [1792, 1792], P(('dp', 'fsdp'))
- new_out: float32 [1792, 1792], P(('dp', 'fsdp'))
- new_gu: float32 [1792, 9728], P(('dp', 'fsdp'))
- new_down: float32 [1792, 4864], P(('dp', 'fsdp'))
- new_small: float32 [1792, 5], P(('dp', 'fsdp'))
- moment_qk: float32 [1792, 512], P(('dp', 'fsdp'))
- moment_value: float32 [1792, 1792], P(('dp', 'fsdp'))
- moment_out: float32 [1792, 1792], P(('dp', 'fsdp'))
- moment_gu: float32 [1792, 9728], P(('dp', 'fsdp'))
- moment_down: float32 [1792, 4864], P(('dp', 'fsdp'))
- moment_small: float32 [1792, 5], P(('dp', 'fsdp'))
Inputs may be any that keep to these rules, and one draw needn't show every extreme that they name: `lengths`: each slot holds one sequence from its first position; positions at or past its length are padding. Some slot has length 2048 and some 2048 // 2.
All inputs are finite; a program needn't handle non-finite values.
Results may differ from a plain program's by a relative error of at most 0.015.
The roundings to bfloat16 on the way count: a program that leaves them out, or rounds other values in their place, can miss the bound.
Values may be sent and summed in bfloat16 or wider, within the bound.
A program may use at most 576 MiB of HBM per device.

v0:
```python
import math

import jax
import jax.numpy as jnp
from jax import lax
from jax.sharding import PartitionSpec as P

D = 1792
H = 16
F = 16
FF = 4864
KS = 3
SLOT = 2048
STEP = 10


norm_epsilon = 1e-06
beta_first = 0.9
beta_second = 0.95
adam_epsilon = 1e-08
weight_decay = 3e-05
highest_precision = lax.Precision.HIGHEST


def passed_along(array, axis, by):
    count = lax.axis_size(axis)
    pairs = [(i, i + by) for i in range(count) if 0 <= i + by < count]
    return lax.ppermute(array, axis, pairs)


def prefix(value, axis, join, neutral):
    count, mine = (lax.axis_size(axis), lax.axis_index(axis))
    pieces = jax.tree.map(lambda part: lax.all_gather(part, axis), value)
    running = jax.tree.map(
        lambda part, zero: jnp.full_like(part, 0) + jnp.asarray(zero, part.dtype), value, neutral
    )

    def prefix_lap(position, running):
        longer = join(running, jax.tree.map(lambda part: part[position], pieces))
        return jax.tree.map(lambda new, old: jnp.where(position < mine, new, old), longer, running)

    return lax.fori_loop(0, count - 1, prefix_lap, running)


def entering(array, axis, combine, identity):
    count, index = (lax.axis_size(axis), lax.axis_index(axis))
    everything = jax.tree.map(
        lambda part, kind: lax.all_gather(part.astype(kind), axis),
        array,
        jax.tree.map(lambda a: jnp.bfloat16 if a.dtype == jnp.float32 else a.dtype, array),
    )
    start = jax.tree.map(
        lambda part, zero: jnp.broadcast_to(jnp.asarray(zero, part.dtype), part.shape),
        array,
        identity,
    )

    def entering_lap(k, before):
        at = count - 1 - k
        reached = at > index
        new = combine(
            before, jax.tree.map(lambda part, own: part[at].astype(own.dtype), everything, array)
        )
        return jax.tree.map(lambda a, b: jnp.where(reached, a, b), new, before)

    return lax.fori_loop(0, count, entering_lap, start)


def taylor_map(vectors):
    ones_part = jnp.ones(vectors.shape[:-1] + (1,), jnp.float32)
    linear_part = vectors / F**0.25
    outer_part = (vectors[..., :, None] * vectors[..., None, :]).reshape(
        vectors.shape[:-1] + (F * F,)
    )
    return jnp.concatenate([ones_part, linear_part, outer_part / math.sqrt(2.0 * F)], axis=-1)


def contract_rows(left_side, right_side):
    return lax.dot_general(
        left_side, right_side, (((0,), (0,)), ((), ())), preferred_element_type=jnp.float32
    )


def contract_columns(left_side, right_side):
    return lax.dot_general(
        left_side, right_side, (((1,), (1,)), ((), ())), preferred_element_type=jnp.float32
    )


def norm_scale(values):
    inverse = lax.rsqrt(jnp.mean(values * values, axis=-1, keepdims=True) + norm_epsilon)
    return (values * inverse, inverse)


def norm_backward(grad_normed, scaled, inverse, gain_row):
    grad_scaled = grad_normed * gain_row[None, :]
    grad_input = inverse * (
        grad_scaled - scaled * jnp.mean(grad_scaled * scaled, axis=-1, keepdims=True)
    )
    return (grad_input, jnp.sum(grad_normed * scaled, axis=0))


def add_pair(earlier, later_part):
    return (earlier[0] + later_part[0], earlier[1] + later_part[1])


def source_total(received):
    return jnp.sum(received, axis=0)


def adam_update(weight, gradient, first_moment, second_moment, learn_rate, decay_rate):
    first_new = beta_first * first_moment + (1.0 - beta_first) * gradient
    second_new = beta_second * second_moment + (1.0 - beta_second) * gradient * gradient
    first_hat = first_new / (1.0 - beta_first**STEP)
    second_hat = second_new / (1.0 - beta_second**STEP)
    new_weight = (
        weight
        - learn_rate * first_hat / (jnp.sqrt(second_hat) + adam_epsilon)
        - decay_rate * weight
    )
    return (new_weight, second_new)


def local(
    tokens,
    cotangent,
    lengths,
    w_qk,
    w_value,
    w_out,
    w_gu,
    w_down,
    small_params,
    m_qk,
    m_value,
    m_out,
    m_gu,
    m_down,
    m_small,
    v_qk,
    v_value,
    v_out,
    v_gu,
    v_down,
    v_small,
):
    slots_here, slot_rows, model_width = tokens.shape
    total_rows = slots_here * slot_rows
    head_width = model_width // H
    feature_count = 1 + F + F * F
    half_qk = H * F
    scale_factor = 1.0 / math.sqrt(F)
    positions = lax.axis_index("fsdp") * slot_rows + jnp.arange(slot_rows, dtype=jnp.int32)
    valid_mask = (positions[None, :] < lengths[:, None]).astype(jnp.float32).reshape(total_rows, 1)
    qk_low = w_qk.astype(jnp.bfloat16)
    value_low = w_value.astype(jnp.bfloat16)
    gate_low = w_gu.astype(jnp.bfloat16)
    down_low = w_down.astype(jnp.bfloat16)
    inputs = tokens.reshape(total_rows, model_width).astype(jnp.float32)
    scaled_first, inverse_first = norm_scale(inputs)
    pieces = (
        lax.all_gather(qk_low, ("dp", "fsdp"), axis=0, tiled=True),
        lax.all_gather(value_low, ("dp", "fsdp"), axis=0, tiled=True),
        lax.all_gather(w_out.astype(jnp.bfloat16), ("dp", "fsdp"), axis=0, tiled=True),
        lax.all_gather(small_params.astype(jnp.bfloat16), ("dp", "fsdp"), axis=0, tiled=True),
    )
    gain_rows = pieces[3][:, KS].astype(jnp.float32)
    normed_rows = (scaled_first * gain_rows[None, :]).astype(jnp.bfloat16)
    acc_qk = jnp.dot(normed_rows, pieces[0], preferred_element_type=jnp.float32)
    acc_value = jnp.dot(normed_rows, pieces[1], preferred_element_type=jnp.float32)
    out_full = pieces[2]
    small_full = pieces[3]
    small_float = small_full.astype(jnp.float32)
    normed_low = (scaled_first * small_float[:, KS][None, :]).astype(jnp.bfloat16)
    query_key = acc_qk.astype(jnp.bfloat16)
    value_pre = acc_value.astype(jnp.bfloat16).reshape(slots_here, slot_rows, model_width)
    earlier_rows = passed_along(value_pre[:, slot_rows - (KS - 1) :, :], "fsdp", 1)
    extended = jnp.concatenate([earlier_rows, value_pre], axis=1).astype(jnp.float32)
    convolved = small_float[:, 0] * extended[:, KS - 1 : KS - 1 + slot_rows, :]
    for tap_index in range(1, KS):
        convolved = (
            convolved
            + small_float[:, tap_index]
            * extended[:, KS - 1 - tap_index : KS - 1 - tap_index + slot_rows, :]
        )
    values_low = convolved.astype(jnp.bfloat16).reshape(slots_here, slot_rows, H, head_width)
    queries_low = query_key[:, :half_qk].reshape(slots_here, slot_rows, H, F)
    keys_low = query_key[:, half_qk:].reshape(slots_here, slot_rows, H, F)
    scores = (
        jnp.einsum("schf,sdhf->shcd", queries_low, keys_low, preferred_element_type=jnp.float32)
        * scale_factor
    )
    local_index = jnp.arange(slot_rows, dtype=jnp.int32)
    allowed = (local_index[None, :] <= local_index[:, None])[None, None]
    kernel = jnp.where(allowed, 1.0 + scores + 0.5 * scores * scores, 0.0)
    values_float = values_low.astype(jnp.float32)
    numerator = jnp.einsum("shcd,sdhe->sche", kernel, values_float, precision=highest_precision)
    denominator = jnp.swapaxes(jnp.sum(kernel, axis=-1), 1, 2)
    queries_float = queries_low.astype(jnp.float32)
    keys_float = keys_low.astype(jnp.float32)
    phi_query = taylor_map(queries_float)
    phi_key = taylor_map(keys_float)
    state_local = jnp.einsum("schf,sche->shfe", phi_key, values_float, precision=highest_precision)
    norm_local = jnp.sum(phi_key, axis=1)
    state_zero = jnp.zeros((slots_here, H * feature_count * head_width), jnp.float32)
    norm_zero = jnp.zeros((slots_here, H * feature_count), jnp.float32)
    state_flat, norm_flat = prefix(
        (state_local.reshape(slots_here, -1), norm_local.reshape(slots_here, -1)),
        "fsdp",
        add_pair,
        (state_zero, norm_zero),
    )
    state_before = state_flat.reshape(slots_here, H, feature_count, head_width)
    norm_before = norm_flat.reshape(slots_here, H, feature_count)
    numerator = numerator + jnp.einsum(
        "schf,shfe->sche", phi_query, state_before, precision=highest_precision
    )
    denominator = denominator + jnp.einsum(
        "schf,shf->sch", phi_query, norm_before, precision=highest_precision
    )
    mixer_float = numerator / denominator[..., None]
    mixer_low = mixer_float.astype(jnp.bfloat16).reshape(total_rows, model_width)
    after_mixer = inputs + jnp.dot(mixer_low, out_full, preferred_element_type=jnp.float32)
    scaled_second, inverse_second = norm_scale(after_mixer)
    second_low = (scaled_second * small_float[:, KS + 1][None, :]).astype(jnp.bfloat16)
    rows_in = second_low
    gate_up = jnp.dot(
        rows_in,
        lax.all_gather(gate_low, ("dp", "fsdp"), axis=0, tiled=True),
        preferred_element_type=jnp.float32,
    )
    gate_part = gate_up[:, :FF]
    upward = gate_up[:, FF:]
    sigmoid_gate = jax.nn.sigmoid(gate_part)
    silu_gate = gate_part * sigmoid_gate
    hidden_low = (silu_gate * upward).astype(jnp.bfloat16)
    down_result = contract_columns(
        hidden_low, lax.all_gather(down_low, ("dp", "fsdp"), axis=0, tiled=True)
    )
    result = after_mixer + down_result
    layer_out = (valid_mask * result).astype(jnp.bfloat16).reshape(tokens.shape)
    grad_result = valid_mask * cotangent.reshape(total_rows, model_width).astype(jnp.float32)
    grad_result_low = grad_result.astype(jnp.bfloat16)
    rows_in = grad_result_low
    grad_hidden = jnp.dot(
        rows_in,
        lax.all_gather(down_low, ("dp", "fsdp"), axis=0, tiled=True),
        preferred_element_type=jnp.float32,
    )
    grad_upward = grad_hidden * silu_gate
    grad_gate = grad_hidden * upward * sigmoid_gate * (1.0 + gate_part * (1.0 - sigmoid_gate))
    grad_gate_up = jnp.concatenate([grad_gate, grad_upward], axis=1).astype(jnp.bfloat16)
    grad_second = contract_columns(
        grad_gate_up, lax.all_gather(gate_low, ("dp", "fsdp"), axis=0, tiled=True)
    )
    grad_after_norm, grad_gain_second = norm_backward(
        grad_second, scaled_second, inverse_second, small_float[:, KS + 1]
    )
    grad_after = grad_result + grad_after_norm
    grad_after_low = grad_after.astype(jnp.bfloat16)
    grad_mixer = contract_columns(grad_after_low, out_full).astype(jnp.bfloat16).astype(jnp.float32)
    grad_mixer = grad_mixer.reshape(slots_here, slot_rows, H, head_width)
    grad_numerator = grad_mixer / denominator[..., None]
    grad_denominator = -jnp.sum(grad_mixer * mixer_float, axis=-1) / denominator
    grad_kernel = jnp.einsum(
        "sche,sdhe->shcd", grad_numerator, values_float, precision=highest_precision
    )
    grad_kernel = grad_kernel + jnp.swapaxes(grad_denominator, 1, 2)[..., None]
    grad_values = jnp.einsum("shcd,sche->sdhe", kernel, grad_numerator, precision=highest_precision)
    grad_scores = jnp.where(allowed, grad_kernel * (1.0 + scores), 0.0) * scale_factor
    grad_queries = jnp.einsum(
        "shcd,sdhf->schf", grad_scores, keys_float, precision=highest_precision
    )
    grad_keys = jnp.einsum(
        "shcd,schf->sdhf", grad_scores, queries_float, precision=highest_precision
    )
    carry_state = jnp.einsum(
        "schf,sche->shfe", phi_query, grad_numerator, precision=highest_precision
    )
    carry_norm = jnp.einsum(
        "schf,sch->shf", phi_query, grad_denominator, precision=highest_precision
    )
    after_state_flat, after_norm_flat = entering(
        (carry_state.reshape(slots_here, -1), carry_norm.reshape(slots_here, -1)),
        "fsdp",
        add_pair,
        (state_zero, norm_zero),
    )
    state_after = after_state_flat.reshape(slots_here, H, feature_count, head_width)
    norm_after = after_norm_flat.reshape(slots_here, H, feature_count)
    grad_phi_query = jnp.einsum(
        "shfe,sche->schf", state_before, grad_numerator, precision=highest_precision
    )
    grad_phi_query = grad_phi_query + norm_before[:, None, :, :] * grad_denominator[..., None]
    grad_values = grad_values + jnp.einsum(
        "schf,shfe->sche", phi_key, state_after, precision=highest_precision
    )
    grad_phi_key = jnp.einsum(
        "shfe,sche->schf", state_after, values_float, precision=highest_precision
    )
    grad_phi_key = grad_phi_key + norm_after[:, None, :, :]
    query_pull = jax.vjp(taylor_map, queries_float)[1]
    key_pull = jax.vjp(taylor_map, keys_float)[1]
    grad_queries = grad_queries + query_pull(grad_phi_query)[0]
    grad_keys = grad_keys + key_pull(grad_phi_key)[0]
    grad_query_key = jnp.concatenate(
        [grad_queries.reshape(total_rows, half_qk), grad_keys.reshape(total_rows, half_qk)], axis=1
    ).astype(jnp.bfloat16)
    grad_values_low = grad_values.reshape(slots_here, slot_rows, model_width).astype(jnp.bfloat16)
    later_rows = passed_along(grad_values_low[:, : KS - 1, :], "fsdp", -1)
    grad_extended = jnp.concatenate([grad_values_low, later_rows], axis=1).astype(jnp.float32)
    grad_pre = small_float[:, 0] * grad_extended[:, :slot_rows, :]
    for tap_index in range(1, KS):
        grad_pre = (
            grad_pre
            + small_float[:, tap_index] * grad_extended[:, tap_index : tap_index + slot_rows, :]
        )
    grad_pre_low = grad_pre.reshape(total_rows, model_width).astype(jnp.bfloat16)
    grad_values_float = grad_values_low.astype(jnp.float32)
    tap_grads = [
        jnp.sum(
            grad_values_float * extended[:, KS - 1 - tap_index : KS - 1 - tap_index + slot_rows, :],
            axis=(0, 1),
        )
        for tap_index in range(KS)
    ]
    pieces = (
        lax.all_gather(qk_low, ("dp", "fsdp"), axis=0, tiled=True),
        lax.all_gather(value_low, ("dp", "fsdp"), axis=0, tiled=True),
    )
    product = contract_columns(grad_query_key, pieces[0]) + contract_columns(
        grad_pre_low, pieces[1]
    )
    grad_input_norm, grad_gain_first = norm_backward(
        product, scaled_first, inverse_first, small_float[:, KS]
    )
    input_grad = (grad_after + grad_input_norm).reshape(tokens.shape)
    grad_small_full = jnp.stack(tap_grads + [grad_gain_first, grad_gain_second], axis=1)
    gradient_terms = jnp.concatenate(
        [
            contract_rows(normed_low, grad_query_key),
            contract_rows(normed_low, grad_pre_low),
            contract_rows(mixer_low, grad_after_low),
            contract_rows(second_low, grad_gate_up),
            contract_rows(grad_result_low, hidden_low),
            grad_small_full,
        ],
        axis=1,
    )
    owned_rows = w_qk.shape[0]
    term_columns = gradient_terms.shape[1]
    dp_count = lax.axis_size("dp")
    fsdp_count = lax.axis_size("fsdp")
    summed = source_total(
        lax.all_to_all(
            gradient_terms.reshape(dp_count * fsdp_count, owned_rows, term_columns).astype(
                jnp.bfloat16
            ),
            ("dp", "fsdp"),
            split_axis=0,
            concat_axis=0,
            tiled=True,
        ).astype(jnp.float32)
    )
    bound_qk = 2 * half_qk
    bound_value = bound_qk + model_width
    bound_out = bound_value + model_width
    bound_gu = bound_out + 2 * FF
    bound_down = bound_gu + FF
    grads_all = (
        summed[:, :bound_qk],
        summed[:, bound_qk:bound_value],
        summed[:, bound_value:bound_out],
        summed[:, bound_out:bound_gu],
        summed[:, bound_gu:bound_down],
        summed[:, bound_down:],
    )
    masters = (w_qk, w_value, w_out, w_gu, w_down, small_params)
    firsts = (m_qk, m_value, m_out, m_gu, m_down, m_small)
    seconds = (v_qk, v_value, v_out, v_gu, v_down, v_small)
    learn_rates = (
        0.05 / math.sqrt(D),
        0.05 / math.sqrt(D),
        0.05 / math.sqrt(max(D // 128, 1)),
        0.05 / math.sqrt(D),
        0.05 / math.sqrt(0.0003 * FF * SLOT**0.825),
        0.014,
    )
    decays = (weight_decay, weight_decay, weight_decay, weight_decay, weight_decay, 0.0)
    new_weights = []
    new_seconds = []
    for position in range(6):
        updated, moment = adam_update(
            masters[position],
            grads_all[position],
            firsts[position],
            seconds[position],
            learn_rates[position],
            decays[position],
        )
        new_weights.append(updated)
        new_seconds.append(moment)
    return (
        layer_out,
        input_grad,
        grads_all[0],
        grads_all[1],
        grads_all[2],
        grads_all[3],
        grads_all[4],
        grads_all[5],
        new_weights[0],
        new_weights[1],
        new_weights[2],
        new_weights[3],
        new_weights[4],
        new_weights[5],
        new_seconds[0],
        new_seconds[1],
        new_seconds[2],
        new_seconds[3],
        new_seconds[4],
        new_seconds[5],
    )


def solution(mesh):
    return jax.shard_map(
        local,
        mesh=mesh,
        in_specs=(
            P("dp", "fsdp", None),
            P("dp", "fsdp", None),
            P("dp"),
            P(("dp", "fsdp"), None),
            P(("dp", "fsdp"), None),
            P(("dp", "fsdp"), None),
            P(("dp", "fsdp"), None),
            P(("dp", "fsdp"), None),
            P(("dp", "fsdp"), None),
            P(("dp", "fsdp"), None),
            P(("dp", "fsdp"), None),
            P(("dp", "fsdp"), None),
            P(("dp", "fsdp"), None),
            P(("dp", "fsdp"), None),
            P(("dp", "fsdp"), None),
            P(("dp", "fsdp"), None),
            P(("dp", "fsdp"), None),
            P(("dp", "fsdp"), None),
            P(("dp", "fsdp"), None),
            P(("dp", "fsdp"), None),
            P(("dp", "fsdp"), None),
        ),
        out_specs=(
            P("dp", "fsdp", None),
            P("dp", "fsdp", None),
            P(("dp", "fsdp"), None),
            P(("dp", "fsdp"), None),
            P(("dp", "fsdp"), None),
            P(("dp", "fsdp"), None),
            P(("dp", "fsdp"), None),
            P(("dp", "fsdp"), None),
            P(("dp", "fsdp"), None),
            P(("dp", "fsdp"), None),
            P(("dp", "fsdp"), None),
            P(("dp", "fsdp"), None),
            P(("dp", "fsdp"), None),
            P(("dp", "fsdp"), None),
            P(("dp", "fsdp"), None),
            P(("dp", "fsdp"), None),
            P(("dp", "fsdp"), None),
            P(("dp", "fsdp"), None),
            P(("dp", "fsdp"), None),
            P(("dp", "fsdp"), None),
        ),
        check_vma=False,
    )
```

profile of v0, /device:TPU:0, one launch (start us, length us, event | category | flops | bytes accessed | tf_op | source)
XLA Modules:
  0.0 2874.2 jit_solution(6828888684776516709)
XLA Ops:
  11.4 43.5 %all-gather = bf16[32,56,5]{1,2,0:T(8,128)(2,1)S(1)} all-gather(bf16[1,56,5]{1,2,0:T(8,128)(2,1)S(1)} %convert_bitcast_fusion), channel_id=1, replica_groups=mesh['dp'=4,'fsdp'=8] {'dp','fsdp'}, dimensions={0}, use_global_device_ids=true | all-gather | bytes 18480 | tf_op jit(solution)/shard_map/all_gather | solution.py:165
  60.1 10.1 all-gather.11.cloned.1.call-done
  79.8 62.9 %all-gather.9.cloned.1.call-done = bf16[1792,1792]{1,0:T(8,128)(2,1)} async-done(((bf16[56,1792]{1,0:T(8,128)(2,1)}), bf16[1792,1792]{1,0:T(8,128)(2,1)}) %all-gather.9.cloned.1.call-update) | async-done | bytes 6422544 | tf_op jit(solution)/shard_map/all_gather | solution.py:163
  142.7 6.9 convolution_convert_fusion.4
  165.5 6.8 fusion.4
  172.2 9.1 all_gather_reshape.6
  192.2 6.9 fusion.3
  199.4 6.1 fusion.33
  205.7 18.1 all_gather.40
  228.4 224.2 %all-gather.13.cloned.1.call-done = f32[8,2,489216]{2,1,0:T(2,128)} async-done(((f32[1,2,489216]{2,1,0:T(2,128)}), f32[8,2,489216]{2,1,0:T(2,128)}) %all-gather.13.cloned.1.call-update) | async-done | bytes 31309840 | tf_op jit(solution)/shard_map/all_gather | solution.py:33
  452.6 46.7 %while.34 = (s32[]{:T(128)}, f32[2,489216]{1,0:T(2,128)}, f32[2,4368]{1,0:T(2,128)S(1)}, s32[]{:T(128)}, f32[8,2,489216]{2,1,0:T(2,128)}, /*index=5*/f32[8,2,4368]{2,1,0:T(2,128)S(1)}, s32[]{:T(128)}, s32[]{:T(128)}) while((s32[]{:T(128)}, f32[2,489216]{1,0:T(2,128)}, f32[2,4368]{1,0:T(2,128)S(1)}, s32[]{:T(128)}, ...), condition=%wide.region_3.4_spmd.clone, body=%wide.region_2.3_spmd.clone.sunk | while | flops 2961508 | bytes 11846139 | solution.py:42
  452.6 5.8 add_select_fusion.13
  458.5 6.8 add_select_fusion.13
  465.3 6.7 add_select_fusion.13
  472.1 6.7 add_select_fusion.13
  478.9 6.9 add_select_fusion.13
  485.8 6.7 add_select_fusion.13
  492.6 6.7 add_select_fusion.13
  499.5 9.9 reshape.299
  509.4 8.2 fusion.80
  517.7 13.8 fusion.81
  531.5 11.3 fusion.89
  546.3 8.9 multiply_reduce_fusion.7
  555.2 172.0 %all-gather.17.cloned.1.call-done = bf16[1792,9728]{1,0:T(8,128)(2,1)} async-done(((bf16[56,9728]{1,0:T(8,128)(2,1)}), bf16[1792,9728]{1,0:T(8,128)(2,1)}) %all-gather.17.cloned.1.call-update) | async-done | bytes 34865168 | tf_op jit(solution)/shard_map/all_gather | solution.py:229
  727.3 28.2 fusion.79
  755.4 91.4 %all-gather.19.cloned.1.call-done = bf16[1792,4864]{1,0:T(8,128)(2,1)} async-done(((bf16[56,4864]{1,0:T(8,128)(2,1)}), bf16[1792,4864]{1,0:T(8,128)(2,1)}) %all-gather.19.cloned.1.call-update) | async-done | bytes 17432592 | tf_op jit(solution)/shard_map/all_gather | solution.py:238
  846.8 23.4 multiply_convert_fusion.1
  870.2 29.5 %multiply_reduce_fusion.4 = (bf16[1792]{0:T(1024)(128)(2,1)}, f32[512]{0:T(512)S(1)}, f32[512,1792]{1,0:T(8,128)}) fusion(f32[512,1792]{1,0:T(8,128)} %get-tuple-element.485, f32[512]{0:T(512)S(1)} %add_rsqrt_fusion, f32[1792]{0:T(1024)S(1)} %get-tuple-element.423, bf16[1792,9728]{1,0:T(8,128)(2,1)} %all-gather.17.cloned.1.call-done, ...), kind=kOutput, calls=%fused_computation.71 | convolution fusion | flops 17876383744 | bytes 52181504 | tf_op jit(solution)/shard_map/dot_general | solution.py:85
  905.8 8.2 fusion.31
  914.0 5.8 reshape.333
  919.8 5.1 copy.247
  924.9 14.8 convolution_convert_fusion.5
  939.7 5.4 reshape.342
  958.3 11.5 fusion.58
  970.6 11.4 bitcast_add_fusion
  983.3 5.3 multiply_reduce_fusion.2
  988.6 9.5 select_multiply_fusion
  1004.1 14.7 all_gather.45
  1018.8 7.7 convolution_convert_fusion.2
  1026.6 15.3 fusion.32
  1041.9 13.2 convolution_convert_fusion.1
  1055.1 26.7 convolution_convert_fusion
  1081.8 8.6 all-gather.21.cloned.1.call-done
  1090.4 50.0 %while.35 = (s32[]{:T(128)}, f32[2,489216]{1,0:T(2,128)}, f32[2,4368]{1,0:T(2,128)S(1)}, s32[]{:T(128)}, bf16[8,2,489216]{2,1,0:T(2,128)(2,1)}, /*index=5*/bf16[...) while((s32[]{:T(128)}, f32[2,489216]{1,0:T(2,128)}, ...), condition=%wide.region_11.12_spmd.clone, body=%wide.region_10.11_spmd.clone.sunk | while | flops 3948680 | bytes 9871865 | solution.py:66
  1090.4 5.4 add_select_fusion.15
  1095.9 6.3 add_select_fusion.15
  1102.2 6.3 add_select_fusion.15
  1108.5 6.3 add_select_fusion.15
  1114.9 6.3 add_select_fusion.15
  1121.2 6.3 add_select_fusion.15
  1127.6 6.3 add_select_fusion.15
  1133.9 6.3 add_select_fusion.15
  1140.4 9.6 reshape.307
  1150.0 16.9 add_convert_fusion
  1168.8 6.3 add_bitcast_fusion
  1181.2 7.4 fusion.43
  1204.5 7.0 fusion.90
  1225.0 5.9 bitcast_convert_fusion
  1231.8 140.4 %concatenate.52 = bf16[32,56,18693]{2,1,0:T(8,128)(2,1)} concatenate(bf16[32,56,512]{2,1,0:T(8,128)(2,1)} %convolution_convert_fusion.6, bf16[32,56,1792]{2,1,0:T(8,128)(2,1)} %bitcast.203, bf16[32,56,1792]{2,1,0:T(8,128)(2,1)} %convolution_convert_fusion.2, bf16[32,56,9728]{2,1,0:T(8,128)(2,1)} %bitcast.191, bf16[32,56,4864]{2,1,0:T(8,128)(2,1)} %convolution_convert_fusion.1, ...), dimensions={2} | concatenate | bytes 133991424 | tf_op jit(solution)/shard_map/concatenate | solution.py:339
  1372.2 5.4 all-to-all-start
  1377.6 17.3 multiply_convert_fusion.3
  1394.9 1433.0 %all-to-all-done = bf16[32,56,18693]{2,1,0:T(8,128)(2,1)} async-done(((bf16[32,56,18693]{2,1,0:T(8,128)(2,1)}), bf16[32,56,18693]{2,1,0:T(8,128)(2,1)}, u32[]{:S(2)}, u32[]{:S(2)}) %all-to-all-start) | async-done | bytes 66995744 | tf_op jit(solution)/shard_map/all_to_all | solution.py:355
  2827.9 23.4 convert_reduce_fusion
  2853.8 6.3 multiply_subtract_fusion
  (299 shorter events, 129.2 us)
Async XLA Ops:
  7.2 51.2 %copy-start.5 = (bf16[2,256,1792]{2,1,0:T(8,128)(2,1)S(1)}, bf16[2,256,1792]{2,1,0:T(8,128)(2,1)}, u32[]{:S(2)}) copy-start(bf16[2,256,1792]{2,1,0:T(8,128)(2,1)} %param.25) | copy-start | bytes 5505028
  7.2 62.9 %all-gather.11.cloned.1.call-start = ((), (), s32[]{:S(2)}) async-start(), calls=%async_computation.2 | async-start | bytes 1892352 | tf_op jit(solution)/shard_map/all_gather | solution.py:162
  8.9 133.8 %all-gather.9.cloned.1.call-start = ((), (), s32[]{:S(2)}) async-start(), calls=%async_computation.1 | async-start | bytes 6623232 | tf_op jit(solution)/shard_map/all_gather | solution.py:163
  10.7 441.9 %all-gather.13.cloned.1.call-start = ((), (), s32[]{:S(2)}) async-start(), calls=%async_computation.3 | async-start | bytes 35223552 | tf_op jit(solution)/shard_map/all_gather | solution.py:33
  57.6 15.7 copy-start.67
  58.3 102.3 %copy-start.57 = (f32[1792]{0:T(1024)}, f32[1792]{0:T(1024)S(1)}, u32[]{:S(2)}) copy-start(f32[1792]{0:T(1024)S(1)} %get-tuple-element.424) | copy-start | bytes 21508
  58.3 102.3 %copy-start.59 = (f32[1792]{0:T(1024)}, f32[1792]{0:T(1024)S(1)}, u32[]{:S(2)}) copy-start(f32[1792]{0:T(1024)S(1)} %get-tuple-element.425) | copy-start | bytes 21508
  58.3 102.3 %copy-start.61 = (f32[1792]{0:T(1024)}, f32[1792]{0:T(1024)S(1)}, u32[]{:S(2)}) copy-start(f32[1792]{0:T(1024)S(1)} %get-tuple-element.426) | copy-start | bytes 21508
  74.3 78.9 %copy-start.26 = (bf16[2,256,16,16]{1,0,3,2:T(2,128)(2,1)}, bf16[2,256,16,16]{1,0,3,2:T(2,128)(2,1)S(1)}, u32[]{:S(2)}) copy-start(bf16[2,256,16,16]{1,0,3,2:T(2,128)(2,1)S(1)} %reshape.298) | copy-start | bytes 786436
  150.8 6.4 collective-permute-start
  153.2 38.9 %copy-start.16 = (f32[2,256,16,16]{1,3,2,0:T(8,128)}, f32[2,256,16,16]{1,3,2,0:T(8,128)S(1)}, u32[]{:S(2)}) copy-start(f32[2,256,16,16]{1,3,2,0:T(8,128)S(1)} %broadcast_multiply_fusion.1) | copy-start | bytes 1572868
  157.8 7.0 slice-start.2
  181.4 6.7 copy-start.78
  181.4 364.9 %all-gather.15.cloned.1.call-start = ((), (), s32[]{:S(2)}) async-start(), calls=%async_computation.4 | async-start | bytes 6623232 | tf_op jit(solution)/shard_map/all_gather | solution.py:164
  183.2 544.0 %all-gather.17.cloned.1.call-start = ((), (), s32[]{:S(2)}) async-start(), calls=%async_computation.5 | async-start | bytes 35954688 | tf_op jit(solution)/shard_map/all_gather | solution.py:229
  186.0 660.8 %all-gather.19.cloned.1.call-start = ((), (), s32[]{:S(2)}) async-start(), calls=%async_computation.6 | async-start | bytes 17977344 | tf_op jit(solution)/shard_map/all_gather | solution.py:238
  186.9 903.4 %all-gather.21.cloned.1.call-start = ((), (), s32[]{:S(2)}) async-start(), calls=%async_computation.7 | async-start | bytes 17611776 | tf_op jit(solution)/shard_map/all_gather | solution.py:48
  192.2 6.9 copy-start.42
  192.2 7.3 copy-start.27
  199.3 6.3 copy-start.24
  199.3 24.4 copy-start.13
  499.4 10.0 copy-start.35
  509.4 8.2 copy-start.52
  509.4 8.2 copy-start.1
  517.6 13.9 copy-start.50
  517.6 471.0 %copy-start.48 = (f32[2,256,16]{1,2,0:T(8,128)}, f32[2,256,16]{1,2,0:T(8,128)S(1)}, u32[]{:S(2)}) copy-start(f32[2,256,16]{1,2,0:T(8,128)S(1)} %fusion.60) | copy-start | bytes 98308
  517.6 13.8 copy-start.8
  517.6 13.8 copy-start.64
  727.3 119.6 %copy-start.18 = (bf16[512,1792]{1,0:T(8,128)(2,1)S(1)}, bf16[512,1792]{1,0:T(8,128)(2,1)}, u32[]{:S(2)}) copy-start(bf16[512,1792]{1,0:T(8,128)(2,1)} %fusion.15) | copy-start | bytes 5505028
  870.2 29.5 %copy-start.19 = (bf16[2,256,1792]{2,1,0:T(8,128)(2,1)S(1)}, bf16[2,256,1792]{2,1,0:T(8,128)(2,1)}, u32[]{:S(2)}) copy-start(bf16[2,256,1792]{2,1,0:T(8,128)(2,1)} %param.26) | copy-start | bytes 5505028
  870.2 29.5 %copy-start.70 = (f32[1,2,2,128]{3,1,2,0:T(2,128)S(1)}, f32[1,2,2,128]{3,1,2,0:T(2,128)}, u32[]{:S(2)}) copy-start(f32[1,2,2,128]{3,1,2,0:T(2,128)} %copy-done.69) | copy-start | bytes 6148
  958.3 12.3 copy-start.51
  958.3 12.3 copy-start.53
  988.6 9.6 copy-start.28
  998.2 5.9 copy-start.63
  998.2 20.6 copy-start.32
  1018.8 7.7 copy-start.4
  1018.8 7.7 copy-start.49
  1018.8 7.7 copy-start.66
  1018.8 23.0 slice-start.4
  1026.5 15.3 copy-start.33
  1026.5 15.3 slice-start.5
  1140.4 9.6 copy-start.17
  1167.3 30.3 %collective-permute-start.1 = (bf16[2,2,1792]{2,1,0:T(2,128)(2,1)S(1)}, bf16[2,2,1792]{2,1,0:T(2,128)(2,1)S(1)}, u32[]{:S(2)}, u32[]{:S(2)}) collective-permute-start(bf16[2,2,1792]{2,1,0:T(2,128)(2,1)S(1)} %copy.259), channel_id=1, source_target_pairs={{1,0},{2,1},{3,2},{4,3},{5,4},{6,5},{7,6},{9,8},{10,9},{11,10},{12... | collective-permute-start | bytes 43016 | tf_op jit(solution)/shard_map/ppermute | solution.py:28
  1181.1 7.4 slice-start
  1181.2 7.4 slice-start.1
  1204.4 7.1 copy-start.6
  1204.4 7.1 copy-start.34
  1204.4 7.1 copy-start.41
  1204.5 7.1 copy-start.56
  1204.5 7.1 copy-start.68
  1217.2 7.8 copy-start.77
  1225.0 6.8 copy-start.30
  1225.0 6.8 copy-start.31
  1372.2 5.4 copy-start.71
  1372.2 1455.7 %all-to-all-start = ((bf16[32,56,18693]{2,1,0:T(8,128)(2,1)}), bf16[32,56,18693]{2,1,0:T(8,128)(2,1)}, u32[]{:S(2)}, u32[]{:S(2)}) async-start(bf16[32,56,18693]{2,1,0:T(8,128)(2,1)} %concatenate.52), calls=%async_computation | async-start | bytes 134873088 | tf_op jit(solution)/shard_map/all_to_all | solution.py:355
  1394.9 1457.2 %copy-start.43 = (f32[56,512]{1,0:T(8,128)S(1)}, f32[56,512]{1,0:T(8,128)}, u32[]{:S(2)}) copy-start(f32[56,512]{1,0:T(8,128)} %param.28) | copy-start | bytes 344068
  1394.9 1457.2 %copy-start.54 = (f32[56,512]{1,0:T(8,128)S(1)}, f32[56,512]{1,0:T(8,128)}, u32[]{:S(2)}) copy-start(f32[56,512]{1,0:T(8,128)} %param.34) | copy-start | bytes 344068
  1394.9 1457.2 %copy-start.55 = (f32[56,512]{1,0:T(8,128)S(1)}, f32[56,512]{1,0:T(8,128)}, u32[]{:S(2)}) copy-start(f32[56,512]{1,0:T(8,128)} %param.40) | copy-start | bytes 344068
  1394.9 1458.9 %copy-start.15 = (f32[56,9728]{1,0:T(8,128)S(1)}, f32[56,9728]{1,0:T(8,128)}, u32[]{:S(2)}) copy-start(f32[56,9728]{1,0:T(8,128)} %param.31) | copy-start | bytes 6537220
  2852.2 11.5 copy-start.73
  2853.8 6.4 copy-start.23
  2853.8 6.4 copy-start.39
  2853.8 6.4 copy-start.40
  (31 other events, 95.1 us)
Sparse Core Ops, SparseCore 0:
  11.5 58.6 all-gather.10
  73.6 69.0 all-gather.8
  181.5 271.1 all-gather.12
  455.9 68.3 all-gather.14
  527.6 199.6 all-gather.16
  730.5 116.2 all-gather.18
  949.2 141.1 all-gather.20
where the time goes:
time: 2890 us; the launch traced here: 2870 us
  waiting for transfers between devices  2000 us (69%)
  matrix products  335 us (12%)
  local copies, waits for them, and re-layouts  228 us (8%)
  other arithmetic  206 us (7%)
  blocking collectives  76.3 us (3%)
    all_to_all x1, waiting for transfers between devices, local(): lax.all_to_all(gradient_terms.reshape(dp_count * fsdp_count, owned_rows,...  1430 us
    all_gather x1, waiting for transfers between devices, prefix(): pieces = jax.tree.map(lambda part: lax.all_gather(part, axis), value)  224 us
    all_gather x1, waiting for transfers between devices, local(): lax.all_gather(gate_low, ('dp', 'fsdp'), axis=0, tiled=True)  172 us
    concatenate x6, local copies, waits for them, and re-layouts, local(): jnp.concatenate([contract_rows(normed_low, grad_query_key), contract_rows...  147 us
    all_gather x1, waiting for transfers between devices, local(): lax.all_gather(down_low, ('dp', 'fsdp'), axis=0, tiled=True)  91.4 us
    dot_general x5, matrix products, contract_columns(): lax.dot_general(left_side, right_side, (((1,), (1,)), ((), ())), preferre...  63.6 us
    all_gather x1, waiting for transfers between devices, local(): lax.all_gather(value_low, ('dp', 'fsdp'), axis=0, tiled=True)  62.9 us
  transfers between devices with their start and end apart: 10, of which 7 were waited for; matrix products, arithmetic and copies ran while one was open for 12% of the time, Pallas kernels for 0%

commit v1 on v0

v1 whole, which is shorter than its diff:
```python
import functools
import math

import jax
import jax.numpy as jnp
import numpy as np
from jax import lax
from jax.experimental import pallas as pl
from jax.experimental.pallas import tpu as pltpu
from jax.sharding import Mesh
from jax.sharding import PartitionSpec as P

D = 1792
H = 16
F = 16
FF = 4864
KS = 3
SLOT = 2048
STEP = 10

CORES = 2
HC = H // CORES
HW = D // H
VC = HC * HW
QC = HC * F
FC = FF // CORES
LANES = 128
FEATS = 256
FROWS = 160
SCALE = 1.0 / math.sqrt(F)

norm_epsilon = 1e-06
beta_first = 0.9
beta_second = 0.95
adam_epsilon = 1e-08
weight_decay = 3e-05

bf16 = jnp.bfloat16
f32 = jnp.float32


def feature_tables():
    index = np.full((8, FEATS), -4096, np.int32)
    scale = np.zeros((8, FEATS), np.float32)
    scale[0, 0] = scale[1, 0] = scale[2, 0] = 1.0
    at = 1
    for i in range(F):
        index[0, at] = i
        scale[1, at] = 1.0
        scale[2, at] = SCALE
        at += 1
    for i in range(F):
        for j in range(i, F):
            index[0, at] = i
            index[1, at] = j
            scale[2, at] = (1.0 if i == j else 2.0) * 0.5 * SCALE * SCALE
            at += 1
    return index, scale


def dot(a, b):
    return lax.dot_general(a, b, (((1,), (0,)), ((), ())), preferred_element_type=f32)


def dot_nt(a, b):
    return lax.dot_general(a, b, (((1,), (1,)), ((), ())), preferred_element_type=f32)


def dot_tn(a, b):
    return lax.dot_general(a, b, (((0,), (0,)), ((), ())), preferred_element_type=f32)


def selectors(index_ref, head):
    lane = lax.broadcasted_iota(jnp.int32, (LANES, FEATS), 0) - head * F
    first = jnp.where(lane == index_ref[0:1, :], 1.0, 0.0).astype(bf16)
    second = jnp.where(lane == index_ref[1:2, :], 1.0, 0.0).astype(bf16)
    return first, second


def factors(rows, first, second, scale_ref):
    return (dot(rows, first) + scale_ref[0:1, :], dot(rows, second) + scale_ref[1:2, :])


def window(head):
    start = head * HW
    base = min(start // LANES * LANES, VC - 2 * LANES)
    return base, start - base


def head_columns(ref, head):
    base, offset = window(head)
    wide = ref[:, base : base + 2 * LANES].astype(f32)
    if offset:
        wide = pltpu.roll(wide, 2 * LANES - offset, 1)
    return wide[:, :LANES]


def add_head_columns(ref, head, block):
    base, offset = window(head)
    wide = jnp.concatenate([block, jnp.zeros_like(block)], axis=1)
    if offset:
        wide = pltpu.roll(wide, offset, 1)
    ref[:, base : base + 2 * LANES] += wide


def with_one(block):
    lane = lax.broadcasted_iota(jnp.int32, block.shape, 1)
    return jnp.where(lane < HW, block, jnp.where(lane == HW, 1.0, 0.0))


def only_head(rows, head):
    lane = lax.broadcasted_iota(jnp.int32, rows.shape, 1)
    inside = (lane >= head * F) & (lane < head * F + F)
    return jnp.where(inside, rows.astype(f32), 0.0).astype(bf16)


def state_kernel(index_ref, scale_ref, k_ref, v_ref, state_ref):
    keys = k_ref[...]
    for head in range(HC):
        first, second = selectors(index_ref, head)
        one, two = factors(keys, first, second, scale_ref)
        phi = (one * two * scale_ref[2:3, :]).astype(bf16)
        values = with_one(head_columns(v_ref, head)).astype(bf16)
        state_ref[0, head] = dot_tn(phi, values)[:FROWS]


def scores_of(q_head, keys):
    scores = dot_nt(q_head, keys) * SCALE
    row = lax.broadcasted_iota(jnp.int32, scores.shape, 0)
    column = lax.broadcasted_iota(jnp.int32, scores.shape, 1)
    return scores, column <= row


def forward_kernel(index_ref, scale_ref, q_ref, k_ref, v_ref, before_ref, mixer_ref, den_ref, wide):
    queries = q_ref[...]
    keys = k_ref[...]
    wide[...] = jnp.zeros_like(wide)
    lane = lax.broadcasted_iota(jnp.int32, (queries.shape[0], LANES), 1)
    dens = jnp.zeros((queries.shape[0], LANES), f32)
    for head in range(HC):
        first, second = selectors(index_ref, head)
        one, two = factors(queries, first, second, scale_ref)
        phi = (one * two).astype(bf16)
        values = with_one(head_columns(v_ref, head)).astype(bf16)
        scores, allowed = scores_of(only_head(queries, head), keys)
        kernel = jnp.where(allowed, 1.0 + scores + 0.5 * scores * scores, 0.0).astype(bf16)
        total = dot(kernel, values) + dot(phi[:, :FROWS], before_ref[0, head])
        den = total[:, HW : HW + 1]
        add_head_columns(wide, head, jnp.where(lane < HW, total / den, 0.0))
        dens = jnp.where(lane == head, den, dens)
    mixer_ref[...] = wide[...].astype(bf16)
    den_ref[...] = dens


def pull_kernel(index_ref, scale_ref, q_ref, gm_ref, mixer_ref, den_ref, state_ref, gnum_ref):
    queries = q_ref[...]
    lane = lax.broadcasted_iota(jnp.int32, (queries.shape[0], LANES), 1)
    for head in range(HC):
        first, second = selectors(index_ref, head)
        one, two = factors(queries, first, second, scale_ref)
        phi = (one * two).astype(bf16)
        den = den_ref[:, head : head + 1]
        grad = jnp.where(lane < HW, head_columns(gm_ref, head), 0.0)
        mixer = head_columns(mixer_ref, head)
        pulled = -jnp.sum(grad * mixer, axis=1, keepdims=True)
        grad = (jnp.where(lane == HW, pulled, grad) / den).astype(bf16)
        gnum_ref[:, head * LANES : (head + 1) * LANES] = grad
        state_ref[0, head] = dot_tn(phi, grad)[:FROWS]


def backward_kernel(
    index_ref, scale_ref, q_ref, k_ref, v_ref, gnum_ref, before_ref, after_ref, gqk_ref, gv_ref, wide
):
    queries = q_ref[...]
    keys = k_ref[...]
    wide[...] = jnp.zeros_like(wide)
    lane = lax.broadcasted_iota(jnp.int32, (queries.shape[0], LANES), 1)
    grad_q = jnp.zeros((queries.shape[0], LANES), f32)
    grad_k = jnp.zeros((queries.shape[0], LANES), f32)
    for head in range(HC):
        first, second = selectors(index_ref, head)
        coef = scale_ref[2:3, :]
        q_one, q_two = factors(queries, first, second, scale_ref)
        k_one, k_two = factors(keys, first, second, scale_ref)
        values = with_one(head_columns(v_ref, head)).astype(bf16)
        gnum = gnum_ref[:, head * LANES : (head + 1) * LANES]
        q_head = only_head(queries, head)
        k_head = only_head(keys, head)
        scores, allowed = scores_of(q_head, keys)
        kernel = jnp.where(allowed, 1.0 + scores + 0.5 * scores * scores, 0.0).astype(bf16)
        grad_kernel = dot_nt(gnum, values)
        grad_scores = (jnp.where(allowed, grad_kernel * (1.0 + scores), 0.0) * SCALE).astype(bf16)
        phi_k = (k_one * k_two * coef).astype(bf16)
        after = after_ref[0, head]
        before = before_ref[0, head]
        grad_v = dot_tn(kernel, gnum) + dot(phi_k[:, :FROWS], after)
        add_head_columns(wide, head, jnp.where(lane < HW, grad_v, 0.0))
        empty = jnp.zeros((FEATS - FROWS, LANES), bf16)
        grad_phi_q = dot_nt(gnum, jnp.concatenate([before, empty], axis=0))
        grad_phi_k = dot_nt(values, jnp.concatenate([after, empty], axis=0)) * coef
        grad_q += dot(grad_scores, k_head)
        grad_q += dot_nt((grad_phi_q * q_two).astype(bf16), first)
        grad_q += dot_nt((grad_phi_q * q_one).astype(bf16), second)
        grad_k += dot_tn(grad_scores, q_head)
        grad_k += dot_nt((grad_phi_k * k_two).astype(bf16), first)
        grad_k += dot_nt((grad_phi_k * k_one).astype(bf16), second)
    gqk_ref[:, :LANES] = grad_q.astype(bf16)
    gqk_ref[:, LANES:] = grad_k.astype(bf16)
    gv_ref[...] = wide[...].astype(bf16)


def per_slot(kernel, slots, rows, ins, outs, scratch, flops):
    def table():
        return pl.BlockSpec((8, FEATS), lambda s: (0, 0))

    def row_spec(width, column=0):
        return pl.BlockSpec((rows, width), lambda s: (s, column))

    def state_spec():
        return pl.BlockSpec((1, HC, FROWS, LANES), lambda s: (s, 0, 0, 0))

    def spec(kind):
        return state_spec() if kind == "state" else row_spec(*kind)

    def shape(kind, dtype):
        if kind == "state":
            return jax.ShapeDtypeStruct((slots, HC, FROWS, LANES), dtype)
        return jax.ShapeDtypeStruct((slots * rows, kind[0]), dtype)

    return pl.pallas_call(
        kernel,
        grid=(slots,),
        in_specs=[table(), table()] + [spec(kind) for kind in ins],
        out_specs=[spec(kind) for kind, _ in outs],
        out_shape=[shape(kind, dtype) for kind, dtype in outs],
        scratch_shapes=scratch,
        compiler_params=pltpu.CompilerParams(vmem_limit_bytes=56 << 20),
        cost_estimate=pl.CostEstimate(flops=flops, bytes_accessed=8 << 20, transcendentals=0),
    )


def shifted(array, axis, by):
    count = lax.axis_size(axis)
    return lax.ppermute(array, axis, [(i, (i + by) % count) for i in range(count)])


def passed_along(array, axis, by):
    count = lax.axis_size(axis)
    pairs = [(i, i + by) for i in range(count) if 0 <= i + by < count]
    return lax.ppermute(array, axis, pairs)


def both_cores(mine, theirs, axis):
    first = lax.axis_index("core") == 0
    return jnp.concatenate(
        [jnp.where(first, mine, theirs), jnp.where(first, theirs, mine)], axis=axis
    )


def swapped(array):
    return lax.ppermute(array, "core", [(0, 1), (1, 0)])


def part_of(array, axis, index):
    return lax.dynamic_index_in_dim(array, index, axis, keepdims=False)


def gather_stage(piece, axis, dim):
    count, mine = lax.axis_size(axis), lax.axis_index(axis)
    arrived = [(mine, piece)]
    for by in range(1, count):
        arrived.append(((mine - by) % count, shifted(piece, axis, by)))
    whole = jnp.zeros(piece.shape[:dim] + (count,) + piece.shape[dim:], piece.dtype)
    for source, block in arrived:
        whole = lax.dynamic_update_index_in_dim(whole, block, source, dim)
    return whole


def gather_rows(piece, x_first):
    block = gather_stage(piece, "z", 0)
    if x_first:
        block = gather_stage(block, "x", 0)
        block = gather_stage(block, "y", 0)
    else:
        block = gather_stage(block, "y", 0)
        block = gather_stage(block, "x", 1)
    return block.reshape(D, piece.shape[1])


def scatter_stage(blocks, axis, out_dtype):
    count, mine = lax.axis_size(axis), lax.axis_index(axis)
    arrived = []
    for by in range(1, count):
        arrived.append(shifted(blocks((mine + by) % count), axis, by))
    total = lax.optimization_barrier(blocks(mine)).astype(f32)
    for block in arrived:
        total = total + block.astype(f32)
    return total.astype(out_dtype)


def scatter_rows(left_t, right, x_first):
    y_size, x_size, z_size = lax.axis_size("y"), lax.axis_size("x"), lax.axis_size("z")
    chip_rows = D // (y_size * x_size * z_size)
    columns = right.shape[1]
    view = left_t.reshape(y_size, x_size, z_size * chip_rows, left_t.shape[1])
    first_axis, first_dim = ("x", 1) if x_first else ("y", 0)
    second_axis = "y" if x_first else "x"

    def product(target):
        rows = part_of(view, first_dim, target).reshape(-1, left_t.shape[1])
        return dot(rows, right).astype(bf16)

    return scatter_tail(scatter_stage(product, first_axis, bf16), second_axis, z_size, chip_rows, columns)


def scatter_tail(total, second_axis, z_size, chip_rows, columns):
    second = total.reshape(lax.axis_size(second_axis), z_size * chip_rows, columns)
    total = scatter_stage(lambda target: part_of(second, 0, target), second_axis, bf16)
    third = total.reshape(z_size, chip_rows, columns)
    return scatter_stage(lambda target: part_of(third, 0, target), "z", f32)


def scatter_array(array, x_first):
    y_size, x_size, z_size = lax.axis_size("y"), lax.axis_size("x"), lax.axis_size("z")
    chip_rows = D // (y_size * x_size * z_size)
    columns = array.shape[1]
    view = array.reshape(y_size, x_size, z_size * chip_rows, columns)
    first_axis, first_dim = ("x", 1) if x_first else ("y", 0)
    second_axis = "y" if x_first else "x"
    total = scatter_stage(
        lambda target: part_of(view, first_dim, target).reshape(-1, columns), first_axis, bf16
    )
    return scatter_tail(total, second_axis, z_size, chip_rows, columns)


def chain(local, up):
    count = lax.axis_size("z")
    total = jnp.zeros_like(local)
    for hop in range(1, count):
        pair = (hop - 1, hop) if up else (count - hop, count - hop - 1)
        message = (total + local).astype(bf16)
        total = total + lax.ppermute(message, "z", [pair]).astype(f32)
    return total.astype(bf16)


def norm_scale(values):
    inverse = lax.rsqrt(jnp.mean(values * values, axis=-1, keepdims=True) + norm_epsilon)
    return (values * inverse, inverse)


def norm_backward(grad_normed, scaled, inverse, gain_row):
    grad_scaled = grad_normed * gain_row[None, :]
    grad_input = inverse * (
        grad_scaled - scaled * jnp.mean(grad_scaled * scaled, axis=-1, keepdims=True)
    )
    return (grad_input, jnp.sum(grad_normed * scaled, axis=0))


def adam_update(weight, gradient, first_moment, second_moment, learn_rate, decay_rate):
    first_new = beta_first * first_moment + (1.0 - beta_first) * gradient
    second_new = beta_second * second_moment + (1.0 - beta_second) * gradient * gradient
    first_hat = first_new / (1.0 - beta_first**STEP)
    second_hat = second_new / (1.0 - beta_second**STEP)
    new_weight = (
        weight
        - learn_rate * first_hat / (jnp.sqrt(second_hat) + adam_epsilon)
        - decay_rate * weight
    )
    return (new_weight, second_new)


def local(
    tokens,
    cotangent,
    lengths,
    w_qk,
    w_value,
    w_out,
    w_gu,
    w_down,
    small_params,
    m_qk,
    m_value,
    m_out,
    m_gu,
    m_down,
    m_small,
    v_qk,
    v_value,
    v_out,
    v_gu,
    v_down,
    v_small,
):
    slots, slot_rows, _ = tokens.shape
    owned = w_qk.shape[0]
    rows = slots * slot_rows
    chip_slot = CORES * slot_rows
    chip_rows = slots * chip_slot
    core, z_at = lax.axis_index("core"), lax.axis_index("z")
    other = 1 - core

    def own_rows(array):
        return part_of(array.reshape(slots, CORES, slot_rows, -1), 1, core).reshape(rows, -1)

    def other_rows(array):
        return part_of(array.reshape(slots, CORES, slot_rows, -1), 1, other).reshape(rows, -1)

    def chip_order(mine, theirs):
        width = mine.shape[-1]
        shape = (slots, 1, slot_rows, width)
        return both_cores(mine.reshape(shape), theirs.reshape(shape), 1).reshape(chip_rows, width)

    def on_chip(array):
        return chip_order(array, swapped(array))

    columns_of = [
        w_qk.astype(bf16).reshape(owned, 2, CORES, QC),
        w_value.astype(bf16).reshape(owned, 1, CORES, VC),
        w_out.astype(bf16).reshape(owned, 1, CORES, VC),
        w_gu.astype(bf16).reshape(owned, 2, CORES, FC),
        w_down.astype(bf16).reshape(owned, 1, CORES, FC),
    ]
    small_low = jnp.pad(small_params.astype(bf16), ((0, 0), (0, LANES - (KS + 2))))

    def shard(which, index):
        parts = [part_of(columns_of[i], 2, index).reshape(owned, -1) for i in which]
        return jnp.concatenate(parts, axis=1) if len(parts) > 1 else parts[0]

    def chip_shard(which, extra=None):
        mine, theirs = shard(which, core), shard(which, other)
        arrived = swapped(theirs if extra is None else jnp.concatenate([theirs, extra], axis=1))
        mine = mine if extra is None else jnp.concatenate([mine, extra], axis=1)
        return both_cores(mine, arrived, 0)

    attention_shard = chip_shard((0, 1), small_low)
    rest_shard = chip_shard((2, 3, 4))
    half = (2 * QC + VC + LANES) // 2
    early = jnp.concatenate(
        [
            gather_rows(attention_shard[:, :half], True),
            gather_rows(attention_shard[:, half:], False),
        ],
        axis=1,
    )
    qk_full = early[:, : 2 * QC]
    value_full = early[:, 2 * QC : 2 * QC + VC]
    small_float = early[:, 2 * QC + VC :][:, : KS + 2].astype(f32)
    out_half = gather_rows(rest_shard[:, :VC], True)
    out_full = both_cores(out_half, swapped(out_half), 1)
    gate_full = gather_rows(rest_shard[:, VC : VC + FC], False)
    up_full = gather_rows(rest_shard[:, VC + FC : VC + 2 * FC], True)
    cut = FC // 2 // LANES * LANES
    down_shard = rest_shard[:, VC + 2 * FC :]
    down_pieces = (gather_rows(down_shard[:, :cut], False), gather_rows(down_shard[:, cut:], True))
    down_full = jnp.concatenate(down_pieces, axis=1)

    gain_first, gain_second = small_float[:, KS], small_float[:, KS + 1]
    taps = [part_of(small_float[:, j].reshape(CORES, VC), 0, core) for j in range(KS)]

    tokens_chip = on_chip(tokens.reshape(rows, D))
    scaled_chip, _ = norm_scale(tokens_chip.astype(f32))
    normed_chip = (scaled_chip * gain_first[None, :]).astype(bf16)
    inputs = tokens.reshape(rows, D).astype(f32)
    scaled_first, inverse_first = norm_scale(inputs)
    query_key = dot(normed_chip, qk_full).astype(bf16)
    value_pre = dot(normed_chip, value_full).astype(bf16).reshape(slots, chip_slot, VC)
    earlier = passed_along(value_pre[:, chip_slot - (KS - 1) :, :], "z", 1)
    extended = jnp.concatenate([earlier, value_pre], axis=1).astype(f32)

    def tap_rows(j):
        return extended[:, KS - 1 - j : KS - 1 - j + chip_slot, :]

    convolved = taps[0] * tap_rows(0)
    for j in range(1, KS):
        convolved = convolved + taps[j] * tap_rows(j)
    values = convolved.astype(bf16).reshape(chip_rows, VC)

    index_np, scale_np = feature_tables()
    tables = (jnp.asarray(index_np), jnp.asarray(scale_np))
    q_spec, k_spec, v_spec = (LANES, 0), (LANES, 1), (VC,)
    call = functools.partial(per_slot, slots=slots, rows=chip_slot)
    unit = 2 * chip_rows * HC * LANES * FEATS
    wide = [pltpu.VMEM((chip_slot, VC), f32)]
    (state_own,) = call(
        state_kernel, ins=[k_spec, v_spec], outs=[("state", f32)], scratch=[], flops=4 * unit
    )(*tables, query_key, values)
    before = chain(state_own, True)
    mixer, dens = call(
        forward_kernel,
        ins=[q_spec, k_spec, v_spec, "state"],
        outs=[(v_spec, bf16), ((LANES,), f32)],
        scratch=wide,
        flops=8 * unit,
    )(*tables, query_key, query_key, values, before)

    mixer_full = both_cores(mixer, swapped(mixer), 1)
    after_mixer = inputs + dot(own_rows(mixer_full), out_full)
    scaled_second, inverse_second = norm_scale(after_mixer)
    second_low = (scaled_second * gain_second[None, :]).astype(bf16)
    second_chip = on_chip(second_low)

    gate = dot(second_chip, gate_full)
    upward = dot(second_chip, up_full)
    sigmoid_gate = jax.nn.sigmoid(gate)
    silu_gate = gate * sigmoid_gate
    hidden = (silu_gate * upward).astype(bf16)

    positions = z_at * chip_slot + jnp.arange(chip_slot, dtype=jnp.int32)
    valid_chip = (positions[None, :] < lengths[:, None]).astype(f32).reshape(chip_rows, 1)
    valid = own_rows(valid_chip)
    cotangent_chip = on_chip(cotangent.reshape(rows, D))
    grad_result_chip = (valid_chip * cotangent_chip.astype(f32)).astype(bf16)
    grad_result = valid * cotangent.reshape(rows, D).astype(f32)

    scattered_down = (
        scatter_rows(jnp.transpose(grad_result_chip), hidden[:, :cut], True),
        scatter_rows(jnp.transpose(grad_result_chip), hidden[:, cut:], False),
    )
    down_other = swapped(dot_nt(other_rows(hidden), down_full))
    down_result = dot_nt(own_rows(hidden), down_full) + down_other
    layer_out = (valid * (after_mixer + down_result)).astype(bf16).reshape(tokens.shape)

    grad_hidden = dot(grad_result_chip, down_full)
    grad_upward = (grad_hidden * silu_gate).astype(bf16)
    grad_gate = (
        grad_hidden * upward * sigmoid_gate * (1.0 + gate * (1.0 - sigmoid_gate))
    ).astype(bf16)
    second_other = dot_nt(other_rows(grad_gate), gate_full) + dot_nt(
        other_rows(grad_upward), up_full
    )
    second_own = dot_nt(own_rows(grad_gate), gate_full) + dot_nt(own_rows(grad_upward), up_full)
    grad_second = second_own + swapped(second_other)
    second_t = jnp.transpose(second_chip)
    scattered_gate = scatter_rows(second_t, grad_gate, False)
    scattered_up = scatter_rows(second_t, grad_upward, True)

    grad_after_norm, grad_gain_second = norm_backward(
        grad_second, scaled_second, inverse_second, gain_second
    )
    grad_after = grad_result + grad_after_norm
    grad_after_low = grad_after.astype(bf16)
    grad_mixer = dot_nt(grad_after_low, out_full).astype(bf16).reshape(rows, CORES, VC)
    grad_mixer_chip = chip_order(
        part_of(grad_mixer, 1, core), swapped(part_of(grad_mixer, 1, other))
    )
    after_columns = grad_after_low.reshape(rows, CORES, VC)
    grad_after_chip = chip_order(
        part_of(after_columns, 1, core), swapped(part_of(after_columns, 1, other))
    )
    scattered_out = scatter_rows(jnp.transpose(mixer_full), grad_after_chip, False)

    wide_spec = (HC * LANES,)
    pulled, grad_num = call(
        pull_kernel,
        ins=[q_spec, v_spec, v_spec, (LANES,)],
        outs=[("state", f32), (wide_spec, bf16)],
        scratch=[],
        flops=4 * unit,
    )(*tables, query_key, grad_mixer_chip, mixer, dens)
    after = chain(pulled, False)
    grad_query_key, grad_values = call(
        backward_kernel,
        ins=[q_spec, k_spec, v_spec, wide_spec, "state", "state"],
        outs=[((2 * LANES,), bf16), (v_spec, bf16)],
        scratch=wide,
        flops=24 * unit,
    )(*tables, query_key, query_key, values, grad_num, before, after)

    grad_values = grad_values.reshape(slots, chip_slot, VC)
    later = passed_along(grad_values[:, : KS - 1, :], "z", -1)
    grad_extended = jnp.concatenate([grad_values, later], axis=1).astype(f32)
    grad_pre = taps[0] * grad_extended[:, :chip_slot, :]
    for j in range(1, KS):
        grad_pre = grad_pre + taps[j] * grad_extended[:, j : j + chip_slot, :]
    grad_pre = grad_pre.reshape(chip_rows, VC).astype(bf16)
    grad_values_float = grad_values.astype(f32)
    tap_grads = [jnp.sum(grad_values_float * tap_rows(j), axis=(0, 1)) for j in range(KS)]

    first_other = dot_nt(other_rows(grad_query_key), qk_full) + dot_nt(
        other_rows(grad_pre), value_full
    )
    first_own = dot_nt(own_rows(grad_query_key), qk_full) + dot_nt(own_rows(grad_pre), value_full)
    grad_first = first_own + swapped(first_other)
    normed_t = jnp.transpose(normed_chip)
    scattered_value = scatter_rows(normed_t, grad_pre, True)
    scattered_qk = scatter_rows(normed_t, grad_query_key, False)
    grad_input_norm, grad_gain_first = norm_backward(
        grad_first, scaled_first, inverse_first, gain_first
    )
    input_grad = (grad_after + grad_input_norm).reshape(tokens.shape)

    def whole_feature(part):
        return lax.dynamic_update_slice(jnp.zeros((D,), f32), part, (core * VC,))

    small_terms = jnp.stack(
        [whole_feature(part) for part in tap_grads] + [grad_gain_first, grad_gain_second], axis=1
    )
    small_terms = jnp.pad(small_terms, ((0, 0), (0, LANES - (KS + 2)))).astype(bf16)
    scattered_small = scatter_array(small_terms, True)

    def rows_of(array, index):
        return part_of(array.reshape(CORES, owned, -1), 0, index)

    def finish(*parts):
        merged = jnp.concatenate(parts, axis=1) if len(parts) > 1 else parts[0]
        return rows_of(merged, core), swapped(rows_of(merged, other))

    def columns(*parts):
        mine, theirs = finish(*parts)
        return both_cores(mine, theirs, 1)

    def two_columns(mine, theirs, width):
        shape = (owned, 2, 1, width)
        return both_cores(mine.reshape(shape), theirs.reshape(shape), 2).reshape(owned, -1)

    grad_down_own = columns(*scattered_down)
    grad_gu_own = two_columns(*finish(scattered_gate, scattered_up), FC)
    grad_out_own = columns(scattered_out)
    grad_value_own = columns(scattered_value)
    grad_qk_own = two_columns(*finish(scattered_qk), QC)
    small_mine, small_theirs = finish(scattered_small)
    grad_small_own = (small_mine + small_theirs)[:, : KS + 2]

    grads_all = (
        grad_qk_own,
        grad_value_own,
        grad_out_own,
        grad_gu_own,
        grad_down_own,
        grad_small_own,
    )
    masters = (w_qk, w_value, w_out, w_gu, w_down, small_params)
    firsts = (m_qk, m_value, m_out, m_gu, m_down, m_small)
    seconds = (v_qk, v_value, v_out, v_gu, v_down, v_small)
    learn_rates = (
        0.05 / math.sqrt(D),
        0.05 / math.sqrt(D),
        0.05 / math.sqrt(max(D // 128, 1)),
        0.05 / math.sqrt(D),
        0.05 / math.sqrt(0.0003 * FF * SLOT**0.825),
        0.014,
    )
    decays = (weight_decay, weight_decay, weight_decay, weight_decay, weight_decay, 0.0)
    new_weights = []
    new_seconds = []
    for position in range(6):
        updated, moment = adam_update(
            masters[position],
            grads_all[position],
            firsts[position],
            seconds[position],
            learn_rates[position],
            decays[position],
        )
        new_weights.append(updated)
        new_seconds.append(moment)
    return (layer_out, input_grad) + grads_all + tuple(new_weights) + tuple(new_seconds)


def solution(mesh):
    dp, fsdp = mesh.shape["dp"], mesh.shape["fsdp"]
    y_size = 2 if dp % 2 == 0 else 1
    split = Mesh(
        mesh.devices.reshape(y_size, dp // y_size, fsdp // CORES, CORES), ("y", "x", "z", "core")
    )
    slot_axes, row_axes = ("y", "x"), ("z", "core")
    activation = P(slot_axes, row_axes, None)
    weight = P(slot_axes + row_axes, None)
    return jax.shard_map(
        local,
        mesh=split,
        in_specs=(activation, activation, P(slot_axes)) + (weight,) * 18,
        out_specs=(activation, activation) + (weight,) * 18,
        check_vma=False,
    )
```

time: 2890 us -> 1150 us (0.40)
  waiting for transfers between devices: 2000 us -> 374 us
  starting transfers between devices: 9.73 us -> 172 us
  matrix products: 335 us -> 196 us
  other arithmetic: 206 us -> 107 us
  blocking collectives: 76.3 us -> 0 us
  Pallas kernels: 0 us -> 59.3 us
    all_to_all x1 -> x0, waiting for transfers between devices: 1430 us -> none  [local(): lax.all_to_all(gradient_terms.reshape(dp_count * fsdp_count, owned_rows,...]
    all_gather x7 -> x0, waiting for transfers between devices: 569 us -> none  [the longest x1 224 us: prefix(): pieces = jax.tree.map(lambda part: lax.all_gather(part, axis), value)]
    ppermute x0 -> x99, waiting for transfers between devices: none -> 373 us  [the longest x75 369 us: shifted(): lax.ppermute(array, axis, [(i, (i + by) % count) for i in range(count)])]
    ppermute x0 -> x99, starting transfers between devices: none -> 169 us  [the longest x75 158 us: shifted(): lax.ppermute(array, axis, [(i, (i + by) % count) for i in range(count)])]
    concatenate x7 -> x2, local copies, waits for them, and re-layouts: 147 us -> 1.53 us  [both_cores(): jnp.concatenate([jnp.where(first, mine, theirs), jnp.where(first, theirs,...]
    dot_general x29 -> x31, matrix products: 335 us -> 196 us  [the longest x20 119 us: dot(): lax.dot_general(a, b, (((1,), (0,)), ((), ())), preferred_element_type=f32)]
    select_n x30 -> x14, other arithmetic: 96.2 us -> 17 us  [both_cores(): jnp.where(first, mine, theirs)]
    all_gather x3 -> x0, blocking collectives: 76.3 us -> none  [the longest x1 43.5 us: local(): lax.all_gather(small_params.astype(jnp.bfloat16), ('dp', 'fsdp'), axis=0,...]
  transfers between devices with their start and end apart: 10 -> 101, of which waited for: 7 -> 47; matrix products, arithmetic and copies ran while one was open for 12% -> 37% of each run, Pallas kernels for 0% -> 5%
where the time goes in v1:
time: 1150 us; the launch traced here: 1140 us
  waiting for transfers between devices  374 us (33%)
  local copies, waits for them, and re-layouts  226 us (20%)
  matrix products  196 us (17%)
  starting transfers between devices  172 us (15%)
  other arithmetic  107 us (9%)
  Pallas kernels  59.3 us (5%)
    ppermute x75, waiting for transfers between devices, shifted(): lax.ppermute(array, axis, [(i, (i + by) % count) for i in range(count)])  369 us
    ppermute x75, starting transfers between devices, shifted(): lax.ppermute(array, axis, [(i, (i + by) % count) for i in range(count)])  158 us
    dot_general x20, matrix products, dot(): lax.dot_general(a, b, (((1,), (0,)), ((), ())), preferred_element_type=f32)  119 us
    dot_general x11, matrix products, dot_nt(): lax.dot_general(a, b, (((1,), (1,)), ((), ())), preferred_element_type=f32)  76.9 us
    dynamic_update_slice x49, local copies, waits for them, and re-layouts, gather_stage(): whole = lax.dynamic_update_index_in_dim(whole, block, source, dim)  71.7 us
    dynamic_slice x25, local copies, waits for them, and re-layouts, part_of(): return lax.dynamic_index_in_dim(array, index, axis, keepdims=False)  54.2 us
    pallas_call x1, Pallas kernels, local(): call(backward_kernel, ins=[q_spec, k_spec, v_spec, wide_spec, 'state', 's...  28.2 us
    unnamed x285, local copies, waits for them, and re-layouts  23.9 us
  transfers between devices with their start and end apart: 101, of which 47 were waited for; matrix products, arithmetic and copies ran while one was open for 37% of the time, Pallas kernels for 5%

profile of v1, /device:TPU:0, one launch (start us, length us, event | category | flops | bytes accessed | tf_op | source)
XLA Modules:
  0.0 1138.7 jit_solution(5057966359269493625)
XLA Ops:
  2.7 7.5 dynamic-slice_reduce_fusion.1
  30.1 6.7 collective-permute-done.2
  42.1 4.9 collective-permute-start.4
  92.9 6.3 collective-permute-done.19
  99.1 5.6 collective-permute-start.20
  112.3 5.9 collective-permute-done.35
  119.0 11.3 collective-permute-done.36
  148.9 15.4 %collective-permute-done.41 = bf16[112,1280]{1,0:T(8,128)(2,1)S(1)} collective-permute-done((bf16[112,1280]{1,0:T(8,128)(2,1)S(1)}, bf16[112,1280]{1,0:T(8,128)(2,1)S(1)}, u32[]{:S(2)}, u32[]{:S(2)}) %collective-permute-start.41) | collective-permute-done | bytes 286752 | tf_op jit(solution)/shard_map/ppermute | solution.py:244
  165.0 6.9 collective-permute-done.42
  172.0 5.5 collective-permute-start.25
  188.5 21.3 %collective-permute-done.26 = bf16[112,2432]{1,0:T(8,128)(2,1)S(1)} collective-permute-done((bf16[112,2432]{1,0:T(8,128)(2,1)S(1)}, bf16[112,2432]{1,0:T(8,128)(2,1)S(1)}, u32[]{:S(2)}, u32[]{:S(2)}) %collective-permute-start.26) | collective-permute-done | bytes 544800 | tf_op jit(solution)/shard_map/ppermute | solution.py:244
  210.7 10.7 collective-permute-done.27
  227.7 5.4 collective-permute-done.30
  233.1 7.0 collective-permute-start.31
  241.0 17.2 %collective-permute-done.31 = bf16[112,2432]{1,0:T(8,128)(2,1)S(1)} collective-permute-done((bf16[112,2432]{1,0:T(8,128)(2,1)S(1)}, bf16[112,2432]{1,0:T(8,128)(2,1)S(1)}, u32[]{:S(2)}, u32[]{:S(2)}) %collective-permute-start.31) | collective-permute-done | bytes 544800 | tf_op jit(solution)/shard_map/ppermute | solution.py:244
  262.8 6.1 collective-permute-done.32
  287.4 6.0 copy.130
  319.0 5.9 copy.124
  324.8 7.1 constant_dynamic-slice_fusion.11
  340.7 8.5 shard_map.374
  370.5 12.9 %collective-permute-done.22 = bf16[2,4,112,896]{3,2,1,0:T(8,128)(2,1)S(1)} collective-permute-done((bf16[2,4,112,896]{3,2,1,0:T(8,128)(2,1)S(1)}, bf16[2,4,112,896]{3,2,1,0:T(8,128)(2,1)S(1)}, u32[]{:S(2)}, u32[]{:S(2)}) %collective-permute-start.22) | collective-permute-done | bytes 1605664 | tf_op jit(solution)/shard_map/ppermute | solution.py:244
  406.2 12.0 %shard_map.375 = (bf16[1024,896]{1,0:T(8,128)(2,1)}, f32[1024,128]{1,0:T(8,128)}) custom-call(s32[8,256]{1,0:T(8,128)} %constant.755.clone.index_ref, f32[8,256]{1,0:T(8,128)} %constant.756.clone.scale_ref, bf16[1024,256]{1,0:T(8,128)(2,1)} %convolution_convert_fusion.13.k_ref.q_ref, bf16[1024,256]{1,0:T(8,128)(2,1)} %convolution_convert_fusion.13.k_ref.q_ref, ...), custom_call_target="tpu_custom_call" | custom-call | flops 4294967296 | bytes 8388608 | tf_op jit(solution)/shard_map/pallas_call | solution.py:489
  421.5 11.1 collective-permute-done.44
  434.5 16.1 %fusion.21 = f32[1024,2432]{1,0:T(8,128)} fusion(bf16[1024,1792]{1,0:T(8,128)(2,1)S(1)} %copy-done.13, bf16[1792,1280]{1,0:T(8,128)(2,1)S(1)} %bitcast.529, bf16[1792,1152]{1,0:T(8,128)(2,1)} %bitcast.542), kind=kOutput, calls=%fused_computation.78 | convolution fusion | flops 8942911488 | bytes 22347776 | tf_op jit(solution)/shard_map/dot_general | solution.py:62
  454.2 6.3 copy.125
  462.3 5.3 broadcast_select_fusion.1
  467.6 6.7 multiply_reduce_fusion.4
  474.9 14.0 %collective-permute-done.29 = bf16[2,4,112,2432]{3,2,1,0:T(8,128)(2,1)} collective-permute-done((bf16[2,4,112,2432]{3,2,1,0:T(8,128)(2,1)}, bf16[2,4,112,2432]{3,2,1,0:T(8,128)(2,1)}, u32[]{:S(2)}, u32[]{:S(2)}) %collective-permute-start.29) | collective-permute-done | bytes 4358176 | tf_op jit(solution)/shard_map/ppermute | solution.py:244
  491.7 22.3 %collective-permute-done.34 = bf16[2,4,112,2432]{3,2,1,0:T(8,128)(2,1)} collective-permute-done((bf16[2,4,112,2432]{3,2,1,0:T(8,128)(2,1)}, bf16[2,4,112,2432]{3,2,1,0:T(8,128)(2,1)}, u32[]{:S(2)}, u32[]{:S(2)}) %collective-permute-start.34) | collective-permute-done | bytes 4358176 | tf_op jit(solution)/shard_map/ppermute | solution.py:244
  520.3 12.0 %fusion.75 = f32[1024,2432]{1,0:T(8,128)} fusion(bf16[1024,1792]{1,0:T(8,128)(2,1)S(1)} %bitcast.472, bf16[1792,2432]{1,0:T(8,128)(2,1)S(1)} %bitcast.489), kind=kOutput, calls=%fused_computation.399 | convolution fusion | flops 8925478912 | bytes 22347776 | tf_op jit(solution)/shard_map/dot_general | solution.py:62
  532.4 24.9 %multiply_convert_fusion.1 = (bf16[1024,2432]{1,0:T(8,128)(2,1)}, bf16[1024,2432]{1,0:T(8,128)(2,1)}, bf16[1024,2432]{1,0:T(8,128)(2,1)}) fusion(f32[1024,2432]{1,0:T(8,128)} %fusion.21, f32[1024,2432]{1,0:T(8,128)} %fusion.75, bf16[1024,1792]{1,0:T(8,128)(2,1)} %bitcast.473, bf16[1792,2432]{1,0:T(8,128)(2,1)} %bitcast.482), kind=kOutput, calls=%fused_computation.1 | convolution fusion | flops 8962834432 | bytes 47251456 | tf_op jit(solution)/shard_map/dot_general | solution.py:62
  560.3 10.3 fusion.77
  573.6 8.6 fusion.76
  582.2 6.8 fusion.78
  589.0 9.7 convolution_add_fusion.1
  614.5 6.0 copy.129
  620.5 6.1 constant_dynamic-slice_fusion.16
  626.6 6.5 convolution_convert_fusion.3
  633.1 6.5 convolution_convert_fusion.2
  645.1 7.0 convolution_convert_fusion.1
  652.1 8.5 fusion.22
  669.7 18.4 %collective-permute-done.85 = bf16[448,1152]{1,0:T(8,128)(2,1)S(1)} collective-permute-done((bf16[448,1152]{1,0:T(8,128)(2,1)S(1)}, bf16[448,1152]{1,0:T(8,128)(2,1)S(1)}, u32[]{:S(2)}, u32[]{:S(2)}) %collective-permute-start.85) | collective-permute-done | bytes 1032224 | tf_op jit(solution)/shard_map/ppermute | solution.py:244
  693.9 6.1 collective-permute-done.86
  701.0 6.4 convolution_convert_fusion
  718.3 4.9 collective-permute-start.92
  723.3 5.7 multiply_reduce_fusion.1
  735.2 10.4 multiply_convert_fusion.3
  745.6 7.7 fusion.20
  759.3 5.6 constant_dynamic-slice_fusion.31
  780.3 25.3 %collective-permute-done.73 = bf16[896,2432]{1,0:T(8,128)(2,1)} collective-permute-done((bf16[896,2432]{1,0:T(8,128)(2,1)}, bf16[896,2432]{1,0:T(8,128)(2,1)}, u32[]{:S(2)}, u32[]{:S(2)}) %collective-permute-start.73) | collective-permute-done | bytes 4358176 | tf_op jit(solution)/shard_map/ppermute | solution.py:244
  813.1 10.6 shard_map.376
  844.3 27.1 %collective-permute-done.67 = bf16[896,896]{1,0:T(8,128)(2,1)S(1)} collective-permute-done((bf16[896,896]{1,0:T(8,128)(2,1)}, bf16[896,896]{1,0:T(8,128)(2,1)S(1)}, u32[]{:S(2)}, u32[]{:S(2)}) %collective-permute-start.67) | collective-permute-done | bytes 1605664 | tf_op jit(solution)/shard_map/ppermute | solution.py:244
  879.7 36.1 %collective-permute-done.79 = bf16[448,2432]{1,0:T(8,128)(2,1)S(1)} collective-permute-done((bf16[448,2432]{1,0:T(8,128)(2,1)S(1)}, bf16[448,2432]{1,0:T(8,128)(2,1)S(1)}, u32[]{:S(2)}, u32[]{:S(2)}) %collective-permute-start.79) | collective-permute-done | bytes 2179104 | tf_op jit(solution)/shard_map/ppermute | solution.py:244
  921.5 28.2 %shard_map.377 = (bf16[1024,256]{1,0:T(8,128)(2,1)}, bf16[1024,896]{1,0:T(8,128)(2,1)}) custom-call(s32[8,256]{1,0:T(8,128)} %constant.755.clone.index_ref, f32[8,256]{1,0:T(8,128)} %constant.756.clone.scale_ref, bf16[1024,256]{1,0:T(8,128)(2,1)} %convolution_convert_fusion.13.k_ref.q_ref, bf16[1024,256]{1,0:T(8,128)(2,1)} %convolution_convert_fusion.13.k_ref.q_ref, ...), custom_call_target="tpu_custom_call" | custom-call | flops 12884901888 | bytes 8388608 | tf_op jit(solution)/shard_map/pallas_call | solution.py:562
  985.5 10.3 collective-permute-done.80
  995.8 20.6 %collective-permute-start.69 = (bf16[112,896]{1,0:T(8,128)(2,1)}, bf16[112,896]{1,0:T(8,128)(2,1)}, u32[]{:S(2)}, u32[]{:S(2)}) collective-permute-start(bf16[112,896]{1,0:T(8,128)(2,1)} %get-tuple-element.185), channel_id=1, source_target_pairs={{0,2},{2,4},{4,6},{6,0},{1,3},{3,5},{5,7},{7,1},{8,10},{10,12},{12... | collective-permute-start | bytes 602120 | tf_op jit(solution)/shard_map/ppermute | solution.py:244
  1021.6 4.8 collective-permute-done.55
  1026.4 13.4 %collective-permute-start.71 = (bf16[112,896]{1,0:T(8,128)(2,1)S(1)}, bf16[112,896]{1,0:T(8,128)(2,1)S(1)}, u32[]{:S(2)}, u32[]{:S(2)}) collective-permute-start(bf16[112,896]{1,0:T(8,128)(2,1)S(1)} %get-tuple-element.183), channel_id=1, source_target_pairs={{0,6},{2,0},{4,2},{6,4},{1,7},{3,1},{5,3},{7,5},{8,14},{10,8},{12,... | collective-permute-start | bytes 602120 | tf_op jit(solution)/shard_map/ppermute | solution.py:244
  1072.3 10.8 collective-permute-done.61
  1088.9 6.8 multiply_subtract_fusion
  1095.6 5.6 collective-permute-done.63
  1102.2 6.2 fusion.13
  1110.7 6.3 collective-permute-done.95
  1131.9 6.0 fusion.12
  (723 shorter events, 460.8 us)
Async XLA Ops:
  14.0 60.0 %collective-permute-start.17 = (bf16[56,8192]{1,0:T(8,128)(2,1)}, bf16[56,8192]{1,0:T(8,128)(2,1)}, u32[]{:S(2)}, u32[]{:S(2)}) collective-permute-start(bf16[56,8192]{1,0:T(8,128)(2,1)} %pad_maximum_fusion.21), channel_id=1, source_target_pairs={{0,1},{1,0},{2,3},{3,2},{4,5},{5,4},{6,7},{7,6},{8,9},{9,8},{10,11... | collective-permute-start | bytes 2752520 | tf_op jit(solution)/shard_map/ppermute | solution.py:261
  17.6 257.8 %collective-permute-start = (bf16[512,1792]{1,0:T(8,128)(2,1)S(1)}, bf16[512,1792]{1,0:T(8,128)(2,1)}, u32[]{:S(2)}, u32[]{:S(2)}) collective-permute-start(bf16[512,1792]{1,0:T(8,128)(2,1)S(1)} %bitcast.468), channel_id=1, source_target_pairs={{0,1},{1,0},{2,3},{3,2},{4,5},{5,4},{6,7},{7,6},{8,9},{9,8},{10,11... | collective-permute-start | bytes 5505032 | tf_op jit(solution)/shard_map/ppermute | solution.py:261
  18.1 261.2 %collective-permute-start.46 = (bf16[512,1792]{1,0:T(8,128)(2,1)}, bf16[512,1792]{1,0:T(8,128)(2,1)}, u32[]{:S(2)}, u32[]{:S(2)}) collective-permute-start(bf16[512,1792]{1,0:T(8,128)(2,1)} %bitcast.511), channel_id=1, source_target_pairs={{0,1},{1,0},{2,3},{3,2},{4,5},{5,4},{6,7},{7,6},{8,9},{9,8},{10,11... | collective-permute-start | bytes 5505032 | tf_op jit(solution)/shard_map/ppermute | solution.py:261
  26.0 12.7 %collective-permute-start.8 = (bf16[112,640]{1,0:T(8,128)(2,1)}, bf16[112,640]{1,0:T(8,128)(2,1)S(1)}, u32[]{:S(2)}, u32[]{:S(2)}) collective-permute-start(bf16[112,640]{1,0:T(8,128)(2,1)} %get-tuple-element.98), channel_id=1, source_target_pairs={{0,4},{2,6},{4,0},{6,2},{1,5},{3,7},{5,1},{7,3},{8,12},{10,14},{12... | collective-permute-start | bytes 430088 | tf_op jit(solution)/shard_map/ppermute | solution.py:244
  38.7 12.6 %collective-permute-start.3 = (bf16[112,640]{1,0:T(8,128)(2,1)S(1)}, bf16[112,640]{1,0:T(8,128)(2,1)S(1)}, u32[]{:S(2)}, u32[]{:S(2)}) collective-permute-start(bf16[112,640]{1,0:T(8,128)(2,1)S(1)} %get-tuple-element.100), channel_id=1, source_target_pairs={{0,4},{2,6},{4,0},{6,2},{1,5},{3,7},{5,1},{7,3},{8,12},{10,14},{12... | collective-permute-start | bytes 430088 | tf_op jit(solution)/shard_map/ppermute | solution.py:244
  52.8 15.0 %collective-permute-start.5 = (bf16[4,112,640]{2,1,0:T(8,128)(2,1)S(1)}, bf16[4,112,640]{2,1,0:T(8,128)(2,1)S(1)}, u32[]{:S(2)}, u32[]{:S(2)}) collective-permute-start(bf16[4,112,640]{2,1,0:T(8,128)(2,1)S(1)} %bitcast_dynamic-update-slice_fusion.52), channel_id=1, source_target_pairs={{0,16},{16,0},{1,17},{17,1},{2,18},{18,2},{3,19},{19,3},{4,20},{20... | collective-permute-start | bytes 1720328 | tf_op jit(solution)/shard_map/ppermute | solution.py:244
  63.5 245.0 %collective-permute-start.11 = (bf16[2,4,112,640]{3,2,1,0:T(8,128)(2,1)}, bf16[2,4,112,640]{3,2,1,0:T(8,128)(2,1)}, u32[]{:S(2)}, u32[]{:S(2)}) collective-permute-start(bf16[2,4,112,640]{3,2,1,0:T(8,128)(2,1)} %bitcast_dynamic-update-slice_fusion.24), channel_id=1, source_target_pairs={{0,16},{16,0},{1,17},{17,1},{2,18},{18,2},{3,19},{19,3},{4,20},{20... | collective-permute-start | bytes 3440648 | tf_op jit(solution)/shard_map/ppermute | solution.py:244
  68.6 234.2 %collective-permute-start.6 = (bf16[2,4,112,640]{3,2,1,0:T(8,128)(2,1)}, bf16[2,4,112,640]{3,2,1,0:T(8,128)(2,1)}, u32[]{:S(2)}, u32[]{:S(2)}) collective-permute-start(bf16[2,4,112,640]{3,2,1,0:T(8,128)(2,1)} %bitcast_dynamic-update-slice_fusion.26), channel_id=1, source_target_pairs={{0,8},{8,0},{1,9},{9,1},{2,10},{10,2},{3,11},{11,3},{4,12},{12,4},... | collective-permute-start | bytes 3440648 | tf_op jit(solution)/shard_map/ppermute | solution.py:244
  147.9 16.4 %collective-permute-start.41 = (bf16[112,1280]{1,0:T(8,128)(2,1)S(1)}, bf16[112,1280]{1,0:T(8,128)(2,1)S(1)}, u32[]{:S(2)}, u32[]{:S(2)}) collective-permute-start(bf16[112,1280]{1,0:T(8,128)(2,1)S(1)} %get-tuple-element.90), channel_id=1, source_target_pairs={{0,4},{2,6},{4,0},{6,2},{1,5},{3,7},{5,1},{7,3},{8,12},{10,14},{12... | collective-permute-start | bytes 860168 | tf_op jit(solution)/shard_map/ppermute | solution.py:244
  172.0 12.4 %collective-permute-start.25 = (bf16[112,2432]{1,0:T(8,128)(2,1)S(1)}, bf16[112,2432]{1,0:T(8,128)(2,1)S(1)}, u32[]{:S(2)}, u32[]{:S(2)}) collective-permute-start(bf16[112,2432]{1,0:T(8,128)(2,1)S(1)} %get-tuple-element.92), channel_id=1, source_target_pairs={{0,2},{2,4},{4,6},{6,0},{1,3},{3,5},{5,7},{7,1},{8,10},{10,12},{12... | collective-permute-start | bytes 1634312 | tf_op jit(solution)/shard_map/ppermute | solution.py:244
  184.4 25.4 %collective-permute-start.26 = (bf16[112,2432]{1,0:T(8,128)(2,1)S(1)}, bf16[112,2432]{1,0:T(8,128)(2,1)S(1)}, u32[]{:S(2)}, u32[]{:S(2)}) collective-permute-start(bf16[112,2432]{1,0:T(8,128)(2,1)S(1)} %get-tuple-element.92), channel_id=1, source_target_pairs={{0,4},{2,6},{4,0},{6,2},{1,5},{3,7},{5,1},{7,3},{8,12},{10,14},{12... | collective-permute-start | bytes 1634312 | tf_op jit(solution)/shard_map/ppermute | solution.py:244
  233.1 25.0 %collective-permute-start.31 = (bf16[112,2432]{1,0:T(8,128)(2,1)S(1)}, bf16[112,2432]{1,0:T(8,128)(2,1)S(1)}, u32[]{:S(2)}, u32[]{:S(2)}) collective-permute-start(bf16[112,2432]{1,0:T(8,128)(2,1)S(1)} %get-tuple-element.94), channel_id=1, source_target_pairs={{0,4},{2,6},{4,0},{6,2},{1,5},{3,7},{5,1},{7,3},{8,12},{10,14},{12... | collective-permute-start | bytes 1634312 | tf_op jit(solution)/shard_map/ppermute | solution.py:244
  268.9 29.4 %collective-permute-start.21 = (bf16[4,112,896]{2,1,0:T(8,128)(2,1)}, bf16[4,112,896]{2,1,0:T(8,128)(2,1)}, u32[]{:S(2)}, u32[]{:S(2)}) collective-permute-start(bf16[4,112,896]{2,1,0:T(8,128)(2,1)} %bitcast_dynamic-update-slice_fusion.44), channel_id=1, source_target_pairs={{0,8},{8,0},{1,9},{9,1},{2,10},{10,2},{3,11},{11,3},{4,12},{12,4},... | collective-permute-start | bytes 2408456 | tf_op jit(solution)/shard_map/ppermute | solution.py:244
  275.5 75.2 %collective-permute-start.38 = (bf16[4,112,1152]{2,1,0:T(8,128)(2,1)}, bf16[4,112,1152]{2,1,0:T(8,128)(2,1)}, u32[]{:S(2)}, u32[]{:S(2)}) collective-permute-start(bf16[4,112,1152]{2,1,0:T(8,128)(2,1)} %bitcast_dynamic-update-slice_fusion.40), channel_id=1, source_target_pairs={{0,16},{16,0},{1,17},{17,1},{2,18},{18,2},{3,19},{19,3},{4,20},{20... | collective-permute-start | bytes 3096584 | tf_op jit(solution)/shard_map/ppermute | solution.py:244
  279.3 84.3 %collective-permute-start.43 = (bf16[4,112,1280]{2,1,0:T(8,128)(2,1)}, bf16[4,112,1280]{2,1,0:T(8,128)(2,1)}, u32[]{:S(2)}, u32[]{:S(2)}) collective-permute-start(bf16[4,112,1280]{2,1,0:T(8,128)(2,1)} %bitcast_dynamic-update-slice_fusion.36), channel_id=1, source_target_pairs={{0,8},{8,0},{1,9},{9,1},{2,10},{10,2},{3,11},{11,3},{4,12},{12,4},... | collective-permute-start | bytes 3440648 | tf_op jit(solution)/shard_map/ppermute | solution.py:244
  298.3 87.0 %collective-permute-start.28 = (bf16[4,112,2432]{2,1,0:T(8,128)(2,1)}, bf16[4,112,2432]{2,1,0:T(8,128)(2,1)}, u32[]{:S(2)}, u32[]{:S(2)}) collective-permute-start(bf16[4,112,2432]{2,1,0:T(8,128)(2,1)} %bitcast_dynamic-update-slice_fusion.32), channel_id=1, source_target_pairs={{0,16},{16,0},{1,17},{17,1},{2,18},{18,2},{3,19},{19,3},{4,20},{20... | collective-permute-start | bytes 6537224 | tf_op jit(solution)/shard_map/ppermute | solution.py:244
  302.9 89.1 %collective-permute-start.33 = (bf16[4,112,2432]{2,1,0:T(8,128)(2,1)}, bf16[4,112,2432]{2,1,0:T(8,128)(2,1)}, u32[]{:S(2)}, u32[]{:S(2)}) collective-permute-start(bf16[4,112,2432]{2,1,0:T(8,128)(2,1)} %bitcast_dynamic-update-slice_fusion.28), channel_id=1, source_target_pairs={{0,8},{8,0},{1,9},{9,1},{2,10},{10,2},{3,11},{11,3},{4,12},{12,4},... | collective-permute-start | bytes 6537224 | tf_op jit(solution)/shard_map/ppermute | solution.py:244
  317.2 17.1 %collective-permute-start.12 = (bf16[2,2,896]{2,1,0:T(2,128)(2,1)S(1)}, bf16[2,2,896]{2,1,0:T(2,128)(2,1)S(1)}, u32[]{:S(2)}, u32[]{:S(2)}) collective-permute-start(bf16[2,2,896]{2,1,0:T(2,128)(2,1)S(1)} %slice.118), channel_id=1, source_target_pairs={{0,2},{2,4},{4,6},{1,3},{3,5},{5,7},{8,10},{10,12},{12,14},{9,11},... | collective-permute-start | bytes 21512 | tf_op jit(solution)/shard_map/ppermute | solution.py:250
  334.4 49.0 %collective-permute-start.22 = (bf16[2,4,112,896]{3,2,1,0:T(8,128)(2,1)S(1)}, bf16[2,4,112,896]{3,2,1,0:T(8,128)(2,1)S(1)}, u32[]{:S(2)}, u32[]{:S(2)}) collective-permute-start(bf16[2,4,112,896]{3,2,1,0:T(8,128)(2,1)S(1)} %bitcast_dynamic-update-slice_fusion.22), channel_id=1, source_target_pairs={{0,16},{16,0},{1,17},{17,1},{2,18},{18,2},{3,19},{19,3},{4,20},{20... | collective-permute-start | bytes 4816904 | tf_op jit(solution)/shard_map/ppermute | solution.py:244
  362.6 55.6 %collective-permute-start.39 = (bf16[2,4,112,1152]{3,2,1,0:T(8,128)(2,1)}, bf16[2,4,112,1152]{3,2,1,0:T(8,128)(2,1)}, u32[]{:S(2)}, u32[]{:S(2)}) collective-permute-start(bf16[2,4,112,1152]{3,2,1,0:T(8,128)(2,1)} %bitcast_dynamic-update-slice_fusion.20), channel_id=1, source_target_pairs={{0,8},{8,0},{1,9},{9,1},{2,10},{10,2},{3,11},{11,3},{4,12},{12,4},... | collective-permute-start | bytes 6193160 | tf_op jit(solution)/shard_map/ppermute | solution.py:244
  369.0 63.6 %collective-permute-start.44 = (bf16[2,4,112,1280]{3,2,1,0:T(8,128)(2,1)}, bf16[2,4,112,1280]{3,2,1,0:T(8,128)(2,1)}, u32[]{:S(2)}, u32[]{:S(2)}) collective-permute-start(bf16[2,4,112,1280]{3,2,1,0:T(8,128)(2,1)} %bitcast_dynamic-update-slice_fusion.15), channel_id=1, source_target_pairs={{0,16},{16,0},{1,17},{17,1},{2,18},{18,2},{3,19},{19,3},{4,20},{20... | collective-permute-start | bytes 6881288 | tf_op jit(solution)/shard_map/ppermute | solution.py:244
  383.3 21.7 %collective-permute-start.15 = (bf16[2,8,160,128]{3,2,1,0:T(8,128)(2,1)}, bf16[2,8,160,128]{3,2,1,0:T(8,128)(2,1)S(1)}, u32[]{:S(2)}, u32[]{:S(2)}) collective-permute-start(bf16[2,8,160,128]{3,2,1,0:T(8,128)(2,1)} %add_convert_fusion.16), channel_id=1, source_target_pairs={{4,6},{5,7},{12,14},{13,15},{20,22},{21,23},{28,30},{29,31}} | collective-permute-start | bytes 1966088 | tf_op jit(solution)/shard_map/ppermute | solution.py:342
  385.3 76.9 %collective-permute-start.23 = (bf16[1792,896]{1,0:T(8,128)(2,1)}, bf16[1792,896]{1,0:T(8,128)(2,1)}, u32[]{:S(2)}, u32[]{:S(2)}) collective-permute-start(bf16[1792,896]{1,0:T(8,128)(2,1)} %bitcast.37), channel_id=1, source_target_pairs={{0,1},{1,0},{2,3},{3,2},{4,5},{5,4},{6,7},{7,6},{8,9},{9,8},{10,11... | collective-permute-start | bytes 9633800 | tf_op jit(solution)/shard_map/ppermute | solution.py:261
  392.0 96.9 %collective-permute-start.29 = (bf16[2,4,112,2432]{3,2,1,0:T(8,128)(2,1)}, bf16[2,4,112,2432]{3,2,1,0:T(8,128)(2,1)}, u32[]{:S(2)}, u32[]{:S(2)}) collective-permute-start(bf16[2,4,112,2432]{3,2,1,0:T(8,128)(2,1)} %bitcast_dynamic-update-slice_fusion.8), channel_id=1, source_target_pairs={{0,8},{8,0},{1,9},{9,1},{2,10},{10,2},{3,11},{11,3},{4,12},{12,4},... | collective-permute-start | bytes 13074440 | tf_op jit(solution)/shard_map/ppermute | solution.py:244
  405.0 109.0 %collective-permute-start.34 = (bf16[2,4,112,2432]{3,2,1,0:T(8,128)(2,1)}, bf16[2,4,112,2432]{3,2,1,0:T(8,128)(2,1)}, u32[]{:S(2)}, u32[]{:S(2)}) collective-permute-start(bf16[2,4,112,2432]{3,2,1,0:T(8,128)(2,1)} %bitcast_dynamic-update-slice_fusion.6), channel_id=1, source_target_pairs={{0,16},{16,0},{1,17},{17,1},{2,18},{18,2},{3,19},{19,3},{4,20},{20... | collective-permute-start | bytes 13074440 | tf_op jit(solution)/shard_map/ppermute | solution.py:244
  418.2 32.4 %collective-permute-start.16 = (bf16[1024,896]{1,0:T(8,128)(2,1)}, bf16[1024,896]{1,0:T(8,128)(2,1)S(1)}, u32[]{:S(2)}, u32[]{:S(2)}) collective-permute-start(bf16[1024,896]{1,0:T(8,128)(2,1)} %get-tuple-element.26.mixer_ref), channel_id=1, source_target_pairs={{0,1},{1,0},{2,3},{3,2},{4,5},{5,4},{6,7},{7,6},{8,9},{9,8},{10,11... | collective-permute-start | bytes 5505032 | tf_op jit(solution)/shard_map/ppermute | solution.py:261
  474.8 42.2 %collective-permute-start.24 = (bf16[512,1792]{1,0:T(8,128)(2,1)S(1)}, bf16[512,1792]{1,0:T(8,128)(2,1)S(1)}, u32[]{:S(2)}, u32[]{:S(2)}) collective-permute-start(bf16[512,1792]{1,0:T(8,128)(2,1)S(1)} %multiply_convert_fusion.4), channel_id=1, source_target_pairs={{0,1},{1,0},{2,3},{3,2},{4,5},{5,4},{6,7},{7,6},{8,9},{9,8},{10,11... | collective-permute-start | bytes 5505032 | tf_op jit(solution)/shard_map/ppermute | solution.py:261
  598.7 119.6 %collective-permute-start.47 = (f32[512,1792]{1,0:T(8,128)}, f32[512,1792]{1,0:T(8,128)}, u32[]{:S(2)}, u32[]{:S(2)}) collective-permute-start(f32[512,1792]{1,0:T(8,128)} %convolution_add_fusion.1), channel_id=1, source_target_pairs={{0,1},{1,0},{2,3},{3,2},{4,5},{5,4},{6,7},{7,6},{8,9},{9,8},{10,11... | collective-permute-start | bytes 11010056 | tf_op jit(solution)/shard_map/ppermute | solution.py:261
  602.6 57.9 %collective-permute-start.84 = (bf16[896,1152]{1,0:T(8,128)(2,1)}, bf16[896,1152]{1,0:T(8,128)(2,1)}, u32[]{:S(2)}, u32[]{:S(2)}) collective-permute-start(bf16[896,1152]{1,0:T(8,128)(2,1)} %convolution_convert_fusion.6), channel_id=1, source_target_pairs={{0,8},{8,0},{1,9},{9,1},{2,10},{10,2},{3,11},{11,3},{4,12},{12,4},... | collective-permute-start | bytes 6193160 | tf_op jit(solution)/shard_map/ppermute | solution.py:244
  612.5 54.9 %collective-permute-start.89 = (bf16[896,1280]{1,0:T(8,128)(2,1)}, bf16[896,1280]{1,0:T(8,128)(2,1)}, u32[]{:S(2)}, u32[]{:S(2)}) collective-permute-start(bf16[896,1280]{1,0:T(8,128)(2,1)} %convolution_convert_fusion.4), channel_id=1, source_target_pairs={{0,16},{16,0},{1,17},{17,1},{2,18},{18,2},{3,19},{19,3},{4,20},{20... | collective-permute-start | bytes 6881288 | tf_op jit(solution)/shard_map/ppermute | solution.py:244
  663.4 24.7 %collective-permute-start.85 = (bf16[448,1152]{1,0:T(8,128)(2,1)S(1)}, bf16[448,1152]{1,0:T(8,128)(2,1)S(1)}, u32[]{:S(2)}, u32[]{:S(2)}) collective-permute-start(bf16[448,1152]{1,0:T(8,128)(2,1)S(1)} %get-tuple-element.155), channel_id=1, source_target_pairs={{0,16},{16,0},{1,17},{17,1},{2,18},{18,2},{3,19},{19,3},{4,20},{20... | collective-permute-start | bytes 3096584 | tf_op jit(solution)/shard_map/ppermute | solution.py:244
  667.3 64.9 %collective-permute-start.45 = (f32[512,1792]{1,0:T(8,128)}, f32[512,1792]{1,0:T(8,128)}, u32[]{:S(2)}, u32[]{:S(2)}) collective-permute-start(f32[512,1792]{1,0:T(8,128)} %fusion.22), channel_id=1, source_target_pairs={{0,1},{1,0},{2,3},{3,2},{4,5},{5,4},{6,7},{7,6},{8,9},{9,8},{10,11... | collective-permute-start | bytes 11010056 | tf_op jit(solution)/shard_map/ppermute | solution.py:261
  688.7 28.0 %collective-permute-start.90 = (bf16[448,1280]{1,0:T(8,128)(2,1)S(1)}, bf16[448,1280]{1,0:T(8,128)(2,1)S(1)}, u32[]{:S(2)}, u32[]{:S(2)}) collective-permute-start(bf16[448,1280]{1,0:T(8,128)(2,1)S(1)} %get-tuple-element.141), channel_id=1, source_target_pairs={{0,8},{8,0},{1,9},{9,1},{2,10},{10,2},{3,11},{11,3},{4,12},{12,4},... | collective-permute-start | bytes 3440648 | tf_op jit(solution)/shard_map/ppermute | solution.py:244
  689.1 20.3 %collective-permute-start.87 = (bf16[112,1152]{1,0:T(8,128)(2,1)S(1)}, bf16[112,1152]{1,0:T(8,128)(2,1)S(1)}, u32[]{:S(2)}, u32[]{:S(2)}) collective-permute-start(bf16[112,1152]{1,0:T(8,128)(2,1)S(1)} %get-tuple-element.180), channel_id=1, source_target_pairs={{0,4},{2,6},{4,0},{6,2},{1,5},{3,7},{5,1},{7,3},{8,12},{10,14},{12... | collective-permute-start | bytes 774152 | tf_op jit(solution)/shard_map/ppermute | solution.py:244
  709.4 96.2 %collective-permute-start.73 = (bf16[896,2432]{1,0:T(8,128)(2,1)}, bf16[896,2432]{1,0:T(8,128)(2,1)}, u32[]{:S(2)}, u32[]{:S(2)}) collective-permute-start(bf16[896,2432]{1,0:T(8,128)(2,1)} %convolution_convert_fusion.2), channel_id=1, source_target_pairs={{0,16},{16,0},{1,17},{17,1},{2,18},{18,2},{3,19},{19,3},{4,20},{20... | collective-permute-start | bytes 13074440 | tf_op jit(solution)/shard_map/ppermute | solution.py:244
  712.1 122.2 %collective-permute-start.78 = (bf16[896,2432]{1,0:T(8,128)(2,1)}, bf16[896,2432]{1,0:T(8,128)(2,1)}, u32[]{:S(2)}, u32[]{:S(2)}) collective-permute-start(bf16[896,2432]{1,0:T(8,128)(2,1)} %convolution_convert_fusion), channel_id=1, source_target_pairs={{0,8},{8,0},{1,9},{9,1},{2,10},{10,2},{3,11},{11,3},{4,12},{12,4},... | collective-permute-start | bytes 13074440 | tf_op jit(solution)/shard_map/ppermute | solution.py:244
  718.1 39.0 %collective-permute-start.91 = (bf16[112,1280]{1,0:T(8,128)(2,1)}, bf16[112,1280]{1,0:T(8,128)(2,1)}, u32[]{:S(2)}, u32[]{:S(2)}) collective-permute-start(bf16[112,1280]{1,0:T(8,128)(2,1)} %get-tuple-element.177), channel_id=1, source_target_pairs={{0,2},{2,4},{4,6},{6,0},{1,3},{3,5},{5,7},{7,1},{8,10},{10,12},{12... | collective-permute-start | bytes 860168 | tf_op jit(solution)/shard_map/ppermute | solution.py:244
  718.3 38.8 %collective-permute-start.92 = (bf16[112,1280]{1,0:T(8,128)(2,1)}, bf16[112,1280]{1,0:T(8,128)(2,1)}, u32[]{:S(2)}, u32[]{:S(2)}) collective-permute-start(bf16[112,1280]{1,0:T(8,128)(2,1)} %get-tuple-element.176), channel_id=1, source_target_pairs={{0,4},{2,6},{4,0},{6,2},{1,5},{3,7},{5,1},{7,3},{8,12},{10,14},{12... | collective-permute-start | bytes 860168 | tf_op jit(solution)/shard_map/ppermute | solution.py:244
  732.2 24.9 %collective-permute-start.93 = (bf16[112,1280]{1,0:T(8,128)(2,1)}, bf16[112,1280]{1,0:T(8,128)(2,1)}, u32[]{:S(2)}, u32[]{:S(2)}) collective-permute-start(bf16[112,1280]{1,0:T(8,128)(2,1)} %get-tuple-element.175), channel_id=1, source_target_pairs={{0,6},{2,0},{4,2},{6,4},{1,7},{3,1},{5,3},{7,5},{8,14},{10,8},{12,... | collective-permute-start | bytes 860168 | tf_op jit(solution)/shard_map/ppermute | solution.py:244
  759.3 17.3 %collective-permute-start.94 = (f32[56,2432]{1,0:T(8,128)}, f32[56,2432]{1,0:T(8,128)S(1)}, u32[]{:S(2)}, u32[]{:S(2)}) collective-permute-start(f32[56,2432]{1,0:T(8,128)} %dynamic-slice_bitcast_fusion.13), channel_id=1, source_target_pairs={{0,1},{1,0},{2,3},{3,2},{4,5},{5,4},{6,7},{7,6},{8,9},{9,8},{10,11... | collective-permute-start | bytes 1634312 | tf_op jit(solution)/shard_map/ppermute | solution.py:261
  770.7 40.7 %collective-permute-start.48 = (bf16[512,896]{1,0:T(8,128)(2,1)S(1)}, bf16[512,896]{1,0:T(8,128)(2,1)S(1)}, u32[]{:S(2)}, u32[]{:S(2)}) collective-permute-start(bf16[512,896]{1,0:T(8,128)(2,1)S(1)} %bitcast.601), channel_id=1, source_target_pairs={{0,1},{1,0},{2,3},{3,2},{4,5},{5,4},{6,7},{7,6},{8,9},{9,8},{10,11... | collective-permute-start | bytes 2752520 | tf_op jit(solution)/shard_map/ppermute | solution.py:261
  776.3 50.0 %collective-permute-start.66 = (bf16[512,896]{1,0:T(8,128)(2,1)}, bf16[512,896]{1,0:T(8,128)(2,1)}, u32[]{:S(2)}, u32[]{:S(2)}) collective-permute-start(bf16[512,896]{1,0:T(8,128)(2,1)} %bitcast.451), channel_id=1, source_target_pairs={{0,1},{1,0},{2,3},{3,2},{4,5},{5,4},{6,7},{7,6},{8,9},{9,8},{10,11... | collective-permute-start | bytes 2752520 | tf_op jit(solution)/shard_map/ppermute | solution.py:261
  810.8 62.7 %collective-permute-start.74 = (bf16[448,2432]{1,0:T(8,128)(2,1)}, bf16[448,2432]{1,0:T(8,128)(2,1)S(1)}, u32[]{:S(2)}, u32[]{:S(2)}) collective-permute-start(bf16[448,2432]{1,0:T(8,128)(2,1)} %get-tuple-element.113), channel_id=1, source_target_pairs={{0,8},{8,0},{1,9},{9,1},{2,10},{10,2},{3,11},{11,3},{4,12},{12,4},... | collective-permute-start | bytes 6537224 | tf_op jit(solution)/shard_map/ppermute | solution.py:244
  825.1 12.6 %collective-permute-start.49 = (bf16[2,8,160,128]{3,2,1,0:T(8,128)(2,1)S(1)}, bf16[2,8,160,128]{3,2,1,0:T(8,128)(2,1)S(1)}, u32[]{:S(2)}, u32[]{:S(2)}) collective-permute-start(bf16[2,8,160,128]{3,2,1,0:T(8,128)(2,1)S(1)} %convert_element_type.487), channel_id=1, source_target_pairs={{6,4},{7,5},{14,12},{15,13},{22,20},{23,21},{30,28},{31,29}} | collective-permute-start | bytes 1966088 | tf_op jit(solution)/shard_map/ppermute | solution.py:342
  833.2 38.2 %collective-permute-start.67 = (bf16[896,896]{1,0:T(8,128)(2,1)}, bf16[896,896]{1,0:T(8,128)(2,1)S(1)}, u32[]{:S(2)}, u32[]{:S(2)}) collective-permute-start(bf16[896,896]{1,0:T(8,128)(2,1)} %convolution_convert_fusion.9), channel_id=1, source_target_pairs={{0,16},{16,0},{1,17},{17,1},{2,18},{18,2},{3,19},{19,3},{4,20},{20... | collective-permute-start | bytes 4816904 | tf_op jit(solution)/shard_map/ppermute | solution.py:244
  839.0 76.9 %collective-permute-start.79 = (bf16[448,2432]{1,0:T(8,128)(2,1)S(1)}, bf16[448,2432]{1,0:T(8,128)(2,1)S(1)}, u32[]{:S(2)}, u32[]{:S(2)}) collective-permute-start(bf16[448,2432]{1,0:T(8,128)(2,1)S(1)} %get-tuple-element.115), channel_id=1, source_target_pairs={{0,16},{16,0},{1,17},{17,1},{2,18},{18,2},{3,19},{19,3},{4,20},{20... | collective-permute-start | bytes 6537224 | tf_op jit(solution)/shard_map/ppermute | solution.py:244
  843.0 77.4 %collective-permute-start.51 = (bf16[2,8,160,128]{3,2,1,0:T(8,128)(2,1)S(1)}, bf16[2,8,160,128]{3,2,1,0:T(8,128)(2,1)S(1)}, u32[]{:S(2)}, u32[]{:S(2)}) collective-permute-start(bf16[2,8,160,128]{3,2,1,0:T(8,128)(2,1)S(1)} %add_convert_fusion.14), channel_id=1, source_target_pairs={{2,0},{3,1},{10,8},{11,9},{18,16},{19,17},{26,24},{27,25}} | collective-permute-start | bytes 1966088 | tf_op jit(solution)/shard_map/ppermute | solution.py:342
  872.0 106.6 %collective-permute-start.68 = (bf16[448,896]{1,0:T(8,128)(2,1)S(1)}, bf16[448,896]{1,0:T(8,128)(2,1)S(1)}, u32[]{:S(2)}, u32[]{:S(2)}) collective-permute-start(bf16[448,896]{1,0:T(8,128)(2,1)S(1)} %get-tuple-element.171), channel_id=1, source_target_pairs={{0,8},{8,0},{1,9},{9,1},{2,10},{10,2},{3,11},{11,3},{4,12},{12,4},... | collective-permute-start | bytes 2408456 | tf_op jit(solution)/shard_map/ppermute | solution.py:244
  875.2 105.9 %collective-permute-start.75 = (bf16[112,2432]{1,0:T(8,128)(2,1)}, bf16[112,2432]{1,0:T(8,128)(2,1)S(1)}, u32[]{:S(2)}, u32[]{:S(2)}) collective-permute-start(bf16[112,2432]{1,0:T(8,128)(2,1)} %get-tuple-element.149), channel_id=1, source_target_pairs={{0,2},{2,4},{4,6},{6,0},{1,3},{3,5},{5,7},{7,1},{8,10},{10,12},{12... | collective-permute-start | bytes 1634312 | tf_op jit(solution)/shard_map/ppermute | solution.py:244
  875.7 108.1 %collective-permute-start.76 = (bf16[112,2432]{1,0:T(8,128)(2,1)}, bf16[112,2432]{1,0:T(8,128)(2,1)S(1)}, u32[]{:S(2)}, u32[]{:S(2)}) collective-permute-start(bf16[112,2432]{1,0:T(8,128)(2,1)} %get-tuple-element.148), channel_id=1, source_target_pairs={{0,4},{2,6},{4,0},{6,2},{1,5},{3,7},{5,1},{7,3},{8,12},{10,14},{12... | collective-permute-start | bytes 1634312 | tf_op jit(solution)/shard_map/ppermute | solution.py:244
  915.9 67.9 %collective-permute-start.77 = (bf16[112,2432]{1,0:T(8,128)(2,1)}, bf16[112,2432]{1,0:T(8,128)(2,1)}, u32[]{:S(2)}, u32[]{:S(2)}) collective-permute-start(bf16[112,2432]{1,0:T(8,128)(2,1)} %get-tuple-element.147), channel_id=1, source_target_pairs={{0,6},{2,0},{4,2},{6,4},{1,7},{3,1},{5,3},{7,5},{8,14},{10,8},{12,... | collective-permute-start | bytes 1634312 | tf_op jit(solution)/shard_map/ppermute | solution.py:244
  958.4 22.4 %collective-permute-start.54 = (bf16[896,256]{1,0:T(8,128)(2,1)S(1)}, bf16[896,256]{1,0:T(8,128)(2,1)S(1)}, u32[]{:S(2)}, u32[]{:S(2)}) collective-permute-start(bf16[896,256]{1,0:T(8,128)(2,1)S(1)} %convolution_convert_fusion.14), channel_id=1, source_target_pairs={{0,16},{16,0},{1,17},{17,1},{2,18},{18,2},{3,19},{19,3},{4,20},{20... | collective-permute-start | bytes 1376264 | tf_op jit(solution)/shard_map/ppermute | solution.py:244
  978.6 17.2 %collective-permute-start.80 = (bf16[112,2432]{1,0:T(8,128)(2,1)S(1)}, bf16[112,2432]{1,0:T(8,128)(2,1)S(1)}, u32[]{:S(2)}, u32[]{:S(2)}) collective-permute-start(bf16[112,2432]{1,0:T(8,128)(2,1)S(1)} %copy-done.72), channel_id=1, source_target_pairs={{0,2},{2,4},{4,6},{6,0},{1,3},{3,5},{5,7},{7,1},{8,10},{10,12},{12... | collective-permute-start | bytes 1634312 | tf_op jit(solution)/shard_map/ppermute | solution.py:244
  980.9 35.6 %collective-permute-start.81 = (bf16[112,2432]{1,0:T(8,128)(2,1)S(1)}, bf16[112,2432]{1,0:T(8,128)(2,1)S(1)}, u32[]{:S(2)}, u32[]{:S(2)}) collective-permute-start(bf16[112,2432]{1,0:T(8,128)(2,1)S(1)} %copy-done.71), channel_id=1, source_target_pairs={{0,4},{2,6},{4,0},{6,2},{1,5},{3,7},{5,1},{7,3},{8,12},{10,14},{12... | collective-permute-start | bytes 1634312 | tf_op jit(solution)/shard_map/ppermute | solution.py:244
  981.2 37.3 %collective-permute-start.82 = (bf16[112,2432]{1,0:T(8,128)(2,1)S(1)}, bf16[112,2432]{1,0:T(8,128)(2,1)S(1)}, u32[]{:S(2)}, u32[]{:S(2)}) collective-permute-start(bf16[112,2432]{1,0:T(8,128)(2,1)S(1)} %copy-done.70), channel_id=1, source_target_pairs={{0,6},{2,0},{4,2},{6,4},{1,7},{3,1},{5,3},{7,5},{8,14},{10,8},{12,... | collective-permute-start | bytes 1634312 | tf_op jit(solution)/shard_map/ppermute | solution.py:244
  983.8 118.3 %collective-permute-start.53 = (f32[512,1792]{1,0:T(8,128)}, f32[512,1792]{1,0:T(8,128)}, u32[]{:S(2)}, u32[]{:S(2)}) collective-permute-start(f32[512,1792]{1,0:T(8,128)} %convolution_add_fusion), channel_id=1, source_target_pairs={{0,1},{1,0},{2,3},{3,2},{4,5},{5,4},{6,7},{7,6},{8,9},{9,8},{10,11... | collective-permute-start | bytes 11010056 | tf_op jit(solution)/shard_map/ppermute | solution.py:261
  983.8 76.2 %collective-permute-start.60 = (bf16[896,896]{1,0:T(8,128)(2,1)}, bf16[896,896]{1,0:T(8,128)(2,1)}, u32[]{:S(2)}, u32[]{:S(2)}) collective-permute-start(bf16[896,896]{1,0:T(8,128)(2,1)} %convolution_convert_fusion.11), channel_id=1, source_target_pairs={{0,8},{8,0},{1,9},{9,1},{2,10},{10,2},{3,11},{11,3},{4,12},{12,4},... | collective-permute-start | bytes 4816904 | tf_op jit(solution)/shard_map/ppermute | solution.py:244
  995.8 44.2 %collective-permute-start.69 = (bf16[112,896]{1,0:T(8,128)(2,1)}, bf16[112,896]{1,0:T(8,128)(2,1)}, u32[]{:S(2)}, u32[]{:S(2)}) collective-permute-start(bf16[112,896]{1,0:T(8,128)(2,1)} %get-tuple-element.185), channel_id=1, source_target_pairs={{0,2},{2,4},{4,6},{6,0},{1,3},{3,5},{5,7},{7,1},{8,10},{10,12},{12... | collective-permute-start | bytes 602120 | tf_op jit(solution)/shard_map/ppermute | solution.py:244
  1016.4 24.2 %collective-permute-start.70 = (bf16[112,896]{1,0:T(8,128)(2,1)S(1)}, bf16[112,896]{1,0:T(8,128)(2,1)}, u32[]{:S(2)}, u32[]{:S(2)}) collective-permute-start(bf16[112,896]{1,0:T(8,128)(2,1)S(1)} %get-tuple-element.184), channel_id=1, source_target_pairs={{0,4},{2,6},{4,0},{6,2},{1,5},{3,7},{5,1},{7,3},{8,12},{10,14},{12... | collective-permute-start | bytes 602120 | tf_op jit(solution)/shard_map/ppermute | solution.py:244
  1026.4 18.5 %collective-permute-start.71 = (bf16[112,896]{1,0:T(8,128)(2,1)S(1)}, bf16[112,896]{1,0:T(8,128)(2,1)S(1)}, u32[]{:S(2)}, u32[]{:S(2)}) collective-permute-start(bf16[112,896]{1,0:T(8,128)(2,1)S(1)} %get-tuple-element.183), channel_id=1, source_target_pairs={{0,6},{2,0},{4,2},{6,4},{1,7},{3,1},{5,3},{7,5},{8,14},{10,8},{12,... | collective-permute-start | bytes 602120 | tf_op jit(solution)/shard_map/ppermute | solution.py:244
  1049.3 14.0 %collective-permute-start.83 = (f32[56,4864]{1,0:T(8,128)}, f32[56,4864]{1,0:T(8,128)}, u32[]{:S(2)}, u32[]{:S(2)}) collective-permute-start(f32[56,4864]{1,0:T(8,128)} %get-tuple-element.145), channel_id=1, source_target_pairs={{0,1},{1,0},{2,3},{3,2},{4,5},{5,4},{6,7},{7,6},{8,9},{9,8},{10,11... | collective-permute-start | bytes 3268616 | tf_op jit(solution)/shard_map/ppermute | solution.py:261
  1062.8 20.2 %collective-permute-start.61 = (bf16[448,896]{1,0:T(8,128)(2,1)}, bf16[448,896]{1,0:T(8,128)(2,1)}, u32[]{:S(2)}, u32[]{:S(2)}) collective-permute-start(bf16[448,896]{1,0:T(8,128)(2,1)} %get-tuple-element.173), channel_id=1, source_target_pairs={{0,16},{16,0},{1,17},{17,1},{2,18},{18,2},{3,19},{19,3},{4,20},{20... | collective-permute-start | bytes 2408456 | tf_op jit(solution)/shard_map/ppermute | solution.py:244
  1085.8 15.5 %collective-permute-start.63 = (bf16[112,896]{1,0:T(8,128)(2,1)S(1)}, bf16[112,896]{1,0:T(8,128)(2,1)S(1)}, u32[]{:S(2)}, u32[]{:S(2)}) collective-permute-start(bf16[112,896]{1,0:T(8,128)(2,1)S(1)} %get-tuple-element.188), channel_id=1, source_target_pairs={{0,4},{2,6},{4,0},{6,2},{1,5},{3,7},{5,1},{7,3},{8,12},{10,14},{12... | collective-permute-start | bytes 602120 | tf_op jit(solution)/shard_map/ppermute | solution.py:244
  1088.4 12.8 %collective-permute-start.64 = (bf16[112,896]{1,0:T(8,128)(2,1)S(1)}, bf16[112,896]{1,0:T(8,128)(2,1)S(1)}, u32[]{:S(2)}, u32[]{:S(2)}) collective-permute-start(bf16[112,896]{1,0:T(8,128)(2,1)S(1)} %get-tuple-element.187), channel_id=1, source_target_pairs={{0,6},{2,0},{4,2},{6,4},{1,7},{3,1},{5,3},{7,5},{8,14},{10,8},{12,... | collective-permute-start | bytes 602120 | tf_op jit(solution)/shard_map/ppermute | solution.py:244
  (169 other events, 1788.7 us)

commit v2 on v1

v2 whole, which is shorter than its diff:
```python
import functools
import math

import jax
import jax.numpy as jnp
import numpy as np
from jax import lax
from jax.experimental import pallas as pl
from jax.experimental.pallas import tpu as pltpu
from jax.sharding import Mesh
from jax.sharding import PartitionSpec as P

D = 1792
H = 16
F = 16
FF = 4864
KS = 3
SLOT = 2048
STEP = 10

CORES = 2
HC = H // CORES
HW = D // H
VC = HC * HW
QC = HC * F
FC = FF // CORES
LANES = 128
FEATS = 256
FROWS = 160
SCALE = 1.0 / math.sqrt(F)

norm_epsilon = 1e-06
beta_first = 0.9
beta_second = 0.95
adam_epsilon = 1e-08
weight_decay = 3e-05

bf16 = jnp.bfloat16
f32 = jnp.float32


def feature_tables():
    index = np.full((8, FEATS), -4096, np.int32)
    scale = np.zeros((8, FEATS), np.float32)
    scale[0, 0] = scale[1, 0] = scale[2, 0] = 1.0
    at = 1
    for i in range(F):
        index[0, at] = i
        scale[1, at] = 1.0
        scale[2, at] = SCALE
        at += 1
    for i in range(F):
        for j in range(i, F):
            index[0, at] = i
            index[1, at] = j
            scale[2, at] = (1.0 if i == j else 2.0) * 0.5 * SCALE * SCALE
            at += 1
    return index, scale


def dot(a, b):
    return lax.dot_general(a, b, (((1,), (0,)), ((), ())), preferred_element_type=f32)


def dot_nt(a, b):
    return lax.dot_general(a, b, (((1,), (1,)), ((), ())), preferred_element_type=f32)


def dot_tn(a, b):
    return lax.dot_general(a, b, (((0,), (0,)), ((), ())), preferred_element_type=f32)


def selectors(index_ref, head):
    lane = lax.broadcasted_iota(jnp.int32, (LANES, FEATS), 0) - head * F
    first = jnp.where(lane == index_ref[0:1, :], 1.0, 0.0).astype(bf16)
    second = jnp.where(lane == index_ref[1:2, :], 1.0, 0.0).astype(bf16)
    return first, second


def factors(rows, first, second, scale_ref):
    return (dot(rows, first) + scale_ref[0:1, :], dot(rows, second) + scale_ref[1:2, :])


def window(head):
    start = head * HW
    base = min(start // LANES * LANES, VC - 2 * LANES)
    return base, start - base


def both_halves(core_ref, ref, columns):
    core = core_ref[0]
    return jnp.concatenate([ref[core, :, columns], ref[1 - core, :, columns]], axis=0)


def store_halves(core_ref, ref, rows, columns):
    core, half = core_ref[0], rows.shape[0] // CORES
    ref[core, :, columns] = rows[:half]
    ref[1 - core, :, columns] = rows[half:]


def head_columns(core_ref, ref, head):
    base, offset = window(head)
    wide = both_halves(core_ref, ref, slice(base, base + 2 * LANES)).astype(f32)
    if offset:
        wide = pltpu.roll(wide, 2 * LANES - offset, 1)
    return wide[:, :LANES]


def add_head_columns(ref, head, block):
    base, offset = window(head)
    wide = jnp.concatenate([block, jnp.zeros_like(block)], axis=1)
    if offset:
        wide = pltpu.roll(wide, offset, 1)
    ref[:, base : base + 2 * LANES] += wide


def with_one(block):
    lane = lax.broadcasted_iota(jnp.int32, block.shape, 1)
    return jnp.where(lane < HW, block, jnp.where(lane == HW, 1.0, 0.0))


def only_head(rows, head):
    lane = lax.broadcasted_iota(jnp.int32, rows.shape, 1)
    inside = (lane >= head * F) & (lane < head * F + F)
    return jnp.where(inside, rows.astype(f32), 0.0).astype(bf16)


def state_kernel(core_ref, index_ref, scale_ref, k_ref, v_ref, state_ref):
    keys = both_halves(core_ref, k_ref, slice(None))
    for head in range(HC):
        first, second = selectors(index_ref, head)
        one, two = factors(keys, first, second, scale_ref)
        phi = (one * two * scale_ref[2:3, :]).astype(bf16)
        values = with_one(head_columns(core_ref, v_ref, head)).astype(bf16)
        state_ref[0, head] = dot_tn(phi, values)[:FROWS]


def scores_of(q_head, keys):
    scores = dot_nt(q_head, keys) * SCALE
    row = lax.broadcasted_iota(jnp.int32, scores.shape, 0)
    column = lax.broadcasted_iota(jnp.int32, scores.shape, 1)
    return scores, column <= row


def forward_kernel(core_ref, index_ref, scale_ref, q_ref, k_ref, v_ref, before_ref, mixer_ref, den_ref, wide):
    queries = both_halves(core_ref, q_ref, slice(None))
    keys = both_halves(core_ref, k_ref, slice(None))
    wide[...] = jnp.zeros_like(wide)
    lane = lax.broadcasted_iota(jnp.int32, (queries.shape[0], LANES), 1)
    dens = jnp.zeros((queries.shape[0], LANES), f32)
    for head in range(HC):
        first, second = selectors(index_ref, head)
        one, two = factors(queries, first, second, scale_ref)
        phi = (one * two).astype(bf16)
        values = with_one(head_columns(core_ref, v_ref, head)).astype(bf16)
        scores, allowed = scores_of(only_head(queries, head), keys)
        kernel = jnp.where(allowed, 1.0 + scores + 0.5 * scores * scores, 0.0).astype(bf16)
        total = dot(kernel, values) + dot(phi[:, :FROWS], before_ref[0, head])
        den = total[:, HW : HW + 1]
        add_head_columns(wide, head, jnp.where(lane < HW, total / den, 0.0))
        dens = jnp.where(lane == head, den, dens)
    store_halves(core_ref, mixer_ref, wide[...].astype(bf16), slice(None))
    store_halves(core_ref, den_ref, dens, slice(None))


def pull_kernel(core_ref, index_ref, scale_ref, q_ref, gm_ref, mixer_ref, den_ref, state_ref, gnum_ref):
    queries = both_halves(core_ref, q_ref, slice(None))
    lane = lax.broadcasted_iota(jnp.int32, (queries.shape[0], LANES), 1)
    dens = both_halves(core_ref, den_ref, slice(None))
    for head in range(HC):
        first, second = selectors(index_ref, head)
        one, two = factors(queries, first, second, scale_ref)
        phi = (one * two).astype(bf16)
        den = dens[:, head : head + 1]
        grad = jnp.where(lane < HW, head_columns(core_ref, gm_ref, head), 0.0)
        mixer = head_columns(core_ref, mixer_ref, head)
        pulled = -jnp.sum(grad * mixer, axis=1, keepdims=True)
        grad = (jnp.where(lane == HW, pulled, grad) / den).astype(bf16)
        store_halves(core_ref, gnum_ref, grad, slice(head * LANES, (head + 1) * LANES))
        state_ref[0, head] = dot_tn(phi, grad)[:FROWS]


def backward_kernel(
    core_ref, index_ref, scale_ref, q_ref, k_ref, v_ref, gnum_ref, before_ref, after_ref, gqk_ref, gv_ref, wide
):
    queries = both_halves(core_ref, q_ref, slice(None))
    keys = both_halves(core_ref, k_ref, slice(None))
    wide[...] = jnp.zeros_like(wide)
    lane = lax.broadcasted_iota(jnp.int32, (queries.shape[0], LANES), 1)
    grad_q = jnp.zeros((queries.shape[0], LANES), f32)
    grad_k = jnp.zeros((queries.shape[0], LANES), f32)
    for head in range(HC):
        first, second = selectors(index_ref, head)
        coef = scale_ref[2:3, :]
        q_one, q_two = factors(queries, first, second, scale_ref)
        k_one, k_two = factors(keys, first, second, scale_ref)
        values = with_one(head_columns(core_ref, v_ref, head)).astype(bf16)
        gnum = both_halves(core_ref, gnum_ref, slice(head * LANES, (head + 1) * LANES))
        q_head = only_head(queries, head)
        k_head = only_head(keys, head)
        scores, allowed = scores_of(q_head, keys)
        kernel = jnp.where(allowed, 1.0 + scores + 0.5 * scores * scores, 0.0).astype(bf16)
        grad_kernel = dot_nt(gnum, values)
        grad_scores = (jnp.where(allowed, grad_kernel * (1.0 + scores), 0.0) * SCALE).astype(bf16)
        phi_k = (k_one * k_two * coef).astype(bf16)
        after = after_ref[0, head]
        before = before_ref[0, head]
        grad_v = dot_tn(kernel, gnum) + dot(phi_k[:, :FROWS], after)
        add_head_columns(wide, head, jnp.where(lane < HW, grad_v, 0.0))
        empty = jnp.zeros((FEATS - FROWS, LANES), bf16)
        grad_phi_q = dot_nt(gnum, jnp.concatenate([before, empty], axis=0))
        grad_phi_k = dot_nt(values, jnp.concatenate([after, empty], axis=0)) * coef
        grad_q += dot(grad_scores, k_head)
        grad_q += dot_nt((grad_phi_q * q_two).astype(bf16), first)
        grad_q += dot_nt((grad_phi_q * q_one).astype(bf16), second)
        grad_k += dot_tn(grad_scores, q_head)
        grad_k += dot_nt((grad_phi_k * k_two).astype(bf16), first)
        grad_k += dot_nt((grad_phi_k * k_one).astype(bf16), second)
    store_halves(core_ref, gqk_ref, grad_q.astype(bf16), slice(0, LANES))
    store_halves(core_ref, gqk_ref, grad_k.astype(bf16), slice(LANES, 2 * LANES))
    store_halves(core_ref, gv_ref, wide[...].astype(bf16), slice(None))


def per_slot(kernel, slots, rows, ins, outs, scratch, flops):
    def table():
        return pl.BlockSpec((8, FEATS), lambda s, core: (0, 0))

    def row_spec(width, column=0):
        return pl.BlockSpec((CORES, None, rows, width), lambda s, core: (0, s, 0, column))

    def state_spec():
        return pl.BlockSpec((1, HC, FROWS, LANES), lambda s, core: (s, 0, 0, 0))

    def spec(kind):
        return state_spec() if kind == "state" else row_spec(*kind)

    def shape(kind, dtype):
        if kind == "state":
            return jax.ShapeDtypeStruct((slots, HC, FROWS, LANES), dtype)
        return jax.ShapeDtypeStruct((CORES, slots, rows, kind[0]), dtype)

    return pl.pallas_call(
        kernel,
        grid_spec=pltpu.PrefetchScalarGridSpec(
            num_scalar_prefetch=1,
            grid=(slots,),
            in_specs=[table(), table()] + [spec(kind) for kind in ins],
            out_specs=[spec(kind) for kind, _ in outs],
            scratch_shapes=scratch,
        ),
        out_shape=[shape(kind, dtype) for kind, dtype in outs],
        compiler_params=pltpu.CompilerParams(vmem_limit_bytes=56 << 20),
        cost_estimate=pl.CostEstimate(flops=flops, bytes_accessed=8 << 20, transcendentals=0),
    )


def passed_along(array, axis, by):
    count = lax.axis_size(axis)
    pairs = [(i, i + by) for i in range(count) if 0 <= i + by < count]
    return lax.ppermute(array, axis, pairs)


def both_cores(mine, theirs, axis):
    first = lax.axis_index("core") == 0
    return jnp.concatenate(
        [jnp.where(first, mine, theirs), jnp.where(first, theirs, mine)], axis=axis
    )


def swapped(array):
    return lax.ppermute(array, "core", [(0, 1), (1, 0)])


def part_of(array, axis, index):
    return lax.dynamic_index_in_dim(array, index, axis, keepdims=False)


def bits_of(axis):
    return [(axis, bit) for bit in reversed(range(lax.axis_size(axis).bit_length() - 1))]


def bit_at(axis, bit):
    return (lax.axis_index(axis) >> bit) & 1


def exchanged(array, axis, bit):
    count = lax.axis_size(axis)
    return lax.ppermute(array, axis, [(i, i ^ (1 << bit)) for i in range(count)])


def tied(*arrays):
    return lax.optimization_barrier(arrays)


class Gather:
    def __init__(self, piece, x_first):
        self.columns = piece.shape[1]
        self.block = piece
        low_first = lambda axis: bits_of(axis)[::-1]
        self.plan = [(step, at) for at, step in enumerate(bits_of("z"))]
        if x_first:
            self.plan += [(step, 0) for step in low_first("x") + low_first("y")]
        else:
            self.plan += [(step, 0) for step in low_first("y")]
            self.plan += [(step, len(bits_of("y"))) for step in low_first("x")]

    def stage(self):
        (axis, bit), dim = self.plan.pop(0)
        mine = bit_at(axis, bit)
        arrived = exchanged(self.block, axis, bit)
        shape = self.block.shape[:dim] + (2,) + self.block.shape[dim:]
        whole = jnp.zeros(shape, self.block.dtype)
        whole = lax.dynamic_update_index_in_dim(whole, self.block, mine, dim)
        self.block = lax.dynamic_update_index_in_dim(whole, arrived, 1 - mine, dim)
        return self

    def along_z(self):
        while self.plan[0][0][0] == "z":
            self.stage()
        return self

    def rest(self):
        while self.plan:
            self.stage()
        return self.block.reshape(D, self.columns)


class Scatter:
    def __init__(self, terms, x_first):
        self.dims = bits_of("y") + bits_of("x") + bits_of("z")
        order = ("x", "y") if x_first else ("y", "x")
        self.plan = bits_of(order[0]) + bits_of(order[1]) + bits_of("z")[::-1]
        rows = D >> len(self.dims)
        self.terms = [terms.reshape((2,) * len(self.dims) + (rows, terms.shape[1]))]

    def total(self, terms):
        total = terms[0].astype(f32)
        for term in terms[1:]:
            total = total + term.astype(f32)
        return total

    def stage(self):
        step = self.plan.pop(0)
        dim, mine = self.dims.index(step), bit_at(*step)
        self.dims.remove(step)
        sent = self.total([part_of(term, dim, 1 - mine) for term in self.terms]).astype(bf16)
        self.terms = [part_of(term, dim, mine) for term in self.terms]
        self.terms.append(exchanged(sent, *step))
        return self

    def rest(self):
        while self.plan:
            self.stage()
        return self.total(self.terms)


def chain(local, up):
    count = lax.axis_size("z")
    total = jnp.zeros_like(local)
    for hop in range(1, count):
        pair = (hop - 1, hop) if up else (count - hop, count - hop - 1)
        message = (total + local).astype(bf16)
        total = total + lax.ppermute(message, "z", [pair]).astype(f32)
    return total.astype(bf16)


def mesh_exchange(y, x, z, core, axis):
    if axis == "y":
        return (1 - y, x, z, core)
    if axis == "x":
        return (y, 1 - x, z, core)
    if axis == "z0":
        return (y, x, z + 1 - 2 * (z % 2), core)
    return (y, x, (z + 2) % 4, core)


ORDERS = (("y", "x", "z0", "z1"), ("x", "y", "z0", "z1"))


def reduce_kernel(
    tiles,
    second_ref,
    normed_ref,
    mixer_ref,
    gate_ref,
    up_ref,
    value_ref,
    after_ref,
    qk_ref,
    small_ref,
    out_ref,
    terms,
    sums,
    halves,
    quarters,
    got_terms,
    got_sums,
    got_halves,
    got_quarters,
    send_sem,
    recv_sem,
):
    y, x, z, core = (lax.axis_index(axis) for axis in ("y", "x", "z", "core"))
    ffn, mid, total = tiles
    places = {"y": y, "x": x, "z0": z % 2, "z1": z // 2}
    block = terms.shape[4]

    barrier = pltpu.get_barrier_semaphore()
    for axis in ORDERS[0]:
        pl.semaphore_signal(
            barrier,
            inc=1,
            device_id=mesh_exchange(y, x, z, core, axis),
            device_id_type=pl.DeviceIdType.MESH,
        )
    pl.semaphore_wait(barrier, len(ORDERS[0]))

    def transfer(stream, stage, chunk):
        axis = ORDERS[stream][stage]
        there = 1 - places[axis]
        slot, landing = chunk % 2, chunk % 4
        if stage == 0 and stream == 0:
            source = terms.at[stream, slot, there]
        elif stage == 0:
            source = terms.at[stream, slot, :, there]
        elif stage == 1:
            source = sums.at[stream, slot, there]
        elif stage == 2:
            source = halves.at[stream, slot, :, there]
        else:
            source = quarters.at[stream, slot, there]
        target = (got_terms, got_sums, got_halves, got_quarters)[stage].at[stream, landing]
        return pltpu.make_async_remote_copy(
            src_ref=source,
            dst_ref=target,
            send_sem=send_sem.at[stream, stage, slot],
            recv_sem=recv_sem.at[stream, stage, landing],
            device_id=mesh_exchange(y, x, z, core, axis),
            device_id_type=pl.DeviceIdType.MESH,
        )

    def add(a, b):
        return a.astype(f32) + b.astype(f32)

    def product(stream, chunk, left_ref, right_ref, tile):
        columns = right_ref[:, pl.ds(pl.multiple_of(tile * LANES, LANES), LANES)]

        @pl.loop(0, 4)
        def _(part):
            rows = left_ref[pl.ds(pl.multiple_of(part * block, block), block), :]
            terms[stream, chunk % 2, part // 2, part % 2] = dot(rows, columns).astype(bf16)

    def begin(chunk):
        @pl.when(chunk < ffn)
        def _():
            product(0, chunk, second_ref, gate_ref, chunk)
            product(1, chunk, second_ref, up_ref, chunk)

        @pl.when((chunk >= ffn) & (chunk < ffn + mid))
        def _():
            product(0, chunk, normed_ref, value_ref, chunk - ffn)
            product(1, chunk, mixer_ref, after_ref, chunk - ffn)

        @pl.when(chunk == ffn + mid)
        def _():
            product(0, chunk, normed_ref, qk_ref, 0)
            product(1, chunk, normed_ref, qk_ref, 1)

        @pl.when(chunk == ffn + mid + 1)
        def _():
            for part in range(4):
                rows = small_ref[part * block : (part + 1) * block, :]
                terms[0, chunk % 2, part // 2, part % 2] = rows
                terms[1, chunk % 2, part // 2, part % 2] = rows

        for stream in range(2):
            transfer(stream, 0, chunk).start()

    def advance(stage, chunk):
        for stream in range(2):
            axis = ORDERS[stream][stage]
            here = places[axis]
            slot, landing = chunk % 2, chunk % 4
            transfer(stream, stage, chunk).wait()
            if stage == 0:
                own = terms[stream, slot, here] if stream == 0 else terms[stream, slot, :, here]
                sums[stream, slot] = add(own, got_terms[stream, landing]).astype(bf16)
            elif stage == 1:
                total = add(sums[stream, slot, here], got_sums[stream, landing]).astype(bf16)
                halves[stream, slot] = total.reshape(halves.shape[2:])
            elif stage == 2:
                own = halves[stream, slot, :, here]
                quarters[stream, slot] = add(own, got_halves[stream, landing]).astype(bf16)
            else:
                total = add(quarters[stream, slot, here], got_quarters[stream, landing])
                out_ref[stream, :, pl.ds(pl.multiple_of(chunk * LANES, LANES), LANES)] = total
            if stage < 3:
                transfer(stream, stage + 1, chunk).start()

    @pl.loop(0, total + 4)
    def _(step):
        @pl.when(step < total)
        def _():
            begin(step)

        for stage in range(4):

            @pl.when((step >= stage + 1) & (step < total + stage + 1))
            def _(stage=stage):
                advance(stage, step - stage - 1)


def reduced(second_t, normed_t, mixer_t, grad_gate, grad_up, grad_pre, grad_after, grad_qk, small):
    ffn, mid = grad_gate.shape[1] // LANES, grad_pre.shape[1] // LANES
    total = ffn + mid + 2
    block, rows = D // 4, D // 16
    dma = pltpu.SemaphoreType.DMA
    tokens = second_t.shape[1]
    return pl.pallas_call(
        functools.partial(reduce_kernel, (ffn, mid, total)),
        out_shape=jax.ShapeDtypeStruct((2, rows, total * LANES), f32),
        in_specs=[pl.BlockSpec(memory_space=pltpu.VMEM)] * 9,
        out_specs=pl.BlockSpec(memory_space=pltpu.VMEM),
        scratch_shapes=[
            pltpu.VMEM((2, 2, 2, 2, block, LANES), bf16),
            pltpu.VMEM((2, 2, 2, block, LANES), bf16),
            pltpu.VMEM((2, 2, 2, 2, rows, LANES), bf16),
            pltpu.VMEM((2, 2, 2, rows, LANES), bf16),
            pltpu.VMEM((2, 4, 2, block, LANES), bf16),
            pltpu.VMEM((2, 4, block, LANES), bf16),
            pltpu.VMEM((2, 4, 2, rows, LANES), bf16),
            pltpu.VMEM((2, 4, rows, LANES), bf16),
            dma((2, 4, 2)),
            dma((2, 4, 4)),
        ],
        compiler_params=pltpu.CompilerParams(
            collective_id=0, has_side_effects=True, vmem_limit_bytes=58 << 20
        ),
        cost_estimate=pl.CostEstimate(
            flops=4 * D * tokens * total * LANES, bytes_accessed=400 << 20, transcendentals=0
        ),
    )(second_t, normed_t, mixer_t, grad_gate, grad_up, grad_pre, grad_after, grad_qk, small)


def norm_scale(values):
    inverse = lax.rsqrt(jnp.mean(values * values, axis=-1, keepdims=True) + norm_epsilon)
    return (values * inverse, inverse)


def norm_backward(grad_normed, scaled, inverse, gain_row):
    grad_scaled = grad_normed * gain_row[None, :]
    grad_input = inverse * (
        grad_scaled - scaled * jnp.mean(grad_scaled * scaled, axis=-1, keepdims=True)
    )
    return (grad_input, jnp.sum(grad_normed * scaled, axis=0))


def adam_update(weight, gradient, first_moment, second_moment, learn_rate, decay_rate):
    first_new = beta_first * first_moment + (1.0 - beta_first) * gradient
    second_new = beta_second * second_moment + (1.0 - beta_second) * gradient * gradient
    first_hat = first_new / (1.0 - beta_first**STEP)
    second_hat = second_new / (1.0 - beta_second**STEP)
    new_weight = (
        weight
        - learn_rate * first_hat / (jnp.sqrt(second_hat) + adam_epsilon)
        - decay_rate * weight
    )
    return (new_weight, second_new)


def local(
    tokens,
    cotangent,
    lengths,
    w_qk,
    w_value,
    w_out,
    w_gu,
    w_down,
    small_params,
    m_qk,
    m_value,
    m_out,
    m_gu,
    m_down,
    m_small,
    v_qk,
    v_value,
    v_out,
    v_gu,
    v_down,
    v_small,
):
    slots, slot_rows, _ = tokens.shape
    owned = w_qk.shape[0]
    rows = slots * slot_rows
    core, z_at = lax.axis_index("core"), lax.axis_index("z")
    other = 1 - core
    first_core = core == 0

    def on_chip(array):
        return jnp.concatenate([array, swapped(array)], axis=0)

    def halves(array):
        return array.reshape(CORES, slots, slot_rows, -1)

    columns_of = [
        w_qk.astype(bf16).reshape(owned, 2, CORES, QC),
        w_value.astype(bf16).reshape(owned, 1, CORES, VC),
        w_out.astype(bf16).reshape(owned, 1, CORES, VC),
        w_gu.astype(bf16).reshape(owned, 2, CORES, FC),
        w_down.astype(bf16).reshape(owned, 1, CORES, FC),
    ]
    small_low = jnp.pad(small_params.astype(bf16), ((0, 0), (0, LANES - (KS + 2))))

    def shard(which, index):
        parts = [part_of(columns_of[i], 2, index).reshape(owned, -1) for i in which]
        return jnp.concatenate(parts, axis=1) if len(parts) > 1 else parts[0]

    def chip_shard(which, extra=None):
        mine, theirs = shard(which, core), shard(which, other)
        arrived = swapped(theirs if extra is None else jnp.concatenate([theirs, extra], axis=1))
        mine = mine if extra is None else jnp.concatenate([mine, extra], axis=1)
        return both_cores(mine, arrived, 0)

    attention_shard = chip_shard((0, 1), small_low)
    rest_shard = chip_shard((2, 3, 4))
    half = (2 * QC + VC + LANES) // 2
    cut = FC // 2 // LANES * LANES
    down_at = VC + 2 * FC
    own_tokens = tokens.reshape(rows, D)
    other_tokens = swapped(own_tokens)
    wide_part = 4 * LANES
    early_a = Gather(attention_shard[:, :half], True)
    early_b = Gather(attention_shard[:, half:], False)
    early_a.along_z(), early_b.along_z()
    early_a.block, other_tokens = tied(early_a.block, other_tokens)
    early = jnp.concatenate([early_a.rest(), early_b.rest()], axis=1)

    def gathered(start, width):
        return lax.all_gather(rest_shard[:, start : start + width], ("y", "x", "z"), axis=0, tiled=True)

    out_half = gathered(0, VC)
    gate_full = gathered(VC, FC)
    up_full = gathered(VC + FC, FC)
    last_shard, early = tied(rest_shard[:, down_at:], early)
    down_a = Gather(last_shard[:, :cut], True)
    down_b = Gather(last_shard[:, cut:], False)
    down_full = jnp.concatenate([down_a.rest(), down_b.rest()], axis=1)

    qk_full = early[:, : 2 * QC]
    value_full = early[:, 2 * QC : 2 * QC + VC]
    small_float = early[:, 2 * QC + VC :][:, : KS + 2].astype(f32)
    out_full = both_cores(out_half, swapped(out_half), 1)
    gain_first, gain_second = small_float[:, KS], small_float[:, KS + 1]
    taps = [part_of(small_float[:, j].reshape(CORES, VC), 0, core) for j in range(KS)]

    inputs = tokens.reshape(rows, D).astype(f32)
    scaled_first, inverse_first = norm_scale(inputs)
    scaled_chip, _ = norm_scale(
        jnp.concatenate([own_tokens, other_tokens], axis=0).astype(f32)
    )
    normed_chip = (scaled_chip * gain_first[None, :]).astype(bf16)
    query_key = halves(dot(normed_chip, qk_full).astype(bf16))
    value_pre = halves(dot(normed_chip, value_full).astype(bf16))
    tail = value_pre[:, :, slot_rows - (KS - 1) :, :]
    from_chip = passed_along(part_of(tail, 0, other), "z", 1)
    from_core = part_of(tail, 0, core)
    earlier = jnp.stack(
        [jnp.where(first_core, from_chip, from_core), jnp.where(first_core, from_core, from_chip)]
    )
    extended = jnp.concatenate([earlier, value_pre], axis=2).astype(f32)

    def tap_rows(j):
        return extended[:, :, KS - 1 - j : KS - 1 - j + slot_rows, :]

    convolved = taps[0] * tap_rows(0)
    for j in range(1, KS):
        convolved = convolved + taps[j] * tap_rows(j)
    values = convolved.astype(bf16)

    index_np, scale_np = feature_tables()
    tables = (core.astype(jnp.int32).reshape(1), jnp.asarray(index_np), jnp.asarray(scale_np))
    q_spec, k_spec, v_spec = (LANES, 0), (LANES, 1), (VC,)
    call = functools.partial(per_slot, slots=slots, rows=slot_rows)
    unit = 2 * CORES * rows * HC * LANES * FEATS
    wide = [pltpu.VMEM((CORES * slot_rows, VC), f32)]
    (state_own,) = call(
        state_kernel, ins=[k_spec, v_spec], outs=[("state", f32)], scratch=[], flops=4 * unit
    )(*tables, query_key, values)
    before = chain(state_own, True)
    mixer, dens = call(
        forward_kernel,
        ins=[q_spec, k_spec, v_spec, "state"],
        outs=[(v_spec, bf16), ((LANES,), f32)],
        scratch=wide,
        flops=8 * unit,
    )(*tables, query_key, query_key, values, before)

    mixer_flat = mixer.reshape(CORES * rows, VC)
    mixer_theirs = swapped(mixer_flat)
    mixer_own = both_cores(mixer_flat[:rows], mixer_theirs[rows:], 1)
    mixer_other = both_cores(mixer_flat[rows:], mixer_theirs[:rows], 1)
    after_mixer = inputs + dot(mixer_own, out_full)
    scaled_second, inverse_second = norm_scale(after_mixer)
    second_low = (scaled_second * gain_second[None, :]).astype(bf16)
    second_chip = on_chip(second_low)

    gate = dot(second_chip, gate_full)
    upward = dot(second_chip, up_full)
    sigmoid_gate = jax.nn.sigmoid(gate)
    silu_gate = gate * sigmoid_gate
    hidden = (silu_gate * upward).astype(bf16)

    half_at = jnp.where(first_core, jnp.arange(CORES), 1 - jnp.arange(CORES))
    positions = (z_at * CORES + half_at)[:, None] * slot_rows + jnp.arange(slot_rows)[None, :]
    valid_chip = positions[:, None, :] < lengths[None, :, None]
    valid_chip = valid_chip.astype(f32).reshape(CORES * rows, 1)
    valid = valid_chip[:rows]
    query_key, cotangent_late = lax.optimization_barrier((query_key, cotangent))
    cotangent_chip = on_chip(cotangent_late.reshape(rows, D))
    mixer, cotangent_chip = tied(mixer, cotangent_chip)
    grad_result_chip = (valid_chip * cotangent_chip.astype(f32)).astype(bf16)
    grad_result = valid * cotangent.reshape(rows, D).astype(f32)

    def scattered(terms):
        return lax.psum_scatter(terms, ("y", "x", "z"), scatter_dimension=0, tiled=True)

    down_terms, grad_result_chip = tied(
        dot_tn(grad_result_chip, hidden).astype(bf16), grad_result_chip
    )
    scatter_down = scattered(down_terms)
    down_other = swapped(dot_nt(hidden[rows:], down_full))
    grad_hidden = dot(grad_result_chip, down_full)
    grad_upward = (grad_hidden * silu_gate).astype(bf16)
    grad_gate = (
        grad_hidden * upward * sigmoid_gate * (1.0 + gate * (1.0 - sigmoid_gate))
    ).astype(bf16)
    second_other = dot_nt(grad_gate[rows:], gate_full) + dot_nt(grad_upward[rows:], up_full)
    second_own = dot_nt(grad_gate[:rows], gate_full) + dot_nt(grad_upward[:rows], up_full)
    second_own, down_other = tied(second_own, down_other)
    grad_second = second_own + swapped(second_other)
    down_result = dot_nt(hidden[:rows], down_full) + down_other
    layer_out = (valid * (after_mixer + down_result)).astype(bf16).reshape(tokens.shape)

    grad_after_norm, grad_gain_second = norm_backward(
        grad_second, scaled_second, inverse_second, gain_second
    )
    grad_after = grad_result + grad_after_norm
    grad_after_low = grad_after.astype(bf16)
    grad_mixer = dot_nt(grad_after_low, out_full).astype(bf16).reshape(rows, CORES, VC)
    grad_mixer_chip = jnp.concatenate(
        [part_of(grad_mixer, 1, core), swapped(part_of(grad_mixer, 1, other))], axis=0
    )
    after_columns = grad_after_low.reshape(rows, CORES, VC)
    grad_after_chip = jnp.concatenate(
        [part_of(after_columns, 1, core), swapped(part_of(after_columns, 1, other))], axis=0
    )
    mixer_chip = jnp.concatenate([mixer_own, mixer_other], axis=0)

    wide_spec = (HC * LANES,)
    pulled, grad_num = call(
        pull_kernel,
        ins=[q_spec, v_spec, v_spec, (LANES,)],
        outs=[("state", f32), (wide_spec, bf16)],
        scratch=[],
        flops=4 * unit,
    )(*tables, query_key, halves(grad_mixer_chip), mixer, dens)
    from_later = chain(pulled, False)
    grad_query_key, grad_values = call(
        backward_kernel,
        ins=[q_spec, k_spec, v_spec, wide_spec, "state", "state"],
        outs=[((2 * LANES,), bf16), (v_spec, bf16)],
        scratch=wide,
        flops=24 * unit,
    )(*tables, query_key, query_key, values, grad_num, before, from_later)

    head = grad_values[:, :, : KS - 1, :]
    from_chip = passed_along(part_of(head, 0, core), "z", -1)
    from_core = part_of(head, 0, other)
    later = jnp.stack(
        [jnp.where(first_core, from_core, from_chip), jnp.where(first_core, from_chip, from_core)]
    )
    grad_extended = jnp.concatenate([grad_values, later], axis=2).astype(f32)
    grad_pre = taps[0] * grad_extended[:, :, :slot_rows, :]
    for j in range(1, KS):
        grad_pre = grad_pre + taps[j] * grad_extended[:, :, j : j + slot_rows, :]
    grad_pre = grad_pre.reshape(CORES * rows, VC).astype(bf16)
    grad_query_key = grad_query_key.reshape(CORES * rows, 2 * QC)
    grad_values_float = grad_values.astype(f32)
    tap_grads = [jnp.sum(grad_values_float * tap_rows(j), axis=(0, 1, 2)) for j in range(KS)]

    first_other = dot_nt(grad_query_key[rows:], qk_full) + dot_nt(grad_pre[rows:], value_full)
    first_own = dot_nt(grad_query_key[:rows], qk_full) + dot_nt(grad_pre[:rows], value_full)
    grad_first = first_own + swapped(first_other)
    grad_gain_first = jnp.sum(first_own * scaled_chip[:rows], axis=0) + jnp.sum(
        first_other * scaled_chip[rows:], axis=0
    )

    def whole_feature(part):
        return lax.dynamic_update_slice(jnp.zeros((D,), f32), part, (core * VC,))

    small_terms = jnp.stack(
        [whole_feature(part) for part in tap_grads] + [grad_gain_first, grad_gain_second], axis=1
    )
    small_terms = jnp.pad(small_terms, ((0, 0), (0, LANES - (KS + 2)))).astype(bf16)
    operands = (
        grad_gate,
        grad_upward,
        grad_pre,
        grad_after_chip,
        grad_query_key,
        small_terms,
    )
    in_kernel = tuple(lax.axis_size(axis) for axis in ("y", "x", "z")) == (2, 2, 4)
    if in_kernel:
        lefts = [jnp.transpose(left) for left in (second_chip, normed_chip, mixer_chip)]
        sums = reduced(*lefts, *operands)
        gate_to, mid_to = FC, FC + VC
        sum_gate, sum_up = sums[0, :, :gate_to], sums[1, :, :gate_to]
        sum_value, sum_out = sums[0, :, gate_to:mid_to], sums[1, :, gate_to:mid_to]
        sum_last = jnp.concatenate(
            [sums[0, :, mid_to : mid_to + QC], sums[1, :, mid_to : mid_to + QC], sums[0, :, mid_to + QC :]],
            axis=1,
        )
    else:
        sum_gate = Scatter(dot_tn(second_chip, grad_gate).astype(bf16), False).rest()
        sum_up = Scatter(dot_tn(second_chip, grad_upward).astype(bf16), True).rest()
        sum_value = Scatter(dot_tn(normed_chip, grad_pre).astype(bf16), False).rest()
        sum_out = Scatter(dot_tn(mixer_chip, grad_after_chip).astype(bf16), True).rest()
        qk_terms = dot_tn(normed_chip, grad_query_key).astype(bf16)
        sum_last = Scatter(jnp.concatenate([qk_terms, small_terms], axis=1), True).rest()
    grad_input_norm, _ = norm_backward(grad_first, scaled_first, inverse_first, gain_first)
    input_grad = (grad_after + grad_input_norm).reshape(tokens.shape)

    def rows_of(array, index):
        return part_of(array.reshape(CORES, owned, -1), 0, index)

    def finish(*parts):
        merged = jnp.concatenate(parts, axis=1) if len(parts) > 1 else parts[0]
        mine, theirs = rows_of(merged, core), swapped(rows_of(merged, other))
        return mine.astype(f32), theirs.astype(f32)

    def columns(*parts):
        mine, theirs = finish(*parts)
        return both_cores(mine, theirs, 1)

    def two_columns(mine, theirs, width):
        shape = (owned, 2, 1, width)
        return both_cores(mine.reshape(shape), theirs.reshape(shape), 2).reshape(owned, -1)

    grad_down_own = columns(scatter_down)
    grad_gu_own = two_columns(*finish(sum_gate, sum_up), FC)
    grad_out_own = columns(sum_out)
    grad_value_own = columns(sum_value)
    last_mine, last_theirs = finish(sum_last)
    grad_qk_own = two_columns(last_mine[:, : 2 * QC], last_theirs[:, : 2 * QC], QC)
    grad_small_own = (last_mine + last_theirs)[:, 2 * QC : 2 * QC + KS + 2]

    grads_all = (
        grad_qk_own,
        grad_value_own,
        grad_out_own,
        grad_gu_own,
        grad_down_own,
        grad_small_own,
    )
    masters = (w_qk, w_value, w_out, w_gu, w_down, small_params)
    firsts = (m_qk, m_value, m_out, m_gu, m_down, m_small)
    seconds = (v_qk, v_value, v_out, v_gu, v_down, v_small)
    learn_rates = (
        0.05 / math.sqrt(D),
        0.05 / math.sqrt(D),
        0.05 / math.sqrt(max(D // 128, 1)),
        0.05 / math.sqrt(D),
        0.05 / math.sqrt(0.0003 * FF * SLOT**0.825),
        0.014,
    )
    decays = (weight_decay, weight_decay, weight_decay, weight_decay, weight_decay, 0.0)
    new_weights = []
    new_seconds = []
    for position in range(6):
        updated, moment = adam_update(
            masters[position],
            grads_all[position],
            firsts[position],
            seconds[position],
            learn_rates[position],
            decays[position],
        )
        new_weights.append(updated)
        new_seconds.append(moment)
    return (layer_out, input_grad) + grads_all + tuple(new_weights) + tuple(new_seconds)


def solution(mesh):
    dp, fsdp = mesh.shape["dp"], mesh.shape["fsdp"]
    y_size = 2 if dp % 2 == 0 else 1
    split = Mesh(
        mesh.devices.reshape(y_size, dp // y_size, fsdp // CORES, CORES), ("y", "x", "z", "core")
    )
    slot_axes, row_axes = ("y", "x"), ("z", "core")
    activation = P(slot_axes, row_axes, None)
    weight = P(slot_axes + row_axes, None)
    return jax.shard_map(
        local,
        mesh=split,
        in_specs=(activation, activation, P(slot_axes)) + (weight,) * 18,
        out_specs=(activation, activation) + (weight,) * 18,
        check_vma=False,
    )
```

time: 1150 us -> 1090 us (0.948)
  Pallas kernels: 59.3 us -> 304 us
  starting transfers between devices: 172 us -> 65.4 us
  local copies, waits for them, and re-layouts: 226 us -> 123 us
  waiting for transfers between devices: 374 us -> 293 us
  matrix products: 196 us -> 160 us
  other arithmetic: 107 us -> 122 us
  between operations: 3.38 us -> 15.7 us
    pallas_call x0 -> x1, Pallas kernels: none -> 245 us  [reduced(): pl.pallas_call(functools.partial(reduce_kernel, (ffn, mid, total)), out_s...]
    ppermute x75 -> x16, waiting for transfers between devices: 369 us -> 169 us  [exchanged(): return lax.ppermute(array, axis, [(i, i ^ 1 << bit) for i in range(count)])]
    ppermute x75 -> x16, starting transfers between devices: 158 us -> 17.4 us  [exchanged(): return lax.ppermute(array, axis, [(i, i ^ 1 << bit) for i in range(count)])]
    ppermute x6, waiting for transfers between devices: 3.47 us -> 93 us  [chain(): total = total + lax.ppermute(message, 'z', [pair]).astype(f32)]
    dot_general x20 -> x6, matrix products: 119 us -> 70.2 us  [dot(): lax.dot_general(a, b, (((1,), (0,)), ((), ())), preferred_element_type=f32)]
    dynamic_update_slice x49 -> x30, local copies, waits for them, and re-layouts: 71.7 us -> 28.7 us  [the longest x14 14.5 us: stage(): whole = lax.dynamic_update_index_in_dim(whole, self.block, mine, dim)]
    dynamic_slice x25 -> x12, local copies, waits for them, and re-layouts: 54.2 us -> 16.5 us  [part_of(): return lax.dynamic_index_in_dim(array, index, axis, keepdims=False)]
    transpose x4 -> x0, local copies, waits for them, and re-layouts: 24.2 us -> none  [the longest x1 6.33 us: local(): jnp.transpose(mixer_full)]
  transfers between devices with their start and end apart: 101 -> 45, of which waited for: 47 -> 18; matrix products, arithmetic and copies ran while one was open for 37% -> 29% of each run, Pallas kernels for 5% -> 27%
where the time goes in v2:
time: 1090 us; the launch traced here: 1080 us
  Pallas kernels  304 us (28%)
  waiting for transfers between devices  293 us (27%)
  matrix products  160 us (15%)
  local copies, waits for them, and re-layouts  123 us (11%)
  other arithmetic  122 us (11%)
  starting transfers between devices  65.4 us (6%)
  between operations  15.7 us (1%)
    pallas_call x1, Pallas kernels, reduced(): pl.pallas_call(functools.partial(reduce_kernel, (ffn, mid, total)), out_s...  245 us
    ppermute x16, waiting for transfers between devices, exchanged(): return lax.ppermute(array, axis, [(i, i ^ 1 << bit) for i in range(count)])  169 us
    ppermute x6, waiting for transfers between devices, chain(): total = total + lax.ppermute(message, 'z', [pair]).astype(f32)  93 us
    dot_general x11, matrix products, dot_nt(): lax.dot_general(a, b, (((1,), (1,)), ((), ())), preferred_element_type=f32)  75.2 us
    dot_general x6, matrix products, dot(): lax.dot_general(a, b, (((1,), (0,)), ((), ())), preferred_element_type=f32)  70.2 us
    pallas_call x1, Pallas kernels, local(): call(backward_kernel, ins=[q_spec, k_spec, v_spec, wide_spec, 'state', 's...  28.1 us
    ppermute x6, starting transfers between devices, chain(): total = total + lax.ppermute(message, 'z', [pair]).astype(f32)  27.7 us
    transpose x3, other arithmetic, local(): jnp.transpose(left)  25.9 us
  transfers between devices with their start and end apart: 45, of which 18 were waited for; matrix products, arithmetic and copies ran while one was open for 29% of the time, Pallas kernels for 27%

profile of v2, /device:TPU:0, one launch (start us, length us, event | category | flops | bytes accessed | tf_op | source)
XLA Modules:
  0.0 1082.9 jit_solution(2628264133453201432)
XLA Ops:
  12.2 7.5 dynamic-slice_reduce_fusion.1
  29.0 9.5 all-gather.6.cloned.1.call-start
  40.8 2.8 copy.330
  44.1 4.0 collective-permute-start.7
  49.5 11.0 %collective-permute-done.7 = bf16[112,640]{1,0:T(8,128)(2,1)S(1)} collective-permute-done((bf16[112,640]{1,0:T(8,128)(2,1)S(1)}, bf16[112,640]{1,0:T(8,128)(2,1)S(1)}, u32[]{:S(2)}, u32[]{:S(2)}) %collective-permute-start.7) | collective-permute-done | bytes 143392 | tf_op jit(solution)/shard_map/ppermute | solution.py:288
  65.0 10.6 collective-permute-done.8
  79.5 4.6 collective-permute-done.2
  91.9 19.5 %collective-permute-done.5 = bf16[2,2,112,640]{3,2,1,0:T(8,128)(2,1)} collective-permute-done((bf16[2,2,112,640]{3,2,1,0:T(8,128)(2,1)}, bf16[2,2,112,640]{3,2,1,0:T(8,128)(2,1)}, u32[]{:S(2)}, u32[]{:S(2)}) %collective-permute-start.5) | collective-permute-done | bytes 573472 | tf_op jit(solution)/shard_map/ppermute | solution.py:288
  116.7 18.6 %collective-permute-done.10 = bf16[2,2,2,112,640]{4,3,2,1,0:T(8,128)(2,1)S(1)} collective-permute-done((bf16[2,2,2,112,640]{4,3,2,1,0:T(8,128)(2,1)S(1)}, bf16[2,2,2,112,640]{4,3,2,1,0:T(8,128)(2,1)S(1)}, u32[]{:S(2)}, u32[]{:S(2)}) %collective-permute-start.10) | collective-permute-done | bytes 1146912 | tf_op jit(solution)/shard_map/ppermute | solution.py:288
  139.1 3.9 convolution_convert_fusion.1
  143.0 5.9 fusion.40
  152.8 5.3 collective-permute-start.11
  165.8 8.5 shard_map.374
  175.8 23.3 %collective-permute-start.12 = (bf16[2,8,160,128]{3,2,1,0:T(8,128)(2,1)S(1)}, bf16[2,8,160,128]{3,2,1,0:T(8,128)(2,1)S(1)}, u32[]{:S(2)}, u32[]{:S(2)}) collective-permute-start(bf16[2,8,160,128]{3,2,1,0:T(8,128)(2,1)S(1)} %convert_element_type.172), channel_id=1, source_target_pairs={{0,2},{1,3},{8,10},{9,11},{16,18},{17,19},{24,26},{25,27}} | collective-permute-start | bytes 1966088 | tf_op jit(solution)/shard_map/ppermute | solution.py:363
  204.3 18.8 %collective-permute-done.12 = bf16[2,8,160,128]{3,2,1,0:T(8,128)(2,1)S(1)} collective-permute-done((bf16[2,8,160,128]{3,2,1,0:T(8,128)(2,1)S(1)}, bf16[2,8,160,128]{3,2,1,0:T(8,128)(2,1)S(1)}, u32[]{:S(2)}, u32[]{:S(2)}) %collective-permute-start.12) | collective-permute-done | bytes 655392 | tf_op jit(solution)/shard_map/ppermute | solution.py:363
  223.9 21.4 %collective-permute-done.19 = bf16[2,112,1152]{2,1,0:T(8,128)(2,1)S(1)} collective-permute-done((bf16[2,112,1152]{2,1,0:T(8,128)(2,1)}, bf16[2,112,1152]{2,1,0:T(8,128)(2,1)S(1)}, u32[]{:S(2)}, u32[]{:S(2)}) %collective-permute-start.19) | collective-permute-done | bytes 516128 | tf_op jit(solution)/shard_map/ppermute | solution.py:288
  249.1 19.6 %collective-permute-done.23 = bf16[2,112,1280]{2,1,0:T(8,128)(2,1)S(1)} collective-permute-done((bf16[2,112,1280]{2,1,0:T(8,128)(2,1)S(1)}, bf16[2,112,1280]{2,1,0:T(8,128)(2,1)S(1)}, u32[]{:S(2)}, u32[]{:S(2)}) %collective-permute-start.23) | collective-permute-done | bytes 573472 | tf_op jit(solution)/shard_map/ppermute | solution.py:288
  276.8 11.7 %shard_map.375 = (bf16[2,2,256,896]{3,2,1,0:T(8,128)(2,1)}, f32[2,2,256,128]{3,2,1,0:T(8,128)}) custom-call(s32[1]{0:T(128)} %bitcast.1.core_ref, s32[8,256]{1,0:T(8,128)} %constant.322.clone.index_ref, f32[8,256]{1,0:T(8,128)} %constant.323.clone.scale_ref, bf16[2,2,256,256]{3,2,1,0:T(8,128)(2,1)} %bitcast.289, bf16[2,2,256,256]{3,2,1,0:T(8,128)(2,1)} %bitcast.290, ...), custom_call_target="tpu_custom_call" | custom-call | flops 4294967296 | bytes 8388608 | tf_op jit(solution)/shard_map/pallas_call | solution.py:692
  288.6 3.8 copy.332
  295.1 3.2 bitcast_dynamic-update-slice_fusion.3
  298.3 4.3 pad_maximum_fusion.7
  308.8 4.7 multiply_convert_fusion.3
  317.2 2.9 broadcast_select_fusion.7
  320.1 3.4 broadcast_select_fusion.1
  323.6 3.9 multiply_reduce_fusion.3
  330.8 3.2 bitcast_dynamic-update-slice_fusion
  334.0 14.6 %collective-permute-done.21 = bf16[2,2,2,112,1152]{4,3,2,1,0:T(8,128)(2,1)} collective-permute-done((bf16[2,2,2,112,1152]{4,3,2,1,0:T(8,128)(2,1)}, bf16[2,2,2,112,1152]{4,3,2,1,0:T(8,128)(2,1)}, u32[]{:S(2)}, u32[]{:S(2)}) %collective-permute-start.21) | collective-permute-done | bytes 2064416 | tf_op jit(solution)/shard_map/ppermute | solution.py:288
  348.6 3.1 bitcast_dynamic-update-slice_fusion.2
  351.7 45.6 %collective-permute-done.25 = bf16[2,2,2,112,1280]{4,3,2,1,0:T(8,128)(2,1)S(1)} collective-permute-done((bf16[2,2,2,112,1280]{4,3,2,1,0:T(8,128)(2,1)}, bf16[2,2,2,112,1280]{4,3,2,1,0:T(8,128)(2,1)S(1)}, u32[]{:S(2)}, u32[]{:S(2)}) %collective-permute-start.25) | collective-permute-done | bytes 2293792 | tf_op jit(solution)/shard_map/ppermute | solution.py:288
  398.9 15.5 %fusion.51 = f32[1024,2432]{1,0:T(8,128)} fusion(bf16[1792,2432]{1,0:T(8,128)(2,1)} %all-gather.6.cloned.1.call-done, bf16[512,1792]{0,1:T(8,128)(2,1)} %collective-permute-done.17, bf16[512,1792]{0,1:T(8,128)(2,1)S(1)} %multiply_convert_fusion.6), kind=kOutput, calls=%fused_computation.134 | convolution fusion | flops 8932818944 | bytes 22347776 | tf_op jit(solution)/shard_map/dot_general | solution.py:62
  414.3 23.1 %all-gather.8.cloned.1.call-done = bf16[1792,2432]{1,0:T(8,128)(2,1)} async-done(((bf16[112,2432]{1,0:T(8,128)(2,1)}), bf16[1792,2432]{1,0:T(8,128)(2,1)}) %all-gather.8.cloned.1.call-update) | async-done | bytes 8716304 | tf_op jit(solution)/shard_map/all_gather | solution.py:641
  437.5 19.4 %multiply_convert_fusion.2 = (bf16[1024,2432]{1,0:T(8,128)(2,1)}, f32[1024,2432]{1,0:T(8,128)}) fusion(f32[1024,2432]{1,0:T(8,128)} %fusion.51, bf16[1792,2432]{1,0:T(8,128)(2,1)} %all-gather.8.cloned.1.call-done, bf16[512,1792]{0,1:T(8,128)(2,1)} %collective-permute-done.17, bf16[512,1792]{0,1:T(8,128)(2,1)S(1)} %multiply_convert_fusion.6), kind=kOutput, calls=%fused_computation.3 | convolution fusion | flops 8947761152 | bytes 37289984 | tf_op jit(solution)/shard_map/dot_general | solution.py:62
  456.9 14.8 %convolution_convert_fusion = bf16[1792,2432]{1,0:T(8,128)(2,1)} fusion(bf16[1024,1792]{1,0:T(8,128)(2,1)S(1)} %copy-done.21, bf16[1024,2432]{1,0:T(8,128)(2,1)} %get-tuple-element.299), kind=kOutput, calls=%fused_computation | convolution fusion | flops 8929837056 | bytes 17367040 | tf_op jit(solution)/shard_map/dot_general | solution.py:70
  471.6 11.1 %fusion.19 = f32[512,1792]{0,1:T(8,128)} fusion(bf16[1792,1280]{1,0:T(8,128)(2,1)} %bitcast.53, bf16[1792,1152]{1,0:T(8,128)(2,1)} %bitcast.42, bf16[1024,2432]{1,0:T(8,128)(2,1)} %get-tuple-element.299), kind=kOutput, calls=%fused_computation.65 | convolution fusion | flops 4480172032 | bytes 14876672 | tf_op jit(solution)/shard_map/dot_general | solution.py:66
  482.7 21.6 %multiply_convert_fusion = (bf16[1024,2432]{1,0:T(8,128)(2,1)}, bf16[1024,2432]{1,0:T(8,128)(2,1)}) fusion(f32[1024,2432]{1,0:T(8,128)} %fusion.51, f32[1024,2432]{1,0:T(8,128)} %get-tuple-element.300, bf16[1024,1792]{1,0:T(8,128)(2,1)} %multiply_convert_fusion.3, bf16[1792,1280]{1,0:T(8,128)(2,1)} %bitcast.53, bf16[1792,1152]{1,0:T(8,128)(2,1)} %bitcast.42), kind=kOutput, calls=%fused_computation.1 | convolution fusion | flops 8975286272 | bytes 42270720 | tf_op jit(solution)/shard_map/dot_general | solution.py:62
  504.3 8.3 fusion.23
  512.7 10.4 convolution_add_fusion.2
  523.6 3.6 bitcast_convert_fusion
  527.1 5.2 copy.334
  532.4 8.5 fusion.27
  540.9 7.1 convolution_add_fusion.3
  548.1 3.5 multiply_reduce_fusion
  551.6 4.6 fusion.94
  557.5 4.8 fusion.18
  562.2 4.0 reshape.417
  566.2 3.8 constant_dynamic-slice_fusion.7
  574.0 10.7 shard_map.376
  591.2 74.2 %collective-permute-done.32 = bf16[2,8,160,128]{3,2,1,0:T(8,128)(2,1)S(1)} collective-permute-done((bf16[2,8,160,128]{3,2,1,0:T(8,128)(2,1)S(1)}, bf16[2,8,160,128]{3,2,1,0:T(8,128)(2,1)S(1)}, u32[]{:S(2)}, u32[]{:S(2)}) %collective-permute-start.32) | collective-permute-done | bytes 655392 | tf_op jit(solution)/shard_map/ppermute | solution.py:363
  666.5 28.1 %shard_map.377 = (bf16[2,2,256,256]{3,2,1,0:T(8,128)(2,1)}, bf16[2,2,256,896]{3,2,1,0:T(8,128)(2,1)}) custom-call(s32[1]{0:T(128)} %bitcast.1.core_ref, s32[8,256]{1,0:T(8,128)} %constant.322.clone.index_ref, f32[8,256]{1,0:T(8,128)} %constant.323.clone.scale_ref, bf16[2,2,256,256]{3,2,1,0:T(8,128)(2,1)} %bitcast.292, bf16[2,2,256,256]{3,2,1,0:T(8,128)(2,1)} %bitcast.293, ...), custom_call_target="tpu_custom_call" | custom-call | flops 12884901888 | bytes 8388608 | tf_op jit(solution)/shard_map/pallas_call | solution.py:770
  698.1 3.9 collective-permute-done.33
  711.4 6.1 fusion.87
  717.5 15.9 %maximum_bitcast_fusion.mixer_ref = bf16[1792,1024]{1,0:T(8,128)(2,1)} fusion(bf16[512,896]{0,1:T(8,128)(2,1)S(1)} %copy-done.23, bf16[512,896]{0,1:T(8,128)(2,1)S(1)} %copy-done.22, bf16[512,896]{0,1:T(8,128)(2,1)S(1)} %copy-done.25, bf16[512,896]{0,1:T(8,128)(2,1)S(1)} %copy-done.27), kind=kLoop, calls=%fused_computation.43 | loop fusion | flops 14680064 | bytes 7340032 | tf_op jit(solution)/shard_map/transpose | solution.py:817
  733.5 3.9 fusion.49.second_ref
  741.6 10.3 multiply_convert_fusion.5
  751.8 4.2 copy.333
  758.8 5.8 fusion.12
  764.7 4.0 fusion.32
  768.7 6.2 fusion.13
  776.2 244.7 %shard_map.378 = f32[2,112,3584]{2,1,0:T(8,128)} custom-call(bf16[1792,1024]{1,0:T(8,128)(2,1)} %fusion.49.second_ref, bf16[1792,1024]{1,0:T(8,128)(2,1)} %get-tuple-element.241.normed_ref, bf16[1792,1024]{1,0:T(8,128)(2,1)} %maximum_bitcast_fusion.mixer_ref, bf16[1024,2432]{1,0:T(8,128)(2,1)} %get-tuple-element.238.gate_ref, ...), custom_call_target="tpu_custom_call" | custom-call | flops 26306674688 | bytes 419430400 | tf_op jit(solution)/shard_map/pallas_call | solution.py:519
  1032.8 7.0 fusion.9
  1039.9 5.4 copy.335
  1059.0 3.3 pad_maximum_fusion.17
  1062.3 4.0 reshape.425
  1067.4 6.7 multiply_subtract_fusion
  (410 shorter events, 154.4 us)
Async XLA Ops:
  7.2 269.6 %all-gather.4.cloned.1.call-start = ((), (), s32[]{:S(2)}) async-start(), calls=%async_computation.1 | async-start | bytes 3411968 | tf_op jit(solution)/shard_map/all_gather | solution.py:641
  23.1 2.8 collective-permute-start.4
  28.3 11.5 %copy-start.44 = (bf16[56,1,1,896]{3,2,0,1:T(2,128)(2,1)S(1)}, bf16[56,1,1,896]{3,2,0,1:T(2,128)(2,1)}, u32[]{:S(2)}) copy-start(bf16[56,1,1,896]{3,2,0,1:T(2,128)(2,1)} %get-tuple-element.302) | copy-start | bytes 301060
  28.3 11.5 %copy-start.47 = (f32[56,512]{1,0:T(8,128)S(1)}, f32[56,512]{1,0:T(8,128)}, u32[]{:S(2)}) copy-start(f32[56,512]{1,0:T(8,128)} %param.26) | copy-start | bytes 344068
  28.3 11.9 %copy-start.62 = (f32[56,5]{0,1:T(8,128)S(1)}, f32[56,5]{0,1:T(8,128)}, u32[]{:S(2)}) copy-start(f32[56,5]{0,1:T(8,128)} %param.31) | copy-start | bytes 3364
  29.0 369.8 %all-gather.6.cloned.1.call-start = ((), (), s32[]{:S(2)}) async-start(), calls=%async_computation.2 | async-start | bytes 9261056 | tf_op jit(solution)/shard_map/all_gather | solution.py:641
  39.7 397.8 %all-gather.8.cloned.1.call-start = ((), (), s32[]{:S(2)}) async-start(), calls=%async_computation.3 | async-start | bytes 9261056 | tf_op jit(solution)/shard_map/all_gather | solution.py:641
  40.4 3.6 collective-permute-start
  43.7 279.9 %copy-start.1 = (bf16[512,1792]{0,1:T(8,128)(2,1)}, bf16[512,1792]{0,1:T(8,128)(2,1)S(1)}, u32[]{:S(2)}) copy-start(bf16[512,1792]{0,1:T(8,128)(2,1)S(1)} %copy.330) | copy-start | bytes 5505028
  43.7 41.2 %collective-permute-start.3 = (bf16[512,1792]{0,1:T(8,128)(2,1)S(1)}, bf16[512,1792]{0,1:T(8,128)(2,1)}, u32[]{:S(2)}, u32[]{:S(2)}) collective-permute-start(bf16[512,1792]{0,1:T(8,128)(2,1)S(1)} %copy.330), channel_id=1, source_target_pairs={{0,1},{1,0},{2,3},{3,2},{4,5},{5,4},{6,7},{7,6},{8,9},{9,8},{10,11... | collective-permute-start | bytes 5505032 | tf_op jit(solution)/shard_map/ppermute | solution.py:271
  44.1 16.4 %collective-permute-start.7 = (bf16[112,640]{1,0:T(8,128)(2,1)S(1)}, bf16[112,640]{1,0:T(8,128)(2,1)S(1)}, u32[]{:S(2)}, u32[]{:S(2)}) collective-permute-start(bf16[112,640]{1,0:T(8,128)(2,1)S(1)} %get-tuple-element.236), channel_id=1, source_target_pairs={{0,4},{2,6},{4,0},{6,2},{1,5},{3,7},{5,1},{7,3},{8,12},{10,14},{12... | collective-permute-start | bytes 430088 | tf_op jit(solution)/shard_map/ppermute | solution.py:288
  49.5 13.9 %collective-permute-start.1 = (bf16[112,640]{1,0:T(8,128)(2,1)S(1)}, bf16[112,640]{1,0:T(8,128)(2,1)S(1)}, u32[]{:S(2)}, u32[]{:S(2)}) collective-permute-start(bf16[112,640]{1,0:T(8,128)(2,1)S(1)} %get-tuple-element.234), channel_id=1, source_target_pairs={{0,4},{2,6},{4,0},{6,2},{1,5},{3,7},{5,1},{7,3},{8,12},{10,14},{12... | collective-permute-start | bytes 430088 | tf_op jit(solution)/shard_map/ppermute | solution.py:288
  60.5 15.1 %collective-permute-start.8 = (bf16[2,112,640]{2,1,0:T(8,128)(2,1)S(1)}, bf16[2,112,640]{2,1,0:T(8,128)(2,1)S(1)}, u32[]{:S(2)}, u32[]{:S(2)}) collective-permute-start(bf16[2,112,640]{2,1,0:T(8,128)(2,1)S(1)} %bitcast_dynamic-update-slice_fusion.28), channel_id=1, source_target_pairs={{0,2},{2,0},{4,6},{6,4},{1,3},{3,1},{5,7},{7,5},{8,10},{10,8},{12,... | collective-permute-start | bytes 860168 | tf_op jit(solution)/shard_map/ppermute | solution.py:288
  63.4 20.8 %collective-permute-start.2 = (bf16[2,112,640]{2,1,0:T(8,128)(2,1)S(1)}, bf16[2,112,640]{2,1,0:T(8,128)(2,1)S(1)}, u32[]{:S(2)}, u32[]{:S(2)}) collective-permute-start(bf16[2,112,640]{2,1,0:T(8,128)(2,1)S(1)} %bitcast_dynamic-update-slice_fusion.30), channel_id=1, source_target_pairs={{0,2},{2,0},{4,6},{6,4},{1,3},{3,1},{5,7},{7,5},{8,10},{10,8},{12,... | collective-permute-start | bytes 860168 | tf_op jit(solution)/shard_map/ppermute | solution.py:288
  76.4 11.8 %collective-permute-start.9 = (bf16[2,2,112,640]{3,2,1,0:T(8,128)(2,1)}, bf16[2,2,112,640]{3,2,1,0:T(8,128)(2,1)}, u32[]{:S(2)}, u32[]{:S(2)}) collective-permute-start(bf16[2,2,112,640]{3,2,1,0:T(8,128)(2,1)} %bitcast_dynamic-update-slice_fusion.20), channel_id=1, source_target_pairs={{0,16},{16,0},{1,17},{17,1},{2,18},{18,2},{3,19},{19,3},{4,20},{20... | collective-permute-start | bytes 1720328 | tf_op jit(solution)/shard_map/ppermute | solution.py:288
  84.9 26.6 %collective-permute-start.5 = (bf16[2,2,112,640]{3,2,1,0:T(8,128)(2,1)}, bf16[2,2,112,640]{3,2,1,0:T(8,128)(2,1)}, u32[]{:S(2)}, u32[]{:S(2)}) collective-permute-start(bf16[2,2,112,640]{3,2,1,0:T(8,128)(2,1)} %bitcast_dynamic-update-slice_fusion.25), channel_id=1, source_target_pairs={{0,8},{8,0},{1,9},{9,1},{2,10},{10,2},{3,11},{11,3},{4,12},{12,4},... | collective-permute-start | bytes 1720328 | tf_op jit(solution)/shard_map/ppermute | solution.py:288
  87.6 978.7 %reduce-scatter.2.cloned.1.call-start = ((), (), s32[]{:S(2)}) async-start(), calls=%async_computation.4 | async-start | bytes 9261056 | tf_op jit(solution)/shard_map/reduce_scatter | solution.py:727
  89.5 45.8 %collective-permute-start.10 = (bf16[2,2,2,112,640]{4,3,2,1,0:T(8,128)(2,1)S(1)}, bf16[2,2,2,112,640]{4,3,2,1,0:T(8,128)(2,1)S(1)}, u32[]{:S(2)}, u32[]{:S(2)}) collective-permute-start(bf16[2,2,2,112,640]{4,3,2,1,0:T(8,128)(2,1)S(1)} %bitcast_dynamic-update-slice_fusion.14), channel_id=1, source_target_pairs={{0,8},{8,0},{1,9},{9,1},{2,10},{10,2},{3,11},{11,3},{4,12},{12,4},... | collective-permute-start | bytes 3440648 | tf_op jit(solution)/shard_map/ppermute | solution.py:288
  112.6 23.3 %collective-permute-start.6 = (bf16[2,2,2,112,640]{4,3,2,1,0:T(8,128)(2,1)S(1)}, bf16[2,2,2,112,640]{4,3,2,1,0:T(8,128)(2,1)S(1)}, u32[]{:S(2)}, u32[]{:S(2)}) collective-permute-start(bf16[2,2,2,112,640]{4,3,2,1,0:T(8,128)(2,1)S(1)} %bitcast_dynamic-update-slice_fusion.16), channel_id=1, source_target_pairs={{0,16},{16,0},{1,17},{17,1},{2,18},{18,2},{3,19},{19,3},{4,20},{20... | collective-permute-start | bytes 3440648 | tf_op jit(solution)/shard_map/ppermute | solution.py:288
  116.7 26.3 %copy-start.64 = (f32[1024]{0:T(1024)}, f32[1024]{0:T(1024)S(1)}, u32[]{:S(2)}) copy-start(f32[1024]{0:T(1024)S(1)} %add_rsqrt_fusion) | copy-start | bytes 12292
  148.9 9.3 copy-start.35
  151.3 47.9 %collective-permute-start.18 = (bf16[112,1152]{1,0:T(8,128)(2,1)}, bf16[112,1152]{1,0:T(8,128)(2,1)}, u32[]{:S(2)}, u32[]{:S(2)}) collective-permute-start(bf16[112,1152]{1,0:T(8,128)(2,1)} %slice.201), channel_id=1, source_target_pairs={{0,4},{2,6},{4,0},{6,2},{1,5},{3,7},{5,1},{7,3},{8,12},{10,14},{12... | collective-permute-start | bytes 774152 | tf_op jit(solution)/shard_map/ppermute | solution.py:288
  152.8 7.9 collective-permute-start.11
  158.2 43.8 %collective-permute-start.22 = (bf16[112,1280]{1,0:T(8,128)(2,1)S(1)}, bf16[112,1280]{1,0:T(8,128)(2,1)S(1)}, u32[]{:S(2)}, u32[]{:S(2)}) collective-permute-start(bf16[112,1280]{1,0:T(8,128)(2,1)S(1)} %slice.202), channel_id=1, source_target_pairs={{0,4},{2,6},{4,0},{6,2},{1,5},{3,7},{5,1},{7,3},{8,12},{10,14},{12... | collective-permute-start | bytes 860168 | tf_op jit(solution)/shard_map/ppermute | solution.py:288
  158.3 139.9 %collective-permute-start.26 = (bf16[512,1792]{1,0:T(8,128)(2,1)}, bf16[512,1792]{1,0:T(8,128)(2,1)}, u32[]{:S(2)}, u32[]{:S(2)}) collective-permute-start(bf16[512,1792]{1,0:T(8,128)(2,1)} %bitcast.54), channel_id=1, source_target_pairs={{0,1},{1,0},{2,3},{3,2},{4,5},{5,4},{6,7},{7,6},{8,9},{9,8},{10,11... | collective-permute-start | bytes 5505032 | tf_op jit(solution)/shard_map/ppermute | solution.py:271
  174.3 48.8 %copy-start.6 = (f32[2,8,160,128]{3,2,1,0:T(8,128)S(1)}, f32[2,8,160,128]{3,2,1,0:T(8,128)}, u32[]{:S(2)}) copy-start(f32[2,8,160,128]{3,2,1,0:T(8,128)} %shard_map.374) | copy-start | bytes 3932164
  175.8 47.3 %collective-permute-start.12 = (bf16[2,8,160,128]{3,2,1,0:T(8,128)(2,1)S(1)}, bf16[2,8,160,128]{3,2,1,0:T(8,128)(2,1)S(1)}, u32[]{:S(2)}, u32[]{:S(2)}) collective-permute-start(bf16[2,8,160,128]{3,2,1,0:T(8,128)(2,1)S(1)} %convert_element_type.172), channel_id=1, source_target_pairs={{0,2},{1,3},{8,10},{9,11},{16,18},{17,19},{24,26},{25,27}} | collective-permute-start | bytes 1966088 | tf_op jit(solution)/shard_map/ppermute | solution.py:363
  200.8 44.5 %collective-permute-start.19 = (bf16[2,112,1152]{2,1,0:T(8,128)(2,1)}, bf16[2,112,1152]{2,1,0:T(8,128)(2,1)S(1)}, u32[]{:S(2)}, u32[]{:S(2)}) collective-permute-start(bf16[2,112,1152]{2,1,0:T(8,128)(2,1)} %bitcast_dynamic-update-slice_fusion.26), channel_id=1, source_target_pairs={{0,2},{2,0},{4,6},{6,4},{1,3},{3,1},{5,7},{7,5},{8,10},{10,8},{12,... | collective-permute-start | bytes 1548296 | tf_op jit(solution)/shard_map/ppermute | solution.py:288
  202.0 66.6 %collective-permute-start.23 = (bf16[2,112,1280]{2,1,0:T(8,128)(2,1)S(1)}, bf16[2,112,1280]{2,1,0:T(8,128)(2,1)S(1)}, u32[]{:S(2)}, u32[]{:S(2)}) collective-permute-start(bf16[2,112,1280]{2,1,0:T(8,128)(2,1)S(1)} %bitcast_dynamic-update-slice_fusion.23), channel_id=1, source_target_pairs={{0,2},{2,0},{4,6},{6,4},{1,3},{3,1},{5,7},{7,5},{8,10},{10,8},{12,... | collective-permute-start | bytes 1720328 | tf_op jit(solution)/shard_map/ppermute | solution.py:288
  223.2 46.8 %collective-permute-start.13 = (bf16[2,8,160,128]{3,2,1,0:T(8,128)(2,1)S(1)}, bf16[2,8,160,128]{3,2,1,0:T(8,128)(2,1)S(1)}, u32[]{:S(2)}, u32[]{:S(2)}) collective-permute-start(bf16[2,8,160,128]{3,2,1,0:T(8,128)(2,1)S(1)} %fusion.43), channel_id=1, source_target_pairs={{2,4},{3,5},{10,12},{11,13},{18,20},{19,21},{26,28},{27,29}} | collective-permute-start | bytes 1966088 | tf_op jit(solution)/shard_map/ppermute | solution.py:363
  245.4 28.5 %collective-permute-start.20 = (bf16[2,2,112,1152]{3,2,1,0:T(8,128)(2,1)S(1)}, bf16[2,2,112,1152]{3,2,1,0:T(8,128)(2,1)S(1)}, u32[]{:S(2)}, u32[]{:S(2)}) collective-permute-start(bf16[2,2,112,1152]{3,2,1,0:T(8,128)(2,1)S(1)} %bitcast_dynamic-update-slice_fusion.19), channel_id=1, source_target_pairs={{0,8},{8,0},{1,9},{9,1},{2,10},{10,2},{3,11},{11,3},{4,12},{12,4},... | collective-permute-start | bytes 3096584 | tf_op jit(solution)/shard_map/ppermute | solution.py:288
  268.7 44.8 %collective-permute-start.24 = (bf16[2,2,112,1280]{3,2,1,0:T(8,128)(2,1)S(1)}, bf16[2,2,112,1280]{3,2,1,0:T(8,128)(2,1)}, u32[]{:S(2)}, u32[]{:S(2)}) collective-permute-start(bf16[2,2,112,1280]{3,2,1,0:T(8,128)(2,1)S(1)} %bitcast_dynamic-update-slice_fusion.13), channel_id=1, source_target_pairs={{0,16},{16,0},{1,17},{17,1},{2,18},{18,2},{3,19},{19,3},{4,20},{20... | collective-permute-start | bytes 3440648 | tf_op jit(solution)/shard_map/ppermute | solution.py:288
  270.2 5.5 collective-permute-start.14
  274.9 73.7 %collective-permute-start.21 = (bf16[2,2,2,112,1152]{4,3,2,1,0:T(8,128)(2,1)}, bf16[2,2,2,112,1152]{4,3,2,1,0:T(8,128)(2,1)}, u32[]{:S(2)}, u32[]{:S(2)}) collective-permute-start(bf16[2,2,2,112,1152]{4,3,2,1,0:T(8,128)(2,1)} %bitcast_dynamic-update-slice_fusion.10), channel_id=1, source_target_pairs={{0,16},{16,0},{1,17},{17,1},{2,18},{18,2},{3,19},{19,3},{4,20},{20... | collective-permute-start | bytes 6193160 | tf_op jit(solution)/shard_map/ppermute | solution.py:288
  276.8 43.3 %collective-permute-start.16 = (bf16[1792,896]{1,0:T(8,128)(2,1)}, bf16[1792,896]{1,0:T(8,128)(2,1)}, u32[]{:S(2)}, u32[]{:S(2)}) collective-permute-start(bf16[1792,896]{1,0:T(8,128)(2,1)} %all-gather.4.cloned.1.call-done), channel_id=1, source_target_pairs={{0,1},{1,0},{2,3},{3,2},{4,5},{5,4},{6,7},{7,6},{8,9},{9,8},{10,11... | collective-permute-start | bytes 9633800 | tf_op jit(solution)/shard_map/ppermute | solution.py:271
  292.3 24.9 %collective-permute-start.15 = (bf16[1024,896]{0,1:T(8,128)(2,1)}, bf16[1024,896]{0,1:T(8,128)(2,1)}, u32[]{:S(2)}, u32[]{:S(2)}) collective-permute-start(bf16[1024,896]{0,1:T(8,128)(2,1)} %copy.332), channel_id=1, source_target_pairs={{0,1},{1,0},{2,3},{3,2},{4,5},{5,4},{6,7},{7,6},{8,9},{9,8},{10,11... | collective-permute-start | bytes 5505032 | tf_op jit(solution)/shard_map/ppermute | solution.py:271
  315.8 81.4 %collective-permute-start.25 = (bf16[2,2,2,112,1280]{4,3,2,1,0:T(8,128)(2,1)}, bf16[2,2,2,112,1280]{4,3,2,1,0:T(8,128)(2,1)S(1)}, u32[]{:S(2)}, u32[]{:S(2)}) collective-permute-start(bf16[2,2,2,112,1280]{4,3,2,1,0:T(8,128)(2,1)} %bitcast_dynamic-update-slice_fusion.6), channel_id=1, source_target_pairs={{0,8},{8,0},{1,9},{9,1},{2,10},{10,2},{3,11},{11,3},{4,12},{12,4},... | collective-permute-start | bytes 6881288 | tf_op jit(solution)/shard_map/ppermute | solution.py:288
  327.9 109.5 %copy-start.13 = (bf16[512,1792]{0,1:T(8,128)(2,1)}, bf16[512,1792]{0,1:T(8,128)(2,1)S(1)}, u32[]{:S(2)}) copy-start(bf16[512,1792]{0,1:T(8,128)(2,1)S(1)} %multiply_convert_fusion.6) | copy-start | bytes 5505028
  328.0 70.9 %collective-permute-start.17 = (bf16[512,1792]{0,1:T(8,128)(2,1)S(1)}, bf16[512,1792]{0,1:T(8,128)(2,1)}, u32[]{:S(2)}, u32[]{:S(2)}) collective-permute-start(bf16[512,1792]{0,1:T(8,128)(2,1)S(1)} %multiply_convert_fusion.6), channel_id=1, source_target_pairs={{0,1},{1,0},{2,3},{3,2},{4,5},{5,4},{6,7},{7,6},{8,9},{9,8},{10,11... | collective-permute-start | bytes 5505032 | tf_op jit(solution)/shard_map/ppermute | solution.py:271
  437.5 19.4 %copy-start.21 = (bf16[1024,1792]{1,0:T(8,128)(2,1)S(1)}, bf16[1024,1792]{1,0:T(8,128)(2,1)}, u32[]{:S(2)}) copy-start(bf16[1024,1792]{1,0:T(8,128)(2,1)} %multiply_convert_fusion.3) | copy-start | bytes 11010052
  482.7 65.3 %collective-permute-start.27 = (f32[512,1792]{0,1:T(8,128)}, f32[512,1792]{0,1:T(8,128)}, u32[]{:S(2)}, u32[]{:S(2)}) collective-permute-start(f32[512,1792]{0,1:T(8,128)} %fusion.19), channel_id=1, source_target_pairs={{0,1},{1,0},{2,3},{3,2},{4,5},{5,4},{6,7},{7,6},{8,9},{9,8},{10,11... | collective-permute-start | bytes 11010056 | tf_op jit(solution)/shard_map/ppermute | solution.py:271
  512.6 10.9 %copy-start.66 = (pred[2,2,256]{2,1,0:T(4,128)(4,1)S(1)}, pred[2,2,256]{2,1,0:T(4,128)(4,1)}, u32[]{:S(2)}) copy-start(pred[2,2,256]{2,1,0:T(4,128)(4,1)} %get-tuple-element.232) | copy-start | bytes 3076
  523.1 25.0 %collective-permute-start.28 = (f32[512,1792]{0,1:T(8,128)}, f32[512,1792]{0,1:T(8,128)}, u32[]{:S(2)}, u32[]{:S(2)}) collective-permute-start(f32[512,1792]{0,1:T(8,128)} %convolution_add_fusion.2), channel_id=1, source_target_pairs={{0,1},{1,0},{2,3},{3,2},{4,5},{5,4},{6,7},{7,6},{8,9},{9,8},{10,11... | collective-permute-start | bytes 11010056 | tf_op jit(solution)/shard_map/ppermute | solution.py:271
  527.1 13.7 %slice-start.4 = ((s8[8716288]{0:T(1024)(128)(4,1)}), s8[327680]{0:T(1024)(128)(4,1)S(1)}, s32[]{:S(2)}) async-start(s8[8716288]{0:T(1024)(128)(4,1)} %bitcast.286), calls=%async_computation.9 | async-start | bytes 655360
  570.1 2.5 collective-permute-start.29
  586.3 0.7 collective-permute-start.30
  588.5 0.7 collective-permute-start.31
  589.4 76.0 %collective-permute-start.32 = (bf16[2,8,160,128]{3,2,1,0:T(8,128)(2,1)S(1)}, bf16[2,8,160,128]{3,2,1,0:T(8,128)(2,1)S(1)}, u32[]{:S(2)}, u32[]{:S(2)}) collective-permute-start(bf16[2,8,160,128]{3,2,1,0:T(8,128)(2,1)S(1)} %add_convert_fusion.2), channel_id=1, source_target_pairs={{2,0},{3,1},{10,8},{11,9},{18,16},{19,17},{26,24},{27,25}} | collective-permute-start | bytes 1966088 | tf_op jit(solution)/shard_map/ppermute | solution.py:363
  694.6 9.3 copy-start.56
  694.6 9.3 copy-start.58
  694.6 9.3 copy-start.60
  695.5 6.5 collective-permute-start.33
  711.3 57.4 %collective-permute-start.34 = (f32[512,1792]{0,1:T(8,128)}, f32[512,1792]{0,1:T(8,128)}, u32[]{:S(2)}, u32[]{:S(2)}) collective-permute-start(f32[512,1792]{0,1:T(8,128)} %convolution_add_fusion), channel_id=1, source_target_pairs={{0,1},{1,0},{2,3},{3,2},{4,5},{5,4},{6,7},{7,6},{8,9},{9,8},{10,11... | collective-permute-start | bytes 11010056 | tf_op jit(solution)/shard_map/ppermute | solution.py:271
  717.5 15.9 %copy-start.14 = (bf16[512,1792]{0,1:T(8,128)(2,1)S(1)}, bf16[512,1792]{0,1:T(8,128)(2,1)}, u32[]{:S(2)}) copy-start(bf16[512,1792]{0,1:T(8,128)(2,1)} %copy-done.13) | copy-start | bytes 5505028
  739.7 16.3 %collective-permute-start.35 = (bf16[512,896]{1,0:T(8,128)(2,1)}, bf16[512,896]{1,0:T(8,128)(2,1)}, u32[]{:S(2)}, u32[]{:S(2)}) collective-permute-start(bf16[512,896]{1,0:T(8,128)(2,1)} %bitcast.261), channel_id=1, source_target_pairs={{0,1},{1,0},{2,3},{3,2},{4,5},{5,4},{6,7},{7,6},{8,9},{9,8},{10,11... | collective-permute-start | bytes 2752520 | tf_op jit(solution)/shard_map/ppermute | solution.py:271
  756.1 12.6 %slice-start = ((s8[7340032]{0:T(1024)(128)(4,1)}), s8[4194304]{0:T(1024)(128)(4,1)S(1)}, s32[]{:S(2)}) async-start(s8[7340032]{0:T(1024)(128)(4,1)} %bitcast.226), calls=%async_computation.5 | async-start | bytes 8388608
  758.8 9.9 slice-start.1
  1022.7 22.6 %collective-permute-start.36 = (f32[56,384]{0,1:T(8,128)}, f32[56,384]{0,1:T(8,128)}, u32[]{:S(2)}, u32[]{:S(2)}) collective-permute-start(f32[56,384]{0,1:T(8,128)} %bitcast.82), channel_id=1, source_target_pairs={{0,1},{1,0},{2,3},{3,2},{4,5},{5,4},{6,7},{7,6},{8,9},{9,8},{10,11... | collective-permute-start | bytes 258056 | tf_op jit(solution)/shard_map/ppermute | solution.py:271
  1026.0 29.1 %collective-permute-start.39 = (f32[56,4864]{1,0:T(8,128)}, f32[56,4864]{1,0:T(8,128)}, u32[]{:S(2)}, u32[]{:S(2)}) collective-permute-start(f32[56,4864]{1,0:T(8,128)} %get-tuple-element.257), channel_id=1, source_target_pairs={{0,1},{1,0},{2,3},{3,2},{4,5},{5,4},{6,7},{7,6},{8,9},{9,8},{10,11... | collective-permute-start | bytes 3268616 | tf_op jit(solution)/shard_map/ppermute | solution.py:271
  1031.6 18.2 %collective-permute-start.38 = (f32[56,896]{1,0:T(8,128)}, f32[56,896]{1,0:T(8,128)}, u32[]{:S(2)}, u32[]{:S(2)}) collective-permute-start(f32[56,896]{1,0:T(8,128)} %dynamic-slice_bitcast_fusion.1), channel_id=1, source_target_pairs={{0,1},{1,0},{2,3},{3,2},{4,5},{5,4},{6,7},{7,6},{8,9},{9,8},{10,11... | collective-permute-start | bytes 602120 | tf_op jit(solution)/shard_map/ppermute | solution.py:271
  1032.3 18.5 %collective-permute-start.37 = (f32[56,896]{1,0:T(8,128)}, f32[56,896]{1,0:T(8,128)}, u32[]{:S(2)}, u32[]{:S(2)}) collective-permute-start(f32[56,896]{1,0:T(8,128)} %dynamic-slice_bitcast_fusion.2), channel_id=1, source_target_pairs={{0,1},{1,0},{2,3},{3,2},{4,5},{5,4},{6,7},{7,6},{8,9},{9,8},{10,11... | collective-permute-start | bytes 602120 | tf_op jit(solution)/shard_map/ppermute | solution.py:271
  1039.9 9.9 copy-start.37
  1045.3 8.7 copy-start.39
  1067.3 6.8 collective-permute-start.40
  (59 other events, 320.4 us)
Sparse Core Ops, SparseCore 0:
  29.1 94.2 all-gather.3
  126.2 157.1 all-gather.5
  286.2 151.2 all-gather.7
  591.4 231.4 reduce-scatter.1

commit v3 on v2

--- a/solution.py
+++ b/solution.py
@@ -365,6 +365,8 @@
 
 
 def mesh_exchange(y, x, z, core, axis):
+    if axis == "core":
+        return (y, x, z, 1 - core)
     if axis == "y":
         return (1 - y, x, z, core)
     if axis == "x":
@@ -378,21 +380,22 @@
 
 
 def reduce_kernel(
-    tiles,
-    second_ref,
-    normed_ref,
-    mixer_ref,
+    down_a_ref,
     gate_ref,
+    down_b_ref,
     up_ref,
+    last_a_ref,
+    last_b_ref,
+    qk_ref,
     value_ref,
-    after_ref,
-    qk_ref,
+    out_ref,
+    gu_ref,
+    down_ref,
     small_ref,
-    out_ref,
-    terms,
     sums,
     halves,
     quarters,
+    finals,
     got_terms,
     got_sums,
     got_halves,
@@ -400,146 +403,427 @@
     send_sem,
     recv_sem,
 ):
+    y, x, z, core = places_of()
+    places = {"y": y, "x": x, "z0": z % 2, "z1": z // 2}
+
+    def tiles(ref):
+        return ref.shape[-1] // LANES
+
+    parts, count = ([], []), 0
+    for stream, refs in enumerate(((down_a_ref, gate_ref, last_a_ref), (down_b_ref, up_ref, last_b_ref))):
+        at = 0
+        for ref in refs:
+            parts[stream].append((ref, len(ref.shape) == 3, at, at + tiles(ref)))
+            at += tiles(ref)
+        count = max(count, at)
+    own_down = core * tiles_of(FC)
+    own_value = core * tiles_of(VC)
+    small_at = parts[1][2][2] + tiles_of(VC) + 1
+    places_out = (
+        (
+            (down_ref, own_down, 0, parts[0][0][3]),
+            (gu_ref, own_down, parts[0][1][2], parts[0][1][3]),
+            (value_ref, own_value, parts[0][2][2], parts[0][2][2] + tiles_of(VC)),
+            (qk_ref, core, parts[0][2][3] - 1, parts[0][2][3]),
+        ),
+        (
+            (down_ref, own_down + parts[0][0][3], 0, parts[1][0][3]),
+            (gu_ref, CORES * tiles_of(FC) + own_down, parts[1][1][2], parts[1][1][3]),
+            (out_ref, own_value, parts[1][2][2], parts[1][2][2] + tiles_of(VC)),
+            (qk_ref, CORES + core, small_at - 1, small_at),
+            (small_ref, core, small_at, small_at + 1),
+        ),
+    )
+    greet(y, x, z, core, True)
+
+    def columns(tile):
+        return pl.ds(pl.multiple_of(tile * LANES, LANES), LANES)
+
+    def transfer(stream, stage, chunk, source, target=None):
+        landing = chunk % 4
+        if target is None:
+            target = (got_terms, got_sums, got_halves, got_quarters)[stage].at[stream, landing]
+        axis = (ORDERS[stream] + ("core",))[stage]
+        return pltpu.make_async_remote_copy(
+            src_ref=source,
+            dst_ref=target,
+            send_sem=send_sem.at[stream, stage, landing],
+            recv_sem=recv_sem.at[stream, stage, landing],
+            device_id=mesh_exchange(y, x, z, core, axis),
+            device_id_type=pl.DeviceIdType.MESH,
+        )
+
+    def first_view(stream, ref, tile, place):
+        ref = ref.at[:, :, :, columns(tile)]
+        return ref.at[place] if stream == 0 else ref.at[:, place]
+
+    def source_of(stream, stage, chunk):
+        there = 1 - places[ORDERS[stream][stage]]
+        if stage == 1:
+            return sums.at[stream, chunk % 2, there]
+        if stage == 2:
+            return halves.at[stream, chunk % 2, :, there]
+        return quarters.at[stream, chunk % 2, there]
+
+    def add(a, b):
+        return a.astype(f32) + b.astype(f32)
+
+    def begin(stream, chunk):
+        ref, _, start, stop = parts[stream][2]
+
+        @pl.when((chunk >= start) & (chunk < stop))
+        def _():
+            there = 1 - places[ORDERS[stream][0]]
+            transfer(stream, 0, chunk, first_view(stream, ref, chunk - start, there)).start()
+
+    def second(stream, chunk):
+        for ref, summed, start, stop in parts[stream]:
+
+            @pl.when((chunk >= start) & (chunk < stop))
+            def _(ref=ref, summed=summed, start=start):
+                tile = chunk - start
+                if summed:
+                    sums[stream, chunk % 2] = ref[:, :, columns(tile)]
+                else:
+                    there = 1 - places[ORDERS[stream][0]]
+                    transfer(stream, 0, chunk, first_view(stream, ref, tile, there)).wait()
+                    own = first_view(stream, ref, tile, places[ORDERS[stream][0]])[...]
+                    sums[stream, chunk % 2] = add(own, got_terms[stream, chunk % 4]).astype(bf16)
+
+        transfer(stream, 1, chunk, source_of(stream, 1, chunk)).start()
+
+    def advance(stream, stage, chunk):
+        here = places[ORDERS[stream][stage]]
+        slot, landing = chunk % 2, chunk % 4
+        transfer(stream, stage, chunk, source_of(stream, stage, chunk)).wait()
+        if stage == 1:
+            total = add(sums[stream, slot, here], got_sums[stream, landing]).astype(bf16)
+            halves[stream, slot] = total.reshape(halves.shape[2:])
+        elif stage == 2:
+            own = halves[stream, slot, :, here]
+            quarters[stream, slot] = add(own, got_halves[stream, landing]).astype(bf16)
+        else:
+            total = add(quarters[stream, slot, here], got_quarters[stream, landing])
+            finals[stream, slot] = total.reshape(finals.shape[2:])
+        if stage < 3:
+            transfer(stream, stage + 1, chunk, source_of(stream, stage + 1, chunk)).start()
+
+    def hand_over(stream, chunk, waiting):
+        for ref, first, start, stop in places_out[stream]:
+
+            @pl.when((chunk >= start) & (chunk < stop))
+            def _(ref=ref, first=first, start=start):
+                target = ref.at[:, columns(first + chunk - start)]
+                copy = transfer(stream, 4, chunk, finals.at[stream, chunk % 2, 1 - core], target)
+                if waiting:
+                    copy.wait()
+                else:
+                    target[...] = finals[stream, chunk % 2, core]
+                    copy.start()
+
+    @pl.loop(0, count + 5)
+    def _(step):
+        for stream in range(2):
+            total = parts[stream][2][3]
+
+            @pl.when(step < total)
+            def _(stream=stream):
+                begin(stream, step)
+
+        for stage in range(5):
+            for stream in range(2):
+                total = parts[stream][2][3]
+
+                @pl.when((step >= stage + 1) & (step < total + stage + 1))
+                def _(stage=stage, stream=stream):
+                    chunk = step - stage - 1
+                    if stage == 0:
+                        second(stream, chunk)
+                    elif stage < 4:
+                        advance(stream, stage, chunk)
+                    else:
+                        hand_over(stream, chunk, True)
+                    if stage == 3:
+                        hand_over(stream, chunk, False)
+
+
+def tiles_of(width):
+    return width // LANES
+
+
+def first_exchange(terms, axis):
+    view = terms.reshape(2, 2, D // 4, terms.shape[1])
+    dim = 0 if axis == "y" else 1
+    mine = bit_at(axis, 0)
+    arrived = exchanged(part_of(view, dim, 1 - mine), axis, 0)
+    return (part_of(view, dim, mine).astype(f32) + arrived.astype(f32)).astype(bf16)
+
+
+def reduced(down_a, gate, down_b, up, last_a, last_b, owned):
+    block, rows = D // 4, D // 16
+    dma = pltpu.SemaphoreType.DMA
+    last_a, last_b = (last.reshape(2, 2, block, last.shape[1]) for last in (last_a, last_b))
+    widths = (2 * CORES * QC, CORES * VC, CORES * VC, 2 * CORES * FC, CORES * FC, CORES * LANES)
+    return pl.pallas_call(
+        reduce_kernel,
+        out_shape=[jax.ShapeDtypeStruct((owned, width), f32) for width in widths],
+        in_specs=[pl.BlockSpec(memory_space=pltpu.VMEM)] * 6,
+        out_specs=[pl.BlockSpec(memory_space=pltpu.VMEM)] * 6,
+        scratch_shapes=[
+            pltpu.VMEM((2, 2, 2, block, LANES), bf16),
+            pltpu.VMEM((2, 2, 2, 2, rows, LANES), bf16),
+            pltpu.VMEM((2, 2, 2, rows, LANES), bf16),
+            pltpu.VMEM((2, 2, CORES, owned, LANES), f32),
+            pltpu.VMEM((2, 4, 2, block, LANES), bf16),
+            pltpu.VMEM((2, 4, block, LANES), bf16),
+            pltpu.VMEM((2, 4, 2, rows, LANES), bf16),
+            pltpu.VMEM((2, 4, rows, LANES), bf16),
+            dma((2, 5, 4)),
+            dma((2, 5, 4)),
+        ],
+        compiler_params=pltpu.CompilerParams(
+            collective_id=0, has_side_effects=True, vmem_limit_bytes=56 << 20
+        ),
+        cost_estimate=pl.CostEstimate(flops=0, bytes_accessed=1024, transcendentals=0),
+    )(down_a, gate, down_b, up, last_a, last_b)
+
+
+def places_of():
     y, x, z, core = (lax.axis_index(axis) for axis in ("y", "x", "z", "core"))
-    ffn, mid, total = tiles
-    places = {"y": y, "x": x, "z0": z % 2, "z1": z // 2}
-    block = terms.shape[4]
-
+    return y, x, z, core
+
+
+def greet(y, x, z, core, both_cores=False):
     barrier = pltpu.get_barrier_semaphore()
-    for axis in ORDERS[0]:
+    partners = ORDERS[0] + (("core",) if both_cores else ())
+    for axis in partners:
         pl.semaphore_signal(
             barrier,
             inc=1,
             device_id=mesh_exchange(y, x, z, core, axis),
             device_id_type=pl.DeviceIdType.MESH,
         )
-    pl.semaphore_wait(barrier, len(ORDERS[0]))
-
-    def transfer(stream, stage, chunk):
-        axis = ORDERS[stream][stage]
-        there = 1 - places[axis]
-        slot, landing = chunk % 2, chunk % 4
-        if stage == 0 and stream == 0:
-            source = terms.at[stream, slot, there]
-        elif stage == 0:
-            source = terms.at[stream, slot, :, there]
-        elif stage == 1:
-            source = sums.at[stream, slot, there]
-        elif stage == 2:
-            source = halves.at[stream, slot, :, there]
-        else:
-            source = quarters.at[stream, slot, there]
-        target = (got_terms, got_sums, got_halves, got_quarters)[stage].at[stream, landing]
+    pl.semaphore_wait(barrier, len(partners))
+
+
+GATHER_ORDERS = (("z1", "z0", "x", "y"), ("z1", "z0", "y", "x"))
+
+
+def gather_view(ref, order, stage, y, x, z):
+    if stage == 0:
+        return ref.at[y, x, z // 2, z % 2]
+    if stage == 1:
+        return ref.at[y, x, :, z % 2]
+    if stage == 2:
+        return ref.at[y, x]
+    return ref.at[y] if order == 0 else ref.at[:, x]
+
+
+def gather_kernel(tiles, shard_ref, full_ref, send_sem, recv_sem):
+    y, x, z, core = places_of()
+    full_ref[y, x, z // 2, z % 2] = shard_ref[...]
+    greet(y, x, z, core)
+
+    def transfer(stage, tile, order):
+        columns = pl.ds(pl.multiple_of(tile * LANES, LANES), LANES)
+        view = gather_view(full_ref.at[:, :, :, :, :, columns], order, stage, y, x, z)
         return pltpu.make_async_remote_copy(
-            src_ref=source,
-            dst_ref=target,
-            send_sem=send_sem.at[stream, stage, slot],
-            recv_sem=recv_sem.at[stream, stage, landing],
-            device_id=mesh_exchange(y, x, z, core, axis),
+            src_ref=view,
+            dst_ref=view,
+            send_sem=send_sem.at[stage, tile],
+            recv_sem=recv_sem.at[stage, tile],
+            device_id=mesh_exchange(y, x, z, core, GATHER_ORDERS[order][stage]),
             device_id_type=pl.DeviceIdType.MESH,
         )
 
-    def add(a, b):
-        return a.astype(f32) + b.astype(f32)
-
-    def product(stream, chunk, left_ref, right_ref, tile):
-        columns = right_ref[:, pl.ds(pl.multiple_of(tile * LANES, LANES), LANES)]
-
-        @pl.loop(0, 4)
-        def _(part):
-            rows = left_ref[pl.ds(pl.multiple_of(part * block, block), block), :]
-            terms[stream, chunk % 2, part // 2, part % 2] = dot(rows, columns).astype(bf16)
-
-    def begin(chunk):
-        @pl.when(chunk < ffn)
-        def _():
-            product(0, chunk, second_ref, gate_ref, chunk)
-            product(1, chunk, second_ref, up_ref, chunk)
-
-        @pl.when((chunk >= ffn) & (chunk < ffn + mid))
-        def _():
-            product(0, chunk, normed_ref, value_ref, chunk - ffn)
-            product(1, chunk, mixer_ref, after_ref, chunk - ffn)
-
-        @pl.when(chunk == ffn + mid)
-        def _():
-            product(0, chunk, normed_ref, qk_ref, 0)
-            product(1, chunk, normed_ref, qk_ref, 1)
-
-        @pl.when(chunk == ffn + mid + 1)
-        def _():
-            for part in range(4):
-                rows = small_ref[part * block : (part + 1) * block, :]
-                terms[0, chunk % 2, part // 2, part % 2] = rows
-                terms[1, chunk % 2, part // 2, part % 2] = rows
-
-        for stream in range(2):
-            transfer(stream, 0, chunk).start()
-
-    def advance(stage, chunk):
-        for stream in range(2):
-            axis = ORDERS[stream][stage]
-            here = places[axis]
-            slot, landing = chunk % 2, chunk % 4
-            transfer(stream, stage, chunk).wait()
-            if stage == 0:
-                own = terms[stream, slot, here] if stream == 0 else terms[stream, slot, :, here]
-                sums[stream, slot] = add(own, got_terms[stream, landing]).astype(bf16)
-            elif stage == 1:
-                total = add(sums[stream, slot, here], got_sums[stream, landing]).astype(bf16)
-                halves[stream, slot] = total.reshape(halves.shape[2:])
-            elif stage == 2:
-                own = halves[stream, slot, :, here]
-                quarters[stream, slot] = add(own, got_halves[stream, landing]).astype(bf16)
-            else:
-                total = add(quarters[stream, slot, here], got_quarters[stream, landing])
-                out_ref[stream, :, pl.ds(pl.multiple_of(chunk * LANES, LANES), LANES)] = total
-            if stage < 3:
-                transfer(stream, stage + 1, chunk).start()
-
-    @pl.loop(0, total + 4)
+    pairs = (tiles + 1) // 2
+
+    def each(step, behind, act):
+        for order in range(2):
+            tile = 2 * (step - behind) + order
+
+            @pl.when((tile >= 0) & (tile < tiles))
+            def _(tile=tile, order=order):
+                act(tile, order)
+
+    @pl.loop(0, pairs + 4)
     def _(step):
-        @pl.when(step < total)
-        def _():
-            begin(step)
-
+        each(step, 0, lambda tile, order: transfer(0, tile, order).start())
         for stage in range(4):
 
-            @pl.when((step >= stage + 1) & (step < total + stage + 1))
-            def _(stage=stage):
-                advance(stage, step - stage - 1)
-
-
-def reduced(second_t, normed_t, mixer_t, grad_gate, grad_up, grad_pre, grad_after, grad_qk, small):
-    ffn, mid = grad_gate.shape[1] // LANES, grad_pre.shape[1] // LANES
-    total = ffn + mid + 2
-    block, rows = D // 4, D // 16
-    dma = pltpu.SemaphoreType.DMA
-    tokens = second_t.shape[1]
-    return pl.pallas_call(
-        functools.partial(reduce_kernel, (ffn, mid, total)),
-        out_shape=jax.ShapeDtypeStruct((2, rows, total * LANES), f32),
-        in_specs=[pl.BlockSpec(memory_space=pltpu.VMEM)] * 9,
+            def act(tile, order, stage=stage):
+                transfer(stage, tile, order).wait()
+                if stage < 3:
+                    transfer(stage + 1, tile, order).start()
+
+            each(step, stage + 1, act)
+
+
+def gathered_rows(shard):
+    rows, width = shard.shape
+    tiles = width // LANES
+    full = pl.pallas_call(
+        functools.partial(gather_kernel, tiles),
+        out_shape=jax.ShapeDtypeStruct((2, 2, 2, 2, rows, width), bf16),
+        in_specs=[pl.BlockSpec(memory_space=pltpu.VMEM)],
         out_specs=pl.BlockSpec(memory_space=pltpu.VMEM),
         scratch_shapes=[
-            pltpu.VMEM((2, 2, 2, 2, block, LANES), bf16),
-            pltpu.VMEM((2, 2, 2, block, LANES), bf16),
-            pltpu.VMEM((2, 2, 2, 2, rows, LANES), bf16),
-            pltpu.VMEM((2, 2, 2, rows, LANES), bf16),
-            pltpu.VMEM((2, 4, 2, block, LANES), bf16),
-            pltpu.VMEM((2, 4, block, LANES), bf16),
-            pltpu.VMEM((2, 4, 2, rows, LANES), bf16),
-            pltpu.VMEM((2, 4, rows, LANES), bf16),
-            dma((2, 4, 2)),
-            dma((2, 4, 4)),
+            pltpu.SemaphoreType.DMA((4, tiles)),
+            pltpu.SemaphoreType.DMA((4, tiles)),
         ],
         compiler_params=pltpu.CompilerParams(
-            collective_id=0, has_side_effects=True, vmem_limit_bytes=58 << 20
+            collective_id=1, has_side_effects=True, vmem_limit_bytes=40 << 20
         ),
-        cost_estimate=pl.CostEstimate(
-            flops=4 * D * tokens * total * LANES, bytes_accessed=400 << 20, transcendentals=0
+        cost_estimate=pl.CostEstimate(flops=0, bytes_accessed=1024, transcendentals=0),
+    )(shard)
+    return full.reshape(D, width)
+
+
+SLOTS = 10
+
+
+def feed_forward_kernel(
+    tiles,
+    second_ref,
+    grad_ref,
+    shard_ref,
+    hidden_ref,
+    grad_gate_ref,
+    grad_up_ref,
+    down_own_ref,
+    down_other_ref,
+    second_own_ref,
+    second_other_ref,
+    held,
+    down_ref,
+    grad_second_ref,
+    send_sem,
+    recv_sem,
+    out_sem,
+):
+    y, x, z, core = places_of()
+    down_ref[...] = jnp.zeros_like(down_ref)
+    grad_second_ref[...] = jnp.zeros_like(grad_second_ref)
+    greet(y, x, z, core)
+    tokens = second_ref.shape[0]
+    block = 256 if tokens % 256 == 0 else tokens
+
+    def transfer(stage, tile, order):
+        slot = tile % SLOTS
+        view = gather_view(held.at[slot], order, stage, y, x, z)
+        return pltpu.make_async_remote_copy(
+            src_ref=view,
+            dst_ref=view,
+            send_sem=send_sem.at[stage, slot],
+            recv_sem=recv_sem.at[stage, slot],
+            device_id=mesh_exchange(y, x, z, core, GATHER_ORDERS[order][stage]),
+            device_id_type=pl.DeviceIdType.MESH,
+        )
+
+    def compute(tile):
+        weights = held.at[tile % SLOTS]
+        columns = pl.ds(pl.multiple_of(tile * LANES, LANES), LANES)
+
+        @pl.loop(0, tokens // block)
+        def _(part):
+            rows = pl.ds(pl.multiple_of(part * block, block), block)
+            both = weights[:, :, :, :, :, : 2 * LANES].reshape(D, 2 * LANES)
+            down = weights[:, :, :, :, :, 2 * LANES :].reshape(D, LANES)
+            gate_up = dot(second_ref[rows, :], both)
+            gate, upward = gate_up[:, :LANES], gate_up[:, LANES:]
+            grad_hidden = dot(grad_ref[rows, :], down)
+            sigmoid_gate = 1.0 / (1.0 + jnp.exp(-gate))
+            silu_gate = gate * sigmoid_gate
+            hidden = (silu_gate * upward).astype(bf16)
+            grad_upward = (grad_hidden * silu_gate).astype(bf16)
+            grad_gate = (
+                grad_hidden * upward * sigmoid_gate * (1.0 + gate * (1.0 - sigmoid_gate))
+            ).astype(bf16)
+            hidden_ref[rows, columns] = hidden
+            grad_up_ref[rows, columns] = grad_upward
+            grad_gate_ref[rows, columns] = grad_gate
+            down_ref[rows, :] += dot_nt(hidden, down)
+            grad_second_ref[rows, :] += dot_nt(
+                jnp.concatenate([grad_gate, grad_upward], axis=1), both
+            )
+
+    pairs = (tiles + 1) // 2
+
+    def each(step, behind, act):
+        for order in range(2):
+            tile = 2 * (step - behind) + order
+
+            @pl.when((tile >= 0) & (tile < tiles))
+            def _(tile=tile, order=order):
+                act(tile, order)
+
+    def send_on(stage):
+        def act(tile, order):
+            transfer(stage, tile, order).wait()
+            transfer(stage + 1, tile, order).start()
+
+        return act
+
+    def finish(tile, order):
+        transfer(3, tile, order).wait()
+        compute(tile)
+
+    def begin(tile, order):
+        held[tile % SLOTS, y, x, z // 2, z % 2] = shard_ref[tile]
+        transfer(0, tile, order).start()
+
+    @pl.loop(0, pairs + 4)
+    def _(step):
+        each(step, 2, send_on(1))
+        each(step, 3, send_on(2))
+        each(step, 4, finish)
+        each(step, 1, send_on(0))
+        each(step, 0, begin)
+
+    half = tokens // 2
+    copies = [
+        pltpu.make_async_copy(source, target, out_sem.at[at])
+        for at, (source, target) in enumerate(
+            (
+                (grad_second_ref.at[half:], second_other_ref),
+                (grad_second_ref.at[:half], second_own_ref),
+                (down_ref.at[half:], down_other_ref),
+                (down_ref.at[:half], down_own_ref),
+            )
+        )
+    ]
+    for copy in copies:
+        copy.start()
+    for copy in copies:
+        copy.wait()
+
+
+def feed_forward(second, grad_result, gate_shard, up_shard, down_shard):
+    tokens = second.shape[0]
+    rows, width = gate_shard.shape
+    tiles = width // LANES
+    parts = [shard.reshape(rows, tiles, LANES) for shard in (gate_shard, up_shard, down_shard)]
+    shard = jnp.transpose(jnp.stack(parts, axis=2), (1, 0, 2, 3)).reshape(tiles, rows, 3 * LANES)
+    narrow = jax.ShapeDtypeStruct((tokens, width), bf16)
+    part = jax.ShapeDtypeStruct((tokens // 2, D), f32)
+    return pl.pallas_call(
+        functools.partial(feed_forward_kernel, tiles),
+        out_shape=(narrow,) * 3 + (part,) * 4,
+        in_specs=[pl.BlockSpec(memory_space=pltpu.VMEM)] * 3,
+        out_specs=[pl.BlockSpec(memory_space=pltpu.VMEM)] * 3 + [pl.BlockSpec(memory_space=pl.ANY)] * 4,
+        scratch_shapes=[
+            pltpu.VMEM((SLOTS, 2, 2, 2, 2, rows, 3 * LANES), bf16),
+            pltpu.VMEM((tokens, D), f32),
+            pltpu.VMEM((tokens, D), f32),
+            pltpu.SemaphoreType.DMA((4, SLOTS)),
+            pltpu.SemaphoreType.DMA((4, SLOTS)),
+            pltpu.SemaphoreType.DMA((4,)),
+        ],
+        compiler_params=pltpu.CompilerParams(
+            collective_id=2, has_side_effects=True, vmem_limit_bytes=60 << 20
         ),
-    )(second_t, normed_t, mixer_t, grad_gate, grad_up, grad_pre, grad_after, grad_qk, small)
+        cost_estimate=pl.CostEstimate(flops=0, bytes_accessed=1024, transcendentals=0),
+    )(second, grad_result, shard)
 
 
 def norm_scale(values):
@@ -625,28 +909,32 @@
 
     attention_shard = chip_shard((0, 1), small_low)
     rest_shard = chip_shard((2, 3, 4))
-    half = (2 * QC + VC + LANES) // 2
+    in_kernel = tuple(lax.axis_size(axis) for axis in ("y", "x", "z")) == (2, 2, 4)
+    early_width = 2 * QC + VC + LANES
+    half = early_width // 2
     cut = FC // 2 // LANES * LANES
     down_at = VC + 2 * FC
     own_tokens = tokens.reshape(rows, D)
     other_tokens = swapped(own_tokens)
     wide_part = 4 * LANES
-    early_a = Gather(attention_shard[:, :half], True)
-    early_b = Gather(attention_shard[:, half:], False)
-    early_a.along_z(), early_b.along_z()
-    early_a.block, other_tokens = tied(early_a.block, other_tokens)
-    early = jnp.concatenate([early_a.rest(), early_b.rest()], axis=1)
-
-    def gathered(start, width):
-        return lax.all_gather(rest_shard[:, start : start + width], ("y", "x", "z"), axis=0, tiled=True)
-
-    out_half = gathered(0, VC)
-    gate_full = gathered(VC, FC)
-    up_full = gathered(VC + FC, FC)
-    last_shard, early = tied(rest_shard[:, down_at:], early)
-    down_a = Gather(last_shard[:, :cut], True)
-    down_b = Gather(last_shard[:, cut:], False)
-    down_full = jnp.concatenate([down_a.rest(), down_b.rest()], axis=1)
+    if in_kernel:
+        full = gathered_rows(jnp.concatenate([attention_shard, rest_shard[:, :VC]], axis=1))
+        early, out_half = full[:, :early_width], full[:, early_width:]
+    else:
+        early_a = Gather(attention_shard[:, :half], True)
+        early_b = Gather(attention_shard[:, half:], False)
+        early = jnp.concatenate([early_a.rest(), early_b.rest()], axis=1)
+
+        def gathered(start, width):
+            return lax.all_gather(rest_shard[:, start : start + width], ("y", "x", "z"), axis=0, tiled=True)
+
+        out_half = gathered(0, VC)
+        gate_full = gathered(VC, FC)
+        up_full = gathered(VC + FC, FC)
+        last_shard, early = tied(rest_shard[:, down_at:], early)
+        down_a = Gather(last_shard[:, :cut], True)
+        down_b = Gather(last_shard[:, cut:], False)
+        down_full = jnp.concatenate([down_a.rest(), down_b.rest()], axis=1)
 
     qk_full = early[:, : 2 * QC]
     value_full = early[:, 2 * QC : 2 * QC + VC]
@@ -706,12 +994,6 @@
     second_low = (scaled_second * gain_second[None, :]).astype(bf16)
     second_chip = on_chip(second_low)
 
-    gate = dot(second_chip, gate_full)
-    upward = dot(second_chip, up_full)
-    sigmoid_gate = jax.nn.sigmoid(gate)
-    silu_gate = gate * sigmoid_gate
-    hidden = (silu_gate * upward).astype(bf16)
-
     half_at = jnp.where(first_core, jnp.arange(CORES), 1 - jnp.arange(CORES))
     positions = (z_at * CORES + half_at)[:, None] * slot_rows + jnp.arange(slot_rows)[None, :]
     valid_chip = positions[:, None, :] < lengths[None, :, None]
@@ -723,24 +1005,44 @@
     grad_result_chip = (valid_chip * cotangent_chip.astype(f32)).astype(bf16)
     grad_result = valid * cotangent.reshape(rows, D).astype(f32)
 
-    def scattered(terms):
-        return lax.psum_scatter(terms, ("y", "x", "z"), scatter_dimension=0, tiled=True)
-
-    down_terms, grad_result_chip = tied(
-        dot_tn(grad_result_chip, hidden).astype(bf16), grad_result_chip
-    )
-    scatter_down = scattered(down_terms)
-    down_other = swapped(dot_nt(hidden[rows:], down_full))
-    grad_hidden = dot(grad_result_chip, down_full)
-    grad_upward = (grad_hidden * silu_gate).astype(bf16)
-    grad_gate = (
-        grad_hidden * upward * sigmoid_gate * (1.0 + gate * (1.0 - sigmoid_gate))
-    ).astype(bf16)
-    second_other = dot_nt(grad_gate[rows:], gate_full) + dot_nt(grad_upward[rows:], up_full)
-    second_own = dot_nt(grad_gate[:rows], gate_full) + dot_nt(grad_upward[:rows], up_full)
-    second_own, down_other = tied(second_own, down_other)
-    grad_second = second_own + swapped(second_other)
-    down_result = dot_nt(hidden[:rows], down_full) + down_other
+    if in_kernel:
+        hidden, grad_gate, grad_upward, *ffn_parts = feed_forward(
+            second_chip,
+            grad_result_chip,
+            rest_shard[:, VC : VC + FC],
+            rest_shard[:, VC + FC : down_at],
+            rest_shard[:, down_at:],
+        )
+        down_own, down_other, second_own, second_other = ffn_parts
+        grad_second = second_own + swapped(second_other)
+        down_result = down_own + swapped(down_other)
+        down_terms = dot_tn(grad_result_chip, hidden).astype(bf16)
+        gate_terms = dot_tn(second_chip, grad_gate).astype(bf16)
+        up_terms = dot_tn(second_chip, grad_upward).astype(bf16)
+        grad_second, gate_terms, up_terms, down_terms = tied(
+            grad_second, gate_terms, up_terms, down_terms
+        )
+        sum_gate, sum_up = first_exchange(gate_terms, "y"), first_exchange(up_terms, "x")
+        at = 10 * LANES
+        sum_down = (
+            first_exchange(down_terms[:, :at], "y"),
+            first_exchange(down_terms[:, at:], "x"),
+        )
+    else:
+        gate = dot(second_chip, gate_full)
+        upward = dot(second_chip, up_full)
+        sigmoid_gate = jax.nn.sigmoid(gate)
+        silu_gate = gate * sigmoid_gate
+        hidden = (silu_gate * upward).astype(bf16)
+        grad_hidden = dot(grad_result_chip, down_full)
+        grad_upward = (grad_hidden * silu_gate).astype(bf16)
+        grad_gate = (
+            grad_hidden * upward * sigmoid_gate * (1.0 + gate * (1.0 - sigmoid_gate))
+        ).astype(bf16)
+        second_part = dot_nt(grad_gate, gate_full) + dot_nt(grad_upward, up_full)
+        grad_second = second_part[:rows] + swapped(second_part[rows:])
+        down_part = dot_nt(hidden, down_full)
+        down_result = down_part[:rows] + swapped(down_part[rows:])
     layer_out = (valid * (after_mixer + down_result)).astype(bf16).reshape(tokens.shape)
 
     grad_after_norm, grad_gain_second = norm_backward(
@@ -804,26 +1106,22 @@
         [whole_feature(part) for part in tap_grads] + [grad_gain_first, grad_gain_second], axis=1
     )
     small_terms = jnp.pad(small_terms, ((0, 0), (0, LANES - (KS + 2)))).astype(bf16)
-    operands = (
-        grad_gate,
-        grad_upward,
-        grad_pre,
-        grad_after_chip,
-        grad_query_key,
-        small_terms,
-    )
-    in_kernel = tuple(lax.axis_size(axis) for axis in ("y", "x", "z")) == (2, 2, 4)
     if in_kernel:
-        lefts = [jnp.transpose(left) for left in (second_chip, normed_chip, mixer_chip)]
-        sums = reduced(*lefts, *operands)
-        gate_to, mid_to = FC, FC + VC
-        sum_gate, sum_up = sums[0, :, :gate_to], sums[1, :, :gate_to]
-        sum_value, sum_out = sums[0, :, gate_to:mid_to], sums[1, :, gate_to:mid_to]
-        sum_last = jnp.concatenate(
-            [sums[0, :, mid_to : mid_to + QC], sums[1, :, mid_to : mid_to + QC], sums[0, :, mid_to + QC :]],
-            axis=1,
+        value_terms = dot_tn(normed_chip, grad_pre).astype(bf16)
+        out_terms = dot_tn(mixer_chip, grad_after_chip).astype(bf16)
+        qk_terms = dot_tn(normed_chip, grad_query_key).astype(bf16)
+        grad_qk_own, grad_value_own, grad_out_own, grad_gu_own, grad_down_own, small_both = reduced(
+            sum_down[0],
+            sum_gate,
+            sum_down[1],
+            sum_up,
+            jnp.concatenate([value_terms, qk_terms[:, :QC]], axis=1),
+            jnp.concatenate([out_terms, qk_terms[:, QC:], small_terms], axis=1),
+            owned,
         )
+        grad_small_own = (small_both[:, :LANES] + small_both[:, LANES:])[:, : KS + 2]
     else:
+        sum_down = Scatter(dot_tn(grad_result_chip, hidden).astype(bf16), True).rest()
         sum_gate = Scatter(dot_tn(second_chip, grad_gate).astype(bf16), False).rest()
         sum_up = Scatter(dot_tn(second_chip, grad_upward).astype(bf16), True).rest()
         sum_value = Scatter(dot_tn(normed_chip, grad_pre).astype(bf16), False).rest()
@@ -849,13 +1147,14 @@
         shape = (owned, 2, 1, width)
         return both_cores(mine.reshape(shape), theirs.reshape(shape), 2).reshape(owned, -1)
 
-    grad_down_own = columns(scatter_down)
-    grad_gu_own = two_columns(*finish(sum_gate, sum_up), FC)
-    grad_out_own = columns(sum_out)
-    grad_value_own = columns(sum_value)
-    last_mine, last_theirs = finish(sum_last)
-    grad_qk_own = two_columns(last_mine[:, : 2 * QC], last_theirs[:, : 2 * QC], QC)
-    grad_small_own = (last_mine + last_theirs)[:, 2 * QC : 2 * QC + KS + 2]
+    if not in_kernel:
+        grad_down_own = columns(sum_down)
+        grad_gu_own = two_columns(*finish(sum_gate, sum_up), FC)
+        grad_out_own = columns(sum_out)
+        grad_value_own = columns(sum_value)
+        last_mine, last_theirs = finish(sum_last)
+        grad_qk_own = two_columns(last_mine[:, : 2 * QC], last_theirs[:, : 2 * QC], QC)
+        grad_small_own = (last_mine + last_theirs)[:, 2 * QC : 2 * QC + KS + 2]
 
     grads_all = (
         grad_qk_own,

time: 1090 us -> 1020 us (0.936)
  Pallas kernels: 304 us -> 617 us
  waiting for transfers between devices: 293 us -> 28.2 us
  matrix products: 160 us -> 109 us
  starting transfers between devices: 65.4 us -> 19.2 us
  between operations: 15.7 us -> 2.49 us
    pallas_call x1 -> x3, Pallas kernels: 245 us -> 558 us  [the longest x1 283 us: feed_forward(): pl.pallas_call(functools.partial(feed_forward_kernel, tiles), out_shape=(...]
    ppermute x16 -> x4, waiting for transfers between devices: 169 us -> 1.95 us  [exchanged(): return lax.ppermute(array, axis, [(i, i ^ 1 << bit) for i in range(count)])]
    ppermute x6, waiting for transfers between devices: 93 us -> 25 us  [chain(): total = total + lax.ppermute(message, 'z', [pair]).astype(f32)]
    dot_general x1 -> x6, matrix products: 14.8 us -> 72.8 us  [dot_tn(): lax.dot_general(a, b, (((0,), (0,)), ((), ())), preferred_element_type=f32)]
    dot_general x6 -> x3, matrix products: 70.2 us -> 13.8 us  [dot(): lax.dot_general(a, b, (((1,), (0,)), ((), ())), preferred_element_type=f32)]
    dot_general x11 -> x5, matrix products: 75.2 us -> 22.1 us  [dot_nt(): lax.dot_general(a, b, (((1,), (1,)), ((), ())), preferred_element_type=f32)]
    dynamic_update_slice x30 -> x0, local copies, waits for them, and re-layouts: 28.7 us -> none  [the longest x14 14.5 us: stage(): whole = lax.dynamic_update_index_in_dim(whole, self.block, mine, dim)]
    transpose x3 -> x1, other arithmetic: 25.9 us -> 1.52 us  [feed_forward(): jnp.transpose(jnp.stack(parts, axis=2), (1, 0, 2, 3))]
  transfers between devices with their start and end apart: 45 -> 24, of which waited for: 18 -> 4; matrix products, arithmetic and copies ran while one was open for 29% -> 21% of each run, Pallas kernels for 27% -> 13%
where the time goes in v3:
time: 1020 us; the launch traced here: 1010 us
  Pallas kernels  617 us (60%)
  local copies, waits for them, and re-layouts  119 us (12%)
  other arithmetic  115 us (11%)
  matrix products  109 us (11%)
  waiting for transfers between devices  28.2 us (3%)
  starting transfers between devices  19.2 us (2%)
    pallas_call x1, Pallas kernels, feed_forward(): pl.pallas_call(functools.partial(feed_forward_kernel, tiles), out_shape=(...  283 us
    pallas_call x1, Pallas kernels, reduced(): pl.pallas_call(reduce_kernel, out_shape=[jax.ShapeDtypeStruct((owned, wid...  192 us
    pallas_call x1, Pallas kernels, gathered_rows(): pl.pallas_call(functools.partial(gather_kernel, tiles), out_shape=jax.Sha...  82.7 us
    dot_general x6, matrix products, dot_tn(): lax.dot_general(a, b, (((0,), (0,)), ((), ())), preferred_element_type=f32)  72.8 us
    unnamed x197, local copies, waits for them, and re-layouts  32.6 us
    pallas_call x1, Pallas kernels, local(): call(backward_kernel, ins=[q_spec, k_spec, v_spec, wide_spec, 'state', 's...  28.2 us
    ppermute x6, waiting for transfers between devices, chain(): total = total + lax.ppermute(message, 'z', [pair]).astype(f32)  25 us
    dynamic_slice x9, local copies, waits for them, and re-layouts, part_of(): return lax.dynamic_index_in_dim(array, index, axis, keepdims=False)  24.8 us
  transfers between devices with their start and end apart: 24, of which 4 were waited for; matrix products, arithmetic and copies ran while one was open for 21% of the time, Pallas kernels for 13%

profile of v3, /device:TPU:0, one launch (start us, length us, event | category | flops | bytes accessed | tf_op | source)
XLA Modules:
  0.0 1009.4 jit_solution(9497203906881926653)
XLA Ops:
  5.3 7.5 dynamic-slice_reduce_fusion.1
  18.7 2.8 constant_dynamic-slice_fusion.14
  32.5 82.7 %shard_map.374 = bf16[2,2,2,2,112,2176]{5,4,3,2,1,0:T(8,128)(2,1)S(1)} custom-call(bf16[112,2176]{1,0:T(8,128)(2,1)S(1)} %fusion.58.shard_ref), custom_call_target="tpu_custom_call" | custom-call | bytes 1024 | tf_op jit(solution)/shard_map/pallas_call | solution.py:665
  115.2 3.0 copy-done
  118.8 2.4 fusion.3
  121.3 6.6 fusion.49
  129.3 3.5 convolution_convert_fusion.5
  133.3 2.5 add_convert_fusion.v_ref
  135.8 8.5 shard_map.375
  145.6 4.2 collective-permute-start.4
  149.8 11.9 %collective-permute-done.4 = bf16[2,8,160,128]{3,2,1,0:T(8,128)(2,1)S(1)} collective-permute-done((bf16[2,8,160,128]{3,2,1,0:T(8,128)(2,1)S(1)}, bf16[2,8,160,128]{3,2,1,0:T(8,128)(2,1)S(1)}, u32[]{:S(2)}, u32[]{:S(2)}) %collective-permute-start.4) | collective-permute-done | bytes 655392 | tf_op jit(solution)/shard_map/ppermute | solution.py:363
  162.5 2.3 fusion.52
  173.4 2.2 add_convert_fusion.3.before_ref
  175.6 11.8 %shard_map.376 = (bf16[2,2,256,896]{3,2,1,0:T(8,128)(2,1)}, f32[2,2,256,128]{3,2,1,0:T(8,128)}) custom-call(s32[1]{0:T(128)} %bitcast.1.core_ref, s32[8,256]{1,0:T(8,128)} %constant.212.clone.index_ref, f32[8,256]{1,0:T(8,128)} %constant.213.clone.scale_ref, bf16[2,2,256,256]{3,2,1,0:T(8,128)(2,1)} %bitcast.226, bf16[2,2,256,256]{3,2,1,0:T(8,128)(2,1)} %bitcast.227, ...), custom_call_target="tpu_custom_call" | custom-call | flops 4294967296 | bytes 8388608 | tf_op jit(solution)/shard_map/pallas_call | solution.py:980
  193.0 3.5 broadcast_select_fusion.1
  197.8 4.6 bitcast_select_fusion.1
  202.5 3.7 multiply_reduce_fusion.3
  211.8 2.1 copy.116
  216.8 4.0 copy.120.shard_ref
  220.9 5.0 convert_multiply_fusion
  225.8 2.3 pad_maximum_fusion.5
  228.1 2.6 multiply_convert_fusion.grad_ref
  230.7 4.1 pad_maximum_fusion.4.second_ref
  234.8 283.4 %shard_map.377 = (bf16[1024,2432]{1,0:T(8,128)(2,1)}, bf16[1024,2432]{1,0:T(8,128)(2,1)}, bf16[1024,2432]{1,0:T(8,128)(2,1)}, f32[512,1792]{1,0:T(8,128)}, f32[5...) custom-call(bf16[1024,1792]{1,0:T(8,128)(2,1)} %pad_maximum_fusion.4.second_ref, ...), custom_call_target="tpu_custom_call" | custom-call | bytes 1024 | tf_op jit(solution)/shard_map/pallas_call | solution.py:809
  518.8 15.0 %convolution_convert_fusion.2 = bf16[1792,2432]{1,0:T(8,128)(2,1)} fusion(bf16[1024,2432]{1,0:T(8,128)(2,1)} %get-tuple-element.54, bf16[512,1792]{1,0:T(8,128)(2,1)} %collective-permute-done.9, bf16[512,1792]{1,0:T(8,128)(2,1)} %multiply_convert_fusion.3), kind=kOutput, calls=%fused_computation.2 | convolution fusion | flops 8937177088 | bytes 17367040 | tf_op jit(solution)/shard_map/dot_general | solution.py:70
  533.7 15.6 %convolution_convert_fusion.1 = bf16[1792,2432]{1,0:T(8,128)(2,1)} fusion(bf16[1024,2432]{1,0:T(8,128)(2,1)} %get-tuple-element.55, bf16[512,1792]{1,0:T(8,128)(2,1)} %collective-permute-done.9, bf16[512,1792]{1,0:T(8,128)(2,1)} %multiply_convert_fusion.3), kind=kOutput, calls=%fused_computation.1 | convolution fusion | flops 8937177088 | bytes 17367040 | tf_op jit(solution)/shard_map/dot_general | solution.py:70
  549.4 14.7 %convolution_convert_fusion = bf16[1792,2432]{1,0:T(8,128)(2,1)} fusion(bf16[1024,1792]{1,0:T(8,128)(2,1)S(1)} %copy-done.11, bf16[1024,2432]{1,0:T(8,128)(2,1)} %get-tuple-element.56), kind=kOutput, calls=%fused_computation | convolution fusion | flops 8929837056 | bytes 17367040 | tf_op jit(solution)/shard_map/dot_general | solution.py:70
  568.1 5.0 fusion.88
  574.4 4.7 fusion.35
  579.1 4.6 reshape.316
  583.8 7.1 constant_dynamic-slice_fusion.5
  591.9 2.6 slice.179
  594.5 2.2 copy-done.8
  598.2 4.4 slice.180
  602.7 4.8 reshape.325
  609.5 3.0 dynamic-slice_bitcast_fusion.3
  612.5 3.8 collective-permute-start.21
  616.3 5.0 constant_dynamic-slice_fusion.1
  623.8 10.8 %shard_map.378 = (f32[2,8,160,128]{3,2,1,0:T(8,128)}, bf16[2,2,256,1024]{3,2,1,0:T(8,128)(2,1)}) custom-call(s32[1]{0:T(128)} %bitcast.1.core_ref, s32[8,256]{1,0:T(8,128)} %constant.212.clone.index_ref, f32[8,256]{1,0:T(8,128)} %constant.213.clone.scale_ref, bf16[2,2,256,256]{3,2,1,0:T(8,128)(2,1)} %bitcast.228, bf16[2,2,256,896]{3,2,1,0:T(8,128)(2,1)} %bitcast.204, ...), custom_call_target="tpu_custom_call" | custom-call | flops 2147483648 | bytes 8388608 | tf_op jit(solution)/shard_map/pallas_call | solution.py:1064
  636.8 4.8 dynamic-slice_bitcast_fusion.1
  641.9 2.5 dynamic-slice_bitcast_fusion
  645.9 19.5 %fusion.32 = bf16[1792,896]{0,1:T(8,128)(2,1)} fusion(bf16[512,896]{1,0:T(8,128)(2,1)S(1)} %copy-done.45, bf16[512,896]{1,0:T(8,128)(2,1)S(1)} %copy-done.44, bf16[512,896]{1,0:T(8,128)(2,1)S(1)} %copy-done.47, bf16[512,896]{1,0:T(8,128)(2,1)S(1)} %copy-done.49, bf16[512,896]{1,0:T(8,128)(2,1)} %collective-permute-done.23, bf16[512,896]{1,0:T(8,128)(2,1)S(1)} %bitcast.211), kind=kOutput, calls=%fused_computation.70 | convolution fusion | flops 3308290048 | bytes 8716288 | tf_op jit(solution)/shard_map/dot_general | solution.py:70
  666.9 3.4 fusion.10.down_b_ref
  670.3 3.7 fusion.4.down_a_ref
  674.0 13.1 %collective-permute-done.16 = bf16[2,8,160,128]{3,2,1,0:T(8,128)(2,1)S(1)} collective-permute-done((bf16[2,8,160,128]{3,2,1,0:T(8,128)(2,1)S(1)}, bf16[2,8,160,128]{3,2,1,0:T(8,128)(2,1)S(1)}, u32[]{:S(2)}, u32[]{:S(2)}) %collective-permute-start.16) | collective-permute-done | bytes 655392 | tf_op jit(solution)/shard_map/ppermute | solution.py:363
  688.2 28.2 %shard_map.379 = (bf16[2,2,256,256]{3,2,1,0:T(8,128)(2,1)}, bf16[2,2,256,896]{3,2,1,0:T(8,128)(2,1)}) custom-call(s32[1]{0:T(128)} %bitcast.1.core_ref, s32[8,256]{1,0:T(8,128)} %constant.212.clone.index_ref, f32[8,256]{1,0:T(8,128)} %constant.213.clone.scale_ref, bf16[2,2,256,256]{3,2,1,0:T(8,128)(2,1)} %bitcast.229, bf16[2,2,256,256]{3,2,1,0:T(8,128)(2,1)} %bitcast.230, ...), custom_call_target="tpu_custom_call" | custom-call | flops 12884901888 | bytes 8388608 | tf_op jit(solution)/shard_map/pallas_call | solution.py:1072
  717.2 2.9 fusion.17
  721.5 2.8 convolution_convert_fusion.4
  729.1 2.1 fusion.36
  731.2 2.5 convolution_add_fusion
  733.8 5.3 convolution_convert_fusion.3
  741.1 6.2 copy.125
  747.3 6.0 fusion.38
  755.2 6.8 fusion.1.gate_ref
  762.1 5.6 fusion.up_ref
  767.7 6.8 fusion.18
  775.2 3.6 fusion.9
  778.7 6.5 copy.128
  785.2 191.5 %shard_map.380 = (f32[56,512]{1,0:T(8,128)}, f32[56,1792]{1,0:T(8,128)}, f32[56,1792]{1,0:T(8,128)}, f32[56,9728]{1,0:T(8,128)}, f32[56,4864]{1,0:T(8,128)}, /*index=5*/f32[56,256]{1,0:T(8,128)}) custom-call(bf16[2,448,1280]{2,1,0:T(8,128)(2,1)} %fusion.4.down_a_ref, bf16[2,448,2432]{2,1,0:T(8,128)(2,1)} %fusion.1.gate_ref, ...), custom_call_target="tpu_custom_call" | custom-call | bytes 1024 | tf_op jit(solution)/shard_map/pallas_call | solution.py:567
  985.9 2.3 multiply_subtract_fusion.3
  988.2 2.3 multiply_subtract_fusion.2
  990.5 6.1 multiply_subtract_fusion
  996.7 2.1 multiply_subtract_fusion.1
  999.3 5.2 fusion.14
  (333 shorter events, 94.7 us)
Async XLA Ops:
  5.3 7.6 copy-start.38
  12.8 11.1 %copy-start.66 = (f32[56,5]{0,1:T(8,128)S(1)}, f32[56,5]{0,1:T(8,128)}, u32[]{:S(2)}) copy-start(f32[56,5]{0,1:T(8,128)} %param.31) | copy-start | bytes 3364
  12.9 14.2 %copy-start.3 = (bf16[2,256,1792]{2,1,0:T(8,128)(2,1)S(1)}, bf16[2,256,1792]{2,1,0:T(8,128)(2,1)}, u32[]{:S(2)}) copy-start(bf16[2,256,1792]{2,1,0:T(8,128)(2,1)} %param.23) | copy-start | bytes 5505028
  12.9 14.6 %copy-start.35 = (bf16[56,1,1,2432]{3,2,0,1:T(2,128)(2,1)S(1)}, bf16[56,1,1,2432]{3,2,0,1:T(2,128)(2,1)}, u32[]{:S(2)}) copy-start(bf16[56,1,1,2432]{3,2,0,1:T(2,128)(2,1)} %get-tuple-element.191) | copy-start | bytes 817156
  23.5 7.4 collective-permute-start.2
  27.0 2.5 collective-permute-start.1
  27.1 91.7 %collective-permute-start = (bf16[512,1792]{1,0:T(8,128)(2,1)S(1)}, bf16[512,1792]{1,0:T(8,128)(2,1)}, u32[]{:S(2)}, u32[]{:S(2)}) collective-permute-start(bf16[512,1792]{1,0:T(8,128)(2,1)S(1)} %bitcast.163), channel_id=1, source_target_pairs={{0,1},{1,0},{2,3},{3,2},{4,5},{5,4},{6,7},{7,6},{8,9},{9,8},{10,11... | collective-permute-start | bytes 5505032 | tf_op jit(solution)/shard_map/ppermute | solution.py:271
  32.4 82.8 %copy-start.18 = (bf16[56,8192]{1,0:T(8,128)(2,1)}, bf16[56,8192]{1,0:T(8,128)(2,1)S(1)}, u32[]{:S(2)}) copy-start(bf16[56,8192]{1,0:T(8,128)(2,1)S(1)} %get-tuple-element.187) | copy-start | bytes 2752516
  32.4 82.8 %copy-start.20 = (bf16[56,8192]{1,0:T(8,128)(2,1)}, bf16[56,8192]{1,0:T(8,128)(2,1)S(1)}, u32[]{:S(2)}) copy-start(bf16[56,8192]{1,0:T(8,128)(2,1)S(1)} %get-tuple-element.188) | copy-start | bytes 2752516
  118.6 10.7 %copy-start.55 = (f32[1792]{0:T(1024)}, f32[1792]{0:T(1024)S(1)}, u32[]{:S(2)}) copy-start(f32[1792]{0:T(1024)S(1)} %get-tuple-element.148) | copy-start | bytes 21508
  118.7 14.5 %copy-start.58 = (f32[896]{0:T(1024)}, f32[896]{0:T(1024)S(1)}, u32[]{:S(2)}) copy-start(f32[896]{0:T(1024)S(1)} %fusion.76) | copy-start | bytes 10756
  118.7 14.5 %copy-start.60 = (f32[896]{0:T(1024)}, f32[896]{0:T(1024)S(1)}, u32[]{:S(2)}) copy-start(f32[896]{0:T(1024)S(1)} %fusion.75) | copy-start | bytes 10756
  118.8 14.5 %copy-start.62 = (f32[896]{0:T(1024)}, f32[896]{0:T(1024)S(1)}, u32[]{:S(2)}) copy-start(f32[896]{0:T(1024)S(1)} %fusion.74) | copy-start | bytes 10756
  118.8 10.5 %slice-start = ((s8[7798784]{0:T(1024)(128)(4,1)}), s8[4194304]{0:T(1024)(128)(4,1)S(1)}, s32[]{:S(2)}) async-start(s8[7798784]{0:T(1024)(128)(4,1)} %bitcast.155), calls=%async_computation | async-start | bytes 8388608
  121.3 8.0 slice-start.1
  128.0 4.9 collective-permute-start.3
  145.6 16.1 %collective-permute-start.4 = (bf16[2,8,160,128]{3,2,1,0:T(8,128)(2,1)S(1)}, bf16[2,8,160,128]{3,2,1,0:T(8,128)(2,1)S(1)}, u32[]{:S(2)}, u32[]{:S(2)}) collective-permute-start(bf16[2,8,160,128]{3,2,1,0:T(8,128)(2,1)S(1)} %convert_element_type.218), channel_id=1, source_target_pairs={{0,2},{1,3},{8,10},{9,11},{16,18},{17,19},{24,26},{25,27}} | collective-permute-start | bytes 1966088 | tf_op jit(solution)/shard_map/ppermute | solution.py:363
  164.8 6.6 copy-start.70
  164.8 3.6 collective-permute-start.5
  168.5 24.5 %collective-permute-start.8 = (bf16[1792,896]{1,0:T(8,128)(2,1)}, bf16[1792,896]{1,0:T(8,128)(2,1)}, u32[]{:S(2)}, u32[]{:S(2)}) collective-permute-start(bf16[1792,896]{1,0:T(8,128)(2,1)} %slice.204), channel_id=1, source_target_pairs={{0,1},{1,0},{2,3},{3,2},{4,5},{5,4},{6,7},{7,6},{8,9},{9,8},{10,11... | collective-permute-start | bytes 9633800 | tf_op jit(solution)/shard_map/ppermute | solution.py:271
  170.4 3.0 collective-permute-start.6
  175.6 13.5 %copy-start.68 = (f32[56,5]{0,1:T(8,128)S(1)}, f32[56,5]{0,1:T(8,128)}, u32[]{:S(2)}) copy-start(f32[56,5]{0,1:T(8,128)} %param.43) | copy-start | bytes 3364
  175.6 15.0 %copy-start.69 = (f32[56,5]{0,1:T(8,128)S(1)}, f32[56,5]{0,1:T(8,128)}, u32[]{:S(2)}) copy-start(f32[56,5]{0,1:T(8,128)} %param.37) | copy-start | bytes 3364
  187.4 9.1 collective-permute-start.7
  191.3 34.5 %collective-permute-start.10 = (bf16[512,1792]{1,0:T(8,128)(2,1)}, bf16[512,1792]{1,0:T(8,128)(2,1)}, u32[]{:S(2)}, u32[]{:S(2)}) collective-permute-start(bf16[512,1792]{1,0:T(8,128)(2,1)} %bitcast.17), channel_id=1, source_target_pairs={{0,1},{1,0},{2,3},{3,2},{4,5},{5,4},{6,7},{7,6},{8,9},{9,8},{10,11... | collective-permute-start | bytes 5505032 | tf_op jit(solution)/shard_map/ppermute | solution.py:271
  207.8 22.8 %collective-permute-start.9 = (bf16[512,1792]{1,0:T(8,128)(2,1)}, bf16[512,1792]{1,0:T(8,128)(2,1)}, u32[]{:S(2)}, u32[]{:S(2)}) collective-permute-start(bf16[512,1792]{1,0:T(8,128)(2,1)} %multiply_convert_fusion.3), channel_id=1, source_target_pairs={{0,1},{1,0},{2,3},{3,2},{4,5},{5,4},{6,7},{7,6},{8,9},{9,8},{10,11... | collective-permute-start | bytes 5505032 | tf_op jit(solution)/shard_map/ppermute | solution.py:271
  518.2 45.8 %collective-permute-start.12 = (f32[512,1792]{1,0:T(8,128)}, f32[512,1792]{1,0:T(8,128)S(1)}, u32[]{:S(2)}, u32[]{:S(2)}) collective-permute-start(f32[512,1792]{1,0:T(8,128)} %get-tuple-element.53), channel_id=1, source_target_pairs={{0,1},{1,0},{2,3},{3,2},{4,5},{5,4},{6,7},{7,6},{8,9},{9,8},{10,11... | collective-permute-start | bytes 11010056 | tf_op jit(solution)/shard_map/ppermute | solution.py:271
  518.3 48.7 %collective-permute-start.11 = (f32[512,1792]{1,0:T(8,128)}, f32[512,1792]{1,0:T(8,128)S(1)}, u32[]{:S(2)}, u32[]{:S(2)}) collective-permute-start(f32[512,1792]{1,0:T(8,128)} %get-tuple-element.51), channel_id=1, source_target_pairs={{0,1},{1,0},{2,3},{3,2},{4,5},{5,4},{6,7},{7,6},{8,9},{9,8},{10,11... | collective-permute-start | bytes 11010056 | tf_op jit(solution)/shard_map/ppermute | solution.py:271
  533.7 15.6 %copy-start.11 = (bf16[1024,1792]{1,0:T(8,128)(2,1)S(1)}, bf16[1024,1792]{1,0:T(8,128)(2,1)}, u32[]{:S(2)}) copy-start(bf16[1024,1792]{1,0:T(8,128)(2,1)} %multiply_convert_fusion.grad_ref) | copy-start | bytes 11010052
  549.4 14.7 %copy-start.30 = (f32[512,1792]{1,0:T(8,128)S(1)}, f32[512,1792]{1,0:T(8,128)}, u32[]{:S(2)}) copy-start(f32[512,1792]{1,0:T(8,128)} %get-tuple-element.52) | copy-start | bytes 11010052
  568.1 6.3 copy-start.32
  568.1 6.3 copy-start.34
  591.9 30.5 %collective-permute-start.13 = (bf16[512,896]{1,0:T(8,128)(2,1)}, bf16[512,896]{1,0:T(8,128)(2,1)S(1)}, u32[]{:S(2)}, u32[]{:S(2)}) collective-permute-start(bf16[512,896]{1,0:T(8,128)(2,1)} %bitcast.140), channel_id=1, source_target_pairs={{0,1},{1,0},{2,3},{3,2},{4,5},{5,4},{6,7},{7,6},{8,9},{9,8},{10,11... | collective-permute-start | bytes 2752520 | tf_op jit(solution)/shard_map/ppermute | solution.py:271
  607.5 8.8 copy-start.9
  609.3 61.0 %collective-permute-start.19 = (bf16[2,448,1280]{2,1,0:T(8,128)(2,1)}, bf16[2,448,1280]{2,1,0:T(8,128)(2,1)}, u32[]{:S(2)}, u32[]{:S(2)}) collective-permute-start(bf16[2,448,1280]{2,1,0:T(8,128)(2,1)} %dynamic-slice_bitcast_fusion.2), channel_id=1, source_target_pairs={{0,16},{16,0},{1,17},{17,1},{2,18},{18,2},{3,19},{19,3},{4,20},{20... | collective-permute-start | bytes 6881288 | tf_op jit(solution)/shard_map/ppermute | solution.py:288
  612.5 54.3 %collective-permute-start.21 = (bf16[2,448,1152]{2,1,0:T(8,128)(2,1)}, bf16[2,448,1152]{2,1,0:T(8,128)(2,1)}, u32[]{:S(2)}, u32[]{:S(2)}) collective-permute-start(bf16[2,448,1152]{2,1,0:T(8,128)(2,1)} %dynamic-slice_bitcast_fusion.3), channel_id=1, source_target_pairs={{0,8},{8,0},{1,9},{9,1},{2,10},{10,2},{3,11},{11,3},{4,12},{12,4},... | collective-permute-start | bytes 6193160 | tf_op jit(solution)/shard_map/ppermute | solution.py:288
  622.4 22.5 %collective-permute-start.23 = (bf16[512,896]{1,0:T(8,128)(2,1)}, bf16[512,896]{1,0:T(8,128)(2,1)}, u32[]{:S(2)}, u32[]{:S(2)}) collective-permute-start(bf16[512,896]{1,0:T(8,128)(2,1)} %bitcast.138), channel_id=1, source_target_pairs={{0,1},{1,0},{2,3},{3,2},{4,5},{5,4},{6,7},{7,6},{8,9},{9,8},{10,11... | collective-permute-start | bytes 2752520 | tf_op jit(solution)/shard_map/ppermute | solution.py:271
  623.8 18.1 %slice-start.8 = ((s8[8716288]{0:T(1024)(128)(4,1)}), s8[327680]{0:T(1024)(128)(4,1)S(1)}, s32[]{:S(2)}) async-start(s8[8716288]{0:T(1024)(128)(4,1)} %bitcast.181), calls=%async_computation.8 | async-start | bytes 655360
  623.8 18.1 %slice-start.9 = ((s8[8716288]{0:T(1024)(128)(4,1)}), s8[4194304]{0:T(1024)(128)(4,1)S(1)}, s32[]{:S(2)}) async-start(s8[8716288]{0:T(1024)(128)(4,1)} %bitcast.181), calls=%async_computation.9 | async-start | bytes 8388608
  636.0 8.4 collective-permute-start.14
  641.5 113.7 %collective-permute-start.20 = (bf16[2,448,2432]{2,1,0:T(8,128)(2,1)}, bf16[2,448,2432]{2,1,0:T(8,128)(2,1)}, u32[]{:S(2)}, u32[]{:S(2)}) collective-permute-start(bf16[2,448,2432]{2,1,0:T(8,128)(2,1)} %dynamic-slice_bitcast_fusion.1), channel_id=1, source_target_pairs={{0,16},{16,0},{1,17},{17,1},{2,18},{18,2},{3,19},{19,3},{4,20},{20... | collective-permute-start | bytes 13074440 | tf_op jit(solution)/shard_map/ppermute | solution.py:288
  644.5 117.6 %collective-permute-start.22 = (bf16[2,448,2432]{2,1,0:T(8,128)(2,1)}, bf16[2,448,2432]{2,1,0:T(8,128)(2,1)}, u32[]{:S(2)}, u32[]{:S(2)}) collective-permute-start(bf16[2,448,2432]{2,1,0:T(8,128)(2,1)} %dynamic-slice_bitcast_fusion), channel_id=1, source_target_pairs={{0,8},{8,0},{1,9},{9,1},{2,10},{10,2},{3,11},{11,3},{4,12},{12,4},... | collective-permute-start | bytes 13074440 | tf_op jit(solution)/shard_map/ppermute | solution.py:288
  644.8 25.5 %slice-start.4 = ((s8[4587520]{0:T(1024)(128)(4,1)}), s8[4194304]{0:T(1024)(128)(4,1)S(1)}, s32[]{:S(2)}) async-start(s8[4587520]{0:T(1024)(128)(4,1)} %bitcast.172), calls=%async_computation.4 | async-start | bytes 8388608
  644.9 20.4 %collective-permute-start.15 = (bf16[2,8,160,128]{3,2,1,0:T(8,128)(2,1)S(1)}, bf16[2,8,160,128]{3,2,1,0:T(8,128)(2,1)S(1)}, u32[]{:S(2)}, u32[]{:S(2)}) collective-permute-start(bf16[2,8,160,128]{3,2,1,0:T(8,128)(2,1)S(1)} %fusion.53), channel_id=1, source_target_pairs={{4,2},{5,3},{12,10},{13,11},{20,18},{21,19},{28,26},{29,27}} | collective-permute-start | bytes 1966088 | tf_op jit(solution)/shard_map/ppermute | solution.py:363
  645.9 21.0 %copy-start.10 = (bf16[1792,1152]{1,0:T(8,128)(2,1)S(1)}, bf16[1792,1152]{1,0:T(8,128)(2,1)}, u32[]{:S(2)}) copy-start(bf16[1792,1152]{1,0:T(8,128)(2,1)} %slice.180) | copy-start | bytes 12386308
  645.9 24.4 %slice-start.5 = ((s8[4587520]{0:T(1024)(128)(4,1)}), s8[393216]{0:T(1024)(128)(4,1)S(1)}, s32[]{:S(2)}) async-start(s8[4587520]{0:T(1024)(128)(4,1)} %bitcast.172), calls=%async_computation.5 | async-start | bytes 786432
  665.6 21.5 %collective-permute-start.16 = (bf16[2,8,160,128]{3,2,1,0:T(8,128)(2,1)S(1)}, bf16[2,8,160,128]{3,2,1,0:T(8,128)(2,1)S(1)}, u32[]{:S(2)}, u32[]{:S(2)}) collective-permute-start(bf16[2,8,160,128]{3,2,1,0:T(8,128)(2,1)S(1)} %add_convert_fusion.2), channel_id=1, source_target_pairs={{2,0},{3,1},{10,8},{11,9},{18,16},{19,17},{26,24},{27,25}} | collective-permute-start | bytes 1966088 | tf_op jit(solution)/shard_map/ppermute | solution.py:363
  688.2 29.0 %copy-start.2 = (f32[2,2,258,896]{3,2,1,0:T(8,128)S(1)}, f32[2,2,258,896]{3,2,1,0:T(8,128)}, u32[]{:S(2)}) copy-start(f32[2,2,258,896]{3,2,1,0:T(8,128)} %copy-done.1) | copy-start | bytes 11096068
  720.1 5.5 collective-permute-start.17
  733.7 34.0 %collective-permute-start.18 = (f32[512,1792]{1,0:T(8,128)}, f32[512,1792]{1,0:T(8,128)}, u32[]{:S(2)}, u32[]{:S(2)}) collective-permute-start(f32[512,1792]{1,0:T(8,128)} %convolution_add_fusion), channel_id=1, source_target_pairs={{0,1},{1,0},{2,3},{3,2},{4,5},{5,4},{6,7},{7,6},{8,9},{9,8},{10,11... | collective-permute-start | bytes 11010056 | tf_op jit(solution)/shard_map/ppermute | solution.py:271
  747.3 14.7 %slice-start.11 = ((s8[8716288]{0:T(1024)(128)(4,1)}), s8[4194304]{0:T(1024)(128)(4,1)S(1)}, s32[]{:S(2)}) async-start(s8[8716288]{0:T(1024)(128)(4,1)} %bitcast.184), calls=%async_computation.11 | async-start | bytes 8388608
  747.3 14.7 %slice-start.12 = ((s8[8716288]{0:T(1024)(128)(4,1)}), s8[4194304]{0:T(1024)(128)(4,1)S(1)}, s32[]{:S(2)}) async-start(s8[8716288]{0:T(1024)(128)(4,1)} %bitcast.184), calls=%async_computation.12 | async-start | bytes 8388608
  753.3 8.8 slice-start.13
  755.2 12.4 %slice-start.6 = ((s8[7340032]{0:T(1024)(128)(4,1)}), s8[4194304]{0:T(1024)(128)(4,1)S(1)}, s32[]{:S(2)}) async-start(s8[7340032]{0:T(1024)(128)(4,1)} %bitcast.175), calls=%async_computation.6 | async-start | bytes 8388608
  785.2 192.4 %copy-start.54 = (f32[56,5]{1,0:T(8,128)S(1)}, f32[56,5]{1,0:T(8,128)}, u32[]{:S(2)}) copy-start(f32[56,5]{1,0:T(8,128)} %copy.131) | copy-start | bytes 3364
  785.2 198.7 %copy-start.52 = (f32[56,512]{1,0:T(8,128)S(1)}, f32[56,512]{1,0:T(8,128)}, u32[]{:S(2)}) copy-start(f32[56,512]{1,0:T(8,128)} %param.26) | copy-start | bytes 344068
  785.2 200.7 %copy-start.37 = (f32[56,1792]{1,0:T(8,128)S(1)}, f32[56,1792]{1,0:T(8,128)}, u32[]{:S(2)}) copy-start(f32[56,1792]{1,0:T(8,128)} %param.27) | copy-start | bytes 1204228
  785.2 200.7 %copy-start.53 = (f32[56,1792]{1,0:T(8,128)S(1)}, f32[56,1792]{1,0:T(8,128)}, u32[]{:S(2)}) copy-start(f32[56,1792]{1,0:T(8,128)} %param.33) | copy-start | bytes 1204228
  976.8 11.4 %copy-start.39 = (f32[56,1792]{1,0:T(8,128)S(1)}, f32[56,1792]{1,0:T(8,128)}, u32[]{:S(2)}) copy-start(f32[56,1792]{1,0:T(8,128)} %param.28) | copy-start | bytes 1204228
  976.8 11.4 %copy-start.40 = (f32[56,1792]{1,0:T(8,128)S(1)}, f32[56,1792]{1,0:T(8,128)}, u32[]{:S(2)}) copy-start(f32[56,1792]{1,0:T(8,128)} %get-tuple-element.238) | copy-start | bytes 1204228
  984.0 6.5 copy-start.16
  984.0 6.5 copy-start.17
  990.5 6.2 copy-start.27
  990.5 8.3 copy-start.13
  (45 other events, 159.9 us)

commit v4 on v3

--- a/solution.py
+++ b/solution.py
@@ -254,6 +254,106 @@
     )
 
 
+def linked(kernel, up, ids):
+    def run(*refs):
+        y, x, z, core = places_of()
+        last = lax.axis_size("z") - 1
+        *refs, sent, send_sem, recv_sem = refs
+        total_ref = refs[-1]
+        by = 1 if up else last
+        receives, sends = (z > 0, z < last) if up else (z < last, z > 0)
+
+        barrier = pltpu.get_barrier_semaphore()
+        for step in (1, last):
+            pl.semaphore_signal(
+                barrier,
+                inc=1,
+                device_id=(y, x, lax.rem(z + step, last + 1), core),
+                device_id_type=pl.DeviceIdType.MESH,
+            )
+        pl.semaphore_wait(barrier, 2)
+
+        def transfer(slot, head):
+            return pltpu.make_async_remote_copy(
+                src_ref=sent.at[slot, head],
+                dst_ref=total_ref.at[slot, head],
+                send_sem=send_sem.at[slot, head],
+                recv_sem=recv_sem.at[slot, head],
+                device_id=(y, x, lax.rem(z + by, last + 1), core),
+                device_id_type=pl.DeviceIdType.MESH,
+            )
+
+        @pl.when(jnp.logical_not(receives))
+        def _():
+            total_ref[...] = jnp.zeros_like(total_ref)
+
+        @pl.loop(0, sent.shape[0])
+        def _(slot):
+            for head in range(HC):
+                term = kernel([core], slot, head, *refs[:-1])
+
+                @pl.when(receives)
+                def _(head=head):
+                    transfer(slot, head).wait_recv()
+
+                @pl.when(sends)
+                def _(head=head, term=term):
+                    sent[slot, head] = (total_ref[slot, head].astype(f32) + term).astype(bf16)
+                    transfer(slot, head).start()
+
+        @pl.when(sends)
+        def _():
+            @pl.loop(0, sent.shape[0])
+            def _(slot):
+                for head in range(HC):
+                    transfer(slot, head).wait_send()
+
+    def call(*operands, slots, extra=()):
+        state = jax.ShapeDtypeStruct((slots, HC, FROWS, LANES), bf16)
+        vmem = pl.BlockSpec(memory_space=pltpu.VMEM)
+        return pl.pallas_call(
+            run,
+            out_shape=list(extra) + [state],
+            in_specs=[vmem] * len(operands),
+            out_specs=[vmem] * (len(extra) + 1),
+            scratch_shapes=[
+                pltpu.VMEM((slots, HC, FROWS, LANES), bf16),
+                pltpu.SemaphoreType.DMA((slots, HC)),
+                pltpu.SemaphoreType.DMA((slots, HC)),
+            ],
+            compiler_params=pltpu.CompilerParams(
+                collective_id=ids, has_side_effects=True, vmem_limit_bytes=40 << 20
+            ),
+            cost_estimate=pl.CostEstimate(flops=0, bytes_accessed=1024, transcendentals=0),
+        )(*operands)
+
+    return call
+
+
+def key_term(core_ref, slot, head, index_ref, scale_ref, qk_ref, v_ref):
+    keys = both_halves(core_ref, qk_ref.at[:, slot], slice(LANES, 2 * LANES))
+    first, second = selectors(index_ref, head)
+    one, two = factors(keys, first, second, scale_ref)
+    phi = (one * two * scale_ref[2:3, :]).astype(bf16)
+    values = with_one(head_columns(core_ref, v_ref.at[:, slot], head)).astype(bf16)
+    return dot_tn(phi, values)[:FROWS]
+
+
+def query_term(core_ref, slot, head, index_ref, scale_ref, qk_ref, gm_ref, mixer_ref, den_ref, gnum_ref):
+    queries = both_halves(core_ref, qk_ref.at[:, slot], slice(0, LANES))
+    first, second = selectors(index_ref, head)
+    one, two = factors(queries, first, second, scale_ref)
+    phi = (one * two).astype(bf16)
+    den = both_halves(core_ref, den_ref.at[:, slot], slice(None))[:, head : head + 1]
+    lane = lax.broadcasted_iota(jnp.int32, (queries.shape[0], LANES), 1)
+    grad = jnp.where(lane < HW, head_columns(core_ref, gm_ref.at[:, slot], head), 0.0)
+    mixer = head_columns(core_ref, mixer_ref.at[:, slot], head)
+    pulled = -jnp.sum(grad * mixer, axis=1, keepdims=True)
+    grad = (jnp.where(lane == HW, pulled, grad) / den).astype(bf16)
+    store_halves(core_ref, gnum_ref.at[:, slot], grad, slice(head * LANES, (head + 1) * LANES))
+    return dot_tn(phi, grad)[:FROWS]
+
+
 def passed_along(array, axis, by):
     count = lax.axis_size(axis)
     pairs = [(i, i + by) for i in range(count) if 0 <= i + by < count]
@@ -379,6 +479,9 @@
 ORDERS = (("y", "x", "z0", "z1"), ("x", "y", "z0", "z1"))
 
 
+WIDE = 2 * LANES
+
+
 def reduce_kernel(
     down_a_ref,
     gate_ref,
@@ -386,6 +489,7 @@
     up_ref,
     last_a_ref,
     last_b_ref,
+    small_terms_ref,
     qk_ref,
     value_ref,
     out_ref,
@@ -406,31 +510,35 @@
     y, x, z, core = places_of()
     places = {"y": y, "x": x, "z0": z % 2, "z1": z // 2}
 
-    def tiles(ref):
-        return ref.shape[-1] // LANES
-
     parts, count = ([], []), 0
-    for stream, refs in enumerate(((down_a_ref, gate_ref, last_a_ref), (down_b_ref, up_ref, last_b_ref))):
+    all_refs = (
+        (down_a_ref, gate_ref, last_a_ref),
+        (down_b_ref, up_ref, last_b_ref, small_terms_ref),
+    )
+    for stream, refs in enumerate(all_refs):
         at = 0
         for ref in refs:
-            parts[stream].append((ref, len(ref.shape) == 3, at, at + tiles(ref)))
-            at += tiles(ref)
+            chunks = ref.shape[-1] // WIDE
+            parts[stream].append((ref, len(ref.shape) == 3, at, at + chunks))
+            at += chunks
         count = max(count, at)
-    own_down = core * tiles_of(FC)
-    own_value = core * tiles_of(VC)
-    small_at = parts[1][2][2] + tiles_of(VC) + 1
+    hidden, width = FC // LANES, VC // LANES
+    down_a = (hidden + 1) // 2
+    down_b = hidden - down_a
+    gate_at, last_a = 2 * parts[0][1][2], 2 * parts[0][2][2]
+    up_at, last_b, small_at = (2 * parts[1][at][2] for at in (1, 2, 3))
     places_out = (
         (
-            (down_ref, own_down, 0, parts[0][0][3]),
-            (gu_ref, own_down, parts[0][1][2], parts[0][1][3]),
-            (value_ref, own_value, parts[0][2][2], parts[0][2][2] + tiles_of(VC)),
-            (qk_ref, core, parts[0][2][3] - 1, parts[0][2][3]),
+            (down_ref, core * hidden, 0, down_a),
+            (gu_ref, core * hidden, gate_at, gate_at + hidden),
+            (value_ref, core * width, last_a, last_a + width),
+            (qk_ref, core, last_a + width, last_a + width + 1),
+            (qk_ref, CORES + core, last_a + width + 1, last_a + width + 2),
         ),
         (
-            (down_ref, own_down + parts[0][0][3], 0, parts[1][0][3]),
-            (gu_ref, CORES * tiles_of(FC) + own_down, parts[1][1][2], parts[1][1][3]),
-            (out_ref, own_value, parts[1][2][2], parts[1][2][2] + tiles_of(VC)),
-            (qk_ref, CORES + core, small_at - 1, small_at),
+            (down_ref, core * hidden + down_a, 0, down_b),
+            (gu_ref, (CORES + core) * hidden, up_at, up_at + hidden),
+            (out_ref, core * width, last_b, last_b + width),
             (small_ref, core, small_at, small_at + 1),
         ),
     )
@@ -438,12 +546,15 @@
 
     def columns(tile):
         return pl.ds(pl.multiple_of(tile * LANES, LANES), LANES)
+
+    def wide_columns(chunk):
+        return pl.ds(pl.multiple_of(chunk * WIDE, WIDE), WIDE)
 
     def transfer(stream, stage, chunk, source, target=None):
         landing = chunk % 4
         if target is None:
             target = (got_terms, got_sums, got_halves, got_quarters)[stage].at[stream, landing]
-        axis = (ORDERS[stream] + ("core",))[stage]
+        axis = (ORDERS[stream] + ("core", "core"))[stage]
         return pltpu.make_async_remote_copy(
             src_ref=source,
             dst_ref=target,
@@ -454,7 +565,7 @@
         )
 
     def first_view(stream, ref, tile, place):
-        ref = ref.at[:, :, :, columns(tile)]
+        ref = ref.at[:, :, :, wide_columns(tile)]
         return ref.at[place] if stream == 0 else ref.at[:, place]
 
     def source_of(stream, stage, chunk):
@@ -469,12 +580,12 @@
         return a.astype(f32) + b.astype(f32)
 
     def begin(stream, chunk):
-        ref, _, start, stop = parts[stream][2]
-
-        @pl.when((chunk >= start) & (chunk < stop))
-        def _():
-            there = 1 - places[ORDERS[stream][0]]
-            transfer(stream, 0, chunk, first_view(stream, ref, chunk - start, there)).start()
+        for ref, _, start, stop in parts[stream][2:]:
+
+            @pl.when((chunk >= start) & (chunk < stop))
+            def _(ref=ref, start=start):
+                there = 1 - places[ORDERS[stream][0]]
+                transfer(stream, 0, chunk, first_view(stream, ref, chunk - start, there)).start()
 
     def second(stream, chunk):
         for ref, summed, start, stop in parts[stream]:
@@ -483,7 +594,7 @@
             def _(ref=ref, summed=summed, start=start):
                 tile = chunk - start
                 if summed:
-                    sums[stream, chunk % 2] = ref[:, :, columns(tile)]
+                    sums[stream, chunk % 2] = ref[:, :, wide_columns(tile)]
                 else:
                     there = 1 - places[ORDERS[stream][0]]
                     transfer(stream, 0, chunk, first_view(stream, ref, tile, there)).wait()
@@ -509,22 +620,26 @@
             transfer(stream, stage + 1, chunk, source_of(stream, stage + 1, chunk)).start()
 
     def hand_over(stream, chunk, waiting):
-        for ref, first, start, stop in places_out[stream]:
-
-            @pl.when((chunk >= start) & (chunk < stop))
-            def _(ref=ref, first=first, start=start):
-                target = ref.at[:, columns(first + chunk - start)]
-                copy = transfer(stream, 4, chunk, finals.at[stream, chunk % 2, 1 - core], target)
-                if waiting:
-                    copy.wait()
-                else:
-                    target[...] = finals[stream, chunk % 2, core]
-                    copy.start()
+        for at in range(2):
+            tile = 2 * chunk + at
+            lanes = slice(at * LANES, (at + 1) * LANES)
+            for ref, first, start, stop in places_out[stream]:
+
+                @pl.when((tile >= start) & (tile < stop))
+                def _(at=at, tile=tile, lanes=lanes, ref=ref, first=first, start=start):
+                    target = ref.at[:, columns(first + tile - start)]
+                    source = finals.at[stream, chunk % 2, 1 - core, :, lanes]
+                    copy = transfer(stream, 4 + at, chunk, source, target)
+                    if waiting:
+                        copy.wait()
+                    else:
+                        target[...] = finals[stream, chunk % 2, core, :, lanes]
+                        copy.start()
 
     @pl.loop(0, count + 5)
     def _(step):
         for stream in range(2):
-            total = parts[stream][2][3]
+            total = parts[stream][-1][3]
 
             @pl.when(step < total)
             def _(stream=stream):
@@ -532,7 +647,7 @@
 
         for stage in range(5):
             for stream in range(2):
-                total = parts[stream][2][3]
+                total = parts[stream][-1][3]
 
                 @pl.when((step >= stage + 1) & (step < total + stage + 1))
                 def _(stage=stage, stream=stream):
@@ -547,45 +662,33 @@
                         hand_over(stream, chunk, False)
 
 
-def tiles_of(width):
-    return width // LANES
-
-
-def first_exchange(terms, axis):
-    view = terms.reshape(2, 2, D // 4, terms.shape[1])
-    dim = 0 if axis == "y" else 1
-    mine = bit_at(axis, 0)
-    arrived = exchanged(part_of(view, dim, 1 - mine), axis, 0)
-    return (part_of(view, dim, mine).astype(f32) + arrived.astype(f32)).astype(bf16)
-
-
-def reduced(down_a, gate, down_b, up, last_a, last_b, owned):
+def reduced(down_a, gate, down_b, up, last_a, last_b, small, owned):
     block, rows = D // 4, D // 16
     dma = pltpu.SemaphoreType.DMA
-    last_a, last_b = (last.reshape(2, 2, block, last.shape[1]) for last in (last_a, last_b))
+    last_a, last_b, small = (last.reshape(2, 2, block, -1) for last in (last_a, last_b, small))
     widths = (2 * CORES * QC, CORES * VC, CORES * VC, 2 * CORES * FC, CORES * FC, CORES * LANES)
     return pl.pallas_call(
         reduce_kernel,
         out_shape=[jax.ShapeDtypeStruct((owned, width), f32) for width in widths],
-        in_specs=[pl.BlockSpec(memory_space=pltpu.VMEM)] * 6,
+        in_specs=[pl.BlockSpec(memory_space=pltpu.VMEM)] * 7,
         out_specs=[pl.BlockSpec(memory_space=pltpu.VMEM)] * 6,
         scratch_shapes=[
-            pltpu.VMEM((2, 2, 2, block, LANES), bf16),
-            pltpu.VMEM((2, 2, 2, 2, rows, LANES), bf16),
-            pltpu.VMEM((2, 2, 2, rows, LANES), bf16),
-            pltpu.VMEM((2, 2, CORES, owned, LANES), f32),
-            pltpu.VMEM((2, 4, 2, block, LANES), bf16),
-            pltpu.VMEM((2, 4, block, LANES), bf16),
-            pltpu.VMEM((2, 4, 2, rows, LANES), bf16),
-            pltpu.VMEM((2, 4, rows, LANES), bf16),
-            dma((2, 5, 4)),
-            dma((2, 5, 4)),
+            pltpu.VMEM((2, 2, 2, block, WIDE), bf16),
+            pltpu.VMEM((2, 2, 2, 2, rows, WIDE), bf16),
+            pltpu.VMEM((2, 2, 2, rows, WIDE), bf16),
+            pltpu.VMEM((2, 2, CORES, owned, WIDE), f32),
+            pltpu.VMEM((2, 4, 2, block, WIDE), bf16),
+            pltpu.VMEM((2, 4, block, WIDE), bf16),
+            pltpu.VMEM((2, 4, 2, rows, WIDE), bf16),
+            pltpu.VMEM((2, 4, rows, WIDE), bf16),
+            dma((2, 6, 4)),
+            dma((2, 6, 4)),
         ],
         compiler_params=pltpu.CompilerParams(
             collective_id=0, has_side_effects=True, vmem_limit_bytes=56 << 20
         ),
         cost_estimate=pl.CostEstimate(flops=0, bytes_accessed=1024, transcendentals=0),
-    )(down_a, gate, down_b, up, last_a, last_b)
+    )(down_a, gate, down_b, up, last_a, last_b, small)
 
 
 def places_of():
@@ -687,9 +790,14 @@
     second_ref,
     grad_ref,
     shard_ref,
-    hidden_ref,
-    grad_gate_ref,
-    grad_up_ref,
+    gate_send_ref,
+    gate_keep_ref,
+    up_send_ref,
+    up_keep_ref,
+    down_a_send_ref,
+    down_a_keep_ref,
+    down_b_send_ref,
+    down_b_keep_ref,
     down_own_ref,
     down_other_ref,
     second_own_ref,
@@ -697,9 +805,14 @@
     held,
     down_ref,
     grad_second_ref,
+    second_t_ref,
+    grad_t_ref,
+    narrow,
+    terms,
     send_sem,
     recv_sem,
     out_sem,
+    terms_sem,
 ):
     y, x, z, core = places_of()
     down_ref[...] = jnp.zeros_like(down_ref)
@@ -720,9 +833,11 @@
             device_id_type=pl.DeviceIdType.MESH,
         )
 
+    down_a = (tiles + 1) // 2
+    down_b = tiles - down_a
+
     def compute(tile):
         weights = held.at[tile % SLOTS]
-        columns = pl.ds(pl.multiple_of(tile * LANES, LANES), LANES)
 
         @pl.loop(0, tokens // block)
         def _(part):
@@ -739,13 +854,65 @@
             grad_gate = (
                 grad_hidden * upward * sigmoid_gate * (1.0 + gate * (1.0 - sigmoid_gate))
             ).astype(bf16)
-            hidden_ref[rows, columns] = hidden
-            grad_up_ref[rows, columns] = grad_upward
-            grad_gate_ref[rows, columns] = grad_gate
+            grads = jnp.concatenate([grad_gate, grad_upward], axis=1)
+            narrow[rows, : 2 * LANES] = grads
+            narrow[rows, 2 * LANES :] = hidden
             down_ref[rows, :] += dot_nt(hidden, down)
-            grad_second_ref[rows, :] += dot_nt(
-                jnp.concatenate([grad_gate, grad_upward], axis=1), both
-            )
+            grad_second_ref[rows, :] += dot_nt(grads, both)
+
+    def weight_terms(tile):
+        slot = tile % 2
+
+        @pl.loop(0, 4)
+        def _(part):
+            rows = pl.ds(pl.multiple_of(part * quarter, quarter), quarter)
+            grads = dot(second_t_ref[rows, :], narrow[:, : 2 * LANES])
+            terms[slot, part // 2, part % 2, :, : 2 * LANES] = grads.astype(bf16)
+            down = dot(grad_t_ref[rows, :], narrow[:, 2 * LANES :])
+            terms[slot, part // 2, part % 2, :, 2 * LANES :] = down.astype(bf16)
+
+    quarter = D // 4
+
+    def terms_copies(tile):
+        slot = tile % 2
+
+        gate, up = (gate_send_ref, gate_keep_ref), (up_send_ref, up_keep_ref)
+        first, second = (down_a_send_ref, down_a_keep_ref), (down_b_send_ref, down_b_keep_ref)
+
+        def pair(index, stream, refs, at, sem):
+            here = (y, x)[stream]
+            columns = pl.ds(pl.multiple_of(at * LANES, LANES), LANES)
+            copies = []
+            for way, (place, ref) in enumerate(zip((1 - here, here), refs)):
+                source = terms.at[slot, :, :, :, index * LANES : (index + 1) * LANES]
+                source = source.at[place] if stream == 0 else source.at[:, place]
+                copies.append(
+                    pltpu.make_async_copy(source, ref.at[:, :, columns], terms_sem.at[slot, sem, way])
+                )
+            return copies
+
+        early = tile < down_a
+        return (
+            (None, pair(0, 0, gate, tile, 0)),
+            (None, pair(1, 1, up, tile, 1)),
+            (early, pair(2, 0, first, jnp.where(early, tile, 0), 2)),
+            (tile >= down_a, pair(2, 1, second, jnp.where(early, 0, tile - down_a), 2)),
+            (tile == tiles - 1, pair(0, 0, gate, tiles, 3)),
+            (tile == tiles - 1, pair(1, 1, up, tiles, 4)),
+            (tile == tiles - 1, pair(2, 1, second, down_b, 5)),
+        )
+
+    def all_copies(tile, act):
+        for condition, copies in terms_copies(tile):
+            if condition is None:
+                for copy in copies:
+                    act(copy)
+            else:
+
+                @pl.when(condition)
+                def _(copies=copies):
+                    for copy in copies:
+                        act(copy)
 
     pairs = (tiles + 1) // 2
 
@@ -767,6 +934,13 @@
     def finish(tile, order):
         transfer(3, tile, order).wait()
         compute(tile)
+
+        @pl.when(tile >= 2)
+        def _():
+            all_copies(tile - 2, lambda copy: copy.wait())
+
+        weight_terms(tile)
+        all_copies(tile, lambda copy: copy.start())
 
     def begin(tile, order):
         held[tile % SLOTS, y, x, z // 2, z % 2] = shard_ref[tile]
@@ -779,6 +953,16 @@
         each(step, 4, finish)
         each(step, 1, send_on(0))
         each(step, 0, begin)
+
+        @pl.when(step < tokens // block)
+        def _():
+            rows = pl.ds(pl.multiple_of(step * block, block), block)
+            second_t_ref[:, rows] = second_ref[rows, :].T
+            grad_t_ref[:, rows] = grad_ref[rows, :].T
+
+    @pl.loop(tiles - 2, tiles)
+    def _(tile):
+        all_copies(tile, lambda copy: copy.wait())
 
     half = tokens // 2
     copies = [
@@ -804,26 +988,38 @@
     tiles = width // LANES
     parts = [shard.reshape(rows, tiles, LANES) for shard in (gate_shard, up_shard, down_shard)]
     shard = jnp.transpose(jnp.stack(parts, axis=2), (1, 0, 2, 3)).reshape(tiles, rows, 3 * LANES)
-    narrow = jax.ShapeDtypeStruct((tokens, width), bf16)
+    down_a = (tiles + 1) // 2
+    terms = [
+        jax.ShapeDtypeStruct((2, D // 4, count * LANES), bf16)
+        for count in (tiles + 1, tiles + 1, down_a, down_a)
+        for _ in range(2)
+    ]
     part = jax.ShapeDtypeStruct((tokens // 2, D), f32)
-    return pl.pallas_call(
+    dma = pltpu.SemaphoreType.DMA
+    results = pl.pallas_call(
         functools.partial(feed_forward_kernel, tiles),
-        out_shape=(narrow,) * 3 + (part,) * 4,
+        out_shape=terms + [part] * 4,
         in_specs=[pl.BlockSpec(memory_space=pltpu.VMEM)] * 3,
-        out_specs=[pl.BlockSpec(memory_space=pltpu.VMEM)] * 3 + [pl.BlockSpec(memory_space=pl.ANY)] * 4,
+        out_specs=[pl.BlockSpec(memory_space=pl.ANY)] * 12,
         scratch_shapes=[
             pltpu.VMEM((SLOTS, 2, 2, 2, 2, rows, 3 * LANES), bf16),
             pltpu.VMEM((tokens, D), f32),
             pltpu.VMEM((tokens, D), f32),
-            pltpu.SemaphoreType.DMA((4, SLOTS)),
-            pltpu.SemaphoreType.DMA((4, SLOTS)),
-            pltpu.SemaphoreType.DMA((4,)),
+            pltpu.VMEM((D, tokens), bf16),
+            pltpu.VMEM((D, tokens), bf16),
+            pltpu.VMEM((tokens, 3 * LANES), bf16),
+            pltpu.VMEM((2, 2, 2, D // 4, 3 * LANES), bf16),
+            dma((4, SLOTS)),
+            dma((4, SLOTS)),
+            dma((4,)),
+            dma((2, 6, 2)),
         ],
         compiler_params=pltpu.CompilerParams(
             collective_id=2, has_side_effects=True, vmem_limit_bytes=60 << 20
         ),
         cost_estimate=pl.CostEstimate(flops=0, bytes_accessed=1024, transcendentals=0),
     )(second, grad_result, shard)
+    return list(zip(results[0:8:2], results[1:8:2])), results[8:]
 
 
 def norm_scale(values):
@@ -973,10 +1169,13 @@
     call = functools.partial(per_slot, slots=slots, rows=slot_rows)
     unit = 2 * CORES * rows * HC * LANES * FEATS
     wide = [pltpu.VMEM((CORES * slot_rows, VC), f32)]
-    (state_own,) = call(
-        state_kernel, ins=[k_spec, v_spec], outs=[("state", f32)], scratch=[], flops=4 * unit
-    )(*tables, query_key, values)
-    before = chain(state_own, True)
+    if in_kernel:
+        (before,) = linked(key_term, True, 3)(*tables[1:], query_key, values, slots=slots)
+    else:
+        (state_own,) = call(
+            state_kernel, ins=[k_spec, v_spec], outs=[("state", f32)], scratch=[], flops=4 * unit
+        )(*tables, query_key, values)
+        before = chain(state_own, True)
     mixer, dens = call(
         forward_kernel,
         ins=[q_spec, k_spec, v_spec, "state"],
@@ -987,8 +1186,15 @@
 
     mixer_flat = mixer.reshape(CORES * rows, VC)
     mixer_theirs = swapped(mixer_flat)
-    mixer_own = both_cores(mixer_flat[:rows], mixer_theirs[rows:], 1)
-    mixer_other = both_cores(mixer_flat[rows:], mixer_theirs[:rows], 1)
+
+    def beside(mine, theirs):
+        whole = jnp.zeros((mine.shape[0], CORES * mine.shape[1]), mine.dtype)
+        for index, part in ((core, mine), (other, theirs)):
+            whole = lax.dynamic_update_slice_in_dim(whole, part, index * mine.shape[1], 1)
+        return whole
+
+    mixer_own = beside(mixer_flat[:rows], mixer_theirs[rows:])
+    mixer_other = beside(mixer_flat[rows:], mixer_theirs[:rows])
     after_mixer = inputs + dot(mixer_own, out_full)
     scaled_second, inverse_second = norm_scale(after_mixer)
     second_low = (scaled_second * gain_second[None, :]).astype(bf16)
@@ -1006,7 +1212,7 @@
     grad_result = valid * cotangent.reshape(rows, D).astype(f32)
 
     if in_kernel:
-        hidden, grad_gate, grad_upward, *ffn_parts = feed_forward(
+        ffn_terms, ffn_parts = feed_forward(
             second_chip,
             grad_result_chip,
             rest_shard[:, VC : VC + FC],
@@ -1016,18 +1222,9 @@
         down_own, down_other, second_own, second_other = ffn_parts
         grad_second = second_own + swapped(second_other)
         down_result = down_own + swapped(down_other)
-        down_terms = dot_tn(grad_result_chip, hidden).astype(bf16)
-        gate_terms = dot_tn(second_chip, grad_gate).astype(bf16)
-        up_terms = dot_tn(second_chip, grad_upward).astype(bf16)
-        grad_second, gate_terms, up_terms, down_terms = tied(
-            grad_second, gate_terms, up_terms, down_terms
-        )
-        sum_gate, sum_up = first_exchange(gate_terms, "y"), first_exchange(up_terms, "x")
-        at = 10 * LANES
-        sum_down = (
-            first_exchange(down_terms[:, :at], "y"),
-            first_exchange(down_terms[:, at:], "x"),
-        )
+        (send_gate, keep_gate), (send_up, keep_up), *down_pairs = ffn_terms
+        (send_down_a, keep_down_a), (send_down_b, keep_down_b) = down_pairs
+        got_gate, got_up = exchanged(send_gate, "y", 0), exchanged(send_up, "x", 0)
     else:
         gate = dot(second_chip, gate_full)
         upward = dot(second_chip, up_full)
@@ -1050,25 +1247,38 @@
     )
     grad_after = grad_result + grad_after_norm
     grad_after_low = grad_after.astype(bf16)
-    grad_mixer = dot_nt(grad_after_low, out_full).astype(bf16).reshape(rows, CORES, VC)
-    grad_mixer_chip = jnp.concatenate(
-        [part_of(grad_mixer, 1, core), swapped(part_of(grad_mixer, 1, other))], axis=0
-    )
-    after_columns = grad_after_low.reshape(rows, CORES, VC)
-    grad_after_chip = jnp.concatenate(
-        [part_of(after_columns, 1, core), swapped(part_of(after_columns, 1, other))], axis=0
-    )
-    mixer_chip = jnp.concatenate([mixer_own, mixer_other], axis=0)
+    grad_mixer = dot_nt(grad_after_low, out_full).astype(bf16)
+
+    def core_columns(array):
+        mine, theirs = (
+            lax.dynamic_slice_in_dim(array, index * VC, VC, axis=1) for index in (core, other)
+        )
+        return jnp.concatenate([mine, swapped(theirs)], axis=0)
+
+    grad_mixer_chip = core_columns(grad_mixer)
+    grad_after_chip = core_columns(grad_after_low)
+    mixer_chip = lax.optimization_barrier(jnp.concatenate([mixer_own, mixer_other], axis=0))
 
     wide_spec = (HC * LANES,)
-    pulled, grad_num = call(
-        pull_kernel,
-        ins=[q_spec, v_spec, v_spec, (LANES,)],
-        outs=[("state", f32), (wide_spec, bf16)],
-        scratch=[],
-        flops=4 * unit,
-    )(*tables, query_key, halves(grad_mixer_chip), mixer, dens)
-    from_later = chain(pulled, False)
+    if in_kernel:
+        grad_num, from_later = linked(query_term, False, 4)(
+            *tables[1:],
+            query_key,
+            halves(grad_mixer_chip),
+            mixer,
+            dens,
+            slots=slots,
+            extra=(jax.ShapeDtypeStruct((CORES, slots, slot_rows, HC * LANES), bf16),),
+        )
+    else:
+        pulled, grad_num = call(
+            pull_kernel,
+            ins=[q_spec, v_spec, v_spec, (LANES,)],
+            outs=[("state", f32), (wide_spec, bf16)],
+            scratch=[],
+            flops=4 * unit,
+        )(*tables, query_key, halves(grad_mixer_chip), mixer, dens)
+        from_later = chain(pulled, False)
     grad_query_key, grad_values = call(
         backward_kernel,
         ins=[q_spec, k_spec, v_spec, wide_spec, "state", "state"],
@@ -1077,6 +1287,17 @@
         flops=24 * unit,
     )(*tables, query_key, query_key, values, grad_num, before, from_later)
 
+    if in_kernel:
+        got_gate, got_up, send_down_a, send_down_b, grad_values = tied(
+            got_gate, got_up, send_down_a, send_down_b, grad_values
+        )
+
+        def summed(keep, got):
+            return (keep.astype(f32) + got.astype(f32)).astype(bf16)
+
+        sum_gate, sum_up = summed(keep_gate, got_gate), summed(keep_up, got_up)
+        sum_down_a = summed(keep_down_a, exchanged(send_down_a, "y", 0))
+        sum_down_b = summed(keep_down_b, exchanged(send_down_b, "x", 0))
     head = grad_values[:, :, : KS - 1, :]
     from_chip = passed_along(part_of(head, 0, core), "z", -1)
     from_core = part_of(head, 0, other)
@@ -1107,16 +1328,17 @@
     )
     small_terms = jnp.pad(small_terms, ((0, 0), (0, LANES - (KS + 2)))).astype(bf16)
     if in_kernel:
-        value_terms = dot_tn(normed_chip, grad_pre).astype(bf16)
-        out_terms = dot_tn(mixer_chip, grad_after_chip).astype(bf16)
-        qk_terms = dot_tn(normed_chip, grad_query_key).astype(bf16)
+        empty = jnp.zeros((CORES * rows, LANES), bf16)
+        last_a = jnp.concatenate([grad_pre, grad_query_key, empty], axis=1)
+        last_b = jnp.concatenate([grad_after_chip, empty], axis=1)
         grad_qk_own, grad_value_own, grad_out_own, grad_gu_own, grad_down_own, small_both = reduced(
-            sum_down[0],
+            sum_down_a,
             sum_gate,
-            sum_down[1],
+            sum_down_b,
             sum_up,
-            jnp.concatenate([value_terms, qk_terms[:, :QC]], axis=1),
-            jnp.concatenate([out_terms, qk_terms[:, QC:], small_terms], axis=1),
+            dot_tn(normed_chip, last_a).astype(bf16),
+            dot_tn(mixer_chip, last_b).astype(bf16),
+            jnp.pad(small_terms, ((0, 0), (0, LANES))),
             owned,
         )
         grad_small_own = (small_both[:, :LANES] + small_both[:, LANES:])[:, : KS + 2]

time: 1020 us -> 886 us (0.87)
  matrix products: 109 us -> 45.9 us
  local copies, waits for them, and re-layouts: 119 us -> 58.9 us
  Pallas kernels: 617 us -> 643 us
  other arithmetic: 115 us -> 91.2 us
    dot_general x6 -> x2, matrix products: 72.8 us -> 16.4 us  [dot_tn(): lax.dot_general(a, b, (((0,), (0,)), ((), ())), preferred_element_type=f32)]
    ppermute x6 -> x0, waiting for transfers between devices: 25 us -> none  [chain(): total = total + lax.ppermute(message, 'z', [pair]).astype(f32)]
    ppermute x4, waiting for transfers between devices: 1.95 us -> 25.3 us  [exchanged(): return lax.ppermute(array, axis, [(i, i ^ 1 << bit) for i in range(count)])]
    pallas_call x3, Pallas kernels: 303 us -> 317 us  [the longest x1 274 us: feed_forward(): pl.pallas_call(functools.partial(feed_forward_kernel, tiles), out_shape=t...]
    dynamic_slice x9 -> x7, local copies, waits for them, and re-layouts: 24.8 us -> 11.9 us  [part_of(): return lax.dynamic_index_in_dim(array, index, axis, keepdims=False)]
    concatenate x2 -> x1, local copies, waits for them, and re-layouts: 12.7 us -> 0.01 us  [local(): last_a = jnp.concatenate([grad_pre, grad_query_key, empty], axis=1)]
    squeeze x6 -> x2, local copies, waits for them, and re-layouts: 11.9 us -> 0.03 us  [part_of(): return lax.dynamic_index_in_dim(array, index, axis, keepdims=False)]
    pallas_call x1, Pallas kernels: 192 us -> 203 us  [reduced(): pl.pallas_call(reduce_kernel, out_shape=[jax.ShapeDtypeStruct((owned, wid...]
  transfers between devices with their start and end apart: 24 -> 18, of which waited for: 4 -> 4; matrix products, arithmetic and copies ran while one was open for 21% -> 14% of each run, Pallas kernels for 13% -> 19%
where the time goes in v4:
time: 886 us; the launch traced here: 883 us
  Pallas kernels  643 us (73%)
  other arithmetic  91.2 us (10%)
  local copies, waits for them, and re-layouts  58.9 us (7%)
  matrix products  45.9 us (5%)
  waiting for transfers between devices  26.8 us (3%)
  starting transfers between devices  14.7 us (2%)
    pallas_call x1, Pallas kernels, feed_forward(): pl.pallas_call(functools.partial(feed_forward_kernel, tiles), out_shape=t...  274 us
    pallas_call x1, Pallas kernels, reduced(): pl.pallas_call(reduce_kernel, out_shape=[jax.ShapeDtypeStruct((owned, wid...  203 us
    pallas_call x1, Pallas kernels, gathered_rows(): pl.pallas_call(functools.partial(gather_kernel, tiles), out_shape=jax.Sha...  83.2 us
    pallas_call x2, Pallas kernels, call(): pl.pallas_call(run, out_shape=list(extra) + [state], in_specs=[vmem] * le...  42.7 us
    pallas_call x1, Pallas kernels, local(): call(backward_kernel, ins=[q_spec, k_spec, v_spec, wide_spec, 'state', 's...  28.4 us
    ppermute x4, waiting for transfers between devices, exchanged(): return lax.ppermute(array, axis, [(i, i ^ 1 << bit) for i in range(count)])  25.3 us
    unnamed x172, local copies, waits for them, and re-layouts  23.1 us
    convert_element_type x4, other arithmetic, summed(): return (keep.astype(f32) + got.astype(f32)).astype(bf16)  19.1 us
  transfers between devices with their start and end apart: 18, of which 4 were waited for; matrix products, arithmetic and copies ran while one was open for 14% of the time, Pallas kernels for 19%

profile of v4, /device:TPU:0, one launch (start us, length us, event | category | flops | bytes accessed | tf_op | source)
XLA Modules:
  0.0 882.7 jit_solution(15337695665367648600)
XLA Ops:
  2.8 1.6 constant_dynamic-slice_fusion.12
  5.1 2.7 convert_element_type.146
  7.8 3.1 reshape.279
  10.9 8.0 dynamic-slice_reduce_fusion.1
  19.8 1.3 reshape.281
  21.2 1.9 constant_dynamic-slice_fusion.11
  23.1 1.9 pad_maximum_fusion.13
  28.8 1.5 broadcast_select_fusion.3
  30.4 83.2 %shard_map.374 = bf16[2,2,2,2,112,2176]{5,4,3,2,1,0:T(8,128)(2,1)S(1)} custom-call(bf16[112,2176]{1,0:T(8,128)(2,1)S(1)} %fusion.47.shard_ref), custom_call_target="tpu_custom_call" | custom-call | bytes 1024 | tf_op jit(solution)/shard_map/pallas_call | solution.py:768
  113.6 3.0 copy-done
  116.7 1.9 slice.188
  119.2 2.3 fusion
  121.5 6.5 fusion.38
  128.0 1.8 collective-permute-start.3
  129.8 2.9 convolution_convert_fusion.2
  135.1 17.3 %shard_map.375.before_ref = bf16[2,8,160,128]{3,2,1,0:T(8,128)(2,1)S(1)} custom-call(s32[8,256]{1,0:T(8,128)S(1)} %copy-done.7, f32[8,256]{1,0:T(8,128)S(1)} %copy-done.9, bf16[2,2,256,256]{3,2,1,0:T(8,128)(2,1)S(1)} %bitcast.110, bf16[2,2,256,896]{3,2,1,0:T(8,128)(2,1)S(1)} %add_convert_fusion.4.refs_3_.v_ref), custom_call_target="tpu_custom_call" | custom-call | bytes 1024 | tf_op jit(solution)/shard_map/pallas_call | solution.py:314
  153.2 11.9 %shard_map.376 = (bf16[2,2,256,896]{3,2,1,0:T(8,128)(2,1)}, f32[2,2,256,128]{3,2,1,0:T(8,128)}) custom-call(s32[1]{0:T(128)} %bitcast.1.core_ref, s32[8,256]{1,0:T(8,128)} %constant.171.clone.refs_0_.index_ref, f32[8,256]{1,0:T(8,128)} %constant.172.clone.refs_1_.scale_ref, bf16[2,2,256,256]{3,2,1,0:T(8,128)(2,1)} %bitcast.111, ...), custom_call_target="tpu_custom_call" | custom-call | flops 4294967296 | bytes 8388608 | tf_op jit(solution)/shard_map/pallas_call | solution.py:1179
  165.7 1.6 fusion.78
  167.8 1.5 collective-permute-done.4
  169.3 1.7 slice_dynamic-update-slice_fusion
  171.0 4.8 broadcast_select_fusion.1
  175.9 3.6 multiply_reduce_fusion.3
  179.6 1.6 multiply_convert_fusion.3
  183.0 1.4 copy.108
  184.3 2.1 copy.109
  186.5 1.5 maximum_bitcast_fusion
  188.0 1.4 copy.110
  189.3 4.1 copy.111.shard_ref
  193.4 2.3 pad_maximum_fusion.5
  195.7 2.4 multiply_convert_fusion.grad_ref
  198.2 4.2 pad_maximum_fusion.4.second_ref
  202.4 274.1 %shard_map.377 = (bf16[2,448,2560]{2,1,0:T(8,128)(2,1)}, bf16[2,448,2560]{2,1,0:T(8,128)(2,1)}, bf16[2,448,2560]{2,1,0:T(8,128)(2,1)}, bf16[2,448,2560]{2,1,0:T(...) custom-call(bf16[1024,1792]{1,0:T(8,128)(2,1)} %pad_maximum_fusion.4, ...), custom_call_target="tpu_custom_call" | custom-call | bytes 1024 | tf_op jit(solution)/shard_map/pallas_call | solution.py:999
  477.9 1.4 collective-permute-start.11
  479.3 4.4 collective-permute-start.12
  483.8 5.4 multiply_reduce_fusion
  490.6 7.4 fusion.76
  498.7 3.5 fusion.20
  502.6 5.1 convert_multiply_fusion
  507.7 2.0 pad_maximum_fusion.6
  511.5 25.4 %shard_map.378 = (bf16[2,2,256,1024]{3,2,1,0:T(8,128)(2,1)S(1)}, bf16[2,8,160,128]{3,2,1,0:T(8,128)(2,1)S(1)}) custom-call(s32[8,256]{1,0:T(8,128)S(1)} %copy-done.8, f32[8,256]{1,0:T(8,128)S(1)} %copy-done.10, bf16[2,2,256,256]{3,2,1,0:T(8,128)(2,1)S(1)} %bitcast.115, bf16[2,2,256,896]{3,2,1,0:T(8,128)(2,1)S(1)} %bitcast.109, ...), custom_call_target="tpu_custom_call" | custom-call | bytes 1024 | tf_op jit(solution)/shard_map/pallas_call | solution.py:314
  536.9 1.3 copy-done.11
  539.0 28.4 %shard_map.379 = (bf16[2,2,256,256]{3,2,1,0:T(8,128)(2,1)}, bf16[2,2,256,896]{3,2,1,0:T(8,128)(2,1)}) custom-call(s32[1]{0:T(128)} %bitcast.1.core_ref, s32[8,256]{1,0:T(8,128)} %constant.171.clone.refs_0_.index_ref, f32[8,256]{1,0:T(8,128)} %constant.172.clone.refs_1_.scale_ref, bf16[2,2,256,256]{3,2,1,0:T(8,128)(2,1)} %bitcast.113, ...), custom_call_target="tpu_custom_call" | custom-call | flops 12884901888 | bytes 8388608 | tf_op jit(solution)/shard_map/pallas_call | solution.py:1282
  567.4 11.9 %collective-permute-done.11 = bf16[2,448,2560]{2,1,0:T(8,128)(2,1)} collective-permute-done((bf16[2,448,2560]{2,1,0:T(8,128)(2,1)}, bf16[2,448,2560]{2,1,0:T(8,128)(2,1)}, u32[]{:S(2)}, u32[]{:S(2)}) %collective-permute-start.11) | collective-permute-done | bytes 4587552 | tf_op jit(solution)/shard_map/ppermute | solution.py:388
  579.3 3.7 collective-permute-done.12
  584.0 3.2 fusion.13
  587.2 1.3 collective-permute-start.13
  588.6 1.8 collective-permute-start.16
  590.4 1.2 collective-permute-start.15
  591.6 5.6 add_convert_fusion.up_ref
  597.2 5.7 add_convert_fusion.1.gate_ref
  602.9 6.9 convolution_convert_fusion.1
  612.0 1.8 slice-done.1
  613.8 2.1 fusion.25
  616.8 3.9 fusion.27
  620.7 9.5 %convolution_convert_fusion = bf16[1792,1280]{1,0:T(8,128)(2,1)} fusion(bf16[1024,256]{1,0:T(8,128)(2,1)S(1)} %bitcast.155, bf16[1024,896]{1,0:T(8,128)(2,1)} %bitcast.128, bf16[1280]{0:T(1024)(128)(2,1)S(1)} %pad.23.clone, f32[1792]{0:T(1024)S(1)} %get-tuple-element.160, f32[1024]{0:T(1024)S(1)} %add_rsqrt_fusion, ...), kind=kOutput, calls=%fused_computation.4 | convolution fusion | flops 4720623616 | bytes 10630656 | tf_op jit(solution)/shard_map/dot_general | solution.py:70
  630.3 9.7 %collective-permute-done.16 = bf16[2,448,1280]{2,1,0:T(8,128)(2,1)} collective-permute-done((bf16[2,448,1280]{2,1,0:T(8,128)(2,1)}, bf16[2,448,1280]{2,1,0:T(8,128)(2,1)}, u32[]{:S(2)}, u32[]{:S(2)}) %collective-permute-start.16) | collective-permute-done | bytes 2293792 | tf_op jit(solution)/shard_map/ppermute | solution.py:388
  640.0 4.2 add_convert_fusion.2.down_b_ref
  644.2 3.6 add_convert_fusion.3.down_a_ref
  647.8 6.3 fusion.14
  655.5 202.8 %shard_map.380 = (f32[56,512]{1,0:T(8,128)}, f32[56,1792]{1,0:T(8,128)}, f32[56,1792]{1,0:T(8,128)}, f32[56,9728]{1,0:T(8,128)}, f32[56,4864]{1,0:T(8,128)}, /*index=5*/f32[56,256]{1,0:T(8,128)}) custom-call(bf16[2,448,1280]{2,1,0:T(8,128)(2,1)} %add_convert_fusion.3.down_a_ref, bf16[2,448,2560]{2,1,0:T(8,128)(2,1)} %add_convert_fusion.1.gate_ref, ...), custom_call_target="tpu_custom_call" | custom-call | bytes 1024 | tf_op jit(solution)/shard_map/pallas_call | solution.py:670
  861.3 7.3 multiply_subtract_fusion
  868.7 2.1 multiply_subtract_fusion.1
  875.0 3.1 fusion.10
  880.2 1.3 copy.173
  (276 shorter events, 36.0 us)
Async XLA Ops:
  7.8 11.1 %copy-start.33 = (f32[56,4864]{1,0:T(8,128)S(1)}, f32[56,4864]{1,0:T(8,128)}, u32[]{:S(2)}) copy-start(f32[56,4864]{1,0:T(8,128)} %param.30) | copy-start | bytes 3268612
  18.9 6.6 copy-start.62
  19.8 6.5 copy-start.15
  19.8 7.9 copy-start.42
  23.1 4.7 copy-start.43
  25.1 3.8 collective-permute-start.2
  26.1 2.6 collective-permute-start.1
  26.3 92.9 %collective-permute-start = (bf16[512,1792]{1,0:T(8,128)(2,1)S(1)}, bf16[512,1792]{1,0:T(8,128)(2,1)}, u32[]{:S(2)}, u32[]{:S(2)}) collective-permute-start(bf16[512,1792]{1,0:T(8,128)(2,1)S(1)} %bitcast.116), channel_id=1, source_target_pairs={{0,1},{1,0},{2,3},{3,2},{4,5},{5,4},{6,7},{7,6},{8,9},{9,8},{10,11... | collective-permute-start | bytes 5505032 | tf_op jit(solution)/shard_map/ppermute | solution.py:371
  30.3 83.2 %copy-start.24 = (bf16[56,8192]{1,0:T(8,128)(2,1)}, bf16[56,8192]{1,0:T(8,128)(2,1)S(1)}, u32[]{:S(2)}) copy-start(bf16[56,8192]{1,0:T(8,128)(2,1)S(1)} %get-tuple-element.196) | copy-start | bytes 2752516
  119.0 52.1 %collective-permute-start.5 = (bf16[1792,896]{1,0:T(8,128)(2,1)}, bf16[1792,896]{1,0:T(8,128)(2,1)}, u32[]{:S(2)}, u32[]{:S(2)}) collective-permute-start(bf16[1792,896]{1,0:T(8,128)(2,1)} %slice.188), channel_id=1, source_target_pairs={{0,1},{1,0},{2,3},{3,2},{4,5},{5,4},{6,7},{7,6},{8,9},{9,8},{10,11... | collective-permute-start | bytes 9633800 | tf_op jit(solution)/shard_map/ppermute | solution.py:371
  128.0 4.7 collective-permute-start.3
  135.1 18.2 %copy-start.1 = (bf16[2,2,256,896]{3,2,1,0:T(8,128)(2,1)}, bf16[2,2,256,896]{3,2,1,0:T(8,128)(2,1)S(1)}, u32[]{:S(2)}) copy-start(bf16[2,2,256,896]{3,2,1,0:T(8,128)(2,1)S(1)} %add_convert_fusion.4.refs_3_.v_ref) | copy-start | bytes 5505028
  165.1 4.1 collective-permute-start.4
  165.2 28.2 %collective-permute-start.7 = (bf16[512,1792]{1,0:T(8,128)(2,1)}, bf16[512,1792]{1,0:T(8,128)(2,1)}, u32[]{:S(2)}, u32[]{:S(2)}) collective-permute-start(bf16[512,1792]{1,0:T(8,128)(2,1)} %bitcast.126), channel_id=1, source_target_pairs={{0,1},{1,0},{2,3},{3,2},{4,5},{5,4},{6,7},{7,6},{8,9},{9,8},{10,11... | collective-permute-start | bytes 5505032 | tf_op jit(solution)/shard_map/ppermute | solution.py:371
  171.0 4.8 copy-start.31
  171.0 4.8 copy-start.29
  181.2 17.0 %collective-permute-start.6 = (bf16[512,1792]{1,0:T(8,128)(2,1)}, bf16[512,1792]{1,0:T(8,128)(2,1)}, u32[]{:S(2)}, u32[]{:S(2)}) collective-permute-start(bf16[512,1792]{1,0:T(8,128)(2,1)} %multiply_convert_fusion.3), channel_id=1, source_target_pairs={{0,1},{1,0},{2,3},{3,2},{4,5},{5,4},{6,7},{7,6},{8,9},{9,8},{10,11... | collective-permute-start | bytes 5505032 | tf_op jit(solution)/shard_map/ppermute | solution.py:371
  202.4 275.2 %copy-start.63 = (f32[56,5]{0,1:T(8,128)S(1)}, f32[56,5]{0,1:T(8,128)}, u32[]{:S(2)}) copy-start(f32[56,5]{0,1:T(8,128)} %param.43) | copy-start | bytes 3364
  202.4 275.4 %copy-start.64 = (f32[56,5]{0,1:T(8,128)S(1)}, f32[56,5]{0,1:T(8,128)}, u32[]{:S(2)}) copy-start(f32[56,5]{0,1:T(8,128)} %param.37) | copy-start | bytes 3364
  476.5 7.3 collective-permute-start.9
  476.5 12.6 %collective-permute-start.8 = (f32[512,1792]{1,0:T(8,128)}, f32[512,1792]{1,0:T(8,128)}, u32[]{:S(2)}, u32[]{:S(2)}) collective-permute-start(f32[512,1792]{1,0:T(8,128)} %get-tuple-element.57), channel_id=1, source_target_pairs={{0,1},{1,0},{2,3},{3,2},{4,5},{5,4},{6,7},{7,6},{8,9},{9,8},{10,11... | collective-permute-start | bytes 11010056 | tf_op jit(solution)/shard_map/ppermute | solution.py:371
  477.9 101.4 %collective-permute-start.11 = (bf16[2,448,2560]{2,1,0:T(8,128)(2,1)}, bf16[2,448,2560]{2,1,0:T(8,128)(2,1)}, u32[]{:S(2)}, u32[]{:S(2)}) collective-permute-start(bf16[2,448,2560]{2,1,0:T(8,128)(2,1)} %get-tuple-element.66), channel_id=1, source_target_pairs={{0,16},{16,0},{1,17},{17,1},{2,18},{18,2},{3,19},{19,3},{4,20},{20... | collective-permute-start | bytes 13762568 | tf_op jit(solution)/shard_map/ppermute | solution.py:388
  479.3 103.7 %collective-permute-start.12 = (bf16[2,448,2560]{2,1,0:T(8,128)(2,1)}, bf16[2,448,2560]{2,1,0:T(8,128)(2,1)}, u32[]{:S(2)}, u32[]{:S(2)}) collective-permute-start(bf16[2,448,2560]{2,1,0:T(8,128)(2,1)} %get-tuple-element.67), channel_id=1, source_target_pairs={{0,8},{8,0},{1,9},{9,1},{2,10},{10,2},{3,11},{11,3},{4,12},{12,4},... | collective-permute-start | bytes 13762568 | tf_op jit(solution)/shard_map/ppermute | solution.py:388
  483.7 5.4 copy-start.17
  483.7 6.3 copy-start.22
  483.8 6.8 copy-start.27
  490.6 7.4 copy-start.38
  490.6 8.1 copy-start.40
  502.5 5.3 copy-start.30
  502.5 5.2 copy-start.32
  502.5 8.0 collective-permute-start.10
  510.1 92.8 %collective-permute-start.17 = (bf16[512,896]{1,0:T(8,128)(2,1)S(1)}, bf16[512,896]{1,0:T(8,128)(2,1)}, u32[]{:S(2)}, u32[]{:S(2)}) collective-permute-start(bf16[512,896]{1,0:T(8,128)(2,1)S(1)} %get-tuple-element.183), channel_id=1, source_target_pairs={{0,1},{1,0},{2,3},{3,2},{4,5},{5,4},{6,7},{7,6},{8,9},{9,8},{10,11... | collective-permute-start | bytes 2752520 | tf_op jit(solution)/shard_map/ppermute | solution.py:371
  539.0 45.0 %copy-start.14 = (f32[2,2,258,896]{3,2,1,0:T(8,128)S(1)}, f32[2,2,258,896]{3,2,1,0:T(8,128)}, u32[]{:S(2)}) copy-start(f32[2,2,258,896]{3,2,1,0:T(8,128)} %copy-done.13) | copy-start | bytes 11096068
  583.0 8.6 slice-start.6
  584.0 7.6 slice-start.7
  584.0 13.1 %slice-start.4 = ((s8[4587520]{0:T(1024)(128)(4,1)}), s8[4194304]{0:T(1024)(128)(4,1)S(1)}, s32[]{:S(2)}) async-start(s8[4587520]{0:T(1024)(128)(4,1)} %bitcast.129), calls=%async_computation.4 | async-start | bytes 8388608
  587.2 22.5 %collective-permute-start.13 = (bf16[2,2,896]{2,1,0:T(2,128)(2,1)S(1)}, bf16[2,2,896]{2,1,0:T(2,128)(2,1)S(1)}, u32[]{:S(2)}, u32[]{:S(2)}) collective-permute-start(bf16[2,2,896]{2,1,0:T(2,128)(2,1)S(1)} %dynamic-slice_bitcast_fusion), channel_id=1, source_target_pairs={{2,0},{4,2},{6,4},{3,1},{5,3},{7,5},{10,8},{12,10},{14,12},{11,9},... | collective-permute-start | bytes 21512 | tf_op jit(solution)/shard_map/ppermute | solution.py:360
  588.5 8.6 slice-start.5
  588.6 51.4 %collective-permute-start.16 = (bf16[2,448,1280]{2,1,0:T(8,128)(2,1)}, bf16[2,448,1280]{2,1,0:T(8,128)(2,1)}, u32[]{:S(2)}, u32[]{:S(2)}) collective-permute-start(bf16[2,448,1280]{2,1,0:T(8,128)(2,1)} %get-tuple-element.77), channel_id=1, source_target_pairs={{0,8},{8,0},{1,9},{9,1},{2,10},{10,2},{3,11},{11,3},{4,12},{12,4},... | collective-permute-start | bytes 6881288 | tf_op jit(solution)/shard_map/ppermute | solution.py:388
  590.4 53.8 %collective-permute-start.15 = (bf16[2,448,1280]{2,1,0:T(8,128)(2,1)}, bf16[2,448,1280]{2,1,0:T(8,128)(2,1)}, u32[]{:S(2)}, u32[]{:S(2)}) collective-permute-start(bf16[2,448,1280]{2,1,0:T(8,128)(2,1)} %get-tuple-element.73), channel_id=1, source_target_pairs={{0,16},{16,0},{1,17},{17,1},{2,18},{18,2},{3,19},{19,3},{4,20},{20... | collective-permute-start | bytes 6881288 | tf_op jit(solution)/shard_map/ppermute | solution.py:388
  597.2 5.7 copy-start.36
  602.9 6.9 copy-start.26
  611.3 4.7 copy-start.28
  616.6 31.2 %collective-permute-start.14 = (f32[512,1792]{1,0:T(8,128)S(1)}, f32[512,1792]{1,0:T(8,128)S(1)}, u32[]{:S(2)}, u32[]{:S(2)}) collective-permute-start(f32[512,1792]{1,0:T(8,128)S(1)} %convolution_add_fusion), channel_id=1, source_target_pairs={{0,1},{1,0},{2,3},{3,2},{4,5},{5,4},{6,7},{7,6},{8,9},{9,8},{10,11... | collective-permute-start | bytes 11010056 | tf_op jit(solution)/shard_map/ppermute | solution.py:371
  616.8 31.0 %slice-start.2 = ((s8[7340032]{0:T(1024)(128)(4,1)}), s8[4194304]{0:T(1024)(128)(4,1)S(1)}, s32[]{:S(2)}) async-start(s8[7340032]{0:T(1024)(128)(4,1)} %bitcast.123), calls=%async_computation.2 | async-start | bytes 8388608
  620.7 27.1 %slice-start.3 = ((s8[7340032]{0:T(1024)(128)(4,1)}), s8[3145728]{0:T(1024)(128)(4,1)S(1)}, s32[]{:S(2)}) async-start(s8[7340032]{0:T(1024)(128)(4,1)} %bitcast.123), calls=%async_computation.3 | async-start | bytes 6291456
  630.3 13.9 %copy-start.41 = (bf16[2,448,1280]{2,1,0:T(8,128)(2,1)S(1)}, bf16[2,448,1280]{2,1,0:T(8,128)(2,1)}, u32[]{:S(2)}) copy-start(bf16[2,448,1280]{2,1,0:T(8,128)(2,1)} %get-tuple-element.72) | copy-start | bytes 6881284
  647.8 6.3 copy-start.18
  861.2 7.4 copy-start.34
  861.2 7.4 copy-start.35
  861.2 7.4 copy-start.48
  861.2 7.4 copy-start.49
  861.2 9.6 %copy-start.44 = (f32[56,1792]{1,0:T(8,128)S(1)}, f32[56,1792]{1,0:T(8,128)}, u32[]{:S(2)}) copy-start(f32[56,1792]{1,0:T(8,128)} %param.27) | copy-start | bytes 1204228
  861.3 9.6 %copy-start.47 = (f32[56,1792]{1,0:T(8,128)S(1)}, f32[56,1792]{1,0:T(8,128)}, u32[]{:S(2)}) copy-start(f32[56,1792]{1,0:T(8,128)} %get-tuple-element.243) | copy-start | bytes 1204228
  861.3 9.6 %copy-start.56 = (f32[56,1792]{1,0:T(8,128)S(1)}, f32[56,1792]{1,0:T(8,128)}, u32[]{:S(2)}) copy-start(f32[56,1792]{1,0:T(8,128)} %param.33) | copy-start | bytes 1204228
  861.3 9.6 %copy-start.57 = (f32[56,1792]{1,0:T(8,128)S(1)}, f32[56,1792]{1,0:T(8,128)}, u32[]{:S(2)}) copy-start(f32[56,1792]{1,0:T(8,128)} %param.39) | copy-start | bytes 1204228
  861.3 10.8 %copy-start.58 = (f32[56,1792]{1,0:T(8,128)S(1)}, f32[56,1792]{1,0:T(8,128)}, u32[]{:S(2)}) copy-start(f32[56,1792]{1,0:T(8,128)} %param.34) | copy-start | bytes 1204228
  861.3 10.8 %copy-start.59 = (f32[56,1792]{1,0:T(8,128)S(1)}, f32[56,1792]{1,0:T(8,128)}, u32[]{:S(2)}) copy-start(f32[56,1792]{1,0:T(8,128)} %param.40) | copy-start | bytes 1204228
  861.3 12.0 %copy-start.60 = (f32[56,512]{1,0:T(8,128)S(1)}, f32[56,512]{1,0:T(8,128)}, u32[]{:S(2)}) copy-start(f32[56,512]{1,0:T(8,128)} %param.32) | copy-start | bytes 344068
  861.3 11.9 %copy-start.61 = (f32[56,512]{1,0:T(8,128)S(1)}, f32[56,512]{1,0:T(8,128)}, u32[]{:S(2)}) copy-start(f32[56,512]{1,0:T(8,128)} %param.38) | copy-start | bytes 344068
  868.7 4.6 copy-start.53
  868.7 5.3 copy-start.20
  868.7 5.3 copy-start.21
  874.9 5.2 copy-start.23
  (28 other events, 75.5 us)

commit v5 on v4

--- a/solution.py
+++ b/solution.py
@@ -709,12 +709,16 @@
     pl.semaphore_wait(barrier, len(partners))
 
 
-GATHER_ORDERS = (("z1", "z0", "x", "y"), ("z1", "z0", "y", "x"))
+GATHER_ORDERS = (("z1", "z0", "x", "y"), ("z1", "z0", "y", "x"), ("x", "y", "z1", "z0"))
 
 
 def gather_view(ref, order, stage, y, x, z):
     if stage == 0:
         return ref.at[y, x, z // 2, z % 2]
+    if order == 2:
+        if stage == 1:
+            return ref.at[y, :, z // 2, z % 2]
+        return ref.at[:, :, z // 2, z % 2] if stage == 2 else ref.at[:, :, :, z % 2]
     if stage == 1:
         return ref.at[y, x, :, z % 2]
     if stage == 2:
@@ -783,6 +787,7 @@
 
 
 SLOTS = 10
+ACROSS = 3
 
 
 def feed_forward_kernel(
@@ -790,6 +795,7 @@
     second_ref,
     grad_ref,
     shard_ref,
+    early_ref,
     gate_send_ref,
     gate_keep_ref,
     up_send_ref,
@@ -813,16 +819,45 @@
     recv_sem,
     out_sem,
     terms_sem,
+    early_sem,
 ):
     y, x, z, core = places_of()
+    streamed = shard_ref.shape[0]
+    ready = tiles - streamed
+    paired = streamed - ACROSS
+    before_across = (ready + paired) // 2 - 2
+    count = (tiles + 1) // 2
+
+    def pair_of(turn):
+        within = turn - before_across
+        between = jnp.where(within % 2 == 0, count - 2 + within // 2, before_across + within // 2)
+        return jnp.where(within < 0, turn, between)
+
+    def early_copies(pair):
+        copies = []
+        for at in range(2):
+            for part in range(3):
+                start = (part * ready + 2 * pair + at) * LANES
+                copies.append(
+                    pltpu.make_async_copy(
+                        early_ref.at[:, :, :, :, :, start : start + LANES],
+                        held.at[SLOTS - 2 + at, :, :, :, :, :, part * LANES : (part + 1) * LANES],
+                        early_sem.at[at, part],
+                    )
+                )
+        return copies
+
+    if ready:
+        for copy in early_copies(0):
+            copy.start()
     down_ref[...] = jnp.zeros_like(down_ref)
     grad_second_ref[...] = jnp.zeros_like(grad_second_ref)
     greet(y, x, z, core)
     tokens = second_ref.shape[0]
-    block = 256 if tokens % 256 == 0 else tokens
+    block = 512 if tokens % 512 == 0 else tokens
 
     def transfer(stage, tile, order):
-        slot = tile % SLOTS
+        slot = SLOTS + tile if order == 2 else tile % SLOTS
         view = gather_view(held.at[slot], order, stage, y, x, z)
         return pltpu.make_async_remote_copy(
             src_ref=view,
@@ -833,77 +868,73 @@
             device_id_type=pl.DeviceIdType.MESH,
         )
 
-    down_a = (tiles + 1) // 2
-    down_b = tiles - down_a
-
-    def compute(tile):
-        weights = held.at[tile % SLOTS]
+
+    def compute(slots):
+        def both(part):
+            lanes = slice(part * LANES, (part + 1) * LANES)
+            return jnp.concatenate(
+                [held[slot, :, :, :, :, :, lanes].reshape(D, LANES) for slot in slots], axis=1
+            )
 
         @pl.loop(0, tokens // block)
-        def _(part):
-            rows = pl.ds(pl.multiple_of(part * block, block), block)
-            both = weights[:, :, :, :, :, : 2 * LANES].reshape(D, 2 * LANES)
-            down = weights[:, :, :, :, :, 2 * LANES :].reshape(D, LANES)
-            gate_up = dot(second_ref[rows, :], both)
-            gate, upward = gate_up[:, :LANES], gate_up[:, LANES:]
-            grad_hidden = dot(grad_ref[rows, :], down)
+        def _(at):
+            rows = pl.ds(pl.multiple_of(at * block, block), block)
+            gate = dot(second_ref[rows, :], both(0))
+            upward = dot(second_ref[rows, :], both(1))
+            grad_hidden = dot(grad_ref[rows, :], both(2))
             sigmoid_gate = 1.0 / (1.0 + jnp.exp(-gate))
             silu_gate = gate * sigmoid_gate
-            hidden = (silu_gate * upward).astype(bf16)
-            grad_upward = (grad_hidden * silu_gate).astype(bf16)
-            grad_gate = (
+            narrow[rows, 2 * WIDE :] = (silu_gate * upward).astype(bf16)
+            narrow[rows, WIDE : 2 * WIDE] = (grad_hidden * silu_gate).astype(bf16)
+            narrow[rows, :WIDE] = (
                 grad_hidden * upward * sigmoid_gate * (1.0 + gate * (1.0 - sigmoid_gate))
             ).astype(bf16)
-            grads = jnp.concatenate([grad_gate, grad_upward], axis=1)
-            narrow[rows, : 2 * LANES] = grads
-            narrow[rows, 2 * LANES :] = hidden
-            down_ref[rows, :] += dot_nt(hidden, down)
-            grad_second_ref[rows, :] += dot_nt(grads, both)
-
-    def weight_terms(tile):
-        slot = tile % 2
+            down_ref[rows, :] += dot_nt(narrow[rows, 2 * WIDE :], both(2))
+            grad_second_ref[rows, :] += dot_nt(narrow[rows, :WIDE], both(0)) + dot_nt(
+                narrow[rows, WIDE : 2 * WIDE], both(1)
+            )
+
+    quarter = D // 4
+
+    def weight_terms(turn):
+        slot = turn % 2
 
         @pl.loop(0, 4)
         def _(part):
             rows = pl.ds(pl.multiple_of(part * quarter, quarter), quarter)
-            grads = dot(second_t_ref[rows, :], narrow[:, : 2 * LANES])
-            terms[slot, part // 2, part % 2, :, : 2 * LANES] = grads.astype(bf16)
-            down = dot(grad_t_ref[rows, :], narrow[:, 2 * LANES :])
-            terms[slot, part // 2, part % 2, :, 2 * LANES :] = down.astype(bf16)
-
-    quarter = D // 4
-
-    def terms_copies(tile):
-        slot = tile % 2
-
+            grads = dot(second_t_ref[rows, :], narrow[:, : 2 * WIDE])
+            terms[slot, part // 2, part % 2, :, : 2 * WIDE] = grads.astype(bf16)
+            down = dot(grad_t_ref[rows, :], narrow[:, 2 * WIDE :])
+            terms[slot, part // 2, part % 2, :, 2 * WIDE :] = down.astype(bf16)
+
+    def terms_copies(turn):
+        slot, pair = turn % 2, pair_of(turn)
         gate, up = (gate_send_ref, gate_keep_ref), (up_send_ref, up_keep_ref)
         first, second = (down_a_send_ref, down_a_keep_ref), (down_b_send_ref, down_b_keep_ref)
 
-        def pair(index, stream, refs, at, sem):
+        def apart(index, stream, refs, at):
             here = (y, x)[stream]
-            columns = pl.ds(pl.multiple_of(at * LANES, LANES), LANES)
+            columns = pl.ds(pl.multiple_of(at * WIDE, WIDE), WIDE)
             copies = []
             for way, (place, ref) in enumerate(zip((1 - here, here), refs)):
-                source = terms.at[slot, :, :, :, index * LANES : (index + 1) * LANES]
+                source = terms.at[slot, :, :, :, index * WIDE : (index + 1) * WIDE]
                 source = source.at[place] if stream == 0 else source.at[:, place]
                 copies.append(
-                    pltpu.make_async_copy(source, ref.at[:, :, columns], terms_sem.at[slot, sem, way])
+                    pltpu.make_async_copy(source, ref.at[:, :, columns], terms_sem.at[slot, index, way])
                 )
             return copies
 
-        early = tile < down_a
+        split = (tiles + 1) // 4
+        early = pair < split
         return (
-            (None, pair(0, 0, gate, tile, 0)),
-            (None, pair(1, 1, up, tile, 1)),
-            (early, pair(2, 0, first, jnp.where(early, tile, 0), 2)),
-            (tile >= down_a, pair(2, 1, second, jnp.where(early, 0, tile - down_a), 2)),
-            (tile == tiles - 1, pair(0, 0, gate, tiles, 3)),
-            (tile == tiles - 1, pair(1, 1, up, tiles, 4)),
-            (tile == tiles - 1, pair(2, 1, second, down_b, 5)),
+            (None, apart(0, 0, gate, pair)),
+            (None, apart(1, 1, up, pair)),
+            (early, apart(2, 0, first, jnp.where(early, pair, 0))),
+            (pair >= split, apart(2, 1, second, jnp.where(early, 0, pair - split))),
         )
 
-    def all_copies(tile, act):
-        for condition, copies in terms_copies(tile):
+    def all_copies(turn, act):
+        for condition, copies in terms_copies(turn):
             if condition is None:
                 for copy in copies:
                     act(copy)
@@ -914,13 +945,13 @@
                     for copy in copies:
                         act(copy)
 
-    pairs = (tiles + 1) // 2
+    pairs = paired // 2
 
     def each(step, behind, act):
         for order in range(2):
             tile = 2 * (step - behind) + order
 
-            @pl.when((tile >= 0) & (tile < tiles))
+            @pl.when((tile >= 0) & (tile < paired))
             def _(tile=tile, order=order):
                 act(tile, order)
 
@@ -931,38 +962,91 @@
 
         return act
 
-    def finish(tile, order):
-        transfer(3, tile, order).wait()
-        compute(tile)
-
-        @pl.when(tile >= 2)
+    def work(slots, turn):
+        compute(slots)
+
+        @pl.when(turn >= 2)
         def _():
-            all_copies(tile - 2, lambda copy: copy.wait())
-
-        weight_terms(tile)
-        all_copies(tile, lambda copy: copy.start())
+            all_copies(turn - 2, lambda copy: copy.wait())
+
+        weight_terms(turn)
+        all_copies(turn, lambda copy: copy.start())
 
     def begin(tile, order):
         held[tile % SLOTS, y, x, z // 2, z % 2] = shard_ref[tile]
         transfer(0, tile, order).start()
+
+    def finish(pair):
+        for order in range(2):
+            transfer(3, 2 * pair + order, order).wait()
+        slots = tuple((2 * pair + order) % SLOTS for order in range(2))
+        turn = ready // 2 + pair
+        work(slots, jnp.where(turn >= before_across, 2 * turn - before_across + 1, turn))
+
+    def begin_across(tile):
+        held[SLOTS + tile, y, x, z // 2, z % 2] = shard_ref[paired + tile]
+        transfer(0, tile, 2).start()
+
+    def advance_across(step):
+        for tile in range(ACROSS):
+
+            @pl.when(step == 2 * tile)
+            def _(tile=tile):
+                begin_across(tile)
+
+            for stage in range(4):
+
+                @pl.when(step == 2 * tile + stage + 1)
+                def _(tile=tile, stage=stage):
+                    transfer(stage, tile, 2).wait()
+                    if stage < 3:
+                        transfer(stage + 1, tile, 2).start()
+
+    def on_early(pair):
+        for copy in early_copies(pair):
+            copy.wait()
+        work((SLOTS - 2, SLOTS - 1), jnp.int32(pair))
+        if 2 * pair + 2 < ready:
+            for copy in early_copies(pair + 1):
+                copy.start()
 
     @pl.loop(0, pairs + 4)
     def _(step):
         each(step, 2, send_on(1))
         each(step, 3, send_on(2))
-        each(step, 4, finish)
+        advance_across(step)
+        for pair in range(ready // 2):
+
+            @pl.when(step == 2 + pair)
+            def _(pair=pair):
+                on_early(pair)
+
+
+        @pl.when(step >= 4)
+        def _():
+            finish(step - 4)
+
+        @pl.when(step == pairs + 1)
+        def _():
+            work((SLOTS, SLOTS + 1), jnp.int32(before_across))
+
+        @pl.when(step == pairs + 2)
+        def _():
+            held[2] = jnp.zeros(held.shape[1:], bf16)
+            work((SLOTS + 2, 2), jnp.int32(before_across + 2))
+
         each(step, 1, send_on(0))
         each(step, 0, begin)
 
-        @pl.when(step < tokens // block)
+        @pl.when(step < 2)
         def _():
-            rows = pl.ds(pl.multiple_of(step * block, block), block)
+            rows = pl.ds(pl.multiple_of(step * (tokens // 2), tokens // 2), tokens // 2)
             second_t_ref[:, rows] = second_ref[rows, :].T
             grad_t_ref[:, rows] = grad_ref[rows, :].T
 
-    @pl.loop(tiles - 2, tiles)
-    def _(tile):
-        all_copies(tile, lambda copy: copy.wait())
+    @pl.loop(count - 2, count)
+    def _(turn):
+        all_copies(turn, lambda copy: copy.wait())
 
     half = tokens // 2
     copies = [
@@ -982,12 +1066,15 @@
         copy.wait()
 
 
-def feed_forward(second, grad_result, gate_shard, up_shard, down_shard):
+EARLY = 4
+
+
+def feed_forward(second, grad_result, shards, early):
     tokens = second.shape[0]
-    rows, width = gate_shard.shape
-    tiles = width // LANES
-    parts = [shard.reshape(rows, tiles, LANES) for shard in (gate_shard, up_shard, down_shard)]
-    shard = jnp.transpose(jnp.stack(parts, axis=2), (1, 0, 2, 3)).reshape(tiles, rows, 3 * LANES)
+    rows, streamed = shards[0].shape[0], shards[0].shape[1] // LANES
+    shard = jnp.stack([part.reshape(rows, streamed, LANES) for part in shards], axis=2)
+    shard = jnp.transpose(shard, (1, 0, 2, 3)).reshape(streamed, rows, 3 * LANES)
+    tiles = streamed + early.shape[-1] // (3 * LANES)
     down_a = (tiles + 1) // 2
     terms = [
         jax.ShapeDtypeStruct((2, D // 4, count * LANES), bf16)
@@ -999,26 +1086,27 @@
     results = pl.pallas_call(
         functools.partial(feed_forward_kernel, tiles),
         out_shape=terms + [part] * 4,
-        in_specs=[pl.BlockSpec(memory_space=pltpu.VMEM)] * 3,
+        in_specs=[pl.BlockSpec(memory_space=pltpu.VMEM)] * 3 + [pl.BlockSpec(memory_space=pl.ANY)],
         out_specs=[pl.BlockSpec(memory_space=pl.ANY)] * 12,
         scratch_shapes=[
-            pltpu.VMEM((SLOTS, 2, 2, 2, 2, rows, 3 * LANES), bf16),
+            pltpu.VMEM((SLOTS + ACROSS, 2, 2, 2, 2, rows, 3 * LANES), bf16),
             pltpu.VMEM((tokens, D), f32),
             pltpu.VMEM((tokens, D), f32),
             pltpu.VMEM((D, tokens), bf16),
             pltpu.VMEM((D, tokens), bf16),
-            pltpu.VMEM((tokens, 3 * LANES), bf16),
-            pltpu.VMEM((2, 2, 2, D // 4, 3 * LANES), bf16),
-            dma((4, SLOTS)),
-            dma((4, SLOTS)),
+            pltpu.VMEM((tokens, 3 * WIDE), bf16),
+            pltpu.VMEM((2, 2, 2, D // 4, 3 * WIDE), bf16),
+            dma((4, SLOTS + ACROSS)),
+            dma((4, SLOTS + ACROSS)),
             dma((4,)),
-            dma((2, 6, 2)),
+            dma((2, 3, 2)),
+            dma((2, 3)),
         ],
         compiler_params=pltpu.CompilerParams(
             collective_id=2, has_side_effects=True, vmem_limit_bytes=60 << 20
         ),
         cost_estimate=pl.CostEstimate(flops=0, bytes_accessed=1024, transcendentals=0),
-    )(second, grad_result, shard)
+    )(second, grad_result, shard, early)
     return list(zip(results[0:8:2], results[1:8:2])), results[8:]
 
 
@@ -1115,7 +1203,13 @@
     wide_part = 4 * LANES
     if in_kernel:
         full = gathered_rows(jnp.concatenate([attention_shard, rest_shard[:, :VC]], axis=1))
+        starts, split = (VC, VC + FC, down_at), EARLY * LANES
+        late_shards = [rest_shard[:, start + split : start + FC] for start in starts]
+        early_shard = jnp.concatenate([rest_shard[:, start : start + split] for start in starts], axis=1)
         early, out_half = full[:, :early_width], full[:, early_width:]
+        early_shard, small_full = tied(early_shard, full[:, early_width - LANES : early_width])
+        early_tiles = lax.all_gather(early_shard, ("y", "x", "z"), axis=0)
+        early_tiles = early_tiles.reshape(2, 2, 2, 2, rest_shard.shape[0], -1)
     else:
         early_a = Gather(attention_shard[:, :half], True)
         early_b = Gather(attention_shard[:, half:], False)
@@ -1131,10 +1225,11 @@
         down_a = Gather(last_shard[:, :cut], True)
         down_b = Gather(last_shard[:, cut:], False)
         down_full = jnp.concatenate([down_a.rest(), down_b.rest()], axis=1)
+        small_full = early[:, early_width - LANES :]
 
     qk_full = early[:, : 2 * QC]
     value_full = early[:, 2 * QC : 2 * QC + VC]
-    small_float = early[:, 2 * QC + VC :][:, : KS + 2].astype(f32)
+    small_float = small_full[:, : KS + 2].astype(f32)
     out_full = both_cores(out_half, swapped(out_half), 1)
     gain_first, gain_second = small_float[:, KS], small_float[:, KS + 1]
     taps = [part_of(small_float[:, j].reshape(CORES, VC), 0, core) for j in range(KS)]
@@ -1213,11 +1308,7 @@
 
     if in_kernel:
         ffn_terms, ffn_parts = feed_forward(
-            second_chip,
-            grad_result_chip,
-            rest_shard[:, VC : VC + FC],
-            rest_shard[:, VC + FC : down_at],
-            rest_shard[:, down_at:],
+            second_chip, grad_result_chip, late_shards, early_tiles
         )
         down_own, down_other, second_own, second_other = ffn_parts
         grad_second = second_own + swapped(second_other)

time: 886 us -> 866 us (0.977)
  Pallas kernels: 643 us -> 609 us
  between operations: 2.14 us -> 15.5 us
    pallas_call x1, Pallas kernels: 274 us -> 230 us  [feed_forward(): pl.pallas_call(functools.partial(feed_forward_kernel, tiles), out_shape=t...]
    pallas_call x2, Pallas kernels: 42.7 us -> 54.9 us  [call(): pl.pallas_call(run, out_shape=list(extra) + [state], in_specs=[vmem] * le...]
    unnamed x172 -> x171, local copies, waits for them, and re-layouts: 23.1 us -> 23.3 us
  transfers between devices with their start and end apart: 18 -> 19, of which waited for: 4 -> 5; matrix products, arithmetic and copies ran while one was open for 14% -> 15% of each run, Pallas kernels for 19% -> 21%
where the time goes in v5:
time: 866 us; the launch traced here: 862 us
  Pallas kernels  609 us (70%)
  other arithmetic  93.1 us (11%)
  local copies, waits for them, and re-layouts  59.8 us (7%)
  matrix products  46 us (5%)
  waiting for transfers between devices  30 us (3%)
  between operations  15.5 us (2%)
  starting transfers between devices  9.17 us (1%)
    pallas_call x1, Pallas kernels, feed_forward(): pl.pallas_call(functools.partial(feed_forward_kernel, tiles), out_shape=t...  230 us
    pallas_call x1, Pallas kernels, reduced(): pl.pallas_call(reduce_kernel, out_shape=[jax.ShapeDtypeStruct((owned, wid...  201 us
    pallas_call x1, Pallas kernels, gathered_rows(): pl.pallas_call(functools.partial(gather_kernel, tiles), out_shape=jax.Sha...  83.1 us
    pallas_call x2, Pallas kernels, call(): pl.pallas_call(run, out_shape=list(extra) + [state], in_specs=[vmem] * le...  54.9 us
    pallas_call x1, Pallas kernels, local(): call(backward_kernel, ins=[q_spec, k_spec, v_spec, wide_spec, 'state', 's...  28.4 us
    ppermute x4, waiting for transfers between devices, exchanged(): return lax.ppermute(array, axis, [(i, i ^ 1 << bit) for i in range(count)])  25.3 us
    unnamed x171, local copies, waits for them, and re-layouts  23.3 us
    convert_element_type x4, other arithmetic, summed(): return (keep.astype(f32) + got.astype(f32)).astype(bf16)  19.2 us
  transfers between devices with their start and end apart: 19, of which 5 were waited for; matrix products, arithmetic and copies ran while one was open for 15% of the time, Pallas kernels for 21%

profile of v5, /device:TPU:0, one launch (start us, length us, event | category | flops | bytes accessed | tf_op | source)
XLA Modules:
  0.0 862.3 jit_solution(7914548164812190919)
XLA Ops:
  9.4 1.6 constant_dynamic-slice_fusion.10
  11.6 2.7 convert_element_type.143
  14.4 3.0 reshape.276
  17.4 8.0 dynamic-slice_reduce_fusion.1
  26.3 1.3 reshape.278
  27.6 1.9 constant_dynamic-slice_fusion.13
  29.6 1.9 pad_maximum_fusion.13
  35.3 1.5 broadcast_select_fusion.3
  36.9 83.1 %shard_map.374 = bf16[2,2,2,2,112,2176]{5,4,3,2,1,0:T(8,128)(2,1)S(1)} custom-call(bf16[112,2176]{1,0:T(8,128)(2,1)S(1)} %fusion.54.shard_ref), custom_call_target="tpu_custom_call" | custom-call | bytes 1024 | tf_op jit(solution)/shard_map/pallas_call | solution.py:772
  119.9 3.1 copy-done
  124.0 1.8 fusion.59
  126.8 3.9 slice.201
  130.8 2.3 fusion
  133.1 6.7 fusion.38
  139.8 1.6 collective-permute-start.3
  141.4 2.9 convolution_convert_fusion.2
  146.8 29.5 %shard_map.375.before_ref = bf16[2,8,160,128]{3,2,1,0:T(8,128)(2,1)S(1)} custom-call(s32[8,256]{1,0:T(8,128)S(1)} %copy-done.7, f32[8,256]{1,0:T(8,128)S(1)} %copy-done.9, bf16[2,2,256,256]{3,2,1,0:T(8,128)(2,1)S(1)} %bitcast.108, bf16[2,2,256,896]{3,2,1,0:T(8,128)(2,1)S(1)} %add_convert_fusion.4.refs_3_.v_ref), custom_call_target="tpu_custom_call" | custom-call | bytes 1024 | tf_op jit(solution)/shard_map/pallas_call | solution.py:314
  177.1 11.9 %shard_map.376 = (bf16[2,2,256,896]{3,2,1,0:T(8,128)(2,1)}, f32[2,2,256,128]{3,2,1,0:T(8,128)}) custom-call(s32[1]{0:T(128)} %bitcast.1.core_ref, s32[8,256]{1,0:T(8,128)} %constant.171.clone.refs_0_.index_ref, f32[8,256]{1,0:T(8,128)} %constant.172.clone.refs_1_.scale_ref, bf16[2,2,256,256]{3,2,1,0:T(8,128)(2,1)} %bitcast.109, ...), custom_call_target="tpu_custom_call" | custom-call | flops 4294967296 | bytes 8388608 | tf_op jit(solution)/shard_map/pallas_call | solution.py:1274
  189.5 1.6 fusion.90
  191.6 1.5 collective-permute-done.4
  193.1 1.8 slice_dynamic-update-slice_fusion
  194.9 4.8 broadcast_select_fusion.1
  199.7 3.6 multiply_reduce_fusion.3
  203.4 1.6 multiply_convert_fusion.3
  206.4 1.4 stack_reshape.10
  208.1 1.4 stack_reshape.9
  209.5 1.4 maximum_bitcast_fusion
  210.9 2.3 copy.104
  213.2 1.8 copy.105.shard_ref
  215.0 2.3 pad_maximum_fusion.5
  217.3 2.5 multiply_convert_fusion.grad_ref
  219.8 4.2 pad_maximum_fusion.4.second_ref
  224.0 229.8 %shard_map.377 = (bf16[2,448,2560]{2,1,0:T(8,128)(2,1)}, bf16[2,448,2560]{2,1,0:T(8,128)(2,1)}, bf16[2,448,2560]{2,1,0:T(8,128)(2,1)}, bf16[2,448,2560]{2,1,0:T(...) custom-call(bf16[1024,1792]{1,0:T(8,128)(2,1)} %pad_maximum_fusion.4, ...), custom_call_target="tpu_custom_call" | custom-call | bytes 1024 | tf_op jit(solution)/shard_map/pallas_call | solution.py:1086
  455.3 2.1 collective-permute-start.11
  457.4 3.2 collective-permute-done.9
  460.6 5.4 multiply_reduce_fusion
  467.5 7.0 fusion.88
  475.6 3.5 fusion.20
  479.5 5.1 convert_multiply_fusion
  484.6 2.0 pad_maximum_fusion.6
  488.4 25.5 %shard_map.378 = (bf16[2,2,256,1024]{3,2,1,0:T(8,128)(2,1)S(1)}, bf16[2,8,160,128]{3,2,1,0:T(8,128)(2,1)S(1)}) custom-call(s32[8,256]{1,0:T(8,128)S(1)} %copy-done.8, f32[8,256]{1,0:T(8,128)S(1)} %copy-done.10, bf16[2,2,256,256]{3,2,1,0:T(8,128)(2,1)S(1)} %bitcast.113, bf16[2,2,256,896]{3,2,1,0:T(8,128)(2,1)S(1)} %bitcast.107, ...), custom_call_target="tpu_custom_call" | custom-call | bytes 1024 | tf_op jit(solution)/shard_map/pallas_call | solution.py:314
  513.9 1.3 copy-done.11
  516.1 28.4 %shard_map.379 = (bf16[2,2,256,256]{3,2,1,0:T(8,128)(2,1)}, bf16[2,2,256,896]{3,2,1,0:T(8,128)(2,1)}) custom-call(s32[1]{0:T(128)} %bitcast.1.core_ref, s32[8,256]{1,0:T(8,128)} %constant.171.clone.refs_0_.index_ref, f32[8,256]{1,0:T(8,128)} %constant.172.clone.refs_1_.scale_ref, bf16[2,2,256,256]{3,2,1,0:T(8,128)(2,1)} %bitcast.111, ...), custom_call_target="tpu_custom_call" | custom-call | flops 12884901888 | bytes 8388608 | tf_op jit(solution)/shard_map/pallas_call | solution.py:1373
  544.5 12.5 %collective-permute-done.11 = bf16[2,448,2560]{2,1,0:T(8,128)(2,1)} collective-permute-done((bf16[2,448,2560]{2,1,0:T(8,128)(2,1)}, bf16[2,448,2560]{2,1,0:T(8,128)(2,1)}, u32[]{:S(2)}, u32[]{:S(2)}) %collective-permute-start.11) | collective-permute-done | bytes 4587552 | tf_op jit(solution)/shard_map/ppermute | solution.py:388
  557.0 1.5 collective-permute-done.12
  559.5 3.2 fusion.13
  562.6 1.3 collective-permute-start.13
  565.0 5.6 add_convert_fusion.up_ref
  570.6 5.7 add_convert_fusion.1.gate_ref
  576.4 6.9 convolution_convert_fusion.1
  585.5 1.8 slice-done.1
  587.3 2.1 fusion.25
  590.3 3.9 fusion.27
  594.2 9.5 %convolution_convert_fusion = bf16[1792,1280]{1,0:T(8,128)(2,1)} fusion(bf16[1024,256]{1,0:T(8,128)(2,1)S(1)} %bitcast.151, bf16[1024,896]{1,0:T(8,128)(2,1)} %bitcast.125, bf16[1280]{0:T(1024)(128)(2,1)S(1)} %pad.23.clone, f32[1792]{0:T(1024)S(1)} %get-tuple-element.164, f32[1024]{0:T(1024)S(1)} %add_rsqrt_fusion, ...), kind=kOutput, calls=%fused_computation.4 | convolution fusion | flops 4720623616 | bytes 10630656 | tf_op jit(solution)/shard_map/dot_general | solution.py:70
  603.7 11.3 %collective-permute-done.16 = bf16[2,448,1280]{2,1,0:T(8,128)(2,1)} collective-permute-done((bf16[2,448,1280]{2,1,0:T(8,128)(2,1)}, bf16[2,448,1280]{2,1,0:T(8,128)(2,1)}, u32[]{:S(2)}, u32[]{:S(2)}) %collective-permute-start.16) | collective-permute-done | bytes 2293792 | tf_op jit(solution)/shard_map/ppermute | solution.py:388
  615.0 4.3 add_convert_fusion.2.down_b_ref
  619.3 3.6 add_convert_fusion.3.down_a_ref
  623.0 6.2 fusion.14
  630.6 200.5 %shard_map.380 = (f32[56,512]{1,0:T(8,128)}, f32[56,1792]{1,0:T(8,128)}, f32[56,1792]{1,0:T(8,128)}, f32[56,9728]{1,0:T(8,128)}, f32[56,4864]{1,0:T(8,128)}, /*index=5*/f32[56,256]{1,0:T(8,128)}) custom-call(bf16[2,448,1280]{2,1,0:T(8,128)(2,1)} %add_convert_fusion.3.down_a_ref, bf16[2,448,2560]{2,1,0:T(8,128)(2,1)} %add_convert_fusion.1.gate_ref, ...), custom_call_target="tpu_custom_call" | custom-call | bytes 1024 | tf_op jit(solution)/shard_map/pallas_call | solution.py:670
  834.1 7.3 multiply_subtract_fusion
  841.5 2.1 multiply_subtract_fusion.1
  844.9 1.2 multiply_subtract_fusion.2
  847.7 3.0 fusion.10
  852.9 1.3 copy.167
  (280 shorter events, 37.8 us)
Async XLA Ops:
  7.2 216.8 %all-gather.3.cloned.1.call-start = ((), (), s32[]{:S(2)}) async-start(), calls=%async_computation | async-start | bytes 5849088 | tf_op jit(solution)/shard_map/all_gather | solution.py:1211
  14.3 11.0 %copy-start.33 = (f32[56,4864]{1,0:T(8,128)S(1)}, f32[56,4864]{1,0:T(8,128)}, u32[]{:S(2)}) copy-start(f32[56,4864]{1,0:T(8,128)} %param.30) | copy-start | bytes 3268612
  25.4 6.6 copy-start.62
  26.3 6.5 copy-start.15
  26.3 7.9 copy-start.42
  29.6 4.7 copy-start.43
  31.5 3.8 collective-permute-start.1
  32.6 2.6 collective-permute-start.2
  32.7 98.1 %collective-permute-start = (bf16[512,1792]{1,0:T(8,128)(2,1)S(1)}, bf16[512,1792]{1,0:T(8,128)(2,1)}, u32[]{:S(2)}, u32[]{:S(2)}) collective-permute-start(bf16[512,1792]{1,0:T(8,128)(2,1)S(1)} %bitcast.114), channel_id=1, source_target_pairs={{0,1},{1,0},{2,3},{3,2},{4,5},{5,4},{6,7},{7,6},{8,9},{9,8},{10,11... | collective-permute-start | bytes 5505032 | tf_op jit(solution)/shard_map/ppermute | solution.py:371
  36.8 83.1 %copy-start.21 = (bf16[56,8192]{1,0:T(8,128)(2,1)}, bf16[56,8192]{1,0:T(8,128)(2,1)S(1)}, u32[]{:S(2)}) copy-start(bf16[56,8192]{1,0:T(8,128)(2,1)S(1)} %get-tuple-element.200) | copy-start | bytes 2752516
  130.6 64.2 %collective-permute-start.5 = (bf16[1792,896]{1,0:T(8,128)(2,1)}, bf16[1792,896]{1,0:T(8,128)(2,1)}, u32[]{:S(2)}, u32[]{:S(2)}) collective-permute-start(bf16[1792,896]{1,0:T(8,128)(2,1)} %slice.201), channel_id=1, source_target_pairs={{0,1},{1,0},{2,3},{3,2},{4,5},{5,4},{6,7},{7,6},{8,9},{9,8},{10,11... | collective-permute-start | bytes 9633800 | tf_op jit(solution)/shard_map/ppermute | solution.py:371
  139.8 4.5 collective-permute-start.3
  146.7 30.3 %copy-start.1 = (bf16[2,2,256,896]{3,2,1,0:T(8,128)(2,1)}, bf16[2,2,256,896]{3,2,1,0:T(8,128)(2,1)S(1)}, u32[]{:S(2)}) copy-start(bf16[2,2,256,896]{3,2,1,0:T(8,128)(2,1)S(1)} %add_convert_fusion.4.refs_3_.v_ref) | copy-start | bytes 5505028
  189.0 4.1 collective-permute-start.4
  189.0 26.0 %collective-permute-start.7 = (bf16[512,1792]{1,0:T(8,128)(2,1)}, bf16[512,1792]{1,0:T(8,128)(2,1)}, u32[]{:S(2)}, u32[]{:S(2)}) collective-permute-start(bf16[512,1792]{1,0:T(8,128)(2,1)} %bitcast.123), channel_id=1, source_target_pairs={{0,1},{1,0},{2,3},{3,2},{4,5},{5,4},{6,7},{7,6},{8,9},{9,8},{10,11... | collective-permute-start | bytes 5505032 | tf_op jit(solution)/shard_map/ppermute | solution.py:371
  194.8 4.8 copy-start.31
  194.9 4.8 copy-start.29
  205.0 14.7 %collective-permute-start.6 = (bf16[512,1792]{1,0:T(8,128)(2,1)}, bf16[512,1792]{1,0:T(8,128)(2,1)}, u32[]{:S(2)}, u32[]{:S(2)}) collective-permute-start(bf16[512,1792]{1,0:T(8,128)(2,1)} %multiply_convert_fusion.3), channel_id=1, source_target_pairs={{0,1},{1,0},{2,3},{3,2},{4,5},{5,4},{6,7},{7,6},{8,9},{9,8},{10,11... | collective-permute-start | bytes 5505032 | tf_op jit(solution)/shard_map/ppermute | solution.py:371
  224.0 231.0 %copy-start.63 = (f32[56,5]{0,1:T(8,128)S(1)}, f32[56,5]{0,1:T(8,128)}, u32[]{:S(2)}) copy-start(f32[56,5]{0,1:T(8,128)} %param.43) | copy-start | bytes 3364
  224.0 231.2 %copy-start.64 = (f32[56,5]{0,1:T(8,128)S(1)}, f32[56,5]{0,1:T(8,128)}, u32[]{:S(2)}) copy-start(f32[56,5]{0,1:T(8,128)} %param.37) | copy-start | bytes 3364
  453.8 6.8 collective-permute-start.9
  453.9 12.1 %collective-permute-start.8 = (f32[512,1792]{1,0:T(8,128)}, f32[512,1792]{1,0:T(8,128)}, u32[]{:S(2)}, u32[]{:S(2)}) collective-permute-start(f32[512,1792]{1,0:T(8,128)} %get-tuple-element.61), channel_id=1, source_target_pairs={{0,1},{1,0},{2,3},{3,2},{4,5},{5,4},{6,7},{7,6},{8,9},{9,8},{10,11... | collective-permute-start | bytes 11010056 | tf_op jit(solution)/shard_map/ppermute | solution.py:371
  455.3 101.7 %collective-permute-start.11 = (bf16[2,448,2560]{2,1,0:T(8,128)(2,1)}, bf16[2,448,2560]{2,1,0:T(8,128)(2,1)}, u32[]{:S(2)}, u32[]{:S(2)}) collective-permute-start(bf16[2,448,2560]{2,1,0:T(8,128)(2,1)} %get-tuple-element.70), channel_id=1, source_target_pairs={{0,16},{16,0},{1,17},{17,1},{2,18},{18,2},{3,19},{19,3},{4,20},{20... | collective-permute-start | bytes 13762568 | tf_op jit(solution)/shard_map/ppermute | solution.py:388
  457.4 101.0 %collective-permute-start.12 = (bf16[2,448,2560]{2,1,0:T(8,128)(2,1)}, bf16[2,448,2560]{2,1,0:T(8,128)(2,1)}, u32[]{:S(2)}, u32[]{:S(2)}) collective-permute-start(bf16[2,448,2560]{2,1,0:T(8,128)(2,1)} %get-tuple-element.71), channel_id=1, source_target_pairs={{0,8},{8,0},{1,9},{9,1},{2,10},{10,2},{3,11},{11,3},{4,12},{12,4},... | collective-permute-start | bytes 13762568 | tf_op jit(solution)/shard_map/ppermute | solution.py:388
  460.6 5.4 copy-start.17
  460.6 6.3 copy-start.24
  460.6 6.8 copy-start.27
  467.5 7.0 copy-start.38
  467.5 8.1 copy-start.40
  479.3 5.3 copy-start.30
  479.4 5.3 copy-start.32
  479.4 8.2 collective-permute-start.10
  487.0 89.4 %collective-permute-start.17 = (bf16[512,896]{1,0:T(8,128)(2,1)S(1)}, bf16[512,896]{1,0:T(8,128)(2,1)}, u32[]{:S(2)}, u32[]{:S(2)}) collective-permute-start(bf16[512,896]{1,0:T(8,128)(2,1)S(1)} %get-tuple-element.187), channel_id=1, source_target_pairs={{0,1},{1,0},{2,3},{3,2},{4,5},{5,4},{6,7},{7,6},{8,9},{9,8},{10,11... | collective-permute-start | bytes 2752520 | tf_op jit(solution)/shard_map/ppermute | solution.py:371
  516.0 43.4 %copy-start.14 = (f32[2,2,258,896]{3,2,1,0:T(8,128)S(1)}, f32[2,2,258,896]{3,2,1,0:T(8,128)}, u32[]{:S(2)}) copy-start(f32[2,2,258,896]{3,2,1,0:T(8,128)} %copy-done.13) | copy-start | bytes 11096068
  558.4 6.6 slice-start.6
  559.4 5.6 slice-start.7
  559.4 11.2 %slice-start.4 = ((s8[4587520]{0:T(1024)(128)(4,1)}), s8[4194304]{0:T(1024)(128)(4,1)S(1)}, s32[]{:S(2)}) async-start(s8[4587520]{0:T(1024)(128)(4,1)} %bitcast.128), calls=%async_computation.5 | async-start | bytes 8388608
  562.6 20.6 %collective-permute-start.13 = (bf16[2,2,896]{2,1,0:T(2,128)(2,1)S(1)}, bf16[2,2,896]{2,1,0:T(2,128)(2,1)S(1)}, u32[]{:S(2)}, u32[]{:S(2)}) collective-permute-start(bf16[2,2,896]{2,1,0:T(2,128)(2,1)S(1)} %dynamic-slice_bitcast_fusion), channel_id=1, source_target_pairs={{2,0},{4,2},{6,4},{3,1},{5,3},{7,5},{10,8},{12,10},{14,12},{11,9},... | collective-permute-start | bytes 21512 | tf_op jit(solution)/shard_map/ppermute | solution.py:360
  563.9 6.7 slice-start.5
  564.0 51.0 %collective-permute-start.16 = (bf16[2,448,1280]{2,1,0:T(8,128)(2,1)}, bf16[2,448,1280]{2,1,0:T(8,128)(2,1)}, u32[]{:S(2)}, u32[]{:S(2)}) collective-permute-start(bf16[2,448,1280]{2,1,0:T(8,128)(2,1)} %get-tuple-element.81), channel_id=1, source_target_pairs={{0,8},{8,0},{1,9},{9,1},{2,10},{10,2},{3,11},{11,3},{4,12},{12,4},... | collective-permute-start | bytes 6881288 | tf_op jit(solution)/shard_map/ppermute | solution.py:388
  564.3 55.0 %collective-permute-start.15 = (bf16[2,448,1280]{2,1,0:T(8,128)(2,1)}, bf16[2,448,1280]{2,1,0:T(8,128)(2,1)}, u32[]{:S(2)}, u32[]{:S(2)}) collective-permute-start(bf16[2,448,1280]{2,1,0:T(8,128)(2,1)} %get-tuple-element.77), channel_id=1, source_target_pairs={{0,16},{16,0},{1,17},{17,1},{2,18},{18,2},{3,19},{19,3},{4,20},{20... | collective-permute-start | bytes 6881288 | tf_op jit(solution)/shard_map/ppermute | solution.py:388
  570.6 5.7 copy-start.36
  576.4 6.9 copy-start.26
  584.8 4.7 copy-start.28
  590.1 32.8 %collective-permute-start.14 = (f32[512,1792]{1,0:T(8,128)S(1)}, f32[512,1792]{1,0:T(8,128)S(1)}, u32[]{:S(2)}, u32[]{:S(2)}) collective-permute-start(f32[512,1792]{1,0:T(8,128)S(1)} %convolution_add_fusion), channel_id=1, source_target_pairs={{0,1},{1,0},{2,3},{3,2},{4,5},{5,4},{6,7},{7,6},{8,9},{9,8},{10,11... | collective-permute-start | bytes 11010056 | tf_op jit(solution)/shard_map/ppermute | solution.py:371
  590.3 32.7 %slice-start.2 = ((s8[7340032]{0:T(1024)(128)(4,1)}), s8[4194304]{0:T(1024)(128)(4,1)S(1)}, s32[]{:S(2)}) async-start(s8[7340032]{0:T(1024)(128)(4,1)} %bitcast.121), calls=%async_computation.3 | async-start | bytes 8388608
  594.2 28.7 %slice-start.3 = ((s8[7340032]{0:T(1024)(128)(4,1)}), s8[3145728]{0:T(1024)(128)(4,1)S(1)}, s32[]{:S(2)}) async-start(s8[7340032]{0:T(1024)(128)(4,1)} %bitcast.121), calls=%async_computation.4 | async-start | bytes 6291456
  603.7 15.6 %copy-start.41 = (bf16[2,448,1280]{2,1,0:T(8,128)(2,1)S(1)}, bf16[2,448,1280]{2,1,0:T(8,128)(2,1)}, u32[]{:S(2)}) copy-start(bf16[2,448,1280]{2,1,0:T(8,128)(2,1)} %get-tuple-element.76) | copy-start | bytes 6881284
  622.9 6.3 copy-start.18
  834.0 7.4 copy-start.34
  834.0 7.4 copy-start.35
  834.0 7.4 copy-start.48
  834.0 7.4 copy-start.49
  834.0 9.6 %copy-start.44 = (f32[56,1792]{1,0:T(8,128)S(1)}, f32[56,1792]{1,0:T(8,128)}, u32[]{:S(2)}) copy-start(f32[56,1792]{1,0:T(8,128)} %param.27) | copy-start | bytes 1204228
  834.0 9.6 %copy-start.47 = (f32[56,1792]{1,0:T(8,128)S(1)}, f32[56,1792]{1,0:T(8,128)}, u32[]{:S(2)}) copy-start(f32[56,1792]{1,0:T(8,128)} %get-tuple-element.247) | copy-start | bytes 1204228
  834.0 9.6 %copy-start.56 = (f32[56,1792]{1,0:T(8,128)S(1)}, f32[56,1792]{1,0:T(8,128)}, u32[]{:S(2)}) copy-start(f32[56,1792]{1,0:T(8,128)} %param.33) | copy-start | bytes 1204228
  834.1 9.6 %copy-start.57 = (f32[56,1792]{1,0:T(8,128)S(1)}, f32[56,1792]{1,0:T(8,128)}, u32[]{:S(2)}) copy-start(f32[56,1792]{1,0:T(8,128)} %param.39) | copy-start | bytes 1204228
  834.1 10.8 %copy-start.58 = (f32[56,1792]{1,0:T(8,128)S(1)}, f32[56,1792]{1,0:T(8,128)}, u32[]{:S(2)}) copy-start(f32[56,1792]{1,0:T(8,128)} %param.34) | copy-start | bytes 1204228
  834.1 10.8 %copy-start.59 = (f32[56,1792]{1,0:T(8,128)S(1)}, f32[56,1792]{1,0:T(8,128)}, u32[]{:S(2)}) copy-start(f32[56,1792]{1,0:T(8,128)} %param.40) | copy-start | bytes 1204228
  834.1 12.0 %copy-start.60 = (f32[56,512]{1,0:T(8,128)S(1)}, f32[56,512]{1,0:T(8,128)}, u32[]{:S(2)}) copy-start(f32[56,512]{1,0:T(8,128)} %param.32) | copy-start | bytes 344068
  834.1 12.0 %copy-start.61 = (f32[56,512]{1,0:T(8,128)S(1)}, f32[56,512]{1,0:T(8,128)}, u32[]{:S(2)}) copy-start(f32[56,512]{1,0:T(8,128)} %param.38) | copy-start | bytes 344068
  841.5 5.4 copy-start.20
  841.5 5.3 copy-start.23
  847.7 5.2 copy-start.25
  (29 other events, 80.1 us)
Sparse Core Ops, SparseCore 0:
  126.0 95.1 all-gather.2

commit v6 on v5

--- a/solution.py
+++ b/solution.py
@@ -726,10 +726,70 @@
     return ref.at[y] if order == 0 else ref.at[:, x]
 
 
-def gather_kernel(tiles, shard_ref, full_ref, send_sem, recv_sem):
+ATTENTION = 2 * QC + 2 * VC + LANES
+
+
+def gather_kernel(
+    qk_ref,
+    value_ref,
+    out_ref,
+    gu_ref,
+    down_ref,
+    small_ref,
+    full_ref,
+    late_ref,
+    early_ref,
+    merged,
+    send_sem,
+    recv_sem,
+    core_send_sem,
+    core_recv_sem,
+    own_sem,
+):
     y, x, z, core = places_of()
-    full_ref[y, x, z // 2, z % 2] = shard_ref[...]
-    greet(y, x, z, core)
+    owned = qk_ref.shape[0]
+    greet(y, x, z, core, True)
+
+    at, parts = 0, []
+    for ref, start, width, apart in (
+        (qk_ref, 0, QC, True),
+        (qk_ref, CORES * QC, QC, True),
+        (value_ref, 0, VC, True),
+        (small_ref, 0, LANES, False),
+        (out_ref, 0, VC, True),
+        (gu_ref, 0, FC, True),
+        (gu_ref, FF, FC, True),
+        (down_ref, 0, FC, True),
+    ):
+        parts.append((ref, start, width, apart, at))
+        at += width
+    my_rows = pl.ds(pl.multiple_of(core * owned, 8), owned)
+
+    def copies(index):
+        ref, start, width, apart, at = parts[index]
+
+        def source(which):
+            first = pl.multiple_of(start + (which * width if apart else 0), LANES)
+            return ref.at[:, pl.ds(first, width)]
+
+        target = merged.at[my_rows, at : at + width]
+        remote = pltpu.make_async_remote_copy(
+            src_ref=source(1 - core),
+            dst_ref=target,
+            send_sem=core_send_sem.at[index],
+            recv_sem=core_recv_sem.at[index],
+            device_id=mesh_exchange(y, x, z, core, "core"),
+            device_id_type=pl.DeviceIdType.MESH,
+        )
+        return remote, pltpu.make_async_copy(source(core), target, own_sem.at[index])
+
+    for index in range(len(parts)):
+        for copy in copies(index):
+            copy.start()
+    for index in range(5):
+        for copy in copies(index):
+            copy.wait()
+    full_ref[y, x, z // 2, z % 2] = merged[:, :ATTENTION].astype(bf16)
 
     def transfer(stage, tile, order):
         columns = pl.ds(pl.multiple_of(tile * LANES, LANES), LANES)
@@ -743,47 +803,89 @@
             device_id_type=pl.DeviceIdType.MESH,
         )
 
-    pairs = (tiles + 1) // 2
+    paired = ATTENTION // LANES - ACROSS
+    pairs = paired // 2
 
     def each(step, behind, act):
         for order in range(2):
             tile = 2 * (step - behind) + order
 
-            @pl.when((tile >= 0) & (tile < tiles))
+            @pl.when((tile >= 0) & (tile < paired))
             def _(tile=tile, order=order):
                 act(tile, order)
+
+    def go_on(tile, order, stage):
+        transfer(stage, tile, order).wait()
+        if stage < 3:
+            transfer(stage + 1, tile, order).start()
+
+    hidden = FC // LANES
 
     @pl.loop(0, pairs + 4)
     def _(step):
         each(step, 0, lambda tile, order: transfer(0, tile, order).start())
         for stage in range(4):
-
-            def act(tile, order, stage=stage):
-                transfer(stage, tile, order).wait()
-                if stage < 3:
-                    transfer(stage + 1, tile, order).start()
-
-            each(step, stage + 1, act)
-
-
-def gathered_rows(shard):
-    rows, width = shard.shape
-    tiles = width // LANES
-    full = pl.pallas_call(
-        functools.partial(gather_kernel, tiles),
-        out_shape=jax.ShapeDtypeStruct((2, 2, 2, 2, rows, width), bf16),
-        in_specs=[pl.BlockSpec(memory_space=pltpu.VMEM)],
-        out_specs=pl.BlockSpec(memory_space=pltpu.VMEM),
+            each(step, stage + 1, functools.partial(go_on, stage=stage))
+        for across in range(ACROSS):
+
+            @pl.when(step == 2 * across)
+            def _(across=across):
+                transfer(0, paired + across, 2).start()
+
+            for stage in range(4):
+
+                @pl.when(step == 2 * across + stage + 1)
+                def _(across=across, stage=stage):
+                    go_on(paired + across, 2, stage)
+
+        @pl.when(step == 0)
+        def _():
+            for index in range(5, len(parts)):
+                for copy in copies(index):
+                    copy.wait()
+
+        for tile in range(hidden):
+
+            @pl.when(step == tile // 2)
+            def _(tile=tile):
+                for part in range(3):
+                    first = ATTENTION + part * FC + tile * LANES
+                    block = merged[:, first : first + LANES].astype(bf16)
+                    if tile < EARLY:
+                        start = (part * EARLY + tile) * LANES
+                        early_ref[:, start : start + LANES] = block
+                    else:
+                        late_ref[tile - EARLY, :, part * LANES : (part + 1) * LANES] = block
+
+
+def gathered_weights(w_qk, w_value, w_out, w_gu, w_down, small):
+    owned = w_qk.shape[0]
+    rows, tiles = CORES * owned, ATTENTION // LANES
+    dma = pltpu.SemaphoreType.DMA
+    vmem = pl.BlockSpec(memory_space=pltpu.VMEM)
+    full, late, early = pl.pallas_call(
+        gather_kernel,
+        out_shape=[
+            jax.ShapeDtypeStruct((2, 2, 2, 2, rows, ATTENTION), bf16),
+            jax.ShapeDtypeStruct((FC // LANES - EARLY, rows, 3 * LANES), bf16),
+            jax.ShapeDtypeStruct((rows, 3 * EARLY * LANES), bf16),
+        ],
+        in_specs=[vmem] * 6,
+        out_specs=[vmem] * 3,
         scratch_shapes=[
-            pltpu.SemaphoreType.DMA((4, tiles)),
-            pltpu.SemaphoreType.DMA((4, tiles)),
+            pltpu.VMEM((rows, ATTENTION + 3 * FC), f32),
+            dma((4, tiles)),
+            dma((4, tiles)),
+            dma((8,)),
+            dma((8,)),
+            dma((8,)),
         ],
         compiler_params=pltpu.CompilerParams(
-            collective_id=1, has_side_effects=True, vmem_limit_bytes=40 << 20
+            collective_id=1, has_side_effects=True, vmem_limit_bytes=48 << 20
         ),
         cost_estimate=pl.CostEstimate(flops=0, bytes_accessed=1024, transcendentals=0),
-    )(shard)
-    return full.reshape(D, width)
+    )(w_qk, w_value, w_out, w_gu, w_down, small)
+    return full.reshape(D, ATTENTION), late, early
 
 
 SLOTS = 10
@@ -1069,11 +1171,9 @@
 EARLY = 4
 
 
-def feed_forward(second, grad_result, shards, early):
+def feed_forward(second, grad_result, shard, early):
     tokens = second.shape[0]
-    rows, streamed = shards[0].shape[0], shards[0].shape[1] // LANES
-    shard = jnp.stack([part.reshape(rows, streamed, LANES) for part in shards], axis=2)
-    shard = jnp.transpose(shard, (1, 0, 2, 3)).reshape(streamed, rows, 3 * LANES)
+    streamed, rows, _ = shard.shape
     tiles = streamed + early.shape[-1] // (3 * LANES)
     down_a = (tiles + 1) // 2
     terms = [
@@ -1191,8 +1291,6 @@
         mine = mine if extra is None else jnp.concatenate([mine, extra], axis=1)
         return both_cores(mine, arrived, 0)
 
-    attention_shard = chip_shard((0, 1), small_low)
-    rest_shard = chip_shard((2, 3, 4))
     in_kernel = tuple(lax.axis_size(axis) for axis in ("y", "x", "z")) == (2, 2, 4)
     early_width = 2 * QC + VC + LANES
     half = early_width // 2
@@ -1202,15 +1300,17 @@
     other_tokens = swapped(own_tokens)
     wide_part = 4 * LANES
     if in_kernel:
-        full = gathered_rows(jnp.concatenate([attention_shard, rest_shard[:, :VC]], axis=1))
-        starts, split = (VC, VC + FC, down_at), EARLY * LANES
-        late_shards = [rest_shard[:, start + split : start + FC] for start in starts]
-        early_shard = jnp.concatenate([rest_shard[:, start : start + split] for start in starts], axis=1)
+        small_wide = jnp.pad(small_params, ((0, 0), (0, LANES - (KS + 2))))
+        full, late_shard, early_shard = gathered_weights(
+            w_qk, w_value, w_out, w_gu, w_down, small_wide
+        )
         early, out_half = full[:, :early_width], full[:, early_width:]
-        early_shard, small_full = tied(early_shard, full[:, early_width - LANES : early_width])
+        small_full = early[:, early_width - LANES :]
         early_tiles = lax.all_gather(early_shard, ("y", "x", "z"), axis=0)
-        early_tiles = early_tiles.reshape(2, 2, 2, 2, rest_shard.shape[0], -1)
+        early_tiles = early_tiles.reshape(2, 2, 2, 2, CORES * owned, -1)
     else:
+        attention_shard = chip_shard((0, 1), small_low)
+        rest_shard = chip_shard((2, 3, 4))
         early_a = Gather(attention_shard[:, :half], True)
         early_b = Gather(attention_shard[:, half:], False)
         early = jnp.concatenate([early_a.rest(), early_b.rest()], axis=1)
@@ -1308,7 +1408,7 @@
 
     if in_kernel:
         ffn_terms, ffn_parts = feed_forward(
-            second_chip, grad_result_chip, late_shards, early_tiles
+            second_chip, grad_result_chip, late_shard, early_tiles
         )
         down_own, down_other, second_own, second_other = ffn_parts
         grad_second = second_own + swapped(second_other)

time: 866 us -> 846 us (0.977)
  local copies, waits for them, and re-layouts: 59.8 us -> 43.1 us
  other arithmetic: 93.1 us -> 79.9 us
    dynamic_slice x7 -> x2, local copies, waits for them, and re-layouts: 11.9 us -> 0.05 us  [part_of(): return lax.dynamic_index_in_dim(array, index, axis, keepdims=False)]
    pallas_call x1, Pallas kernels: 230 us -> 239 us  [feed_forward(): pl.pallas_call(functools.partial(feed_forward_kernel, tiles), out_shape=t...]
    unnamed x171 -> x200, local copies, waits for them, and re-layouts: 23.3 us -> 25.6 us
  transfers between devices with their start and end apart: 19 -> 17, of which waited for: 5 -> 5; matrix products, arithmetic and copies ran while one was open for 15% -> 15% of each run, Pallas kernels for 21% -> 21%
where the time goes in v6:
time: 846 us; the launch traced here: 839 us
  Pallas kernels  617 us (73%)
  other arithmetic  79.9 us (9%)
  matrix products  47.9 us (6%)
  local copies, waits for them, and re-layouts  43.1 us (5%)
  waiting for transfers between devices  26.3 us (3%)
  between operations  15.4 us (2%)
  starting transfers between devices  9.29 us (1%)
    pallas_call x1, Pallas kernels, feed_forward(): pl.pallas_call(functools.partial(feed_forward_kernel, tiles), out_shape=t...  239 us
    pallas_call x1, Pallas kernels, reduced(): pl.pallas_call(reduce_kernel, out_shape=[jax.ShapeDtypeStruct((owned, wid...  200 us
    pallas_call x1, Pallas kernels, gathered_weights(): pl.pallas_call(gather_kernel, out_shape=[jax.ShapeDtypeStruct((2, 2, 2, 2...  77.1 us
    pallas_call x2, Pallas kernels, call(): pl.pallas_call(run, out_shape=list(extra) + [state], in_specs=[vmem] * le...  60.5 us
    pallas_call x1, Pallas kernels, local(): call(backward_kernel, ins=[q_spec, k_spec, v_spec, wide_spec, 'state', 's...  28.4 us
    unnamed x200, local copies, waits for them, and re-layouts  25.6 us
    ppermute x4, waiting for transfers between devices, exchanged(): return lax.ppermute(array, axis, [(i, i ^ 1 << bit) for i in range(count)])  25 us
    convert_element_type x4, other arithmetic, summed(): return (keep.astype(f32) + got.astype(f32)).astype(bf16)  19.2 us
  transfers between devices with their start and end apart: 17, of which 5 were waited for; matrix products, arithmetic and copies ran while one was open for 15% of the time, Pallas kernels for 21%

profile of v6, /device:TPU:0, one launch (start us, length us, event | category | flops | bytes accessed | tf_op | source)
XLA Modules:
  0.0 838.6 jit_solution(13432242853307014005)
XLA Ops:
  8.6 1.6 copy-done
  10.2 1.2 copy-done.4
  11.4 1.0 copy-done.8
  12.4 1.0 copy-done.10
  13.4 0.9 copy-done.15
  14.3 77.1 %shard_map.374 = (bf16[2,2,2,2,112,2176]{5,4,3,2,1,0:T(8,128)(2,1)}, bf16[15,112,384]{2,1,0:T(8,128)(2,1)S(1)}, bf16[112,1536]{1,0:T(8,128)(2,1)}) custom-call(f32[56,512]{1,0:T(8,128)S(1)} %copy-done.15, f32[56,1792]{1,0:T(8,128)S(1)} %copy-done.8, f32[56,1792]{1,0:T(8,128)S(1)} %copy-done.10, f32[56,9728]{1,0:T(8,128)S(1)} %copy-done, ...), custom_call_target="tpu_custom_call" | custom-call | bytes 1024 | tf_op jit(solution)/shard_map/pallas_call | solution.py:866
  91.5 1.1 copy-done.12
  92.6 4.0 slice.172
  96.6 1.0 slice.160
  98.1 2.3 fusion
  100.4 6.7 fusion.38
  107.2 1.3 collective-permute-start.1
  108.5 2.9 convolution_convert_fusion.2
  111.9 1.2 add_convert_fusion.4.refs_3_.v_ref
  113.8 35.1 %shard_map.375.before_ref = bf16[2,8,160,128]{3,2,1,0:T(8,128)(2,1)S(1)} custom-call(s32[8,256]{1,0:T(8,128)S(1)} %copy-done.17, f32[8,256]{1,0:T(8,128)S(1)} %copy-done.19, bf16[2,2,256,256]{3,2,1,0:T(8,128)(2,1)S(1)} %bitcast.64, bf16[2,2,256,896]{3,2,1,0:T(8,128)(2,1)S(1)} %add_convert_fusion.4.refs_3_.v_ref), custom_call_target="tpu_custom_call" | custom-call | bytes 1024 | tf_op jit(solution)/shard_map/pallas_call | solution.py:314
  149.7 11.7 %shard_map.376 = (bf16[2,2,256,896]{3,2,1,0:T(8,128)(2,1)}, f32[2,2,256,128]{3,2,1,0:T(8,128)}) custom-call(s32[1]{0:T(128)} %bitcast.1.core_ref, s32[8,256]{1,0:T(8,128)} %constant.143.clone.refs_0_.index_ref, f32[8,256]{1,0:T(8,128)} %constant.144.clone.refs_1_.scale_ref, bf16[2,2,256,256]{3,2,1,0:T(8,128)(2,1)} %bitcast.65, ...), custom_call_target="tpu_custom_call" | custom-call | flops 4294967296 | bytes 8388608 | tf_op jit(solution)/shard_map/pallas_call | solution.py:1374
  161.9 1.6 fusion.74
  164.1 3.5 broadcast_select_fusion.1
  167.6 3.1 slice_dynamic-update-slice_fusion
  170.8 5.4 multiply_reduce_fusion.3
  176.2 3.8 multiply_convert_fusion.3
  180.2 2.3 pad_maximum_fusion.5
  182.5 2.6 multiply_convert_fusion.grad_ref
  185.1 4.1 pad_maximum_fusion.4.second_ref
  189.8 238.5 %shard_map.377 = (bf16[2,448,2560]{2,1,0:T(8,128)(2,1)}, bf16[2,448,2560]{2,1,0:T(8,128)(2,1)}, bf16[2,448,2560]{2,1,0:T(8,128)(2,1)}, bf16[2,448,2560]{2,1,0:T(...) custom-call(bf16[1024,1792]{1,0:T(8,128)(2,1)} %pad_maximum_fusion.4, ...), custom_call_target="tpu_custom_call" | custom-call | bytes 1024 | tf_op jit(solution)/shard_map/pallas_call | solution.py:1186
  432.7 1.4 collective-permute-start.10
  435.1 5.4 multiply_reduce_fusion
  440.9 1.1 copy-done.42
  442.0 6.9 fusion.72
  449.0 1.1 copy-done.46
  450.1 3.5 fusion.20
  454.0 5.2 convert_multiply_fusion
  459.2 2.1 pad_maximum_fusion.6
  463.7 25.5 %shard_map.378 = (bf16[2,2,256,1024]{3,2,1,0:T(8,128)(2,1)S(1)}, bf16[2,8,160,128]{3,2,1,0:T(8,128)(2,1)S(1)}) custom-call(s32[8,256]{1,0:T(8,128)S(1)} %copy-done.18, f32[8,256]{1,0:T(8,128)S(1)} %copy-done.20, bf16[2,2,256,256]{3,2,1,0:T(8,128)(2,1)S(1)} %bitcast.69, bf16[2,2,256,896]{3,2,1,0:T(8,128)(2,1)S(1)} %bitcast.63, ...), custom_call_target="tpu_custom_call" | custom-call | bytes 1024 | tf_op jit(solution)/shard_map/pallas_call | solution.py:314
  489.2 1.3 copy-done.21
  490.5 0.8 copy-done.22
  491.3 28.4 %shard_map.379 = (bf16[2,2,256,256]{3,2,1,0:T(8,128)(2,1)}, bf16[2,2,256,896]{3,2,1,0:T(8,128)(2,1)}) custom-call(s32[1]{0:T(128)} %bitcast.1.core_ref, s32[8,256]{1,0:T(8,128)} %constant.143.clone.refs_0_.index_ref, f32[8,256]{1,0:T(8,128)} %constant.144.clone.refs_1_.scale_ref, bf16[2,2,256,256]{3,2,1,0:T(8,128)(2,1)} %bitcast.67, ...), custom_call_target="tpu_custom_call" | custom-call | flops 12884901888 | bytes 8388608 | tf_op jit(solution)/shard_map/pallas_call | solution.py:1473
  519.7 14.3 %collective-permute-done.10 = bf16[2,448,2560]{2,1,0:T(8,128)(2,1)} collective-permute-done((bf16[2,448,2560]{2,1,0:T(8,128)(2,1)}, bf16[2,448,2560]{2,1,0:T(8,128)(2,1)}, u32[]{:S(2)}, u32[]{:S(2)}) %collective-permute-start.10) | collective-permute-done | bytes 4587552 | tf_op jit(solution)/shard_map/ppermute | solution.py:388
  534.0 1.2 collective-permute-done.9
  535.1 1.0 slice.141
  536.2 3.7 fusion.13
  539.9 1.3 collective-permute-start.11
  542.0 1.7 collective-permute-start.13
  543.7 5.7 add_convert_fusion.up_ref
  549.4 5.7 add_convert_fusion.1.gate_ref
  555.1 6.8 convolution_convert_fusion.1
  562.7 1.2 fusion.17
  564.2 1.9 slice-done.3
  566.2 2.1 fusion.25
  569.2 4.0 fusion.27
  573.2 9.6 %convolution_convert_fusion = bf16[1792,1280]{1,0:T(8,128)(2,1)} fusion(bf16[1024,256]{1,0:T(8,128)(2,1)S(1)} %bitcast.111, bf16[1024,896]{1,0:T(8,128)(2,1)} %bitcast.92, bf16[1280]{0:T(1024)(128)(2,1)S(1)} %copy-done.81, f32[1792]{0:T(1024)S(1)} %copy-done.67, f32[1024]{0:T(1024)S(1)} %copy-done.77, bf16[512,1792]{1,0:T(8,128)(2,1)} %collective-permute-done, ...), kind=kOutput, calls=%fused_computation.4 | convolution fusion | flops 4720623616 | bytes 10630656 | tf_op jit(solution)/shard_map/dot_general | solution.py:70
  582.8 9.5 %collective-permute-done.14 = bf16[2,448,1280]{2,1,0:T(8,128)(2,1)} collective-permute-done((bf16[2,448,1280]{2,1,0:T(8,128)(2,1)}, bf16[2,448,1280]{2,1,0:T(8,128)(2,1)}, u32[]{:S(2)}, u32[]{:S(2)}) %collective-permute-start.14) | collective-permute-done | bytes 2293792 | tf_op jit(solution)/shard_map/ppermute | solution.py:388
  592.3 4.3 add_convert_fusion.2.down_b_ref
  596.6 3.5 add_convert_fusion.3.down_a_ref
  600.2 6.3 fusion.14
  606.9 1.1 pad.42
  608.0 200.5 %shard_map.380 = (f32[56,512]{1,0:T(8,128)}, f32[56,1792]{1,0:T(8,128)}, f32[56,1792]{1,0:T(8,128)}, f32[56,9728]{1,0:T(8,128)}, f32[56,4864]{1,0:T(8,128)}, /*index=5*/f32[56,256]{1,0:T(8,128)}) custom-call(bf16[2,448,1280]{2,1,0:T(8,128)(2,1)} %add_convert_fusion.3.down_a_ref, bf16[2,448,2560]{2,1,0:T(8,128)(2,1)} %add_convert_fusion.1.gate_ref, ...), custom_call_target="tpu_custom_call" | custom-call | bytes 1024 | tf_op jit(solution)/shard_map/pallas_call | solution.py:670
  811.4 6.7 multiply_subtract_fusion
  818.2 2.1 multiply_subtract_fusion.1
  820.4 1.2 multiply_subtract_fusion.3
  821.6 1.2 multiply_subtract_fusion.2
  824.1 3.1 fusion.10
  829.3 1.3 copy.101
  830.6 1.0 copy.102
  (276 shorter events, 23.6 us)
Async XLA Ops:
  7.2 182.6 %all-gather.3.cloned.1.call-start = ((), (), s32[]{:S(2)}) async-start(), calls=%async_computation | async-start | bytes 5849088 | tf_op jit(solution)/shard_map/all_gather | solution.py:1309
  7.2 90.9 %collective-permute-start = (bf16[512,1792]{1,0:T(8,128)(2,1)}, bf16[512,1792]{1,0:T(8,128)(2,1)}, u32[]{:S(2)}, u32[]{:S(2)}) collective-permute-start(bf16[512,1792]{1,0:T(8,128)(2,1)} %bitcast.70), channel_id=1, source_target_pairs={{0,1},{1,0},{2,3},{3,2},{4,5},{5,4},{6,7},{7,6},{8,9},{9,8},{10,11... | collective-permute-start | bytes 5505032 | tf_op jit(solution)/shard_map/ppermute | solution.py:371
  8.5 88.0 %copy-start.59 = (f32[56,5]{1,0:T(8,128)}, f32[56,5]{1,0:T(8,128)S(1)}, u32[]{:S(2)}) copy-start(f32[56,5]{1,0:T(8,128)S(1)} %copy.67) | copy-start | bytes 3364
  92.6 5.6 copy-start.25
  96.5 67.5 %collective-permute-start.3 = (bf16[1792,896]{1,0:T(8,128)(2,1)}, bf16[1792,896]{1,0:T(8,128)(2,1)}, u32[]{:S(2)}, u32[]{:S(2)}) collective-permute-start(bf16[1792,896]{1,0:T(8,128)(2,1)} %slice.172), channel_id=1, source_target_pairs={{0,1},{1,0},{2,3},{3,2},{4,5},{5,4},{6,7},{7,6},{8,9},{9,8},{10,11... | collective-permute-start | bytes 9633800 | tf_op jit(solution)/shard_map/ppermute | solution.py:371
  97.9 10.5 %copy-start.66 = (f32[1792]{0:T(1024)}, f32[1792]{0:T(1024)S(1)}, u32[]{:S(2)}) copy-start(f32[1792]{0:T(1024)S(1)} %get-tuple-element.164) | copy-start | bytes 21508
  98.0 13.8 %copy-start.68 = (f32[896]{0:T(1024)}, f32[896]{0:T(1024)S(1)}, u32[]{:S(2)}) copy-start(f32[896]{0:T(1024)S(1)} %fusion.57) | copy-start | bytes 10756
  98.1 13.8 %copy-start.70 = (f32[896]{0:T(1024)}, f32[896]{0:T(1024)S(1)}, u32[]{:S(2)}) copy-start(f32[896]{0:T(1024)S(1)} %get-tuple-element.205) | copy-start | bytes 10756
  98.1 13.8 %copy-start.72 = (f32[896]{0:T(1024)}, f32[896]{0:T(1024)S(1)}, u32[]{:S(2)}) copy-start(f32[896]{0:T(1024)S(1)} %get-tuple-element.206) | copy-start | bytes 10756
  100.4 353.6 %copy-start.76 = (f32[1024]{0:T(1024)}, f32[1024]{0:T(1024)S(1)}, u32[]{:S(2)}) copy-start(f32[1024]{0:T(1024)S(1)} %add_rsqrt_fusion) | copy-start | bytes 12292
  107.2 4.2 collective-permute-start.1
  113.7 35.9 %copy-start.2 = (bf16[2,2,256,896]{3,2,1,0:T(8,128)(2,1)}, bf16[2,2,256,896]{3,2,1,0:T(8,128)(2,1)S(1)}, u32[]{:S(2)}) copy-start(bf16[2,2,256,896]{3,2,1,0:T(8,128)(2,1)S(1)} %add_convert_fusion.4.refs_3_.v_ref) | copy-start | bytes 5505028
  161.4 6.2 collective-permute-start.2
  161.4 18.8 %collective-permute-start.5 = (bf16[512,1792]{1,0:T(8,128)(2,1)}, bf16[512,1792]{1,0:T(8,128)(2,1)}, u32[]{:S(2)}, u32[]{:S(2)}) collective-permute-start(bf16[512,1792]{1,0:T(8,128)(2,1)} %bitcast.90), channel_id=1, source_target_pairs={{0,1},{1,0},{2,3},{3,2},{4,5},{5,4},{6,7},{7,6},{8,9},{9,8},{10,11... | collective-permute-start | bytes 5505032 | tf_op jit(solution)/shard_map/ppermute | solution.py:371
  167.6 8.6 %copy-start.43 = (bf16[1792,896]{1,0:T(8,128)(2,1)}, bf16[1792,896]{1,0:T(8,128)(2,1)S(1)}, u32[]{:S(2)}) copy-start(bf16[1792,896]{1,0:T(8,128)(2,1)S(1)} %get-tuple-element.181) | copy-start | bytes 9633796
  167.6 8.6 %copy-start.45 = (bf16[1792,896]{1,0:T(8,128)(2,1)}, bf16[1792,896]{1,0:T(8,128)(2,1)S(1)}, u32[]{:S(2)}) copy-start(bf16[1792,896]{1,0:T(8,128)(2,1)S(1)} %get-tuple-element.182) | copy-start | bytes 9633796
  170.7 5.4 copy-start.36
  170.8 5.4 copy-start.38
  180.0 5.1 collective-permute-start.4
  189.8 240.1 %copy-start.82 = (f32[56,5]{0,1:T(8,128)S(1)}, f32[56,5]{0,1:T(8,128)}, u32[]{:S(2)}) copy-start(f32[56,5]{0,1:T(8,128)} %param.43) | copy-start | bytes 3364
  189.8 240.8 %copy-start.83 = (f32[56,5]{0,1:T(8,128)S(1)}, f32[56,5]{0,1:T(8,128)}, u32[]{:S(2)}) copy-start(f32[56,5]{0,1:T(8,128)} %param.37) | copy-start | bytes 3364
  189.8 241.6 %copy-start.78 = (f32[56,5]{0,1:T(8,128)S(1)}, f32[56,5]{0,1:T(8,128)}, u32[]{:S(2)}) copy-start(f32[56,5]{0,1:T(8,128)} %param.31) | copy-start | bytes 3364
  428.3 6.8 collective-permute-start.7
  428.4 12.1 %collective-permute-start.6 = (f32[512,1792]{1,0:T(8,128)}, f32[512,1792]{1,0:T(8,128)}, u32[]{:S(2)}, u32[]{:S(2)}) collective-permute-start(f32[512,1792]{1,0:T(8,128)} %get-tuple-element.63), channel_id=1, source_target_pairs={{0,1},{1,0},{2,3},{3,2},{4,5},{5,4},{6,7},{7,6},{8,9},{9,8},{10,11... | collective-permute-start | bytes 11010056 | tf_op jit(solution)/shard_map/ppermute | solution.py:371
  432.7 101.3 %collective-permute-start.10 = (bf16[2,448,2560]{2,1,0:T(8,128)(2,1)}, bf16[2,448,2560]{2,1,0:T(8,128)(2,1)}, u32[]{:S(2)}, u32[]{:S(2)}) collective-permute-start(bf16[2,448,2560]{2,1,0:T(8,128)(2,1)} %get-tuple-element.73), channel_id=1, source_target_pairs={{0,8},{8,0},{1,9},{9,1},{2,10},{10,2},{3,11},{11,3},{4,12},{12,4},... | collective-permute-start | bytes 13762568 | tf_op jit(solution)/shard_map/ppermute | solution.py:388
  434.1 101.0 %collective-permute-start.9 = (bf16[2,448,2560]{2,1,0:T(8,128)(2,1)}, bf16[2,448,2560]{2,1,0:T(8,128)(2,1)}, u32[]{:S(2)}, u32[]{:S(2)}) collective-permute-start(bf16[2,448,2560]{2,1,0:T(8,128)(2,1)} %get-tuple-element.72), channel_id=1, source_target_pairs={{0,16},{16,0},{1,17},{17,1},{2,18},{18,2},{3,19},{19,3},{4,20},{20... | collective-permute-start | bytes 13762568 | tf_op jit(solution)/shard_map/ppermute | solution.py:388
  435.1 5.8 copy-start.34
  435.1 6.9 copy-start.42
  442.0 7.0 copy-start.44
  442.0 8.1 copy-start.46
  453.9 8.9 %collective-permute-start.8 = (bf16[512,896]{1,0:T(8,128)(2,1)S(1)}, bf16[512,896]{1,0:T(8,128)(2,1)S(1)}, u32[]{:S(2)}, u32[]{:S(2)}) collective-permute-start(bf16[512,896]{1,0:T(8,128)(2,1)S(1)} %get-tuple-element.193), channel_id=1, source_target_pairs={{0,1},{1,0},{2,3},{3,2},{4,5},{5,4},{6,7},{7,6},{8,9},{9,8},{10,11... | collective-permute-start | bytes 2752520 | tf_op jit(solution)/shard_map/ppermute | solution.py:371
  462.2 92.9 %collective-permute-start.15 = (bf16[512,896]{1,0:T(8,128)(2,1)S(1)}, bf16[512,896]{1,0:T(8,128)(2,1)}, u32[]{:S(2)}, u32[]{:S(2)}) collective-permute-start(bf16[512,896]{1,0:T(8,128)(2,1)S(1)} %get-tuple-element.185), channel_id=1, source_target_pairs={{0,1},{1,0},{2,3},{3,2},{4,5},{5,4},{6,7},{7,6},{8,9},{9,8},{10,11... | collective-permute-start | bytes 2752520 | tf_op jit(solution)/shard_map/ppermute | solution.py:371
  491.3 44.8 %copy-start.24 = (f32[2,2,258,896]{3,2,1,0:T(8,128)S(1)}, f32[2,2,258,896]{3,2,1,0:T(8,128)}, u32[]{:S(2)}) copy-start(f32[2,2,258,896]{3,2,1,0:T(8,128)} %copy-done.23) | copy-start | bytes 11096068
  535.1 8.6 %slice-start.6 = ((s8[4587520]{0:T(1024)(128)(4,1)}), s8[4194304]{0:T(1024)(128)(4,1)S(1)}, s32[]{:S(2)}) async-start(s8[4587520]{0:T(1024)(128)(4,1)} %bitcast.96), calls=%async_computation.7 | async-start | bytes 8388608
  536.1 7.6 slice-start.7
  536.1 13.2 %slice-start.4 = ((s8[4587520]{0:T(1024)(128)(4,1)}), s8[4194304]{0:T(1024)(128)(4,1)S(1)}, s32[]{:S(2)}) async-start(s8[4587520]{0:T(1024)(128)(4,1)} %bitcast.94), calls=%async_computation.5 | async-start | bytes 8388608
  539.9 22.1 %collective-permute-start.11 = (bf16[2,2,896]{2,1,0:T(2,128)(2,1)S(1)}, bf16[2,2,896]{2,1,0:T(2,128)(2,1)S(1)}, u32[]{:S(2)}, u32[]{:S(2)}) collective-permute-start(bf16[2,2,896]{2,1,0:T(2,128)(2,1)S(1)} %dynamic-slice_bitcast_fusion), channel_id=1, source_target_pairs={{2,0},{4,2},{6,4},{3,1},{5,3},{7,5},{10,8},{12,10},{14,12},{11,9},... | collective-permute-start | bytes 21512 | tf_op jit(solution)/shard_map/ppermute | solution.py:360
  541.2 8.2 slice-start.5
  541.2 51.0 %collective-permute-start.14 = (bf16[2,448,1280]{2,1,0:T(8,128)(2,1)}, bf16[2,448,1280]{2,1,0:T(8,128)(2,1)}, u32[]{:S(2)}, u32[]{:S(2)}) collective-permute-start(bf16[2,448,1280]{2,1,0:T(8,128)(2,1)} %get-tuple-element.83), channel_id=1, source_target_pairs={{0,8},{8,0},{1,9},{9,1},{2,10},{10,2},{3,11},{11,3},{4,12},{12,4},... | collective-permute-start | bytes 6881288 | tf_op jit(solution)/shard_map/ppermute | solution.py:388
  542.0 54.6 %collective-permute-start.13 = (bf16[2,448,1280]{2,1,0:T(8,128)(2,1)}, bf16[2,448,1280]{2,1,0:T(8,128)(2,1)}, u32[]{:S(2)}, u32[]{:S(2)}) collective-permute-start(bf16[2,448,1280]{2,1,0:T(8,128)(2,1)} %get-tuple-element.79), channel_id=1, source_target_pairs={{0,16},{16,0},{1,17},{17,1},{2,18},{18,2},{3,19},{19,3},{4,20},{20... | collective-permute-start | bytes 6881288 | tf_op jit(solution)/shard_map/ppermute | solution.py:388
  549.4 5.7 copy-start.41
  555.1 6.9 copy-start.33
  569.0 31.2 %collective-permute-start.12 = (f32[512,1792]{1,0:T(8,128)S(1)}, f32[512,1792]{1,0:T(8,128)S(1)}, u32[]{:S(2)}, u32[]{:S(2)}) collective-permute-start(f32[512,1792]{1,0:T(8,128)S(1)} %convolution_add_fusion), channel_id=1, source_target_pairs={{0,1},{1,0},{2,3},{3,2},{4,5},{5,4},{6,7},{7,6},{8,9},{9,8},{10,11... | collective-permute-start | bytes 11010056 | tf_op jit(solution)/shard_map/ppermute | solution.py:371
  569.2 31.0 %slice-start = ((s8[7340032]{0:T(1024)(128)(4,1)}), s8[4194304]{0:T(1024)(128)(4,1)S(1)}, s32[]{:S(2)}) async-start(s8[7340032]{0:T(1024)(128)(4,1)} %bitcast.77), calls=%async_computation.1 | async-start | bytes 8388608
  573.2 27.0 %slice-start.1 = ((s8[7340032]{0:T(1024)(128)(4,1)}), s8[3145728]{0:T(1024)(128)(4,1)S(1)}, s32[]{:S(2)}) async-start(s8[7340032]{0:T(1024)(128)(4,1)} %bitcast.77), calls=%async_computation.2 | async-start | bytes 6291456
  582.8 13.9 %copy-start.47 = (bf16[2,448,1280]{2,1,0:T(8,128)(2,1)S(1)}, bf16[2,448,1280]{2,1,0:T(8,128)(2,1)}, u32[]{:S(2)}) copy-start(bf16[2,448,1280]{2,1,0:T(8,128)(2,1)} %get-tuple-element.78) | copy-start | bytes 6881284
  600.2 6.3 copy-start.27
  600.2 6.3 copy-start.74
  607.9 201.3 %copy-start.61 = (f32[56,5]{1,0:T(8,128)S(1)}, f32[56,5]{1,0:T(8,128)}, u32[]{:S(2)}) copy-start(f32[56,5]{1,0:T(8,128)} %copy.72) | copy-start | bytes 3364
  607.9 202.0 %copy-start.60 = (f32[56,5]{1,0:T(8,128)S(1)}, f32[56,5]{1,0:T(8,128)}, u32[]{:S(2)}) copy-start(f32[56,5]{1,0:T(8,128)} %copy-done.59) | copy-start | bytes 3364
  607.9 202.0 %copy-start.62 = (f32[56,5]{1,0:T(8,128)S(1)}, f32[56,5]{1,0:T(8,128)}, u32[]{:S(2)}) copy-start(f32[56,5]{1,0:T(8,128)} %copy.71) | copy-start | bytes 3364
  607.9 202.0 %copy-start.63 = (f32[56,5]{1,0:T(8,128)S(1)}, f32[56,5]{1,0:T(8,128)}, u32[]{:S(2)}) copy-start(f32[56,5]{1,0:T(8,128)} %copy.74) | copy-start | bytes 3364
  607.9 203.4 %copy-start.1 = (f32[56,9728]{1,0:T(8,128)S(1)}, f32[56,9728]{1,0:T(8,128)}, u32[]{:S(2)}) copy-start(f32[56,9728]{1,0:T(8,128)} %gu_ref.1) | copy-start | bytes 6537220
  811.3 6.8 copy-start.5
  811.3 6.8 copy-start.40
  811.3 6.8 copy-start.50
  811.3 6.8 copy-start.51
  811.3 9.0 %copy-start.49 = (f32[56,1792]{1,0:T(8,128)S(1)}, f32[56,1792]{1,0:T(8,128)}, u32[]{:S(2)}) copy-start(f32[56,1792]{1,0:T(8,128)} %get-tuple-element.230) | copy-start | bytes 1204228
  811.3 9.0 %copy-start.55 = (f32[56,1792]{1,0:T(8,128)S(1)}, f32[56,1792]{1,0:T(8,128)}, u32[]{:S(2)}) copy-start(f32[56,1792]{1,0:T(8,128)} %param.33) | copy-start | bytes 1204228
  811.3 9.0 %copy-start.56 = (f32[56,1792]{1,0:T(8,128)S(1)}, f32[56,1792]{1,0:T(8,128)}, u32[]{:S(2)}) copy-start(f32[56,1792]{1,0:T(8,128)} %param.39) | copy-start | bytes 1204228
  811.4 10.2 %copy-start.58 = (f32[56,1792]{1,0:T(8,128)S(1)}, f32[56,1792]{1,0:T(8,128)}, u32[]{:S(2)}) copy-start(f32[56,1792]{1,0:T(8,128)} %param.40) | copy-start | bytes 1204228
  811.4 12.2 %copy-start.30 = (f32[512,1792]{1,0:T(8,128)S(1)}, f32[512,1792]{1,0:T(8,128)}, u32[]{:S(2)}) copy-start(f32[512,1792]{1,0:T(8,128)} %get-tuple-element.178) | copy-start | bytes 11010052
  818.1 5.4 copy-start.28
  818.1 5.4 copy-start.29
  (46 other events, 116.0 us)
Sparse Core Ops, SparseCore 0:
  92.7 97.0 all-gather.2

commit v7 on v6

--- a/solution.py
+++ b/solution.py
@@ -506,6 +506,7 @@
     got_quarters,
     send_sem,
     recv_sem,
+    load_sem,
 ):
     y, x, z, core = places_of()
     places = {"y": y, "x": x, "z0": z % 2, "z1": z // 2}
@@ -571,7 +572,7 @@
     def source_of(stream, stage, chunk):
         there = 1 - places[ORDERS[stream][stage]]
         if stage == 1:
-            return sums.at[stream, chunk % 2, there]
+            return sums.at[stream, chunk % 4, there]
         if stage == 2:
             return halves.at[stream, chunk % 2, :, there]
         return quarters.at[stream, chunk % 2, there]
@@ -579,7 +580,20 @@
     def add(a, b):
         return a.astype(f32) + b.astype(f32)
 
+    def load(stream, chunk, ref, start):
+        slot = chunk % 4
+        return pltpu.make_async_copy(
+            ref.at[:, :, wide_columns(chunk - start)], sums.at[stream, slot], load_sem.at[stream, slot]
+        )
+
     def begin(stream, chunk):
+        for ref, summed, start, stop in parts[stream]:
+            if summed:
+
+                @pl.when((chunk >= start) & (chunk < stop))
+                def _(ref=ref, start=start):
+                    load(stream, chunk, ref, start).start()
+
         for ref, _, start, stop in parts[stream][2:]:
 
             @pl.when((chunk >= start) & (chunk < stop))
@@ -594,12 +608,12 @@
             def _(ref=ref, summed=summed, start=start):
                 tile = chunk - start
                 if summed:
-                    sums[stream, chunk % 2] = ref[:, :, wide_columns(tile)]
+                    load(stream, chunk, ref, start).wait()
                 else:
                     there = 1 - places[ORDERS[stream][0]]
                     transfer(stream, 0, chunk, first_view(stream, ref, tile, there)).wait()
                     own = first_view(stream, ref, tile, places[ORDERS[stream][0]])[...]
-                    sums[stream, chunk % 2] = add(own, got_terms[stream, chunk % 4]).astype(bf16)
+                    sums[stream, chunk % 4] = add(own, got_terms[stream, chunk % 4]).astype(bf16)
 
         transfer(stream, 1, chunk, source_of(stream, 1, chunk)).start()
 
@@ -608,7 +622,7 @@
         slot, landing = chunk % 2, chunk % 4
         transfer(stream, stage, chunk, source_of(stream, stage, chunk)).wait()
         if stage == 1:
-            total = add(sums[stream, slot, here], got_sums[stream, landing]).astype(bf16)
+            total = add(sums[stream, landing, here], got_sums[stream, landing]).astype(bf16)
             halves[stream, slot] = total.reshape(halves.shape[2:])
         elif stage == 2:
             own = halves[stream, slot, :, here]
@@ -670,10 +684,11 @@
     return pl.pallas_call(
         reduce_kernel,
         out_shape=[jax.ShapeDtypeStruct((owned, width), f32) for width in widths],
-        in_specs=[pl.BlockSpec(memory_space=pltpu.VMEM)] * 7,
+        in_specs=[pl.BlockSpec(memory_space=pl.ANY)] * 4
+        + [pl.BlockSpec(memory_space=pltpu.VMEM)] * 3,
         out_specs=[pl.BlockSpec(memory_space=pltpu.VMEM)] * 6,
         scratch_shapes=[
-            pltpu.VMEM((2, 2, 2, block, WIDE), bf16),
+            pltpu.VMEM((2, 4, 2, block, WIDE), bf16),
             pltpu.VMEM((2, 2, 2, 2, rows, WIDE), bf16),
             pltpu.VMEM((2, 2, 2, rows, WIDE), bf16),
             pltpu.VMEM((2, 2, CORES, owned, WIDE), f32),
@@ -683,6 +698,7 @@
             pltpu.VMEM((2, 4, rows, WIDE), bf16),
             dma((2, 6, 4)),
             dma((2, 6, 4)),
+            dma((2, 4)),
         ],
         compiler_params=pltpu.CompilerParams(
             collective_id=0, has_side_effects=True, vmem_limit_bytes=56 << 20
@@ -1078,12 +1094,18 @@
         held[tile % SLOTS, y, x, z // 2, z % 2] = shard_ref[tile]
         transfer(0, tile, order).start()
 
-    def finish(pair):
-        for order in range(2):
-            transfer(3, 2 * pair + order, order).wait()
-        slots = tuple((2 * pair + order) % SLOTS for order in range(2))
-        turn = ready // 2 + pair
-        work(slots, jnp.where(turn >= before_across, 2 * turn - before_across + 1, turn))
+    def work_of(step, across):
+        late, first = step - 4, step == pairs + 1
+        turn = ready // 2 + late
+        turn = jnp.where(turn >= before_across, 2 * turn - before_across + 1, turn)
+        turn = jnp.where(step < 4, step - 4 + ready // 2, turn)
+        slots = [
+            jnp.where(step < 4, SLOTS - 2 + order, (2 * late + order + 2 * SLOTS) % SLOTS)
+            for order in range(2)
+        ]
+        others = (jnp.where(first, SLOTS, SLOTS + 2), jnp.where(first, SLOTS + 1, 2))
+        slots = [jnp.where(across == 1, there, here) for here, there in zip(slots, others)]
+        return slots, jnp.where(across == 1, before_across + 2 * (step - pairs - 1), turn)
 
     def begin_across(tile):
         held[SLOTS + tile, y, x, z // 2, z % 2] = shard_ref[paired + tile]
@@ -1103,14 +1125,6 @@
                     transfer(stage, tile, 2).wait()
                     if stage < 3:
                         transfer(stage + 1, tile, 2).start()
-
-    def on_early(pair):
-        for copy in early_copies(pair):
-            copy.wait()
-        work((SLOTS - 2, SLOTS - 1), jnp.int32(pair))
-        if 2 * pair + 2 < ready:
-            for copy in early_copies(pair + 1):
-                copy.start()
 
     @pl.loop(0, pairs + 4)
     def _(step):
@@ -1119,23 +1133,35 @@
         advance_across(step)
         for pair in range(ready // 2):
 
-            @pl.when(step == 2 + pair)
+            @pl.when(step == 4 - ready // 2 + pair)
             def _(pair=pair):
-                on_early(pair)
-
+                for copy in early_copies(pair):
+                    copy.wait()
 
         @pl.when(step >= 4)
         def _():
-            finish(step - 4)
-
-        @pl.when(step == pairs + 1)
-        def _():
-            work((SLOTS, SLOTS + 1), jnp.int32(before_across))
+            for order in range(2):
+                transfer(3, 2 * (step - 4) + order, order).wait()
 
         @pl.when(step == pairs + 2)
         def _():
             held[2] = jnp.zeros(held.shape[1:], bf16)
-            work((SLOTS + 2, 2), jnp.int32(before_across + 2))
+
+        works = jnp.where((step == pairs + 1) | (step == pairs + 2), 2, 1)
+
+        @pl.loop(0, 2)
+        def _(across):
+            @pl.when((step >= 4 - ready // 2) & (across < works))
+            def _():
+                slots, turn = work_of(step, across)
+                work(slots, turn)
+
+        for pair in range(ready // 2 - 1):
+
+            @pl.when(step == 4 - ready // 2 + pair)
+            def _(pair=pair):
+                for copy in early_copies(pair + 1):
+                    copy.start()
 
         each(step, 1, send_on(0))
         each(step, 0, begin)

time: 846 us -> 831 us (0.982)
  Pallas kernels: 617 us -> 603 us
    pallas_call x1, Pallas kernels: 239 us -> 227 us  [feed_forward(): pl.pallas_call(functools.partial(feed_forward_kernel, tiles), out_shape=t...]
  transfers between devices with their start and end apart: 17 -> 17, of which waited for: 5 -> 5; matrix products, arithmetic and copies ran while one was open for 15% -> 15% of each run, Pallas kernels for 21% -> 22%
where the time goes in v7:
time: 831 us; the launch traced here: 824 us
  Pallas kernels  603 us (73%)
  other arithmetic  79.9 us (10%)
  matrix products  47.9 us (6%)
  local copies, waits for them, and re-layouts  43.1 us (5%)
  waiting for transfers between devices  25.7 us (3%)
  between operations  15.5 us (2%)
  starting transfers between devices  9.26 us (1%)
    pallas_call x1, Pallas kernels, feed_forward(): pl.pallas_call(functools.partial(feed_forward_kernel, tiles), out_shape=t...  227 us
    pallas_call x1, Pallas kernels, reduced(): pl.pallas_call(reduce_kernel, out_shape=[jax.ShapeDtypeStruct((owned, wid...  198 us
    pallas_call x1, Pallas kernels, gathered_weights(): pl.pallas_call(gather_kernel, out_shape=[jax.ShapeDtypeStruct((2, 2, 2, 2...  77.1 us
    pallas_call x2, Pallas kernels, call(): pl.pallas_call(run, out_shape=list(extra) + [state], in_specs=[vmem] * le...  60.7 us
    pallas_call x1, Pallas kernels, local(): call(backward_kernel, ins=[q_spec, k_spec, v_spec, wide_spec, 'state', 's...  28 us
    unnamed x200, local copies, waits for them, and re-layouts  25.6 us
    ppermute x4, waiting for transfers between devices, exchanged(): return lax.ppermute(array, axis, [(i, i ^ 1 << bit) for i in range(count)])  24.6 us
    convert_element_type x4, other arithmetic, summed(): return (keep.astype(f32) + got.astype(f32)).astype(bf16)  19.2 us
  transfers between devices with their start and end apart: 17, of which 5 were waited for; matrix products, arithmetic and copies ran while one was open for 15% of the time, Pallas kernels for 22%

profile of v7, /device:TPU:0, one launch (start us, length us, event | category | flops | bytes accessed | tf_op | source)
XLA Modules:
  0.0 824.2 jit_solution(8181553067700253506)
XLA Ops:
  8.6 1.6 copy-done
  10.2 1.2 copy-done.4
  11.4 1.0 copy-done.8
  12.4 1.0 copy-done.10
  13.4 0.9 copy-done.15
  14.3 77.1 %shard_map.374 = (bf16[2,2,2,2,112,2176]{5,4,3,2,1,0:T(8,128)(2,1)}, bf16[15,112,384]{2,1,0:T(8,128)(2,1)S(1)}, bf16[112,1536]{1,0:T(8,128)(2,1)}) custom-call(f32[56,512]{1,0:T(8,128)S(1)} %copy-done.15, f32[56,1792]{1,0:T(8,128)S(1)} %copy-done.8, f32[56,1792]{1,0:T(8,128)S(1)} %copy-done.10, f32[56,9728]{1,0:T(8,128)S(1)} %copy-done, ...), custom_call_target="tpu_custom_call" | custom-call | bytes 1024 | tf_op jit(solution)/shard_map/pallas_call | solution.py:882
  91.5 1.1 copy-done.12
  92.6 4.0 slice.172
  96.6 1.0 slice.160
  98.1 2.3 fusion
  100.4 6.7 fusion.38
  107.2 1.3 collective-permute-start.1
  108.5 2.9 convolution_convert_fusion.2
  111.9 1.2 add_convert_fusion.4.refs_3_.v_ref
  113.8 34.8 %shard_map.375.before_ref = bf16[2,8,160,128]{3,2,1,0:T(8,128)(2,1)S(1)} custom-call(s32[8,256]{1,0:T(8,128)S(1)} %copy-done.17, f32[8,256]{1,0:T(8,128)S(1)} %copy-done.19, bf16[2,2,256,256]{3,2,1,0:T(8,128)(2,1)S(1)} %bitcast.64, bf16[2,2,256,896]{3,2,1,0:T(8,128)(2,1)S(1)} %add_convert_fusion.4.refs_3_.v_ref), custom_call_target="tpu_custom_call" | custom-call | bytes 1024 | tf_op jit(solution)/shard_map/pallas_call | solution.py:314
  149.4 12.2 %shard_map.376 = (bf16[2,2,256,896]{3,2,1,0:T(8,128)(2,1)}, f32[2,2,256,128]{3,2,1,0:T(8,128)}) custom-call(s32[1]{0:T(128)} %bitcast.1.core_ref, s32[8,256]{1,0:T(8,128)} %constant.143.clone.refs_0_.index_ref, f32[8,256]{1,0:T(8,128)} %constant.144.clone.refs_1_.scale_ref, bf16[2,2,256,256]{3,2,1,0:T(8,128)(2,1)} %bitcast.65, ...), custom_call_target="tpu_custom_call" | custom-call | flops 4294967296 | bytes 8388608 | tf_op jit(solution)/shard_map/pallas_call | solution.py:1400
  162.3 1.6 fusion.74
  164.4 3.5 broadcast_select_fusion.1
  167.9 3.1 slice_dynamic-update-slice_fusion
  171.1 5.4 multiply_reduce_fusion.3
  176.5 3.8 multiply_convert_fusion.3
  180.5 2.3 pad_maximum_fusion.5
  182.8 2.6 multiply_convert_fusion.grad_ref
  185.4 4.1 pad_maximum_fusion.4.second_ref
  189.7 227.1 %shard_map.377 = (bf16[2,448,2560]{2,1,0:T(8,128)(2,1)}, bf16[2,448,2560]{2,1,0:T(8,128)(2,1)}, bf16[2,448,2560]{2,1,0:T(8,128)(2,1)}, bf16[2,448,2560]{2,1,0:T(...) custom-call(bf16[1024,1792]{1,0:T(8,128)(2,1)} %pad_maximum_fusion.4, ...), custom_call_target="tpu_custom_call" | custom-call | bytes 1024 | tf_op jit(solution)/shard_map/pallas_call | solution.py:1212
  421.2 1.2 collective-permute-start.10
  423.7 5.4 multiply_reduce_fusion
  429.5 1.1 copy-done.42
  430.6 6.9 fusion.72
  437.5 1.1 copy-done.46
  438.6 3.5 fusion.20
  442.6 5.2 convert_multiply_fusion
  447.8 2.1 pad_maximum_fusion.6
  452.2 25.9 %shard_map.378 = (bf16[2,2,256,1024]{3,2,1,0:T(8,128)(2,1)S(1)}, bf16[2,8,160,128]{3,2,1,0:T(8,128)(2,1)S(1)}) custom-call(s32[8,256]{1,0:T(8,128)S(1)} %copy-done.18, f32[8,256]{1,0:T(8,128)S(1)} %copy-done.20, bf16[2,2,256,256]{3,2,1,0:T(8,128)(2,1)S(1)} %bitcast.69, bf16[2,2,256,896]{3,2,1,0:T(8,128)(2,1)S(1)} %bitcast.63, ...), custom_call_target="tpu_custom_call" | custom-call | bytes 1024 | tf_op jit(solution)/shard_map/pallas_call | solution.py:314
  478.1 1.3 copy-done.21
  480.3 28.0 %shard_map.379 = (bf16[2,2,256,256]{3,2,1,0:T(8,128)(2,1)}, bf16[2,2,256,896]{3,2,1,0:T(8,128)(2,1)}) custom-call(s32[1]{0:T(128)} %bitcast.1.core_ref, s32[8,256]{1,0:T(8,128)} %constant.143.clone.refs_0_.index_ref, f32[8,256]{1,0:T(8,128)} %constant.144.clone.refs_1_.scale_ref, bf16[2,2,256,256]{3,2,1,0:T(8,128)(2,1)} %bitcast.67, ...), custom_call_target="tpu_custom_call" | custom-call | flops 12884901888 | bytes 8388608 | tf_op jit(solution)/shard_map/pallas_call | solution.py:1499
  508.2 14.3 %collective-permute-done.10 = bf16[2,448,2560]{2,1,0:T(8,128)(2,1)} collective-permute-done((bf16[2,448,2560]{2,1,0:T(8,128)(2,1)}, bf16[2,448,2560]{2,1,0:T(8,128)(2,1)}, u32[]{:S(2)}, u32[]{:S(2)}) %collective-permute-start.10) | collective-permute-done | bytes 4587552 | tf_op jit(solution)/shard_map/ppermute | solution.py:388
  522.5 0.9 collective-permute-done.9
  523.4 1.0 slice.141
  524.4 3.7 fusion.13
  528.2 1.3 collective-permute-start.11
  529.5 0.9 collective-permute-start.14
  530.4 1.6 collective-permute-start.13
  532.1 5.7 add_convert_fusion.up_ref
  537.8 5.7 add_convert_fusion.1.gate_ref
  543.5 6.8 convolution_convert_fusion.1
  551.1 1.2 fusion.17
  552.6 1.9 slice-done.3
  554.5 2.1 fusion.25
  557.6 4.0 fusion.27
  561.5 9.6 %convolution_convert_fusion = bf16[1792,1280]{1,0:T(8,128)(2,1)} fusion(bf16[1024,256]{1,0:T(8,128)(2,1)S(1)} %bitcast.111, bf16[1024,896]{1,0:T(8,128)(2,1)} %bitcast.92, bf16[1280]{0:T(1024)(128)(2,1)S(1)} %copy-done.81, f32[1792]{0:T(1024)S(1)} %copy-done.67, f32[1024]{0:T(1024)S(1)} %copy-done.77, bf16[512,1792]{1,0:T(8,128)(2,1)} %collective-permute-done, ...), kind=kOutput, calls=%fused_computation.4 | convolution fusion | flops 4720623616 | bytes 10630656 | tf_op jit(solution)/shard_map/dot_general | solution.py:70
  571.1 9.4 %collective-permute-done.14 = bf16[2,448,1280]{2,1,0:T(8,128)(2,1)} collective-permute-done((bf16[2,448,1280]{2,1,0:T(8,128)(2,1)}, bf16[2,448,1280]{2,1,0:T(8,128)(2,1)}, u32[]{:S(2)}, u32[]{:S(2)}) %collective-permute-start.14) | collective-permute-done | bytes 2293792 | tf_op jit(solution)/shard_map/ppermute | solution.py:388
  580.6 4.3 add_convert_fusion.2.down_b_ref
  584.9 3.5 add_convert_fusion.3.down_a_ref
  588.5 6.3 fusion.14
  595.2 1.1 pad.42
  596.2 197.7 %shard_map.380 = (f32[56,512]{1,0:T(8,128)}, f32[56,1792]{1,0:T(8,128)}, f32[56,1792]{1,0:T(8,128)}, f32[56,9728]{1,0:T(8,128)}, f32[56,4864]{1,0:T(8,128)}, /*index=5*/f32[56,256]{1,0:T(8,128)}) custom-call(bf16[2,448,1280]{2,1,0:T(8,128)(2,1)} %add_convert_fusion.3.down_a_ref, bf16[2,448,2560]{2,1,0:T(8,128)(2,1)} %add_convert_fusion.1.gate_ref, ...), custom_call_target="tpu_custom_call" | custom-call | bytes 1024 | tf_op jit(solution)/shard_map/pallas_call | solution.py:684
  796.9 6.7 multiply_subtract_fusion
  803.7 2.1 multiply_subtract_fusion.1
  805.9 1.2 multiply_subtract_fusion.3
  807.1 1.2 multiply_subtract_fusion.2
  809.6 3.1 fusion.10
  814.8 1.3 copy.101
  816.1 1.0 copy.102
  (276 shorter events, 23.6 us)
Async XLA Ops:
  7.2 182.5 %all-gather.3.cloned.1.call-start = ((), (), s32[]{:S(2)}) async-start(), calls=%async_computation | async-start | bytes 5849088 | tf_op jit(solution)/shard_map/all_gather | solution.py:1335
  7.2 90.9 %collective-permute-start = (bf16[512,1792]{1,0:T(8,128)(2,1)}, bf16[512,1792]{1,0:T(8,128)(2,1)}, u32[]{:S(2)}, u32[]{:S(2)}) collective-permute-start(bf16[512,1792]{1,0:T(8,128)(2,1)} %bitcast.70), channel_id=1, source_target_pairs={{0,1},{1,0},{2,3},{3,2},{4,5},{5,4},{6,7},{7,6},{8,9},{9,8},{10,11... | collective-permute-start | bytes 5505032 | tf_op jit(solution)/shard_map/ppermute | solution.py:371
  8.5 88.0 %copy-start.59 = (f32[56,5]{1,0:T(8,128)}, f32[56,5]{1,0:T(8,128)S(1)}, u32[]{:S(2)}) copy-start(f32[56,5]{1,0:T(8,128)S(1)} %copy.67) | copy-start | bytes 3364
  92.6 5.6 copy-start.25
  96.5 67.9 %collective-permute-start.3 = (bf16[1792,896]{1,0:T(8,128)(2,1)}, bf16[1792,896]{1,0:T(8,128)(2,1)}, u32[]{:S(2)}, u32[]{:S(2)}) collective-permute-start(bf16[1792,896]{1,0:T(8,128)(2,1)} %slice.172), channel_id=1, source_target_pairs={{0,1},{1,0},{2,3},{3,2},{4,5},{5,4},{6,7},{7,6},{8,9},{9,8},{10,11... | collective-permute-start | bytes 9633800 | tf_op jit(solution)/shard_map/ppermute | solution.py:371
  97.9 10.5 %copy-start.66 = (f32[1792]{0:T(1024)}, f32[1792]{0:T(1024)S(1)}, u32[]{:S(2)}) copy-start(f32[1792]{0:T(1024)S(1)} %get-tuple-element.164) | copy-start | bytes 21508
  98.0 13.8 %copy-start.68 = (f32[896]{0:T(1024)}, f32[896]{0:T(1024)S(1)}, u32[]{:S(2)}) copy-start(f32[896]{0:T(1024)S(1)} %fusion.57) | copy-start | bytes 10756
  98.1 13.8 %copy-start.70 = (f32[896]{0:T(1024)}, f32[896]{0:T(1024)S(1)}, u32[]{:S(2)}) copy-start(f32[896]{0:T(1024)S(1)} %get-tuple-element.205) | copy-start | bytes 10756
  98.1 13.8 %copy-start.72 = (f32[896]{0:T(1024)}, f32[896]{0:T(1024)S(1)}, u32[]{:S(2)}) copy-start(f32[896]{0:T(1024)S(1)} %get-tuple-element.206) | copy-start | bytes 10756
  100.4 342.1 %copy-start.76 = (f32[1024]{0:T(1024)}, f32[1024]{0:T(1024)S(1)}, u32[]{:S(2)}) copy-start(f32[1024]{0:T(1024)S(1)} %add_rsqrt_fusion) | copy-start | bytes 12292
  107.2 4.2 collective-permute-start.1
  113.7 35.7 %copy-start.2 = (bf16[2,2,256,896]{3,2,1,0:T(8,128)(2,1)}, bf16[2,2,256,896]{3,2,1,0:T(8,128)(2,1)S(1)}, u32[]{:S(2)}) copy-start(bf16[2,2,256,896]{3,2,1,0:T(8,128)(2,1)S(1)} %add_convert_fusion.4.refs_3_.v_ref) | copy-start | bytes 5505028
  161.7 6.3 collective-permute-start.2
  161.8 18.8 %collective-permute-start.5 = (bf16[512,1792]{1,0:T(8,128)(2,1)}, bf16[512,1792]{1,0:T(8,128)(2,1)}, u32[]{:S(2)}, u32[]{:S(2)}) collective-permute-start(bf16[512,1792]{1,0:T(8,128)(2,1)} %bitcast.90), channel_id=1, source_target_pairs={{0,1},{1,0},{2,3},{3,2},{4,5},{5,4},{6,7},{7,6},{8,9},{9,8},{10,11... | collective-permute-start | bytes 5505032 | tf_op jit(solution)/shard_map/ppermute | solution.py:371
  167.9 8.6 %copy-start.43 = (bf16[1792,896]{1,0:T(8,128)(2,1)}, bf16[1792,896]{1,0:T(8,128)(2,1)S(1)}, u32[]{:S(2)}) copy-start(bf16[1792,896]{1,0:T(8,128)(2,1)S(1)} %get-tuple-element.181) | copy-start | bytes 9633796
  167.9 8.6 %copy-start.45 = (bf16[1792,896]{1,0:T(8,128)(2,1)}, bf16[1792,896]{1,0:T(8,128)(2,1)S(1)}, u32[]{:S(2)}) copy-start(bf16[1792,896]{1,0:T(8,128)(2,1)S(1)} %get-tuple-element.182) | copy-start | bytes 9633796
  171.1 5.4 copy-start.36
  171.1 5.4 copy-start.38
  180.3 5.1 collective-permute-start.4
  189.7 228.8 %copy-start.82 = (f32[56,5]{0,1:T(8,128)S(1)}, f32[56,5]{0,1:T(8,128)}, u32[]{:S(2)}) copy-start(f32[56,5]{0,1:T(8,128)} %param.43) | copy-start | bytes 3364
  189.7 229.5 %copy-start.83 = (f32[56,5]{0,1:T(8,128)S(1)}, f32[56,5]{0,1:T(8,128)}, u32[]{:S(2)}) copy-start(f32[56,5]{0,1:T(8,128)} %param.37) | copy-start | bytes 3364
  189.7 230.2 %copy-start.78 = (f32[56,5]{0,1:T(8,128)S(1)}, f32[56,5]{0,1:T(8,128)}, u32[]{:S(2)}) copy-start(f32[56,5]{0,1:T(8,128)} %param.31) | copy-start | bytes 3364
  416.9 6.8 collective-permute-start.7
  416.9 12.1 %collective-permute-start.6 = (f32[512,1792]{1,0:T(8,128)}, f32[512,1792]{1,0:T(8,128)}, u32[]{:S(2)}, u32[]{:S(2)}) collective-permute-start(f32[512,1792]{1,0:T(8,128)} %get-tuple-element.63), channel_id=1, source_target_pairs={{0,1},{1,0},{2,3},{3,2},{4,5},{5,4},{6,7},{7,6},{8,9},{9,8},{10,11... | collective-permute-start | bytes 11010056 | tf_op jit(solution)/shard_map/ppermute | solution.py:371
  421.2 101.3 %collective-permute-start.10 = (bf16[2,448,2560]{2,1,0:T(8,128)(2,1)}, bf16[2,448,2560]{2,1,0:T(8,128)(2,1)}, u32[]{:S(2)}, u32[]{:S(2)}) collective-permute-start(bf16[2,448,2560]{2,1,0:T(8,128)(2,1)} %get-tuple-element.73), channel_id=1, source_target_pairs={{0,8},{8,0},{1,9},{9,1},{2,10},{10,2},{3,11},{11,3},{4,12},{12,4},... | collective-permute-start | bytes 13762568 | tf_op jit(solution)/shard_map/ppermute | solution.py:388
  422.4 101.0 %collective-permute-start.9 = (bf16[2,448,2560]{2,1,0:T(8,128)(2,1)}, bf16[2,448,2560]{2,1,0:T(8,128)(2,1)}, u32[]{:S(2)}, u32[]{:S(2)}) collective-permute-start(bf16[2,448,2560]{2,1,0:T(8,128)(2,1)} %get-tuple-element.72), channel_id=1, source_target_pairs={{0,16},{16,0},{1,17},{17,1},{2,18},{18,2},{3,19},{19,3},{4,20},{20... | collective-permute-start | bytes 13762568 | tf_op jit(solution)/shard_map/ppermute | solution.py:388
  423.7 5.8 copy-start.34
  423.7 6.9 copy-start.42
  430.6 7.0 copy-start.44
  430.6 8.1 copy-start.46
  442.4 8.9 %collective-permute-start.8 = (bf16[512,896]{1,0:T(8,128)(2,1)S(1)}, bf16[512,896]{1,0:T(8,128)(2,1)S(1)}, u32[]{:S(2)}, u32[]{:S(2)}) collective-permute-start(bf16[512,896]{1,0:T(8,128)(2,1)S(1)} %get-tuple-element.193), channel_id=1, source_target_pairs={{0,1},{1,0},{2,3},{3,2},{4,5},{5,4},{6,7},{7,6},{8,9},{9,8},{10,11... | collective-permute-start | bytes 2752520 | tf_op jit(solution)/shard_map/ppermute | solution.py:371
  450.8 92.7 %collective-permute-start.15 = (bf16[512,896]{1,0:T(8,128)(2,1)S(1)}, bf16[512,896]{1,0:T(8,128)(2,1)}, u32[]{:S(2)}, u32[]{:S(2)}) collective-permute-start(bf16[512,896]{1,0:T(8,128)(2,1)S(1)} %get-tuple-element.185), channel_id=1, source_target_pairs={{0,1},{1,0},{2,3},{3,2},{4,5},{5,4},{6,7},{7,6},{8,9},{9,8},{10,11... | collective-permute-start | bytes 2752520 | tf_op jit(solution)/shard_map/ppermute | solution.py:371
  480.3 44.1 %copy-start.24 = (f32[2,2,258,896]{3,2,1,0:T(8,128)S(1)}, f32[2,2,258,896]{3,2,1,0:T(8,128)}, u32[]{:S(2)}) copy-start(f32[2,2,258,896]{3,2,1,0:T(8,128)} %copy-done.23) | copy-start | bytes 11096068
  523.4 8.7 %slice-start.6 = ((s8[4587520]{0:T(1024)(128)(4,1)}), s8[4194304]{0:T(1024)(128)(4,1)S(1)}, s32[]{:S(2)}) async-start(s8[4587520]{0:T(1024)(128)(4,1)} %bitcast.96), calls=%async_computation.7 | async-start | bytes 8388608
  524.4 7.7 slice-start.7
  524.4 13.3 %slice-start.4 = ((s8[4587520]{0:T(1024)(128)(4,1)}), s8[4194304]{0:T(1024)(128)(4,1)S(1)}, s32[]{:S(2)}) async-start(s8[4587520]{0:T(1024)(128)(4,1)} %bitcast.94), calls=%async_computation.5 | async-start | bytes 8388608
  528.2 22.2 %collective-permute-start.11 = (bf16[2,2,896]{2,1,0:T(2,128)(2,1)S(1)}, bf16[2,2,896]{2,1,0:T(2,128)(2,1)S(1)}, u32[]{:S(2)}, u32[]{:S(2)}) collective-permute-start(bf16[2,2,896]{2,1,0:T(2,128)(2,1)S(1)} %dynamic-slice_bitcast_fusion), channel_id=1, source_target_pairs={{2,0},{4,2},{6,4},{3,1},{5,3},{7,5},{10,8},{12,10},{14,12},{11,9},... | collective-permute-start | bytes 21512 | tf_op jit(solution)/shard_map/ppermute | solution.py:360
  529.5 8.3 %slice-start.5 = ((s8[4587520]{0:T(1024)(128)(4,1)}), s8[393216]{0:T(1024)(128)(4,1)S(1)}, s32[]{:S(2)}) async-start(s8[4587520]{0:T(1024)(128)(4,1)} %bitcast.94), calls=%async_computation.6 | async-start | bytes 786432
  529.5 51.0 %collective-permute-start.14 = (bf16[2,448,1280]{2,1,0:T(8,128)(2,1)}, bf16[2,448,1280]{2,1,0:T(8,128)(2,1)}, u32[]{:S(2)}, u32[]{:S(2)}) collective-permute-start(bf16[2,448,1280]{2,1,0:T(8,128)(2,1)} %get-tuple-element.83), channel_id=1, source_target_pairs={{0,8},{8,0},{1,9},{9,1},{2,10},{10,2},{3,11},{11,3},{4,12},{12,4},... | collective-permute-start | bytes 6881288 | tf_op jit(solution)/shard_map/ppermute | solution.py:388
  530.4 54.4 %collective-permute-start.13 = (bf16[2,448,1280]{2,1,0:T(8,128)(2,1)}, bf16[2,448,1280]{2,1,0:T(8,128)(2,1)}, u32[]{:S(2)}, u32[]{:S(2)}) collective-permute-start(bf16[2,448,1280]{2,1,0:T(8,128)(2,1)} %get-tuple-element.79), channel_id=1, source_target_pairs={{0,16},{16,0},{1,17},{17,1},{2,18},{18,2},{3,19},{19,3},{4,20},{20... | collective-permute-start | bytes 6881288 | tf_op jit(solution)/shard_map/ppermute | solution.py:388
  537.8 5.7 copy-start.41
  543.5 6.9 copy-start.33
  557.3 31.1 %collective-permute-start.12 = (f32[512,1792]{1,0:T(8,128)S(1)}, f32[512,1792]{1,0:T(8,128)S(1)}, u32[]{:S(2)}, u32[]{:S(2)}) collective-permute-start(f32[512,1792]{1,0:T(8,128)S(1)} %convolution_add_fusion), channel_id=1, source_target_pairs={{0,1},{1,0},{2,3},{3,2},{4,5},{5,4},{6,7},{7,6},{8,9},{9,8},{10,11... | collective-permute-start | bytes 11010056 | tf_op jit(solution)/shard_map/ppermute | solution.py:371
  557.6 30.9 %slice-start = ((s8[7340032]{0:T(1024)(128)(4,1)}), s8[4194304]{0:T(1024)(128)(4,1)S(1)}, s32[]{:S(2)}) async-start(s8[7340032]{0:T(1024)(128)(4,1)} %bitcast.77), calls=%async_computation.1 | async-start | bytes 8388608
  561.5 26.9 %slice-start.1 = ((s8[7340032]{0:T(1024)(128)(4,1)}), s8[3145728]{0:T(1024)(128)(4,1)S(1)}, s32[]{:S(2)}) async-start(s8[7340032]{0:T(1024)(128)(4,1)} %bitcast.77), calls=%async_computation.2 | async-start | bytes 6291456
  571.1 13.8 %copy-start.47 = (bf16[2,448,1280]{2,1,0:T(8,128)(2,1)S(1)}, bf16[2,448,1280]{2,1,0:T(8,128)(2,1)}, u32[]{:S(2)}) copy-start(bf16[2,448,1280]{2,1,0:T(8,128)(2,1)} %get-tuple-element.78) | copy-start | bytes 6881284
  588.4 6.3 copy-start.27
  588.5 6.3 copy-start.74
  596.2 198.5 %copy-start.61 = (f32[56,5]{1,0:T(8,128)S(1)}, f32[56,5]{1,0:T(8,128)}, u32[]{:S(2)}) copy-start(f32[56,5]{1,0:T(8,128)} %copy.72) | copy-start | bytes 3364
  596.2 199.2 %copy-start.60 = (f32[56,5]{1,0:T(8,128)S(1)}, f32[56,5]{1,0:T(8,128)}, u32[]{:S(2)}) copy-start(f32[56,5]{1,0:T(8,128)} %copy-done.59) | copy-start | bytes 3364
  596.2 199.2 %copy-start.62 = (f32[56,5]{1,0:T(8,128)S(1)}, f32[56,5]{1,0:T(8,128)}, u32[]{:S(2)}) copy-start(f32[56,5]{1,0:T(8,128)} %copy.71) | copy-start | bytes 3364
  596.2 199.2 %copy-start.63 = (f32[56,5]{1,0:T(8,128)S(1)}, f32[56,5]{1,0:T(8,128)}, u32[]{:S(2)}) copy-start(f32[56,5]{1,0:T(8,128)} %copy.74) | copy-start | bytes 3364
  596.2 200.6 %copy-start.1 = (f32[56,9728]{1,0:T(8,128)S(1)}, f32[56,9728]{1,0:T(8,128)}, u32[]{:S(2)}) copy-start(f32[56,9728]{1,0:T(8,128)} %gu_ref.1) | copy-start | bytes 6537220
  796.8 6.8 copy-start.5
  796.8 6.8 copy-start.40
  796.8 6.8 copy-start.50
  796.8 6.8 copy-start.51
  796.8 9.0 %copy-start.49 = (f32[56,1792]{1,0:T(8,128)S(1)}, f32[56,1792]{1,0:T(8,128)}, u32[]{:S(2)}) copy-start(f32[56,1792]{1,0:T(8,128)} %get-tuple-element.230) | copy-start | bytes 1204228
  796.8 9.0 %copy-start.55 = (f32[56,1792]{1,0:T(8,128)S(1)}, f32[56,1792]{1,0:T(8,128)}, u32[]{:S(2)}) copy-start(f32[56,1792]{1,0:T(8,128)} %param.33) | copy-start | bytes 1204228
  796.9 9.0 %copy-start.56 = (f32[56,1792]{1,0:T(8,128)S(1)}, f32[56,1792]{1,0:T(8,128)}, u32[]{:S(2)}) copy-start(f32[56,1792]{1,0:T(8,128)} %param.39) | copy-start | bytes 1204228
  796.9 10.2 %copy-start.58 = (f32[56,1792]{1,0:T(8,128)S(1)}, f32[56,1792]{1,0:T(8,128)}, u32[]{:S(2)}) copy-start(f32[56,1792]{1,0:T(8,128)} %param.40) | copy-start | bytes 1204228
  796.9 12.2 %copy-start.30 = (f32[512,1792]{1,0:T(8,128)S(1)}, f32[512,1792]{1,0:T(8,128)}, u32[]{:S(2)}) copy-start(f32[512,1792]{1,0:T(8,128)} %get-tuple-element.178) | copy-start | bytes 11010052
  803.6 5.4 copy-start.28
  803.7 5.4 copy-start.29
  (46 other events, 115.9 us)
Sparse Core Ops, SparseCore 0:
  92.7 96.9 all-gather.2

commit v8 on v7

--- a/solution.py
+++ b/solution.py
@@ -1017,13 +1017,13 @@
     def weight_terms(turn):
         slot = turn % 2
 
-        @pl.loop(0, 4)
+        @pl.loop(0, 2)
         def _(part):
-            rows = pl.ds(pl.multiple_of(part * quarter, quarter), quarter)
-            grads = dot(second_t_ref[rows, :], narrow[:, : 2 * WIDE])
-            terms[slot, part // 2, part % 2, :, : 2 * WIDE] = grads.astype(bf16)
-            down = dot(grad_t_ref[rows, :], narrow[:, 2 * WIDE :])
-            terms[slot, part // 2, part % 2, :, 2 * WIDE :] = down.astype(bf16)
+            rows = pl.ds(pl.multiple_of(part * 2 * quarter, 2 * quarter), 2 * quarter)
+            grads = dot(second_t_ref[rows, :], narrow[:, : 2 * WIDE]).astype(bf16)
+            terms[slot, part, :, :, : 2 * WIDE] = grads.reshape(2, quarter, 2 * WIDE)
+            down = dot(grad_t_ref[rows, :], narrow[:, 2 * WIDE :]).astype(bf16)
+            terms[slot, part, :, :, 2 * WIDE :] = down.reshape(2, quarter, WIDE)
 
     def terms_copies(turn):
         slot, pair = turn % 2, pair_of(turn)

time: 831 us -> 828 us (level)
  transfers between devices with their start and end apart: 17 -> 17, of which waited for: 5 -> 4; matrix products, arithmetic and copies ran while one was open for 15% -> 15% of each run, Pallas kernels for 22% -> 22%
where the time goes in v8:
time: 828 us; the launch traced here: 820 us
  Pallas kernels  599 us (72%)
  other arithmetic  80.1 us (10%)
  matrix products  47.9 us (6%)
  local copies, waits for them, and re-layouts  42.8 us (5%)
  waiting for transfers between devices  25.2 us (3%)
  between operations  15.5 us (2%)
  starting transfers between devices  9.04 us (1%)
    pallas_call x1, Pallas kernels, feed_forward(): pl.pallas_call(functools.partial(feed_forward_kernel, tiles), out_shape=t...  225 us
    pallas_call x1, Pallas kernels, reduced(): pl.pallas_call(reduce_kernel, out_shape=[jax.ShapeDtypeStruct((owned, wid...  196 us
    pallas_call x1, Pallas kernels, gathered_weights(): pl.pallas_call(gather_kernel, out_shape=[jax.ShapeDtypeStruct((2, 2, 2, 2...  77.1 us
    pallas_call x2, Pallas kernels, call(): pl.pallas_call(run, out_shape=list(extra) + [state], in_specs=[vmem] * le...  60.3 us
    pallas_call x1, Pallas kernels, local(): call(backward_kernel, ins=[q_spec, k_spec, v_spec, wide_spec, 'state', 's...  28.5 us
    unnamed x200, local copies, waits for them, and re-layouts  25.4 us
    ppermute x4, waiting for transfers between devices, exchanged(): return lax.ppermute(array, axis, [(i, i ^ 1 << bit) for i in range(count)])  23.5 us
    convert_element_type x4, other arithmetic, summed(): return (keep.astype(f32) + got.astype(f32)).astype(bf16)  19.2 us
  transfers between devices with their start and end apart: 17, of which 4 were waited for; matrix products, arithmetic and copies ran while one was open for 15% of the time, Pallas kernels for 22%

profile of v8, /device:TPU:0, one launch (start us, length us, event | category | flops | bytes accessed | tf_op | source)
XLA Modules:
  0.0 819.8 jit_solution(7236784148661302294)
XLA Ops:
  8.6 1.6 copy-done
  10.2 1.2 copy-done.4
  11.4 1.0 copy-done.8
  12.4 1.0 copy-done.10
  13.4 0.9 copy-done.15
  14.3 77.1 %shard_map.374 = (bf16[2,2,2,2,112,2176]{5,4,3,2,1,0:T(8,128)(2,1)}, bf16[15,112,384]{2,1,0:T(8,128)(2,1)S(1)}, bf16[112,1536]{1,0:T(8,128)(2,1)}) custom-call(f32[56,512]{1,0:T(8,128)S(1)} %copy-done.15, f32[56,1792]{1,0:T(8,128)S(1)} %copy-done.8, f32[56,1792]{1,0:T(8,128)S(1)} %copy-done.10, f32[56,9728]{1,0:T(8,128)S(1)} %copy-done, ...), custom_call_target="tpu_custom_call" | custom-call | bytes 1024 | tf_op jit(solution)/shard_map/pallas_call | solution.py:882
  91.5 1.1 copy-done.12
  92.6 4.0 slice.172
  96.6 1.0 slice.160
  98.1 2.3 fusion
  100.4 6.7 fusion.38
  107.2 1.3 collective-permute-start.1
  108.5 2.9 convolution_convert_fusion.2
  111.9 1.2 add_convert_fusion.4.refs_3_.v_ref
  113.8 34.8 %shard_map.375.before_ref = bf16[2,8,160,128]{3,2,1,0:T(8,128)(2,1)S(1)} custom-call(s32[8,256]{1,0:T(8,128)S(1)} %copy-done.17, f32[8,256]{1,0:T(8,128)S(1)} %copy-done.19, bf16[2,2,256,256]{3,2,1,0:T(8,128)(2,1)S(1)} %bitcast.64, bf16[2,2,256,896]{3,2,1,0:T(8,128)(2,1)S(1)} %add_convert_fusion.4.refs_3_.v_ref), custom_call_target="tpu_custom_call" | custom-call | bytes 1024 | tf_op jit(solution)/shard_map/pallas_call | solution.py:314
  149.4 12.2 %shard_map.376 = (bf16[2,2,256,896]{3,2,1,0:T(8,128)(2,1)}, f32[2,2,256,128]{3,2,1,0:T(8,128)}) custom-call(s32[1]{0:T(128)} %bitcast.1.core_ref, s32[8,256]{1,0:T(8,128)} %constant.143.clone.refs_0_.index_ref, f32[8,256]{1,0:T(8,128)} %constant.144.clone.refs_1_.scale_ref, bf16[2,2,256,256]{3,2,1,0:T(8,128)(2,1)} %bitcast.65, ...), custom_call_target="tpu_custom_call" | custom-call | flops 4294967296 | bytes 8388608 | tf_op jit(solution)/shard_map/pallas_call | solution.py:1400
  162.3 1.6 fusion.74
  164.4 3.5 broadcast_select_fusion.1
  167.9 3.1 slice_dynamic-update-slice_fusion
  171.1 5.4 multiply_reduce_fusion.3
  176.5 3.8 multiply_convert_fusion.3
  180.5 2.3 pad_maximum_fusion.5
  182.8 2.6 multiply_convert_fusion.grad_ref
  185.4 4.1 pad_maximum_fusion.4.second_ref
  189.7 224.6 %shard_map.377 = (bf16[2,448,2560]{2,1,0:T(8,128)(2,1)}, bf16[2,448,2560]{2,1,0:T(8,128)(2,1)}, bf16[2,448,2560]{2,1,0:T(8,128)(2,1)}, bf16[2,448,2560]{2,1,0:T(...) custom-call(bf16[1024,1792]{1,0:T(8,128)(2,1)} %pad_maximum_fusion.4, ...), custom_call_target="tpu_custom_call" | custom-call | bytes 1024 | tf_op jit(solution)/shard_map/pallas_call | solution.py:1212
  418.7 1.1 collective-permute-start.9
  419.8 1.4 collective-permute-done.7
  421.1 5.4 multiply_reduce_fusion
  426.9 1.1 copy-done.42
  428.0 7.1 fusion.72
  435.2 0.9 copy-done.46
  436.1 3.5 fusion.20
  440.0 5.2 convert_multiply_fusion
  445.2 2.1 pad_maximum_fusion.6
  449.7 25.5 %shard_map.378 = (bf16[2,2,256,1024]{3,2,1,0:T(8,128)(2,1)S(1)}, bf16[2,8,160,128]{3,2,1,0:T(8,128)(2,1)S(1)}) custom-call(s32[8,256]{1,0:T(8,128)S(1)} %copy-done.18, f32[8,256]{1,0:T(8,128)S(1)} %copy-done.20, bf16[2,2,256,256]{3,2,1,0:T(8,128)(2,1)S(1)} %bitcast.69, bf16[2,2,256,896]{3,2,1,0:T(8,128)(2,1)S(1)} %bitcast.63, ...), custom_call_target="tpu_custom_call" | custom-call | bytes 1024 | tf_op jit(solution)/shard_map/pallas_call | solution.py:314
  475.2 1.3 copy-done.21
  477.3 28.5 %shard_map.379 = (bf16[2,2,256,256]{3,2,1,0:T(8,128)(2,1)}, bf16[2,2,256,896]{3,2,1,0:T(8,128)(2,1)}) custom-call(s32[1]{0:T(128)} %bitcast.1.core_ref, s32[8,256]{1,0:T(8,128)} %constant.143.clone.refs_0_.index_ref, f32[8,256]{1,0:T(8,128)} %constant.144.clone.refs_1_.scale_ref, bf16[2,2,256,256]{3,2,1,0:T(8,128)(2,1)} %bitcast.67, ...), custom_call_target="tpu_custom_call" | custom-call | flops 12884901888 | bytes 8388608 | tf_op jit(solution)/shard_map/pallas_call | solution.py:1499
  505.9 14.1 %collective-permute-done.10 = bf16[2,448,2560]{2,1,0:T(8,128)(2,1)} collective-permute-done((bf16[2,448,2560]{2,1,0:T(8,128)(2,1)}, bf16[2,448,2560]{2,1,0:T(8,128)(2,1)}, u32[]{:S(2)}, u32[]{:S(2)}) %collective-permute-start.10) | collective-permute-done | bytes 4587552 | tf_op jit(solution)/shard_map/ppermute | solution.py:388
  520.0 1.0 slice.141
  521.0 3.7 fusion.13
  524.7 1.3 collective-permute-start.11
  526.1 1.8 collective-permute-start.14
  527.9 1.1 collective-permute-start.13
  529.0 5.7 add_convert_fusion.up_ref
  534.7 5.7 add_convert_fusion.1.gate_ref
  540.4 6.8 convolution_convert_fusion.1
  548.0 1.2 fusion.17
  549.5 1.9 slice-done.3
  551.4 2.1 fusion.25
  554.5 4.0 fusion.27
  558.5 9.6 %convolution_convert_fusion = bf16[1792,1280]{1,0:T(8,128)(2,1)} fusion(bf16[1024,256]{1,0:T(8,128)(2,1)S(1)} %bitcast.111, bf16[1024,896]{1,0:T(8,128)(2,1)} %bitcast.92, bf16[1280]{0:T(1024)(128)(2,1)S(1)} %copy-done.81, f32[1792]{0:T(1024)S(1)} %copy-done.67, f32[1024]{0:T(1024)S(1)} %copy-done.77, bf16[512,1792]{1,0:T(8,128)(2,1)} %collective-permute-done, ...), kind=kOutput, calls=%fused_computation.4 | convolution fusion | flops 4720623616 | bytes 10630656 | tf_op jit(solution)/shard_map/dot_general | solution.py:70
  568.0 9.4 %collective-permute-done.14 = bf16[2,448,1280]{2,1,0:T(8,128)(2,1)} collective-permute-done((bf16[2,448,1280]{2,1,0:T(8,128)(2,1)}, bf16[2,448,1280]{2,1,0:T(8,128)(2,1)}, u32[]{:S(2)}, u32[]{:S(2)}) %collective-permute-start.14) | collective-permute-done | bytes 2293792 | tf_op jit(solution)/shard_map/ppermute | solution.py:388
  577.5 4.3 add_convert_fusion.2.down_b_ref
  581.8 3.5 add_convert_fusion.3.down_a_ref
  585.4 6.3 fusion.14
  592.0 1.1 pad.42
  593.1 196.5 %shard_map.380 = (f32[56,512]{1,0:T(8,128)}, f32[56,1792]{1,0:T(8,128)}, f32[56,1792]{1,0:T(8,128)}, f32[56,9728]{1,0:T(8,128)}, f32[56,4864]{1,0:T(8,128)}, /*index=5*/f32[56,256]{1,0:T(8,128)}) custom-call(bf16[2,448,1280]{2,1,0:T(8,128)(2,1)} %add_convert_fusion.3.down_a_ref, bf16[2,448,2560]{2,1,0:T(8,128)(2,1)} %add_convert_fusion.1.gate_ref, ...), custom_call_target="tpu_custom_call" | custom-call | bytes 1024 | tf_op jit(solution)/shard_map/pallas_call | solution.py:684
  792.5 6.7 multiply_subtract_fusion
  799.3 2.1 multiply_subtract_fusion.1
  801.5 1.2 multiply_subtract_fusion.3
  802.7 1.2 multiply_subtract_fusion.2
  805.2 3.1 fusion.10
  810.4 1.3 copy.101
  811.7 1.0 copy.102
  (276 shorter events, 22.4 us)
Async XLA Ops:
  7.2 182.5 %all-gather.3.cloned.1.call-start = ((), (), s32[]{:S(2)}) async-start(), calls=%async_computation | async-start | bytes 5849088 | tf_op jit(solution)/shard_map/all_gather | solution.py:1335
  7.2 90.9 %collective-permute-start = (bf16[512,1792]{1,0:T(8,128)(2,1)}, bf16[512,1792]{1,0:T(8,128)(2,1)}, u32[]{:S(2)}, u32[]{:S(2)}) collective-permute-start(bf16[512,1792]{1,0:T(8,128)(2,1)} %bitcast.70), channel_id=1, source_target_pairs={{0,1},{1,0},{2,3},{3,2},{4,5},{5,4},{6,7},{7,6},{8,9},{9,8},{10,11... | collective-permute-start | bytes 5505032 | tf_op jit(solution)/shard_map/ppermute | solution.py:371
  8.5 88.0 %copy-start.59 = (f32[56,5]{1,0:T(8,128)}, f32[56,5]{1,0:T(8,128)S(1)}, u32[]{:S(2)}) copy-start(f32[56,5]{1,0:T(8,128)S(1)} %copy.67) | copy-start | bytes 3364
  92.6 5.6 copy-start.25
  96.5 67.9 %collective-permute-start.3 = (bf16[1792,896]{1,0:T(8,128)(2,1)}, bf16[1792,896]{1,0:T(8,128)(2,1)}, u32[]{:S(2)}, u32[]{:S(2)}) collective-permute-start(bf16[1792,896]{1,0:T(8,128)(2,1)} %slice.172), channel_id=1, source_target_pairs={{0,1},{1,0},{2,3},{3,2},{4,5},{5,4},{6,7},{7,6},{8,9},{9,8},{10,11... | collective-permute-start | bytes 9633800 | tf_op jit(solution)/shard_map/ppermute | solution.py:371
  97.9 10.5 %copy-start.66 = (f32[1792]{0:T(1024)}, f32[1792]{0:T(1024)S(1)}, u32[]{:S(2)}) copy-start(f32[1792]{0:T(1024)S(1)} %get-tuple-element.164) | copy-start | bytes 21508
  98.0 13.8 %copy-start.68 = (f32[896]{0:T(1024)}, f32[896]{0:T(1024)S(1)}, u32[]{:S(2)}) copy-start(f32[896]{0:T(1024)S(1)} %fusion.57) | copy-start | bytes 10756
  98.1 13.8 %copy-start.70 = (f32[896]{0:T(1024)}, f32[896]{0:T(1024)S(1)}, u32[]{:S(2)}) copy-start(f32[896]{0:T(1024)S(1)} %get-tuple-element.205) | copy-start | bytes 10756
  98.1 13.8 %copy-start.72 = (f32[896]{0:T(1024)}, f32[896]{0:T(1024)S(1)}, u32[]{:S(2)}) copy-start(f32[896]{0:T(1024)S(1)} %get-tuple-element.206) | copy-start | bytes 10756
  100.4 339.6 %copy-start.76 = (f32[1024]{0:T(1024)}, f32[1024]{0:T(1024)S(1)}, u32[]{:S(2)}) copy-start(f32[1024]{0:T(1024)S(1)} %add_rsqrt_fusion) | copy-start | bytes 12292
  107.2 4.2 collective-permute-start.1
  113.7 35.7 %copy-start.2 = (bf16[2,2,256,896]{3,2,1,0:T(8,128)(2,1)}, bf16[2,2,256,896]{3,2,1,0:T(8,128)(2,1)S(1)}, u32[]{:S(2)}) copy-start(bf16[2,2,256,896]{3,2,1,0:T(8,128)(2,1)S(1)} %add_convert_fusion.4.refs_3_.v_ref) | copy-start | bytes 5505028
  161.7 6.3 collective-permute-start.2
  161.8 18.8 %collective-permute-start.5 = (bf16[512,1792]{1,0:T(8,128)(2,1)}, bf16[512,1792]{1,0:T(8,128)(2,1)}, u32[]{:S(2)}, u32[]{:S(2)}) collective-permute-start(bf16[512,1792]{1,0:T(8,128)(2,1)} %bitcast.90), channel_id=1, source_target_pairs={{0,1},{1,0},{2,3},{3,2},{4,5},{5,4},{6,7},{7,6},{8,9},{9,8},{10,11... | collective-permute-start | bytes 5505032 | tf_op jit(solution)/shard_map/ppermute | solution.py:371
  167.9 8.6 %copy-start.43 = (bf16[1792,896]{1,0:T(8,128)(2,1)}, bf16[1792,896]{1,0:T(8,128)(2,1)S(1)}, u32[]{:S(2)}) copy-start(bf16[1792,896]{1,0:T(8,128)(2,1)S(1)} %get-tuple-element.181) | copy-start | bytes 9633796
  167.9 8.6 %copy-start.45 = (bf16[1792,896]{1,0:T(8,128)(2,1)}, bf16[1792,896]{1,0:T(8,128)(2,1)S(1)}, u32[]{:S(2)}) copy-start(bf16[1792,896]{1,0:T(8,128)(2,1)S(1)} %get-tuple-element.182) | copy-start | bytes 9633796
  171.1 5.4 copy-start.36
  171.1 5.4 copy-start.38
  180.3 5.1 collective-permute-start.4
  189.7 226.2 %copy-start.82 = (f32[56,5]{0,1:T(8,128)S(1)}, f32[56,5]{0,1:T(8,128)}, u32[]{:S(2)}) copy-start(f32[56,5]{0,1:T(8,128)} %param.43) | copy-start | bytes 3364
  189.7 226.9 %copy-start.83 = (f32[56,5]{0,1:T(8,128)S(1)}, f32[56,5]{0,1:T(8,128)}, u32[]{:S(2)}) copy-start(f32[56,5]{0,1:T(8,128)} %param.37) | copy-start | bytes 3364
  189.7 227.6 %copy-start.78 = (f32[56,5]{0,1:T(8,128)S(1)}, f32[56,5]{0,1:T(8,128)}, u32[]{:S(2)}) copy-start(f32[56,5]{0,1:T(8,128)} %param.31) | copy-start | bytes 3364
  414.3 6.8 collective-permute-start.7
  414.4 12.1 %collective-permute-start.6 = (f32[512,1792]{1,0:T(8,128)}, f32[512,1792]{1,0:T(8,128)}, u32[]{:S(2)}, u32[]{:S(2)}) collective-permute-start(f32[512,1792]{1,0:T(8,128)} %get-tuple-element.63), channel_id=1, source_target_pairs={{0,1},{1,0},{2,3},{3,2},{4,5},{5,4},{6,7},{7,6},{8,9},{9,8},{10,11... | collective-permute-start | bytes 11010056 | tf_op jit(solution)/shard_map/ppermute | solution.py:371
  418.7 101.3 %collective-permute-start.10 = (bf16[2,448,2560]{2,1,0:T(8,128)(2,1)}, bf16[2,448,2560]{2,1,0:T(8,128)(2,1)}, u32[]{:S(2)}, u32[]{:S(2)}) collective-permute-start(bf16[2,448,2560]{2,1,0:T(8,128)(2,1)} %get-tuple-element.73), channel_id=1, source_target_pairs={{0,8},{8,0},{1,9},{9,1},{2,10},{10,2},{3,11},{11,3},{4,12},{12,4},... | collective-permute-start | bytes 13762568 | tf_op jit(solution)/shard_map/ppermute | solution.py:388
  418.7 101.3 %collective-permute-start.9 = (bf16[2,448,2560]{2,1,0:T(8,128)(2,1)}, bf16[2,448,2560]{2,1,0:T(8,128)(2,1)}, u32[]{:S(2)}, u32[]{:S(2)}) collective-permute-start(bf16[2,448,2560]{2,1,0:T(8,128)(2,1)} %get-tuple-element.72), channel_id=1, source_target_pairs={{0,16},{16,0},{1,17},{17,1},{2,18},{18,2},{3,19},{19,3},{4,20},{20... | collective-permute-start | bytes 13762568 | tf_op jit(solution)/shard_map/ppermute | solution.py:388
  421.1 5.8 copy-start.34
  421.1 6.9 copy-start.42
  428.0 7.2 copy-start.44
  428.0 8.1 copy-start.46
  439.9 8.9 %collective-permute-start.8 = (bf16[512,896]{1,0:T(8,128)(2,1)S(1)}, bf16[512,896]{1,0:T(8,128)(2,1)S(1)}, u32[]{:S(2)}, u32[]{:S(2)}) collective-permute-start(bf16[512,896]{1,0:T(8,128)(2,1)S(1)} %get-tuple-element.193), channel_id=1, source_target_pairs={{0,1},{1,0},{2,3},{3,2},{4,5},{5,4},{6,7},{7,6},{8,9},{9,8},{10,11... | collective-permute-start | bytes 2752520 | tf_op jit(solution)/shard_map/ppermute | solution.py:371
  448.2 92.2 %collective-permute-start.15 = (bf16[512,896]{1,0:T(8,128)(2,1)S(1)}, bf16[512,896]{1,0:T(8,128)(2,1)}, u32[]{:S(2)}, u32[]{:S(2)}) collective-permute-start(bf16[512,896]{1,0:T(8,128)(2,1)S(1)} %get-tuple-element.185), channel_id=1, source_target_pairs={{0,1},{1,0},{2,3},{3,2},{4,5},{5,4},{6,7},{7,6},{8,9},{9,8},{10,11... | collective-permute-start | bytes 2752520 | tf_op jit(solution)/shard_map/ppermute | solution.py:371
  477.3 43.6 %copy-start.24 = (f32[2,2,258,896]{3,2,1,0:T(8,128)S(1)}, f32[2,2,258,896]{3,2,1,0:T(8,128)}, u32[]{:S(2)}) copy-start(f32[2,2,258,896]{3,2,1,0:T(8,128)} %copy-done.23) | copy-start | bytes 11096068
  520.0 9.0 %slice-start.6 = ((s8[4587520]{0:T(1024)(128)(4,1)}), s8[4194304]{0:T(1024)(128)(4,1)S(1)}, s32[]{:S(2)}) async-start(s8[4587520]{0:T(1024)(128)(4,1)} %bitcast.96), calls=%async_computation.7 | async-start | bytes 8388608
  521.0 8.0 slice-start.7
  521.0 13.7 %slice-start.4 = ((s8[4587520]{0:T(1024)(128)(4,1)}), s8[4194304]{0:T(1024)(128)(4,1)S(1)}, s32[]{:S(2)}) async-start(s8[4587520]{0:T(1024)(128)(4,1)} %bitcast.94), calls=%async_computation.5 | async-start | bytes 8388608
  524.7 22.5 %collective-permute-start.11 = (bf16[2,2,896]{2,1,0:T(2,128)(2,1)S(1)}, bf16[2,2,896]{2,1,0:T(2,128)(2,1)S(1)}, u32[]{:S(2)}, u32[]{:S(2)}) collective-permute-start(bf16[2,2,896]{2,1,0:T(2,128)(2,1)S(1)} %dynamic-slice_bitcast_fusion), channel_id=1, source_target_pairs={{2,0},{4,2},{6,4},{3,1},{5,3},{7,5},{10,8},{12,10},{14,12},{11,9},... | collective-permute-start | bytes 21512 | tf_op jit(solution)/shard_map/ppermute | solution.py:360
  526.0 8.6 %slice-start.5 = ((s8[4587520]{0:T(1024)(128)(4,1)}), s8[393216]{0:T(1024)(128)(4,1)S(1)}, s32[]{:S(2)}) async-start(s8[4587520]{0:T(1024)(128)(4,1)} %bitcast.94), calls=%async_computation.6 | async-start | bytes 786432
  526.1 51.4 %collective-permute-start.14 = (bf16[2,448,1280]{2,1,0:T(8,128)(2,1)}, bf16[2,448,1280]{2,1,0:T(8,128)(2,1)}, u32[]{:S(2)}, u32[]{:S(2)}) collective-permute-start(bf16[2,448,1280]{2,1,0:T(8,128)(2,1)} %get-tuple-element.83), channel_id=1, source_target_pairs={{0,8},{8,0},{1,9},{9,1},{2,10},{10,2},{3,11},{11,3},{4,12},{12,4},... | collective-permute-start | bytes 6881288 | tf_op jit(solution)/shard_map/ppermute | solution.py:388
  527.9 53.9 %collective-permute-start.13 = (bf16[2,448,1280]{2,1,0:T(8,128)(2,1)}, bf16[2,448,1280]{2,1,0:T(8,128)(2,1)}, u32[]{:S(2)}, u32[]{:S(2)}) collective-permute-start(bf16[2,448,1280]{2,1,0:T(8,128)(2,1)} %get-tuple-element.79), channel_id=1, source_target_pairs={{0,16},{16,0},{1,17},{17,1},{2,18},{18,2},{3,19},{19,3},{4,20},{20... | collective-permute-start | bytes 6881288 | tf_op jit(solution)/shard_map/ppermute | solution.py:388
  534.7 5.7 copy-start.41
  540.4 6.9 copy-start.33
  554.3 31.1 %collective-permute-start.12 = (f32[512,1792]{1,0:T(8,128)S(1)}, f32[512,1792]{1,0:T(8,128)S(1)}, u32[]{:S(2)}, u32[]{:S(2)}) collective-permute-start(f32[512,1792]{1,0:T(8,128)S(1)} %convolution_add_fusion), channel_id=1, source_target_pairs={{0,1},{1,0},{2,3},{3,2},{4,5},{5,4},{6,7},{7,6},{8,9},{9,8},{10,11... | collective-permute-start | bytes 11010056 | tf_op jit(solution)/shard_map/ppermute | solution.py:371
  554.5 30.8 %slice-start = ((s8[7340032]{0:T(1024)(128)(4,1)}), s8[4194304]{0:T(1024)(128)(4,1)S(1)}, s32[]{:S(2)}) async-start(s8[7340032]{0:T(1024)(128)(4,1)} %bitcast.77), calls=%async_computation.1 | async-start | bytes 8388608
  558.4 26.9 %slice-start.1 = ((s8[7340032]{0:T(1024)(128)(4,1)}), s8[3145728]{0:T(1024)(128)(4,1)S(1)}, s32[]{:S(2)}) async-start(s8[7340032]{0:T(1024)(128)(4,1)} %bitcast.77), calls=%async_computation.2 | async-start | bytes 6291456
  568.0 13.7 %copy-start.47 = (bf16[2,448,1280]{2,1,0:T(8,128)(2,1)S(1)}, bf16[2,448,1280]{2,1,0:T(8,128)(2,1)}, u32[]{:S(2)}) copy-start(bf16[2,448,1280]{2,1,0:T(8,128)(2,1)} %get-tuple-element.78) | copy-start | bytes 6881284
  585.3 6.3 copy-start.27
  585.3 6.3 copy-start.74
  593.1 197.3 %copy-start.61 = (f32[56,5]{1,0:T(8,128)S(1)}, f32[56,5]{1,0:T(8,128)}, u32[]{:S(2)}) copy-start(f32[56,5]{1,0:T(8,128)} %copy.72) | copy-start | bytes 3364
  593.1 198.0 %copy-start.60 = (f32[56,5]{1,0:T(8,128)S(1)}, f32[56,5]{1,0:T(8,128)}, u32[]{:S(2)}) copy-start(f32[56,5]{1,0:T(8,128)} %copy-done.59) | copy-start | bytes 3364
  593.1 198.0 %copy-start.62 = (f32[56,5]{1,0:T(8,128)S(1)}, f32[56,5]{1,0:T(8,128)}, u32[]{:S(2)}) copy-start(f32[56,5]{1,0:T(8,128)} %copy.71) | copy-start | bytes 3364
  593.1 198.0 %copy-start.63 = (f32[56,5]{1,0:T(8,128)S(1)}, f32[56,5]{1,0:T(8,128)}, u32[]{:S(2)}) copy-start(f32[56,5]{1,0:T(8,128)} %copy.74) | copy-start | bytes 3364
  593.1 199.3 %copy-start.1 = (f32[56,9728]{1,0:T(8,128)S(1)}, f32[56,9728]{1,0:T(8,128)}, u32[]{:S(2)}) copy-start(f32[56,9728]{1,0:T(8,128)} %gu_ref.1) | copy-start | bytes 6537220
  792.4 6.8 copy-start.5
  792.4 6.8 copy-start.40
  792.4 6.8 copy-start.50
  792.5 6.8 copy-start.51
  792.5 9.0 %copy-start.49 = (f32[56,1792]{1,0:T(8,128)S(1)}, f32[56,1792]{1,0:T(8,128)}, u32[]{:S(2)}) copy-start(f32[56,1792]{1,0:T(8,128)} %get-tuple-element.230) | copy-start | bytes 1204228
  792.5 9.0 %copy-start.55 = (f32[56,1792]{1,0:T(8,128)S(1)}, f32[56,1792]{1,0:T(8,128)}, u32[]{:S(2)}) copy-start(f32[56,1792]{1,0:T(8,128)} %param.33) | copy-start | bytes 1204228
  792.5 9.0 %copy-start.56 = (f32[56,1792]{1,0:T(8,128)S(1)}, f32[56,1792]{1,0:T(8,128)}, u32[]{:S(2)}) copy-start(f32[56,1792]{1,0:T(8,128)} %param.39) | copy-start | bytes 1204228
  792.5 10.2 %copy-start.58 = (f32[56,1792]{1,0:T(8,128)S(1)}, f32[56,1792]{1,0:T(8,128)}, u32[]{:S(2)}) copy-start(f32[56,1792]{1,0:T(8,128)} %param.40) | copy-start | bytes 1204228
  792.5 12.2 %copy-start.30 = (f32[512,1792]{1,0:T(8,128)S(1)}, f32[512,1792]{1,0:T(8,128)}, u32[]{:S(2)}) copy-start(f32[512,1792]{1,0:T(8,128)} %get-tuple-element.178) | copy-start | bytes 11010052
  799.3 5.4 copy-start.28
  799.3 5.4 copy-start.29
  (46 other events, 115.9 us)
Sparse Core Ops, SparseCore 0:
  92.7 96.9 all-gather.2
